TPU v7x, 32 devices: a whole 2x2x4 slice. The times are simulated.
32 devices in a mesh: src: 4 (over z), dst: 8 (over y, x, core).
Axes of the slice: x: 2, y: 2, z: 4, core: 2. Of those that a mesh axis runs over, the one named last changes fastest.
Arguments:
- table: float32 [65536, 400], P(('src', 'dst')), may hold values from -2 to 2
- state: float32 [65536], P(('src', 'dst')), may hold values from 0.0001 to 0.01
- relations: float32 [4096, 400], replicated, may hold values from -4 to 4
- rel_ids: int32 [65536], P(('src', 'dst')), may hold values from 0 to 4095
- block_list: int32 [32, 32], P(('src', 'dst')), may hold values from 0 to 15
- src_pos: int32 [65536], P(('src', 'dst')), may hold values from 0 to 4095, as said below
- dst_pos: int32 [65536], P(('src', 'dst')), may hold values from 0 to 4095, as said below
- neg_pos: int32 [4096], P(('src', 'dst')), may hold values from 0 to 4095, as said below
Outputs:
- new_table: float32 [65536, 400], P(('src', 'dst'))
- new_state: float32 [65536], P(('src', 'dst'))
Inputs may be any that keep to these rules, and one draw needn't show every extreme that they name: Each entry is owner * 128 + row of a block the device requested; one device's src_pos, dst_pos and neg_pos name the same 16 owners, and its src_pos names each of them. `dst_pos`: rows of the same 16 owners as the device's src_pos. `neg_pos`: rows of the same 16 owners as the device's src_pos.
All inputs are finite; a program needn't handle non-finite values.
Results may differ from a plain program's by a relative error of at most 0.0004.
The roundings to bfloat16 on the way count: a program that leaves them out, or rounds other values in their place, can miss the bound.
Values may be sent and summed in bfloat16 or wider, within the bound.
No kernel may reach another device: no remote copies, remote signals or barrier semaphores. Data moves between devices by JAX's collectives and lax.ppermute only.
A program may use at most 192 MiB of HBM per device.

v0:
```python
import jax
import jax.numpy as jnp
from jax import lax
from jax.sharding import PartitionSpec as P

BLK = 128


def per_device(table, state, relations, rel_ids, block_list, src_pos, dst_pos, neg_pos):
    devices = lax.axis_size(("src", "dst"))
    rows_dev, width = table.shape
    blocks = rows_dev // BLK
    wanted = lax.all_to_all(
        block_list.reshape(devices, 1), ("src", "dst"), split_axis=0, concat_axis=0, tiled=True
    )
    asked = wanted.reshape(devices)
    outgoing = table.reshape(blocks, BLK, width).astype(jnp.bfloat16)[asked]
    fetched = lax.all_to_all(outgoing, ("src", "dst"), split_axis=0, concat_axis=0, tiled=True)
    flat = fetched.reshape(devices * BLK, width)
    source = flat[src_pos].astype(jnp.float32)
    target = flat[dst_pos].astype(jnp.float32)
    own_negs = flat[neg_pos]
    negs = lax.all_gather(own_negs, "dst", axis=0, tiled=True)
    operator = relations[rel_ids]
    u_full = source * operator
    u_half = u_full.astype(jnp.bfloat16)
    positive = jnp.sum(u_full * target, axis=1)
    scores = jnp.dot(u_half, negs.T, preferred_element_type=jnp.float32)
    g_pos = -jax.nn.sigmoid(-positive)
    g_neg = (jax.nn.sigmoid(scores) / negs.shape[0]).astype(jnp.bfloat16)
    grad_u = g_pos[:, None] * target + jnp.dot(g_neg, negs, preferred_element_type=jnp.float32)
    grad_src = grad_u * operator
    grad_dst = g_pos[:, None] * u_full
    own_neg_grad = lax.psum_scatter(
        jnp.dot(g_neg.T, u_half, preferred_element_type=jnp.float32).astype(jnp.bfloat16),
        "dst",
        scatter_dimension=0,
        tiled=True,
    ).astype(jnp.float32)
    slots = jnp.zeros((devices * BLK, width), jnp.float32)
    slots = slots.at[src_pos].add(grad_src).at[dst_pos].add(grad_dst).at[neg_pos].add(own_neg_grad)
    returned = lax.all_to_all(
        slots.reshape(devices, BLK, width), ("src", "dst"), split_axis=0, concat_axis=0, tiled=True
    )
    selector = (asked[None, :] == jnp.arange(blocks, dtype=jnp.int32)[:, None]).astype(jnp.float32)
    grad = jnp.einsum("bq,qrw->brw", selector, returned, precision=lax.Precision.HIGHEST).reshape(
        rows_dev, width
    )
    new_state = state + jnp.mean(grad * grad, axis=1)
    new_table = table - 0.1 * grad / (jnp.sqrt(new_state)[:, None] + 1e-10)
    return (new_table, new_state)


def solution(mesh):
    in_specs = (
        P(("src", "dst"), None),
        P(("src", "dst")),
        P(),
        P(("src", "dst")),
        P(("src", "dst"), None),
        P(("src", "dst")),
        P(("src", "dst")),
        P(("src", "dst")),
    )
    out_specs = (P(("src", "dst"), None), P(("src", "dst")))
    return jax.shard_map(
        per_device, mesh=mesh, in_specs=in_specs, out_specs=out_specs, check_vma=False
    )
```

profile of v0, /device:TPU:0, one launch (start us, length us, event | category | flops | bytes accessed | tf_op | source)
XLA Modules:
  0.0 411.0 jit_solution(8003938198328237329)
XLA Ops:
  7.2 1.3 copy.54
  8.5 7.3 %all-to-all-start = ((s32[32,1,1]{2,1,0:T(1,128)}), s32[32,1,1]{2,1,0:T(1,128)S(1)}, u32[]{:S(2)}, u32[]{:S(2)}) async-start(s32[32,1,1]{2,1,0:T(1,128)} %copy.54), calls=%async_computation | async-start | bytes 32768 | tf_op jit(solution)/shard_map/all_to_all | solution.py:13
  15.8 2.1 copy_bitcast_fusion
  18.0 4.9 %all-to-all-done = s32[32,1,1]{2,1,0:T(1,128)S(1)} async-done(((s32[32,1,1]{2,1,0:T(1,128)}), s32[32,1,1]{2,1,0:T(1,128)S(1)}, u32[]{:S(2)}, u32[]{:S(2)}) %all-to-all-start) | async-done | bytes 160 | tf_op jit(solution)/shard_map/all_to_all | solution.py:13
  22.9 0.7 reduce.1
  23.6 2.7 gather_fusion
  26.2 3.5 all-to-all-start.1
  29.8 0.0 copy-start.6
  29.8 0.0 reduce-scatter.4.cloned.1.call-start
  29.9 8.5 %copy.59 = f32[4096,400]{1,0:T(8,128)} copy(f32[4096,400]{0,1:T(8,128)} %param.10) | data formatting | bytes 13107200 | tf_op args[2]
  38.4 0.0 copy-done.6
  38.4 12.9 %gather_fusion.2 = f32[2048,400]{1,0:T(8,128)} fusion(f32[4096,400]{1,0:T(8,128)} %copy.59, s32[2048]{0:T(1024)S(1)} %fusion.9), kind=kCustom, calls=%fused_computation.2 | custom fusion | bytes 6561792 | tf_op jit(solution)/shard_map/gather | solution.py:24
  51.3 0.0 copy-start.8
  51.3 0.0 copy-start.4
  51.3 0.0 copy-start.5
  51.4 3.8 copy.60
  55.1 0.0 copy-done.8
  55.1 0.0 copy-done.4
  55.2 0.0 copy-done.5
  55.2 48.9 %all-to-all-done.1 = bf16[32,128,400]{1,2,0:T(8,128)(2,1)} async-done(((bf16[32,128,400]{1,2,0:T(8,128)(2,1)}), bf16[32,128,400]{1,2,0:T(8,128)(2,1)}, u32[]{:S(2)}, u32[]{:S(2)}) %all-to-all-start.1) | async-done | bytes 3276832 | tf_op jit(solution)/shard_map/all_to_all | solution.py:18
  104.1 6.0 %copy.72 = bf16[32,128,400]{2,1,0:T(8,128)(2,1)} copy(bf16[32,128,400]{1,2,0:T(8,128)(2,1)} %all-to-all-done.1) | data formatting | bytes 6553600 | tf_op jit(solution)/shard_map/reshape | solution.py:19
  110.1 3.6 gather_fusion.4
  113.7 11.9 %all-gather = bf16[1024,400]{1,0:T(8,128)(2,1)} all-gather(bf16[128,400]{1,0:T(8,128)(2,1)S(1)} %gather_fusion.4), channel_id=2, replica_groups=mesh['src'=4,'dst'=8] {'dst'}, dimensions={0}, use_global_device_ids=true | all-gather | bytes 921600 | tf_op jit(solution)/shard_map/all_gather | solution.py:23
  125.6 12.0 %gather_fusion.3 = bf16[2048,400]{1,0:T(8,128)(2,1)} fusion(bf16[4096,400]{1,0:T(8,128)(2,1)} %bitcast.33, s32[2048]{0:T(1024)S(1)} %get-tuple-element.7), kind=kCustom, calls=%fused_computation.3 | custom fusion | bytes 3284992 | tf_op jit(solution)/shard_map/gather | solution.py:21
  137.6 12.0 %gather_fusion.1 = bf16[2048,400]{1,0:T(8,128)(2,1)} fusion(bf16[4096,400]{1,0:T(8,128)(2,1)} %bitcast.34, s32[2048]{0:T(1024)S(1)} %get-tuple-element.8), kind=kCustom, calls=%fused_computation.1 | custom fusion | bytes 3284992 | tf_op jit(solution)/shard_map/gather | solution.py:20
  149.5 3.9 copy.58
  153.4 3.8 copy.62
  157.2 0.0 copy-start
  157.3 0.0 copy-start.3
  157.3 2.8 fusion.4
  160.0 0.0 copy-done
  160.0 0.0 copy-done.3
  160.0 4.1 %multiply_convert_fusion = bf16[2048,1024]{1,0:T(8,128)(2,1)S(1)} fusion(bf16[1024,400]{1,0:T(8,128)(2,1)S(1)} %copy-done.3, f32[2048,400]{0,1:T(8,128)S(1)} %copy.60, bf16[2048,400]{0,1:T(8,128)(2,1)S(1)} %copy-done), kind=kOutput, calls=%fused_computation.8 | convolution fusion | flops 1690664960 | bytes 9928704 | tf_op jit(solution)/shard_map/dot_general | solution.py:28
  164.2 0.0 copy-start.1
  164.2 1.9 copy-done.1
  166.1 2.9 convolution_convert_fusion
  169.0 2.2 copy.70
  171.2 0.0 reduce-scatter.4.cloned.1.call-update
  171.2 3.6 broadcast_multiply_fusion.1
  174.8 5.1 %copy.66 = f32[2048,400]{1,0:T(8,128)} copy(f32[2048,400]{0,1:T(8,128)} %broadcast_multiply_fusion.1) | data formatting | bytes 6553600 | tf_op jit(solution)/shard_map/mul | solution.py:33
  179.9 6.9 %fusion.6 = f32[2048,400]{0,1:T(8,128)} fusion(f32[2048,400]{0,1:T(8,128)S(1)} %copy.60, bf16[2048,400]{0,1:T(8,128)(2,1)} %copy.62, bf16[2048,1024]{1,0:T(8,128)(2,1)} %copy-done.1, bf16[1024,400]{1,0:T(8,128)(2,1)} %all-gather, f32[2048]{0:T(1024)S(1)} %divide_negate_fusion), kind=kOutput, calls=%fused_computation.17 | convolution fusion | flops 1680998400 | bytes 13213696 | tf_op jit(solution)/shard_map/dot_general | solution.py:31
  186.9 5.0 %copy.65 = f32[2048,400]{1,0:T(8,128)} copy(f32[2048,400]{0,1:T(8,128)} %fusion.6) | data formatting | bytes 6553600 | tf_op jit(solution)/shard_map/mul | solution.py:32
  191.9 17.2 %scatter_custom_fusion = f32[4096,400]{1,0:T(8,128)} fusion(s32[2048]{0:T(1024)S(1)} %get-tuple-element.9, f32[2048,400]{1,0:T(8,128)} %copy.65, f32[]{:T(128)} %constant.9.clone.1), kind=kCustom, calls=%fused_computation.11 | custom fusion | flops 819200 | bytes 6554112 | tf_op jit(solution)/shard_map/scatter-add | solution.py:41
  209.0 19.8 %scatter_fusion = f32[4096,400]{1,0:T(8,128)} fusion(f32[4096,400]{1,0:T(8,128)} %scatter_custom_fusion, s32[2048]{0:T(1024)S(1)} %get-tuple-element.6, f32[2048,400]{1,0:T(8,128)} %copy.66), kind=kCustom, calls=%fused_computation.6 | custom fusion | flops 819200 | bytes 9838592 | tf_op jit(solution)/shard_map/scatter-add | solution.py:41
  228.8 0.0 reduce-scatter.4.cloned.1.call-done
  228.8 1.0 copy.71
  229.8 0.1 copy.67
  230.0 7.9 %scatter_fusion.1 = f32[4096,400]{1,0:T(8,128)} fusion(f32[4096,400]{1,0:T(8,128)} %scatter_fusion, s32[128]{0:T(128)S(1)} %compare_select_fusion.3, f32[128,400]{1,0:T(8,128)S(1)} %copy.67), kind=kCustom, calls=%fused_computation.7 | custom fusion | flops 51200 | bytes 614912 | tf_op jit(solution)/shard_map/scatter-add | solution.py:41
  237.8 8.7 %copy.68 = f32[32,128,400]{1,2,0:T(8,128)} copy(f32[32,128,400]{2,1,0:T(8,128)} %bitcast.35) | data formatting | bytes 13107200 | tf_op jit(solution)/shard_map/reshape | solution.py:43
  246.5 149.1 %all_to_all.22 = f32[32,128,400]{1,2,0:T(8,128)S(1)} all-to-all(f32[32,128,400]{1,2,0:T(8,128)} %copy.68), channel_id=1, replica_groups=mesh['src'=4,'dst'=8] {'src','dst'}, dimensions={0} | all-to-all | bytes 13107200 | tf_op jit(solution)/shard_map/all_to_all | solution.py:42
  395.6 0.0 copy-start.7
  395.6 0.0 copy-start.2
  395.6 4.5 %multiply_reduce_fusion = (f32[16,128]{1,0:T(8,128)S(1)}, f32[16,128,400]{1,0,2:T(8,128)S(1)}) fusion(f32[32,128,400]{1,2,0:T(8,128)S(1)} %all_to_all.22, s32[32]{0:T(128)S(1)} %reduce.1), kind=kOutput, calls=%fused_computation.20 | convolution fusion | flops 317028864 | bytes 9838720 | tf_op jit(solution)/shard_map/bq,qrw->brw/dot_general | solution.py:46
  400.1 0.0 copy-done.7
  400.1 0.6 sqrt_add_fusion
  400.7 0.0 copy-done.2
  400.7 3.5 fusion.7
  (8 shorter events, 0.1 us)
Async XLA Ops:
  8.5 14.4 %all-to-all-start = ((s32[32,1,1]{2,1,0:T(1,128)}), s32[32,1,1]{2,1,0:T(1,128)S(1)}, u32[]{:S(2)}, u32[]{:S(2)}) async-start(s32[32,1,1]{2,1,0:T(1,128)} %copy.54), calls=%async_computation | async-start | bytes 32768 | tf_op jit(solution)/shard_map/all_to_all | solution.py:13
  26.2 77.8 %all-to-all-start.1 = ((bf16[32,128,400]{1,2,0:T(8,128)(2,1)}), bf16[32,128,400]{1,2,0:T(8,128)(2,1)}, u32[]{:S(2)}, u32[]{:S(2)}) async-start(bf16[32,128,400]{1,2,0:T(8,128)(2,1)} %gather_fusion), calls=%async_computation.1 | async-start | bytes 6553600 | tf_op jit(solution)/shard_map/all_to_all | solution.py:18
  29.8 8.6 %copy-start.6 = (s32[2048]{0:T(1024)S(1)}, s32[2048]{0:T(1024)}, u32[]{:S(2)}) copy-start(s32[2048]{0:T(1024)} %param.11) | copy-start | bytes 24580
  29.8 199.0 %reduce-scatter.4.cloned.1.call-start = ((), (), s32[]{:S(2)}) async-start(), calls=%async_computation.4 | async-start | bytes 1179648
  51.3 3.8 copy-start.8
  51.3 3.8 copy-start.4
  51.3 3.8 copy-start.5
  157.2 2.8 copy-start
  157.3 2.8 copy-start.3
  164.2 1.9 copy-start.1
  395.6 4.5 %copy-start.7 = (f32[2048]{0:T(1024)S(1)}, f32[2048]{0:T(1024)}, u32[]{:S(2)}) copy-start(f32[2048]{0:T(1024)} %param.9) | copy-start | bytes 24580
  395.6 5.1 %copy-start.2 = (f32[2048,400]{0,1:T(8,128)S(1)}, f32[2048,400]{0,1:T(8,128)}, u32[]{:S(2)}) copy-start(f32[2048,400]{0,1:T(8,128)} %param.8) | copy-start | bytes 9830404
Sparse Core Ops, SparseCore 0:
  171.4 34.9 reduce-scatter.3
where the time goes:
time: 412 us; the launch traced here: 411 us
  blocking collectives  161 us (39%)
  local copies, waits for them, and re-layouts  94.6 us (23%)
  other arithmetic  58.1 us (14%)
  waiting for transfers between devices  53.8 us (13%)
  matrix products  18.4 us (4%)
  between operations  14.2 us (3%)
  starting transfers between devices  10.9 us (3%)
    all_to_all x1, blocking collectives, per_device(): lax.all_to_all(slots.reshape(devices, BLK, width), ('src', 'dst'), split_...  149 us
    all_to_all x1, waiting for transfers between devices, per_device(): lax.all_to_all(outgoing, ('src', 'dst'), split_axis=0, concat_axis=0, til...  48.9 us
    scatter-add x3, other arithmetic, per_device(): slots.at[src_pos].add(grad_src).at[dst_pos].add(grad_dst).at[neg_pos]  44.8 us
    gather x2, local copies, waits for them, and re-layouts, per_device(): operator = relations[rel_ids]  16.7 us
    gather x2, local copies, waits for them, and re-layouts, per_device(): source = flat[src_pos].astype(jnp.float32)  15.8 us
    gather x2, local copies, waits for them, and re-layouts, per_device(): target = flat[dst_pos].astype(jnp.float32)  15.8 us
    unnamed x21, local copies, waits for them, and re-layouts  13.7 us
    all_gather x1, blocking collectives, per_device(): negs = lax.all_gather(own_negs, 'dst', axis=0, tiled=True)  11.9 us
  transfers between devices with their start and end apart: 3, of which 2 were waited for; matrix products, arithmetic and copies ran while one was open for 21% of the time, Pallas kernels for 0%

commit v1 on v0

v1 whole, which is shorter than its diff:
```python
import jax
import jax.numpy as jnp
from jax import lax
from jax.experimental import pallas as pl
from jax.experimental.pallas import tpu as pltpu
from jax.sharding import PartitionSpec as P

BLK = 128
TAIL = 8
AXES = ("src", "dst")
VMEM_LIMIT = 40 * 1024 * 1024
F32 = jnp.float32
BF16 = jnp.bfloat16
NT = (((1,), (1,)), ((), ()))


def params():
    return pltpu.CompilerParams(vmem_limit_bytes=VMEM_LIMIT)


def whole():
    return pl.BlockSpec(memory_space=pltpu.VMEM)


def smem():
    return pl.BlockSpec(memory_space=pltpu.SMEM)


def anywhere():
    return pl.BlockSpec(memory_space=pl.ANY)


def load_live(live_ref, fetched, rows, sem):
    count = live_ref.shape[0]

    def copy(k):
        lanes = pl.ds(pl.multiple_of(k * BLK, BLK), BLK)
        return pltpu.make_async_copy(fetched.at[live_ref[k]], rows.at[:, lanes], sem)

    def start(k, _):
        copy(k).start()
        return 0

    def wait(k, _):
        copy(k).wait()
        return 0

    lax.fori_loop(0, count, start, 0)
    lax.fori_loop(0, count, wait, 0)


def pick(rows, positions):
    total = rows.shape[1]
    step = min(total, 2048)
    out = None
    for first in range(0, total, step):
        index = lax.broadcasted_iota(jnp.int32, (step, positions.shape[1]), 0) + first
        hot = jnp.where(index == positions, 1.0, 0.0).astype(BF16)
        part = jnp.dot(rows[:, first : first + step], hot, preferred_element_type=F32)
        out = part if out is None else out + part
    return out


def neg_kernel(live_ref, fetched, pos_ref, out_ref, rows, sem):
    load_live(live_ref, fetched, rows, sem)
    out_ref[...] = pick(rows, pos_ref[...]).astype(BF16)


def gather_negs(live, fetched, pos):
    width = fetched.shape[1]
    return pl.pallas_call(
        neg_kernel,
        out_shape=jax.ShapeDtypeStruct((width, pos.shape[1]), BF16),
        in_specs=[smem(), anywhere(), whole()],
        out_specs=whole(),
        scratch_shapes=[
            pltpu.VMEM((width, live.shape[0] * BLK), BF16),
            pltpu.SemaphoreType.DMA,
        ],
        compiler_params=params(),
        name="gather_negs",
    )(live, fetched, pos)


def edge_kernel(live_ref, fetched, spos, dpos, op_ref, src_ref, dst_ref, gpos_ref, rows, sem):
    @pl.when(pl.program_id(0) == 0)
    def _():
        load_live(live_ref, fetched, rows, sem)

    source = pick(rows, spos[...])
    target = pick(rows, dpos[...])
    u = source * op_ref[...]
    positive = jnp.sum(u * target, axis=0, keepdims=True)
    gpos_ref[...] = -jax.nn.sigmoid(-positive)
    src_ref[...] = source.astype(BF16)
    dst_ref[...] = target.astype(BF16)


def gather_edges(live, fetched, spos, dpos, operator, tile=256):
    width = fetched.shape[1]
    edges = spos.shape[1]
    lane = pl.BlockSpec((1, tile), lambda i: (0, i))
    column = pl.BlockSpec((width, tile), lambda i: (0, i))
    return pl.pallas_call(
        edge_kernel,
        grid=(edges // tile,),
        out_shape=(
            jax.ShapeDtypeStruct((width, edges), BF16),
            jax.ShapeDtypeStruct((width, edges), BF16),
            jax.ShapeDtypeStruct((1, edges), F32),
        ),
        in_specs=[smem(), anywhere(), lane, lane, column],
        out_specs=(column, column, lane),
        scratch_shapes=[
            pltpu.VMEM((width, live.shape[0] * BLK), BF16),
            pltpu.SemaphoreType.DMA,
        ],
        compiler_params=params(),
        name="gather_edges",
    )(live, fetched, spos, dpos, operator)


def split(x):
    high = x.astype(BF16)
    return high, (x - high.astype(F32)).astype(BF16)


def score_kernel(negs_ref, src_ref, dst_ref, op_ref, gpos_ref, gs_ref, gd_ref, gn_ref, wide, tall, acc):
    groups, width, _ = negs_ref.shape
    step = pl.program_id(0)
    count = groups * negs_ref.shape[2]
    each = negs_ref.shape[2]

    @pl.when(step == 0)
    def _():
        for g in range(groups):
            block = negs_ref[g]
            wide[:, g * each : (g + 1) * each] = block
            tall[g * each : (g + 1) * each, :] = block.T
        acc[...] = jnp.zeros_like(acc)

    operator = op_ref[...]
    u = src_ref[...].astype(F32) * operator
    u_half = u.astype(BF16)
    scores = jnp.dot(tall[...], u_half, preferred_element_type=F32)
    g_neg = (jax.nn.sigmoid(scores) / count).astype(BF16)
    g_pos = gpos_ref[...]
    grad_u = g_pos * dst_ref[...].astype(F32) + jnp.dot(wide[...], g_neg, preferred_element_type=F32)
    acc[...] += lax.dot_general(u_half, g_neg, NT, preferred_element_type=F32)
    gs_ref[0], gs_ref[1] = split(grad_u * operator)
    gd_ref[0], gd_ref[1] = split(g_pos * u)

    @pl.when(step == pl.num_programs(0) - 1)
    def _():
        for g in range(groups):
            gn_ref[g] = acc[:, g * each : (g + 1) * each].astype(BF16)


def score(negs, source, target, operator, g_pos, tile=256):
    groups, width, each = negs.shape
    edges = source.shape[1]
    lane = pl.BlockSpec((1, tile), lambda i: (0, i))
    column = pl.BlockSpec((width, tile), lambda i: (0, i))
    pair = pl.BlockSpec((2, width, tile), lambda i: (0, 0, i))
    return pl.pallas_call(
        score_kernel,
        grid=(edges // tile,),
        out_shape=(
            jax.ShapeDtypeStruct((2, width, edges), BF16),
            jax.ShapeDtypeStruct((2, width, edges), BF16),
            jax.ShapeDtypeStruct((groups, width, each), BF16),
        ),
        in_specs=[whole(), column, column, column, lane],
        out_specs=(pair, pair, pl.BlockSpec((groups, width, each), lambda i: (0, 0, 0))),
        scratch_shapes=[
            pltpu.VMEM((width, groups * each), BF16),
            pltpu.VMEM((groups * each, width), BF16),
            pltpu.VMEM((width, groups * each), F32),
        ],
        compiler_params=params(),
        name="score",
    )(negs, source, target, operator, g_pos)


def scatter_kernel(gs_ref, gd_ref, spos, dpos, out_ref):
    tile = out_ref.shape[1]
    width = gs_ref.shape[1]
    edges = gs_ref.shape[2]
    index = lax.broadcasted_iota(jnp.int32, (tile, edges), 0) + pl.program_id(0) * tile
    both = None
    for grads, pos in ((gs_ref, spos), (gd_ref, dpos)):
        hot = jnp.where(index == pos[...], 1.0, 0.0).astype(BF16)
        part = lax.dot_general(
            grads[...].reshape(2 * width, edges), hot, NT, preferred_element_type=F32
        )
        both = part if both is None else both + part
    out_ref[...] = both[:width] + both[width:]


def scatter(grads_src, grads_dst, spos, dpos, rows, tile=256):
    width = grads_src.shape[1]
    return pl.pallas_call(
        scatter_kernel,
        grid=(rows // tile,),
        out_shape=jax.ShapeDtypeStruct((width, rows), F32),
        in_specs=[whole(), whole(), whole(), whole()],
        out_specs=pl.BlockSpec((width, tile), lambda i: (0, i)),
        compiler_params=params(),
        name="scatter",
    )(grads_src, grads_dst, spos, dpos)


def encode(x, out_ref):
    width = x.shape[0]
    top = jnp.max(jnp.abs(x), axis=0, keepdims=True)
    power = jnp.ceil(jnp.log2(jnp.maximum(top, 1e-30)))
    code = jnp.clip(jnp.round(x * jnp.exp2(15.0 - power)), -32767.0, 32767.0)
    out_ref[:width, :] = code.astype(jnp.int32).astype(jnp.int16)
    tail = jnp.broadcast_to(power, (TAIL, x.shape[1]))
    out_ref[width:, :] = tail.astype(jnp.int32).astype(jnp.int16)


def decode(code, width):
    power = code[width : width + 1, :].astype(jnp.int32).astype(F32)
    return code[:width, :].astype(jnp.int32).astype(F32) * jnp.exp2(power - 15.0)


def pack_kernel(rank_ref, live_ref, slots_ref, gn_ref, npos, out_ref):
    group = out_ref.shape[0]
    first = pl.program_id(0) * group
    for k in range(group):
        alive = live_ref[first + k] > 0

        @pl.when(alive)
        def _():
            start = pl.multiple_of(rank_ref[first + k] * BLK, BLK)
            index = lax.broadcasted_iota(jnp.int32, (BLK, npos.shape[1]), 0) + start
            hot = jnp.where(index == npos[...], 1.0, 0.0).astype(BF16)
            part = lax.dot_general(gn_ref[...], hot, NT, preferred_element_type=F32)
            encode(slots_ref[:, pl.ds(start, BLK)] + part, out_ref.at[k])

        @pl.when(jnp.logical_not(alive))
        def _():
            out_ref[k] = jnp.zeros(out_ref.shape[1:], jnp.int16)


def pack(rank, live, slots, grad_negs, npos, group=8):
    devices = rank.shape[0]
    width = slots.shape[0]
    return pl.pallas_call(
        pack_kernel,
        grid=(devices // group,),
        out_shape=jax.ShapeDtypeStruct((devices, width + TAIL, BLK), jnp.int16),
        in_specs=[smem(), smem(), whole(), whole(), whole()],
        out_specs=pl.BlockSpec((group, width + TAIL, BLK), lambda i: (i, 0, 0)),
        compiler_params=params(),
        name="pack",
    )(rank, live, slots, grad_negs, npos)


def update_kernel(asked_ref, back_ref, table_ref, state_ref, table_out, state_out, grad):
    group = back_ref.shape[0]
    width = grad.shape[0]
    step = pl.program_id(0)

    @pl.when(step == 0)
    def _():
        grad[...] = jnp.zeros_like(grad)

    for k in range(group):
        lanes = pl.ds(pl.multiple_of(asked_ref[step * group + k] * BLK, BLK), BLK)
        grad[:, lanes] += decode(back_ref[k], width)

    @pl.when(step == pl.num_programs(0) - 1)
    def _():
        def block(b, _):
            lanes = pl.ds(pl.multiple_of(b * BLK, BLK), BLK)
            g = grad[:, lanes]
            new_state = state_ref[:, lanes] + jnp.sum(g * g, axis=0, keepdims=True) / width
            state_out[:, lanes] = new_state
            table_out[:, lanes] = table_ref[:, lanes] - 0.1 * g / (jnp.sqrt(new_state) + 1e-10)
            return 0

        lax.fori_loop(0, grad.shape[1] // BLK, block, 0)


def update(asked, returned, table, state, group=8):
    devices, coded, _ = returned.shape
    width, rows = table.shape
    return pl.pallas_call(
        update_kernel,
        grid=(devices // group,),
        out_shape=(
            jax.ShapeDtypeStruct((width, rows), F32),
            jax.ShapeDtypeStruct((1, rows), F32),
        ),
        in_specs=[
            smem(),
            pl.BlockSpec((group, coded, BLK), lambda i: (i, 0, 0)),
            pl.BlockSpec((width, rows), lambda i: (0, 0)),
            pl.BlockSpec((1, rows), lambda i: (0, 0)),
        ],
        out_specs=(
            pl.BlockSpec((width, rows), lambda i: (0, 0)),
            pl.BlockSpec((1, rows), lambda i: (0, 0)),
        ),
        scratch_shapes=[pltpu.VMEM((width, rows), F32)],
        compiler_params=params(),
        name="update",
    )(asked, returned, table, state)


def per_device(table, state, relations, rel_ids, block_list, src_pos, dst_pos, neg_pos):
    devices = lax.axis_size(AXES)
    named = devices // 2
    rows_dev, width = table.shape
    blocks = rows_dev // BLK
    wanted = lax.all_to_all(
        block_list.reshape(devices, 1), AXES, split_axis=0, concat_axis=0, tiled=True
    )
    asked = wanted.reshape(devices)
    outgoing = table.reshape(blocks, BLK, width).astype(BF16)[asked]
    fetched = lax.all_to_all(
        outgoing.transpose(0, 2, 1), AXES, split_axis=0, concat_axis=0, tiled=True
    )
    operator = relations[rel_ids].T

    ids = jnp.arange(devices, dtype=jnp.int32)
    alive = jnp.max((src_pos // BLK)[:, None] == ids[None, :], axis=0).astype(jnp.int32)
    rank = jnp.sum(jnp.where(ids[None, :] < ids[:, None], alive[None, :], 0), axis=1)
    slot = jnp.arange(named, dtype=jnp.int32)
    live = jnp.sum(
        jnp.where((rank[None, :] == slot[:, None]) & (alive[None, :] > 0), ids[None, :], 0), axis=1
    )

    def compact(pos):
        place = jnp.sum(jnp.where((pos // BLK)[:, None] == ids[None, :], rank[None, :], 0), axis=1)
        return (place * BLK + pos % BLK).reshape(1, -1)

    spos, dpos, npos = compact(src_pos), compact(dst_pos), compact(neg_pos)

    own_negs = gather_negs(live, fetched, npos)
    negs = lax.all_gather(own_negs, "dst", axis=0, tiled=False)
    source, target, g_pos = gather_edges(live, fetched, spos, dpos, operator)
    grads_src, grads_dst, part_negs = score(negs, source, target, operator, g_pos)
    own_grad = lax.psum_scatter(part_negs, "dst", scatter_dimension=0, tiled=False)
    slots = scatter(grads_src, grads_dst, spos, dpos, named * BLK)
    packed = pack(rank, alive, slots, own_grad, npos)
    returned = lax.all_to_all(packed, AXES, split_axis=0, concat_axis=0, tiled=True)
    new_table, new_state = update(asked, returned, table.T, state.reshape(1, rows_dev))
    return (new_table.T, new_state.reshape(rows_dev))


def solution(mesh):
    in_specs = (
        P(AXES, None),
        P(AXES),
        P(),
        P(AXES),
        P(AXES, None),
        P(AXES),
        P(AXES),
        P(AXES),
    )
    out_specs = (P(AXES, None), P(AXES))
    return jax.shard_map(
        per_device, mesh=mesh, in_specs=in_specs, out_specs=out_specs, check_vma=False
    )
```

time: 412 us -> 279 us (0.68)
  blocking collectives: 161 us -> 91.5 us
  local copies, waits for them, and re-layouts: 94.6 us -> 38.9 us
  other arithmetic: 58.1 us -> 3.49 us
  Pallas kernels: 0 us -> 54 us
  matrix products: 18.4 us -> 0 us
  waiting for transfers between devices: 53.8 us -> 65.9 us
    all_to_all x1, blocking collectives: 149 us -> 81.3 us  [per_device(): lax.all_to_all(packed, AXES, split_axis=0, concat_axis=0, tiled=True)]
    pallas_call x0 -> x6, Pallas kernels: none -> 54 us  [the longest x1 15.3 us: scatter(): pl.pallas_call(scatter_kernel, grid=(rows // tile,), out_shape=jax.ShapeD...]
    scatter-add x3 -> x0, other arithmetic: 44.8 us -> none  [per_device(): slots.at[src_pos].add(grad_src).at[dst_pos].add(grad_dst).at[neg_pos]]
    gather x8 -> x3, local copies, waits for them, and re-layouts: 54.6 us -> 20.9 us  [the longest x2 18.2 us: per_device(): operator = relations[rel_ids].T]
    dot_general x4 -> x0, matrix products: 18.4 us -> none  [the longest x1 6.95 us: per_device(): jnp.dot(g_neg, negs, preferred_element_type=jnp.float32)]
    reshape x2 -> x0, local copies, waits for them, and re-layouts: 14.7 us -> none  [the longest x1 8.67 us: per_device(): slots.reshape(devices, BLK, width)]
    reduce_scatter x0 -> x1, waiting for transfers between devices: none -> 14.2 us  [per_device(): lax.psum_scatter(part_negs, 'dst', scatter_dimension=0, tiled=False)]
    mul x2 -> x0, local copies, waits for them, and re-layouts: 10.1 us -> none  [the longest x1 5.07 us: per_device(): grad_dst = g_pos[:, None] * u_full]
  transfers between devices with their start and end apart: 3 -> 3, of which waited for: 2 -> 3; matrix products, arithmetic and copies ran while one was open for 21% -> 11% of each run, Pallas kernels for 0% -> 5%
where the time goes in v1:
time: 279 us; the launch traced here: 278 us
  blocking collectives  91.5 us (33%)
  waiting for transfers between devices  65.9 us (24%)
  Pallas kernels  54 us (19%)
  local copies, waits for them, and re-layouts  38.9 us (14%)
  between operations  14.2 us (5%)
  starting transfers between devices  10.1 us (4%)
  other arithmetic  3.49 us (1%)
    all_to_all x1, blocking collectives, per_device(): lax.all_to_all(packed, AXES, split_axis=0, concat_axis=0, tiled=True)  81.3 us
    all_to_all x1, waiting for transfers between devices, per_device(): lax.all_to_all(outgoing.transpose(0, 2, 1), AXES, split_axis=0, concat_ax...  46.8 us
    gather x2, local copies, waits for them, and re-layouts, per_device(): operator = relations[rel_ids].T  18.2 us
    unnamed x25, local copies, waits for them, and re-layouts  16.7 us
    pallas_call x1, Pallas kernels, scatter(): pl.pallas_call(scatter_kernel, grid=(rows // tile,), out_shape=jax.ShapeD...  15.3 us
    pallas_call x1, Pallas kernels, score(): pl.pallas_call(score_kernel, grid=(edges // tile,), out_shape=(jax.ShapeD...  14.6 us
    reduce_scatter x1, waiting for transfers between devices, per_device(): lax.psum_scatter(part_negs, 'dst', scatter_dimension=0, tiled=False)  14.2 us
    pallas_call x1, Pallas kernels, gather_edges(): pl.pallas_call(edge_kernel, grid=(edges // tile,), out_shape=(jax.ShapeDt...  10.3 us
  transfers between devices with their start and end apart: 3, of which 3 were waited for; matrix products, arithmetic and copies ran while one was open for 11% of the time, Pallas kernels for 5%

profile of v1, /device:TPU:0, one launch (start us, length us, event | category | flops | bytes accessed | tf_op | source)
XLA Modules:
  0.0 278.1 jit_solution(9741507052971854001)
XLA Ops:
  7.2 1.3 copy.25
  8.5 7.3 %all-to-all-start = ((s32[32,1,1]{2,1,0:T(1,128)}), s32[32,1,1]{2,1,0:T(1,128)S(1)}, u32[]{:S(2)}, u32[]{:S(2)}) async-start(s32[32,1,1]{2,1,0:T(1,128)} %copy.25), calls=%async_computation | async-start | bytes 32768 | tf_op jit(solution)/shard_map/all_to_all | solution.py:318
  15.8 2.1 copy_bitcast_fusion
  18.0 4.9 %all-to-all-done = s32[32,1,1]{2,1,0:T(1,128)S(1)} async-done(((s32[32,1,1]{2,1,0:T(1,128)}), s32[32,1,1]{2,1,0:T(1,128)S(1)}, u32[]{:S(2)}, u32[]{:S(2)}) %all-to-all-start) | async-done | bytes 160 | tf_op jit(solution)/shard_map/all_to_all | solution.py:318
  22.9 0.7 reduce.asked_ref
  23.6 2.7 gather_fusion
  26.2 2.8 %all-to-all-start.1 = ((bf16[32,400,128]{2,1,0:T(8,128)(2,1)}), bf16[32,400,128]{2,1,0:T(8,128)(2,1)S(1)}, u32[]{:S(2)}, u32[]{:S(2)}) async-start(bf16[32,400,128]{2,1,0:T(8,128)(2,1)} %bitcast.32), calls=%async_computation.1 | async-start | bytes 6553600 | tf_op jit(solution)/shard_map/all_to_all | solution.py:323
  29.0 0.0 copy-start.10
  29.0 0.0 reduce-scatter.2.cloned.1.call-start
  29.1 8.5 %copy.27 = f32[4096,400]{1,0:T(8,128)} copy(f32[4096,400]{0,1:T(8,128)} %param.10) | data formatting | bytes 13107200 | tf_op args[2]
  37.6 0.0 copy-done.10
  37.6 13.0 %gather_fusion.1 = f32[2048,400]{1,0:T(8,128)} fusion(f32[4096,400]{1,0:T(8,128)} %copy.27, s32[2048]{0:T(1024)S(1)} %fusion.3), kind=kCustom, calls=%fused_computation.1 | custom fusion | bytes 6561792 | tf_op jit(solution)/shard_map/gather | solution.py:326
  50.6 0.0 copy-start.8
  50.6 0.0 copy-start.11
  50.6 0.0 copy-start.9
  50.6 5.3 %copy.28 = f32[2048,400]{0,1:T(8,128)} copy(f32[2048,400]{1,0:T(8,128)} %gather_fusion.1) | data formatting | bytes 6553600 | tf_op jit(solution)/shard_map/gather | solution.py:326
  55.8 0.0 copy-done.8
  55.9 0.1 fusion
  56.0 0.1 select_reduce_fusion.3.rank_ref
  56.1 0.1 select_reduce_fusion.4.live_ref
  56.2 0.0 copy-done.11
  56.3 0.1 select_reduce_fusion.2
  56.4 0.0 copy-done.9
  56.4 0.2 select_reduce_fusion
  56.6 46.8 %all-to-all-done.1.fetched = bf16[32,400,128]{2,1,0:T(8,128)(2,1)S(1)} async-done(((bf16[32,400,128]{2,1,0:T(8,128)(2,1)}), bf16[32,400,128]{2,1,0:T(8,128)(2,1)S(1)}, u32[]{:S(2)}, u32[]{:S(2)}) %all-to-all-start.1) | async-done | bytes 3276832 | tf_op jit(solution)/shard_map/all_to_all | solution.py:323
  103.3 0.0 copy-start
  103.3 1.7 gather_negs.1
  105.0 10.2 %all-gather = bf16[3200,128]{1,0:T(8,128)(2,1)S(1)} all-gather(bf16[400,128]{1,0:T(8,128)(2,1)S(1)} %gather_negs.1), channel_id=2, replica_groups=mesh['src'=4,'dst'=8] {'dst'}, dimensions={0}, use_global_device_ids=true | all-gather | bytes 921600 | tf_op jit(solution)/shard_map/all_gather | solution.py:343
  115.3 0.0 copy-done
  115.3 10.3 %gather_edges.1 = (bf16[400,2048]{1,0:T(8,128)(2,1)S(1)}, bf16[400,2048]{1,0:T(8,128)(2,1)S(1)}, f32[1,2048]{1,0:T(1,128)S(1)}) custom-call(s32[16]{0:T(128)S(1)} %select_reduce_fusion.4.live_ref, bf16[32,400,128]{2,1,0:T(8,128)(2,1)S(1)} %all-to-all-done.1.fetched, s32[1,2048]{1,0:T(1,128)S(1)} %bitcast.27, s32[1,2048]{1,0:T(1,128)S(1)} %bitcast.29, ...), custom_call_target="tpu_custom_call" | custom-call | tf_op jit(solution)/shard_map/gather_edges/pallas_call | solution.py:104
  125.6 14.6 %score.1 = (bf16[2,400,2048]{2,1,0:T(8,128)(2,1)S(1)}, bf16[2,400,2048]{2,1,0:T(8,128)(2,1)S(1)}, bf16[8,400,128]{2,1,0:T(8,128)(2,1)}) custom-call(bf16[8,400,128]{2,1,0:T(8,128)(2,1)S(1)} %bitcast.25, bf16[400,2048]{1,0:T(8,128)(2,1)S(1)} %get-tuple-element.10.src_ref, bf16[400,2048]{1,0:T(8,128)(2,1)S(1)} %get-tuple-element.11.dst_ref, ...), custom_call_target="tpu_custom_call" | custom-call | tf_op jit(solution)/shard_map/score/pallas_call | solution.py:165
  140.2 0.0 copy-start.2
  140.2 1.7 copy-done.2
  141.9 0.0 copy-start.4
  141.9 1.7 copy-done.4
  143.6 0.0 reduce-scatter.2.cloned.1.call-update
  143.6 0.0 copy-start.3
  143.6 1.9 copy-done.3
  145.5 0.0 copy-start.5
  145.5 1.9 copy-done.5
  147.4 15.3 %scatter.1.slots_ref = f32[400,2048]{1,0:T(8,128)S(1)} custom-call(bf16[2,400,2048]{2,1,0:T(8,128)(2,1)S(1)} %copy-done.3, bf16[2,400,2048]{2,1,0:T(8,128)(2,1)S(1)} %copy-done.5, s32[1,2048]{1,0:T(1,128)S(1)} %bitcast.28, s32[1,2048]{1,0:T(1,128)S(1)} %bitcast.30), custom_call_target="tpu_custom_call" | custom-call | tf_op jit(solution)/shard_map/scatter/pallas_call | solution.py:202
  162.7 14.2 %reduce-scatter.2.cloned.1.call-done = bf16[1,400,128]{2,1,0:T(8,128)(2,1)} async-done(((bf16[8,400,128]{2,1,0:T(8,128)(2,1)}), bf16[1,400,128]{2,1,0:T(8,128)(2,1)}) %reduce-scatter.2.cloned.1.call-update) | async-done | bytes 102416 | tf_op jit(solution)/shard_map/reduce_scatter | solution.py:346
  176.9 0.0 copy-start.6
  176.9 0.9 copy-done.6
  177.8 5.6 %pack.1 = s16[32,408,128]{2,1,0:T(8,128)(2,1)S(1)} custom-call(s32[32]{0:T(128)S(1)} %select_reduce_fusion.3.rank_ref, s32[32]{0:T(128)S(1)} %get-tuple-element.21.live_ref, f32[400,2048]{1,0:T(8,128)S(1)} %scatter.1.slots_ref, bf16[400,128]{1,0:T(8,128)(2,1)S(1)} %bitcast.26, s32[1,128]{1,0:T(1,128)S(1)} %fusion.11.pos_ref.npos), custom_call_target="tpu_custom_call" | custom-call | tf_op jit(solution)/shard_map/pack/pallas_call | solution.py:250
  183.4 0.0 copy-start.1
  183.4 0.0 copy-start.7
  183.4 81.3 %all_to_all.22.back_ref = s16[32,408,128]{2,1,0:T(8,128)(2,1)S(1)} all-to-all(s16[32,408,128]{2,1,0:T(8,128)(2,1)S(1)} %pack.1), channel_id=1, replica_groups=mesh['src'=4,'dst'=8] {'src','dst'}, dimensions={0} | all-to-all | bytes 6684672 | tf_op jit(solution)/shard_map/all_to_all | solution.py:349
  264.7 0.0 copy-done.1
  264.7 0.0 copy-done.7
  264.7 6.5 %update.1 = (f32[400,2048]{1,0:T(8,128)}, f32[1,2048]{1,0:T(1,128)}) custom-call(s32[32]{0:T(128)S(1)} %reduce.asked_ref, s16[32,408,128]{2,1,0:T(8,128)(2,1)S(1)} %all_to_all.22.back_ref, f32[400,2048]{1,0:T(8,128)S(1)} %bitcast.24, f32[1,2048]{1,0:T(1,128)S(1)} %bitcast.31), custom_call_target="tpu_custom_call" | custom-call | tf_op jit(solution)/shard_map/update/pallas_call | solution.py:290
  (9 shorter events, 0.1 us)
Async XLA Ops:
  8.5 14.4 %all-to-all-start = ((s32[32,1,1]{2,1,0:T(1,128)}), s32[32,1,1]{2,1,0:T(1,128)S(1)}, u32[]{:S(2)}, u32[]{:S(2)}) async-start(s32[32,1,1]{2,1,0:T(1,128)} %copy.25), calls=%async_computation | async-start | bytes 32768 | tf_op jit(solution)/shard_map/all_to_all | solution.py:318
  26.2 77.1 %all-to-all-start.1 = ((bf16[32,400,128]{2,1,0:T(8,128)(2,1)}), bf16[32,400,128]{2,1,0:T(8,128)(2,1)S(1)}, u32[]{:S(2)}, u32[]{:S(2)}) async-start(bf16[32,400,128]{2,1,0:T(8,128)(2,1)} %bitcast.32), calls=%async_computation.1 | async-start | bytes 6553600 | tf_op jit(solution)/shard_map/all_to_all | solution.py:323
  29.0 8.6 %copy-start.10 = (s32[2048]{0:T(1024)S(1)}, s32[2048]{0:T(1024)}, u32[]{:S(2)}) copy-start(s32[2048]{0:T(1024)} %param.11) | copy-start | bytes 24580
  29.0 147.8 %reduce-scatter.2.cloned.1.call-start = ((), (), s32[]{:S(2)}) async-start(), calls=%async_computation.4 | async-start | bytes 921600 | tf_op jit(solution)/shard_map/reduce_scatter | solution.py:346
  50.6 5.3 %copy-start.8 = (s32[2048]{0:T(1024)S(1)}, s32[2048]{0:T(1024)}, u32[]{:S(2)}) copy-start(s32[2048]{0:T(1024)} %param.13) | copy-start | bytes 24580
  50.6 5.7 %copy-start.11 = (s32[128]{0:T(128)S(1)}, s32[128]{0:T(128)}, u32[]{:S(2)}) copy-start(s32[128]{0:T(128)} %param.15) | copy-start | bytes 1540
  50.6 5.8 %copy-start.9 = (s32[2048]{0:T(1024)S(1)}, s32[2048]{0:T(1024)}, u32[]{:S(2)}) copy-start(s32[2048]{0:T(1024)} %param.14) | copy-start | bytes 24580
  103.3 11.9 %copy-start = (f32[2048,400]{0,1:T(8,128)S(1)}, f32[2048,400]{0,1:T(8,128)}, u32[]{:S(2)}) copy-start(f32[2048,400]{0,1:T(8,128)} %copy.28) | copy-start | bytes 9830404
  140.2 1.7 copy-start.2
  141.9 1.7 copy-start.4
  143.6 1.9 copy-start.3
  145.5 1.9 copy-start.5
  176.9 0.9 copy-start.6
  183.4 81.3 %copy-start.1 = (f32[2048,400]{0,1:T(8,128)S(1)}, f32[2048,400]{0,1:T(8,128)}, u32[]{:S(2)}) copy-start(f32[2048,400]{0,1:T(8,128)} %param.8) | copy-start | bytes 9830404
  183.4 81.3 %copy-start.7 = (f32[2048]{0:T(1024)S(1)}, f32[2048]{0:T(1024)}, u32[]{:S(2)}) copy-start(f32[2048]{0:T(1024)} %param.9) | copy-start | bytes 24580
Sparse Core Ops, SparseCore 0:
  143.7 33.1 reduce-scatter.1

commit v2 on v1

--- a/solution.py
+++ b/solution.py
@@ -1,3 +1,5 @@
+import functools
+
 import jax
 import jax.numpy as jnp
 from jax import lax
@@ -8,14 +10,13 @@
 BLK = 128
 TAIL = 8
 AXES = ("src", "dst")
-VMEM_LIMIT = 40 * 1024 * 1024
 F32 = jnp.float32
 BF16 = jnp.bfloat16
 NT = (((1,), (1,)), ((), ()))
 
 
-def params():
-    return pltpu.CompilerParams(vmem_limit_bytes=VMEM_LIMIT)
+def params(held):
+    return pltpu.CompilerParams(vmem_limit_bytes=14 * 1024 * 1024 + held)
 
 
 def whole():
@@ -77,7 +78,7 @@
             pltpu.VMEM((width, live.shape[0] * BLK), BF16),
             pltpu.SemaphoreType.DMA,
         ],
-        compiler_params=params(),
+        compiler_params=params(4 * width * live.shape[0] * BLK),
         name="gather_negs",
     )(live, fetched, pos)
 
@@ -115,7 +116,7 @@
             pltpu.VMEM((width, live.shape[0] * BLK), BF16),
             pltpu.SemaphoreType.DMA,
         ],
-        compiler_params=params(),
+        compiler_params=params(4 * width * live.shape[0] * BLK),
         name="gather_edges",
     )(live, fetched, spos, dpos, operator)
 
@@ -125,16 +126,19 @@
     return high, (x - high.astype(F32)).astype(BF16)
 
 
-def score_kernel(negs_ref, src_ref, dst_ref, op_ref, gpos_ref, gs_ref, gd_ref, gn_ref, wide, tall, acc):
-    groups, width, _ = negs_ref.shape
+def score_kernel(groups, *refs):
+    negs = refs[:groups]
+    src_ref, dst_ref, op_ref, gpos_ref, gs_ref, gd_ref = refs[groups : groups + 6]
+    outs = refs[groups + 6 : 2 * groups + 6]
+    wide, tall, acc = refs[2 * groups + 6 :]
     step = pl.program_id(0)
-    count = groups * negs_ref.shape[2]
-    each = negs_ref.shape[2]
+    each = negs[0].shape[1]
+    count = groups * each
 
     @pl.when(step == 0)
     def _():
         for g in range(groups):
-            block = negs_ref[g]
+            block = negs[g][...]
             wide[:, g * each : (g + 1) * each] = block
             tall[g * each : (g + 1) * each, :] = block.T
         acc[...] = jnp.zeros_like(acc)
@@ -153,33 +157,35 @@
     @pl.when(step == pl.num_programs(0) - 1)
     def _():
         for g in range(groups):
-            gn_ref[g] = acc[:, g * each : (g + 1) * each].astype(BF16)
+            outs[g][...] = acc[:, g * each : (g + 1) * each].astype(BF16)
 
 
 def score(negs, source, target, operator, g_pos, tile=256):
-    groups, width, each = negs.shape
+    groups = len(negs)
+    width, each = negs[0].shape
     edges = source.shape[1]
     lane = pl.BlockSpec((1, tile), lambda i: (0, i))
     column = pl.BlockSpec((width, tile), lambda i: (0, i))
     pair = pl.BlockSpec((2, width, tile), lambda i: (0, 0, i))
-    return pl.pallas_call(
-        score_kernel,
+    out = pl.pallas_call(
+        functools.partial(score_kernel, groups),
         grid=(edges // tile,),
         out_shape=(
             jax.ShapeDtypeStruct((2, width, edges), BF16),
             jax.ShapeDtypeStruct((2, width, edges), BF16),
-            jax.ShapeDtypeStruct((groups, width, each), BF16),
+            *[jax.ShapeDtypeStruct((width, each), BF16)] * groups,
         ),
-        in_specs=[whole(), column, column, column, lane],
-        out_specs=(pair, pair, pl.BlockSpec((groups, width, each), lambda i: (0, 0, 0))),
+        in_specs=[whole()] * groups + [column, column, column, lane],
+        out_specs=(pair, pair, *[pl.BlockSpec((width, each), lambda i: (0, 0))] * groups),
         scratch_shapes=[
             pltpu.VMEM((width, groups * each), BF16),
             pltpu.VMEM((groups * each, width), BF16),
             pltpu.VMEM((width, groups * each), F32),
         ],
-        compiler_params=params(),
+        compiler_params=params(0),
         name="score",
-    )(negs, source, target, operator, g_pos)
+    )(*negs, source, target, operator, g_pos)
+    return out[0], out[1], out[2:]
 
 
 def scatter_kernel(gs_ref, gd_ref, spos, dpos, out_ref):
@@ -205,7 +211,7 @@
         out_shape=jax.ShapeDtypeStruct((width, rows), F32),
         in_specs=[whole(), whole(), whole(), whole()],
         out_specs=pl.BlockSpec((width, tile), lambda i: (0, i)),
-        compiler_params=params(),
+        compiler_params=params(8 * grads_src.size),
         name="scatter",
     )(grads_src, grads_dst, spos, dpos)
 
@@ -225,9 +231,17 @@
     return code[:width, :].astype(jnp.int32).astype(F32) * jnp.exp2(power - 15.0)
 
 
-def pack_kernel(rank_ref, live_ref, slots_ref, gn_ref, npos, out_ref):
+def pack_kernel(rank_ref, live_ref, slots_ref, npos, *refs):
+    grads, out_ref, total = refs[:-2], refs[-2], refs[-1]
     group = out_ref.shape[0]
     first = pl.program_id(0) * group
+    width = slots_ref.shape[0]
+
+    @pl.when(pl.program_id(0) == 0)
+    def _():
+        summed = sum(g[...].astype(F32) for g in grads)
+        total[:width], total[width:] = split(summed)
+
     for k in range(group):
         alive = live_ref[first + k] > 0
 
@@ -236,7 +250,8 @@
             start = pl.multiple_of(rank_ref[first + k] * BLK, BLK)
             index = lax.broadcasted_iota(jnp.int32, (BLK, npos.shape[1]), 0) + start
             hot = jnp.where(index == npos[...], 1.0, 0.0).astype(BF16)
-            part = lax.dot_general(gn_ref[...], hot, NT, preferred_element_type=F32)
+            both = lax.dot_general(total[...], hot, NT, preferred_element_type=F32)
+            part = both[:width] + both[width:]
             encode(slots_ref[:, pl.ds(start, BLK)] + part, out_ref.at[k])
 
         @pl.when(jnp.logical_not(alive))
@@ -246,16 +261,17 @@
 
 def pack(rank, live, slots, grad_negs, npos, group=8):
     devices = rank.shape[0]
-    width = slots.shape[0]
+    width, rows = slots.shape
     return pl.pallas_call(
         pack_kernel,
         grid=(devices // group,),
         out_shape=jax.ShapeDtypeStruct((devices, width + TAIL, BLK), jnp.int16),
-        in_specs=[smem(), smem(), whole(), whole(), whole()],
+        in_specs=[smem(), smem(), whole(), whole()] + [whole()] * len(grad_negs),
         out_specs=pl.BlockSpec((group, width + TAIL, BLK), lambda i: (i, 0, 0)),
-        compiler_params=params(),
+        scratch_shapes=[pltpu.VMEM((2 * width, npos.shape[1]), BF16)],
+        compiler_params=params(6 * width * rows),
         name="pack",
-    )(rank, live, slots, grad_negs, npos)
+    )(rank, live, slots, npos, *grad_negs)
 
 
 def update_kernel(asked_ref, back_ref, table_ref, state_ref, table_out, state_out, grad):
@@ -305,7 +321,7 @@
             pl.BlockSpec((1, rows), lambda i: (0, 0)),
         ),
         scratch_shapes=[pltpu.VMEM((width, rows), F32)],
-        compiler_params=params(),
+        compiler_params=params(12 * width * rows),
         name="update",
     )(asked, returned, table, state)
 
@@ -339,11 +355,21 @@
 
     spos, dpos, npos = compact(src_pos), compact(dst_pos), compact(neg_pos)
 
+    fetched, operator, live, rank, spos, dpos, npos = lax.optimization_barrier(
+        (fetched, operator, live, rank, spos, dpos, npos)
+    )
     own_negs = gather_negs(live, fetched, npos)
-    negs = lax.all_gather(own_negs, "dst", axis=0, tiled=False)
+    peers = lax.axis_size("dst")
+    negs = [own_negs]
+    for shift in range(1, peers):
+        pairs = [(i, i ^ shift) for i in range(peers)]
+        negs.append(lax.ppermute(own_negs, "dst", pairs))
     source, target, g_pos = gather_edges(live, fetched, spos, dpos, operator)
     grads_src, grads_dst, part_negs = score(negs, source, target, operator, g_pos)
-    own_grad = lax.psum_scatter(part_negs, "dst", scatter_dimension=0, tiled=False)
+    own_grad = [part_negs[0]]
+    for shift in range(1, peers):
+        pairs = [(i, i ^ shift) for i in range(peers)]
+        own_grad.append(lax.ppermute(part_negs[shift], "dst", pairs))
     slots = scatter(grads_src, grads_dst, spos, dpos, named * BLK)
     packed = pack(rank, alive, slots, own_grad, npos)
     returned = lax.all_to_all(packed, AXES, split_axis=0, concat_axis=0, tiled=True)

time: 279 us -> 248 us (0.89)
  between operations: 14.2 us -> 0.89 us
  starting transfers between devices: 10.1 us -> 23.3 us
  waiting for transfers between devices: 65.9 us -> 54.7 us
  blocking collectives: 91.5 us -> 81 us
  local copies, waits for them, and re-layouts: 38.9 us -> 29.3 us
    reduce_scatter x1 -> x0, waiting for transfers between devices: 14.2 us -> none  [per_device(): lax.psum_scatter(part_negs, 'dst', scatter_dimension=0, tiled=False)]
    ppermute x0 -> x14, starting transfers between devices: none -> 12.5 us  [the longest x7 6.69 us: per_device(): negs.append(lax.ppermute(own_negs, 'dst', pairs))]
    all_gather x1 -> x0, blocking collectives: 10.2 us -> none  [per_device(): negs = lax.all_gather(own_negs, 'dst', axis=0, tiled=False)]
    unnamed x25 -> x13, local copies, waits for them, and re-layouts: 16.7 us -> 8.57 us
  transfers between devices with their start and end apart: 3 -> 16, of which waited for: 3 -> 4; matrix products, arithmetic and copies ran while one was open for 11% -> 11% of each run, Pallas kernels for 5% -> 11%
where the time goes in v2:
time: 248 us; the launch traced here: 247 us
  blocking collectives  81 us (33%)
  waiting for transfers between devices  54.7 us (22%)
  Pallas kernels  54.6 us (22%)
  local copies, waits for them, and re-layouts  29.3 us (12%)
  starting transfers between devices  23.3 us (9%)
  other arithmetic  3.49 us (1%)
    all_to_all x1, blocking collectives, per_device(): lax.all_to_all(packed, AXES, split_axis=0, concat_axis=0, tiled=True)  81 us
    all_to_all x1, waiting for transfers between devices, per_device(): lax.all_to_all(outgoing.transpose(0, 2, 1), AXES, split_axis=0, concat_ax...  48.3 us
    gather x2, local copies, waits for them, and re-layouts, per_device(): operator = relations[rel_ids].T  16.7 us
    pallas_call x1, Pallas kernels, scatter(): pl.pallas_call(scatter_kernel, grid=(rows // tile,), out_shape=jax.ShapeD...  15.2 us
    pallas_call x1, Pallas kernels, score(): pl.pallas_call(functools.partial(score_kernel, groups), grid=(edges // ti...  13.1 us
    pallas_call x1, Pallas kernels, gather_edges(): pl.pallas_call(edge_kernel, grid=(edges // tile,), out_shape=(jax.ShapeDt...  11.1 us
    unnamed x13, local copies, waits for them, and re-layouts  8.57 us
    all_to_all x1, starting transfers between devices, per_device(): lax.all_to_all(block_list.reshape(devices, 1), AXES, split_axis=0, concat...  7.3 us
  transfers between devices with their start and end apart: 16, of which 4 were waited for; matrix products, arithmetic and copies ran while one was open for 11% of the time, Pallas kernels for 11%

profile of v2, /device:TPU:0, one launch (start us, length us, event | category | flops | bytes accessed | tf_op | source)
XLA Modules:
  0.0 247.2 jit_solution(8940819024057140037)
XLA Ops:
  0.6 1.3 copy.25
  2.0 7.3 %all-to-all-start = ((s32[32,1,1]{2,1,0:T(1,128)}), s32[32,1,1]{2,1,0:T(1,128)S(1)}, u32[]{:S(2)}, u32[]{:S(2)}) async-start(s32[32,1,1]{2,1,0:T(1,128)} %copy.25), calls=%async_computation | async-start | bytes 32768 | tf_op jit(solution)/shard_map/all_to_all | solution.py:334
  9.3 2.1 copy_bitcast_fusion
  11.4 4.9 %all-to-all-done = s32[32,1,1]{2,1,0:T(1,128)S(1)} async-done(((s32[32,1,1]{2,1,0:T(1,128)}), s32[32,1,1]{2,1,0:T(1,128)S(1)}, u32[]{:S(2)}, u32[]{:S(2)}) %all-to-all-start) | async-done | bytes 160 | tf_op jit(solution)/shard_map/all_to_all | solution.py:334
  16.3 0.7 reduce.asked_ref
  17.0 2.7 %gather_fusion = bf16[32,128,400]{1,2,0:T(8,128)(2,1)} fusion(bf16[16,128,400]{1,2,0:T(8,128)(2,1)S(1)} %copy_bitcast_fusion, s32[1024]{0:T(1024)S(1)} %pad_clamp_fusion), kind=kCustom, calls=%fused_computation | custom fusion | bytes 6553728 | tf_op jit(solution)/shard_map/gather | solution.py:338
  19.7 3.5 %all-to-all-start.1 = ((bf16[32,400,128]{2,1,0:T(8,128)(2,1)}), bf16[32,400,128]{2,1,0:T(8,128)(2,1)}, u32[]{:S(2)}, u32[]{:S(2)}) async-start(bf16[32,400,128]{2,1,0:T(8,128)(2,1)} %bitcast.28), calls=%async_computation.1 | async-start | bytes 6553600 | tf_op jit(solution)/shard_map/all_to_all | solution.py:339
  23.3 0.0 copy-start.4
  23.3 8.5 %copy.27 = f32[4096,400]{1,0:T(8,128)} copy(f32[4096,400]{0,1:T(8,128)} %param.10) | data formatting | bytes 13107200 | tf_op args[2]
  31.8 0.0 copy-done.4
  31.8 12.9 %gather_fusion.1 = f32[2048,400]{1,0:T(8,128)} fusion(f32[4096,400]{1,0:T(8,128)} %copy.27, s32[2048]{0:T(1024)S(1)} %fusion.3), kind=kCustom, calls=%fused_computation.1 | custom fusion | bytes 6561792 | tf_op jit(solution)/shard_map/gather | solution.py:342
  44.8 0.0 copy-start.2
  44.8 0.0 copy-start.5
  44.8 0.0 copy-start.3
  44.8 3.8 %copy.28 = f32[2048,400]{0,1:T(8,128)S(1)} copy(f32[2048,400]{1,0:T(8,128)} %gather_fusion.1) | data formatting | bytes 6553600 | tf_op jit(solution)/shard_map/gather | solution.py:342
  48.5 0.0 copy-done.2
  48.6 0.1 fusion
  48.7 0.1 select_reduce_fusion.3.rank_ref
  48.8 0.1 select_reduce_fusion.4.live_ref
  48.9 0.0 copy-done.5
  49.0 0.1 select_reduce_fusion.2
  49.1 0.0 copy-done.3
  49.1 0.2 select_reduce_fusion
  49.3 48.3 %all-to-all-done.1.fetched = bf16[32,400,128]{2,1,0:T(8,128)(2,1)} async-done(((bf16[32,400,128]{2,1,0:T(8,128)(2,1)}), bf16[32,400,128]{2,1,0:T(8,128)(2,1)}, u32[]{:S(2)}, u32[]{:S(2)}) %all-to-all-start.1) | async-done | bytes 3276832 | tf_op jit(solution)/shard_map/all_to_all | solution.py:339
  97.6 2.6 %gather_negs.1.refs_0_ = bf16[400,128]{1,0:T(8,128)(2,1)S(1)} custom-call(s32[16]{0:T(128)S(1)} %select_reduce_fusion.4.live_ref, bf16[32,400,128]{2,1,0:T(8,128)(2,1)} %all-to-all-done.1.fetched, s32[1,128]{1,0:T(1,128)S(1)} %fusion.11.pos_ref.npos), custom_call_target="tpu_custom_call" | custom-call | tf_op jit(solution)/shard_map/gather_negs/pallas_call | solution.py:72
  100.2 0.1 collective-permute-start
  100.3 1.3 collective-permute-start.1
  101.5 0.6 collective-permute-start.2
  102.1 1.2 collective-permute-start.3
  103.3 0.5 collective-permute-start.4
  103.8 0.0 collective-permute-done.refs_1_
  103.8 2.1 collective-permute-start.5
  106.0 0.1 collective-permute-done.1.refs_2_
  106.0 0.9 collective-permute-start.6
  107.0 11.1 %gather_edges.1 = (bf16[400,2048]{1,0:T(8,128)(2,1)S(1)}, bf16[400,2048]{1,0:T(8,128)(2,1)S(1)}, f32[1,2048]{1,0:T(1,128)S(1)}) custom-call(s32[16]{0:T(128)S(1)} %select_reduce_fusion.4.live_ref, bf16[32,400,128]{2,1,0:T(8,128)(2,1)} %all-to-all-done.1.fetched, s32[1,2048]{1,0:T(1,128)S(1)} %bitcast.23, s32[1,2048]{1,0:T(1,128)S(1)} %bitcast.25, ...), custom_call_target="tpu_custom_call" | custom-call | tf_op jit(solution)/shard_map/gather_edges/pallas_call | solution.py:105
  118.1 0.0 collective-permute-done.2.refs_3_
  118.1 0.0 collective-permute-done.3.refs_4_
  118.1 0.0 collective-permute-done.4.refs_5_
  118.1 0.0 collective-permute-done.5.refs_6_
  118.2 0.0 collective-permute-done.6.refs_7_
  118.2 13.1 %score.1 = (bf16[2,400,2048]{2,1,0:T(8,128)(2,1)S(1)}, bf16[2,400,2048]{2,1,0:T(8,128)(2,1)S(1)}, bf16[400,128]{1,0:T(8,128)(2,1)S(1)}, bf16[400,128]{1,0:T(8,12...) custom-call(bf16[400,128]{1,0:T(8,128)(2,1)S(1)} %gather_negs.1.refs, ...), custom_call_target="tpu_custom_call" | custom-call | tf_op jit(solution)/shard_map/score/pallas_call | solution.py:170
  131.3 1.4 collective-permute-start.7
  132.6 0.5 collective-permute-start.8
  133.1 0.9 collective-permute-start.9
  134.1 0.5 collective-permute-start.10
  134.6 1.5 collective-permute-start.11
  136.2 0.0 collective-permute-done.7.refs_1_
  136.2 0.8 collective-permute-start.12
  137.0 1.4 collective-permute-done.8.refs_2_
  138.4 0.1 collective-permute-start.13
  138.5 15.2 %scatter.1.slots_ref = f32[400,2048]{1,0:T(8,128)S(1)} custom-call(bf16[2,400,2048]{2,1,0:T(8,128)(2,1)S(1)} %get-tuple-element.34.gs_ref, bf16[2,400,2048]{2,1,0:T(8,128)(2,1)S(1)} %get-tuple-element.35.gd_ref, s32[1,2048]{1,0:T(1,128)S(1)} %bitcast.24, s32[1,2048]{1,0:T(1,128)S(1)} %bitcast.26), custom_call_target="tpu_custom_call" | custom-call | tf_op jit(solution)/shard_map/scatter/pallas_call | solution.py:208
  153.7 0.0 collective-permute-done.9.refs_3_
  153.7 0.0 collective-permute-done.10.refs_4_
  153.7 0.0 collective-permute-done.11.refs_5_
  153.8 0.0 collective-permute-done.12.refs_6_
  153.8 0.0 collective-permute-done.13.refs_7_
  153.8 5.9 %pack.1 = s16[32,408,128]{2,1,0:T(8,128)(2,1)S(1)} custom-call(s32[32]{0:T(128)S(1)} %select_reduce_fusion.3.rank_ref, s32[32]{0:T(128)S(1)} %get-tuple-element.49.live_ref, f32[400,2048]{1,0:T(8,128)S(1)} %scatter.1.slots_ref, s32[1,128]{1,0:T(1,128)S(1)} %fusion.11.pos_ref.npos, bf16[400,128]{1,0:T(8,128)(2,1)S(1)} %get-tuple-element.36.refs_0_, ...), custom_call_target="tpu_custom_call" | custom-call | tf_op jit(solution)/shard_map/pack/pallas_call | solution.py:265
  159.7 0.0 copy-start
  159.7 0.0 copy-start.1
  159.7 81.0 %all_to_all.22.back_ref = s16[32,408,128]{2,1,0:T(8,128)(2,1)S(1)} all-to-all(s16[32,408,128]{2,1,0:T(8,128)(2,1)S(1)} %pack.1), channel_id=1, replica_groups=mesh['src'=4,'dst'=8] {'src','dst'}, dimensions={0} | all-to-all | bytes 6684672 | tf_op jit(solution)/shard_map/all_to_all | solution.py:375
  240.7 0.0 copy-done
  240.7 0.0 copy-done.1
  240.7 6.5 %update.1 = (f32[400,2048]{1,0:T(8,128)}, f32[1,2048]{1,0:T(1,128)}) custom-call(s32[32]{0:T(128)S(1)} %reduce.asked_ref, s16[32,408,128]{2,1,0:T(8,128)(2,1)S(1)} %all_to_all.22.back_ref, f32[400,2048]{1,0:T(8,128)S(1)} %bitcast.22, f32[1,2048]{1,0:T(1,128)S(1)} %bitcast.27), custom_call_target="tpu_custom_call" | custom-call | tf_op jit(solution)/shard_map/update/pallas_call | solution.py:306
  (9 shorter events, 0.1 us)
Async XLA Ops:
  2.0 14.4 %all-to-all-start = ((s32[32,1,1]{2,1,0:T(1,128)}), s32[32,1,1]{2,1,0:T(1,128)S(1)}, u32[]{:S(2)}, u32[]{:S(2)}) async-start(s32[32,1,1]{2,1,0:T(1,128)} %copy.25), calls=%async_computation | async-start | bytes 32768 | tf_op jit(solution)/shard_map/all_to_all | solution.py:334
  19.7 77.8 %all-to-all-start.1 = ((bf16[32,400,128]{2,1,0:T(8,128)(2,1)}), bf16[32,400,128]{2,1,0:T(8,128)(2,1)}, u32[]{:S(2)}, u32[]{:S(2)}) async-start(bf16[32,400,128]{2,1,0:T(8,128)(2,1)} %bitcast.28), calls=%async_computation.1 | async-start | bytes 6553600 | tf_op jit(solution)/shard_map/all_to_all | solution.py:339
  23.3 8.6 %copy-start.4 = (s32[2048]{0:T(1024)S(1)}, s32[2048]{0:T(1024)}, u32[]{:S(2)}) copy-start(s32[2048]{0:T(1024)} %param.11) | copy-start | bytes 24580
  44.8 3.8 %copy-start.2 = (s32[2048]{0:T(1024)S(1)}, s32[2048]{0:T(1024)}, u32[]{:S(2)}) copy-start(s32[2048]{0:T(1024)} %param.13) | copy-start | bytes 24580
  44.8 4.2 %copy-start.5 = (s32[128]{0:T(128)S(1)}, s32[128]{0:T(128)}, u32[]{:S(2)}) copy-start(s32[128]{0:T(128)} %param.15) | copy-start | bytes 1540
  44.8 4.3 %copy-start.3 = (s32[2048]{0:T(1024)S(1)}, s32[2048]{0:T(1024)}, u32[]{:S(2)}) copy-start(s32[2048]{0:T(1024)} %param.14) | copy-start | bytes 24580
  100.2 3.6 %collective-permute-start = (bf16[400,128]{1,0:T(8,128)(2,1)S(1)}, bf16[400,128]{1,0:T(8,128)(2,1)S(1)}, u32[]{:S(2)}, u32[]{:S(2)}) collective-permute-start(bf16[400,128]{1,0:T(8,128)(2,1)S(1)} %gather_negs.1.refs_0_), channel_id=1, source_target_pairs={{0,1},{1,0},{2,3},{3,2},{4,5},{5,4},{6,7},{7,6},{8,9},{9,8},{10,11... | collective-permute-start | bytes 307208 | tf_op jit(solution)/shard_map/ppermute | solution.py:366
  100.3 5.7 %collective-permute-start.1 = (bf16[400,128]{1,0:T(8,128)(2,1)S(1)}, bf16[400,128]{1,0:T(8,128)(2,1)S(1)}, u32[]{:S(2)}, u32[]{:S(2)}) collective-permute-start(bf16[400,128]{1,0:T(8,128)(2,1)S(1)} %gather_negs.1.refs_0_), channel_id=1, source_target_pairs={{0,2},{1,3},{2,0},{3,1},{4,6},{5,7},{6,4},{7,5},{8,10},{9,11},{10,... | collective-permute-start | bytes 307208 | tf_op jit(solution)/shard_map/ppermute | solution.py:366
  101.5 16.6 %collective-permute-start.2 = (bf16[400,128]{1,0:T(8,128)(2,1)S(1)}, bf16[400,128]{1,0:T(8,128)(2,1)S(1)}, u32[]{:S(2)}, u32[]{:S(2)}) collective-permute-start(bf16[400,128]{1,0:T(8,128)(2,1)S(1)} %gather_negs.1.refs_0_), channel_id=1, source_target_pairs={{0,3},{1,2},{2,1},{3,0},{4,7},{5,6},{6,5},{7,4},{8,11},{9,10},{10,... | collective-permute-start | bytes 307208 | tf_op jit(solution)/shard_map/ppermute | solution.py:366
  102.1 16.0 %collective-permute-start.3 = (bf16[400,128]{1,0:T(8,128)(2,1)S(1)}, bf16[400,128]{1,0:T(8,128)(2,1)S(1)}, u32[]{:S(2)}, u32[]{:S(2)}) collective-permute-start(bf16[400,128]{1,0:T(8,128)(2,1)S(1)} %gather_negs.1.refs_0_), channel_id=1, source_target_pairs={{0,4},{1,5},{2,6},{3,7},{4,0},{5,1},{6,2},{7,3},{8,12},{9,13},{10,... | collective-permute-start | bytes 307208 | tf_op jit(solution)/shard_map/ppermute | solution.py:366
  103.3 14.8 %collective-permute-start.4 = (bf16[400,128]{1,0:T(8,128)(2,1)S(1)}, bf16[400,128]{1,0:T(8,128)(2,1)S(1)}, u32[]{:S(2)}, u32[]{:S(2)}) collective-permute-start(bf16[400,128]{1,0:T(8,128)(2,1)S(1)} %gather_negs.1.refs_0_), channel_id=1, source_target_pairs={{0,5},{1,4},{2,7},{3,6},{4,1},{5,0},{6,3},{7,2},{8,13},{9,12},{10,... | collective-permute-start | bytes 307208 | tf_op jit(solution)/shard_map/ppermute | solution.py:366
  103.8 14.3 %collective-permute-start.5 = (bf16[400,128]{1,0:T(8,128)(2,1)S(1)}, bf16[400,128]{1,0:T(8,128)(2,1)S(1)}, u32[]{:S(2)}, u32[]{:S(2)}) collective-permute-start(bf16[400,128]{1,0:T(8,128)(2,1)S(1)} %gather_negs.1.refs_0_), channel_id=1, source_target_pairs={{0,6},{1,7},{2,4},{3,5},{4,2},{5,3},{6,0},{7,1},{8,14},{9,15},{10,... | collective-permute-start | bytes 307208 | tf_op jit(solution)/shard_map/ppermute | solution.py:366
  106.0 12.1 %collective-permute-start.6 = (bf16[400,128]{1,0:T(8,128)(2,1)S(1)}, bf16[400,128]{1,0:T(8,128)(2,1)S(1)}, u32[]{:S(2)}, u32[]{:S(2)}) collective-permute-start(bf16[400,128]{1,0:T(8,128)(2,1)S(1)} %gather_negs.1.refs_0_), channel_id=1, source_target_pairs={{0,7},{1,6},{2,5},{3,4},{4,3},{5,2},{6,1},{7,0},{8,15},{9,14},{10,... | collective-permute-start | bytes 307208 | tf_op jit(solution)/shard_map/ppermute | solution.py:366
  131.3 4.9 %collective-permute-start.7 = (bf16[400,128]{1,0:T(8,128)(2,1)S(1)}, bf16[400,128]{1,0:T(8,128)(2,1)S(1)}, u32[]{:S(2)}, u32[]{:S(2)}) collective-permute-start(bf16[400,128]{1,0:T(8,128)(2,1)S(1)} %get-tuple-element.37), channel_id=1, source_target_pairs={{0,1},{1,0},{2,3},{3,2},{4,5},{5,4},{6,7},{7,6},{8,9},{9,8},{10,11... | collective-permute-start | bytes 307208 | tf_op jit(solution)/shard_map/ppermute | solution.py:372
  132.6 5.7 %collective-permute-start.8 = (bf16[400,128]{1,0:T(8,128)(2,1)S(1)}, bf16[400,128]{1,0:T(8,128)(2,1)S(1)}, u32[]{:S(2)}, u32[]{:S(2)}) collective-permute-start(bf16[400,128]{1,0:T(8,128)(2,1)S(1)} %get-tuple-element.38), channel_id=1, source_target_pairs={{0,2},{1,3},{2,0},{3,1},{4,6},{5,7},{6,4},{7,5},{8,10},{9,11},{10,... | collective-permute-start | bytes 307208 | tf_op jit(solution)/shard_map/ppermute | solution.py:372
  133.1 20.6 %collective-permute-start.9 = (bf16[400,128]{1,0:T(8,128)(2,1)S(1)}, bf16[400,128]{1,0:T(8,128)(2,1)S(1)}, u32[]{:S(2)}, u32[]{:S(2)}) collective-permute-start(bf16[400,128]{1,0:T(8,128)(2,1)S(1)} %get-tuple-element.39), channel_id=1, source_target_pairs={{0,3},{1,2},{2,1},{3,0},{4,7},{5,6},{6,5},{7,4},{8,11},{9,10},{10,... | collective-permute-start | bytes 307208 | tf_op jit(solution)/shard_map/ppermute | solution.py:372
  134.1 19.7 %collective-permute-start.10 = (bf16[400,128]{1,0:T(8,128)(2,1)S(1)}, bf16[400,128]{1,0:T(8,128)(2,1)S(1)}, u32[]{:S(2)}, u32[]{:S(2)}) collective-permute-start(bf16[400,128]{1,0:T(8,128)(2,1)S(1)} %get-tuple-element.40), channel_id=1, source_target_pairs={{0,4},{1,5},{2,6},{3,7},{4,0},{5,1},{6,2},{7,3},{8,12},{9,13},{10,... | collective-permute-start | bytes 307208 | tf_op jit(solution)/shard_map/ppermute | solution.py:372
  134.6 19.1 %collective-permute-start.11 = (bf16[400,128]{1,0:T(8,128)(2,1)S(1)}, bf16[400,128]{1,0:T(8,128)(2,1)S(1)}, u32[]{:S(2)}, u32[]{:S(2)}) collective-permute-start(bf16[400,128]{1,0:T(8,128)(2,1)S(1)} %get-tuple-element.41), channel_id=1, source_target_pairs={{0,5},{1,4},{2,7},{3,6},{4,1},{5,0},{6,3},{7,2},{8,13},{9,12},{10,... | collective-permute-start | bytes 307208 | tf_op jit(solution)/shard_map/ppermute | solution.py:372
  136.2 17.6 %collective-permute-start.12 = (bf16[400,128]{1,0:T(8,128)(2,1)S(1)}, bf16[400,128]{1,0:T(8,128)(2,1)S(1)}, u32[]{:S(2)}, u32[]{:S(2)}) collective-permute-start(bf16[400,128]{1,0:T(8,128)(2,1)S(1)} %get-tuple-element.42), channel_id=1, source_target_pairs={{0,6},{1,7},{2,4},{3,5},{4,2},{5,3},{6,0},{7,1},{8,14},{9,15},{10,... | collective-permute-start | bytes 307208 | tf_op jit(solution)/shard_map/ppermute | solution.py:372
  138.4 15.4 %collective-permute-start.13 = (bf16[400,128]{1,0:T(8,128)(2,1)S(1)}, bf16[400,128]{1,0:T(8,128)(2,1)S(1)}, u32[]{:S(2)}, u32[]{:S(2)}) collective-permute-start(bf16[400,128]{1,0:T(8,128)(2,1)S(1)} %get-tuple-element.43), channel_id=1, source_target_pairs={{0,7},{1,6},{2,5},{3,4},{4,3},{5,2},{6,1},{7,0},{8,15},{9,14},{10,... | collective-permute-start | bytes 307208 | tf_op jit(solution)/shard_map/ppermute | solution.py:372
  159.7 81.0 %copy-start = (f32[2048,400]{0,1:T(8,128)S(1)}, f32[2048,400]{0,1:T(8,128)}, u32[]{:S(2)}) copy-start(f32[2048,400]{0,1:T(8,128)} %param.8) | copy-start | bytes 9830404
  159.7 81.0 %copy-start.1 = (f32[2048]{0:T(1024)S(1)}, f32[2048]{0:T(1024)}, u32[]{:S(2)}) copy-start(f32[2048]{0:T(1024)} %param.9) | copy-start | bytes 24580

commit v3 on v2

v3 whole, which is shorter than its diff:
```python
import functools

import jax
import jax.numpy as jnp
from jax import lax
from jax.experimental import pallas as pl
from jax.experimental.pallas import tpu as pltpu
from jax.sharding import PartitionSpec as P

BLK = 128
TAIL = 8
GROUPS = 4
TILE = 256
AXES = ("src", "dst")
F32 = jnp.float32
BF16 = jnp.bfloat16
NT = (((1,), (1,)), ((), ()))


def params(held):
    return pltpu.CompilerParams(vmem_limit_bytes=14 * 1024 * 1024 + held)


MIB = 1024 * 1024


def cost(flops):
    return pl.CostEstimate(flops=flops, bytes_accessed=flops // 512, transcendentals=0)


def whole():
    return pl.BlockSpec(memory_space=pltpu.VMEM)


def smem():
    return pl.BlockSpec(memory_space=pltpu.SMEM)


def anywhere():
    return pl.BlockSpec(memory_space=pl.ANY)


def load_live(live_ref, fetched, rows, sem):
    count = live_ref.shape[0]

    def copy(k):
        lanes = pl.ds(pl.multiple_of(k * BLK, BLK), BLK)
        return pltpu.make_async_copy(fetched.at[live_ref[k]], rows.at[:, lanes], sem)

    def start(k, _):
        copy(k).start()
        return 0

    def wait(k, _):
        copy(k).wait()
        return 0

    lax.fori_loop(0, count, start, 0)
    lax.fori_loop(0, count, wait, 0)


def pick(rows, positions):
    total = rows.shape[1]
    step = min(total, 2048)
    out = None
    for first in range(0, total, step):
        index = lax.broadcasted_iota(jnp.int32, (step, positions.shape[1]), 0) + first
        hot = jnp.where(index == positions, 1.0, 0.0).astype(BF16)
        part = jnp.dot(rows[:, first : first + step], hot, preferred_element_type=F32)
        out = part if out is None else out + part
    return out


def neg_kernel(live_ref, fetched, pos_ref, out_ref, rows, sem):
    load_live(live_ref, fetched, rows, sem)
    out_ref[...] = pick(rows, pos_ref[...]).astype(BF16)


def gather_negs(live, fetched, pos):
    width = fetched.shape[1]
    total = live.shape[0] * BLK
    return pl.pallas_call(
        neg_kernel,
        out_shape=(
            jax.ShapeDtypeStruct((width, pos.shape[1]), BF16),
            jax.ShapeDtypeStruct((width, total), BF16),
        ),
        in_specs=[smem(), anywhere(), whole()],
        out_specs=(whole(), whole()),
        scratch_shapes=[pltpu.SemaphoreType.DMA],
        compiler_params=params(4 * width * total),
        name="gather_negs",
    )(live, fetched, pos)


def edge_kernel(rows, spos, dpos, op_ref, src_ref, dst_ref, gpos_ref):
    source = pick(rows, spos[...])
    target = pick(rows, dpos[...])
    u = source * op_ref[...]
    positive = jnp.sum(u * target, axis=0, keepdims=True)
    gpos_ref[...] = -jax.nn.sigmoid(-positive)
    src_ref[...] = source.astype(BF16)
    dst_ref[...] = target.astype(BF16)


def gather_edges(rows, spos, dpos, operator, tile=512):
    width, total = rows.shape
    edges = spos.shape[1]
    lane = pl.BlockSpec((1, tile), lambda i: (0, i))
    column = pl.BlockSpec((width, tile), lambda i: (0, i))
    return pl.pallas_call(
        edge_kernel,
        grid=(edges // tile,),
        out_shape=(
            jax.ShapeDtypeStruct((width, edges), BF16),
            jax.ShapeDtypeStruct((width, edges), BF16),
            jax.ShapeDtypeStruct((1, edges), F32),
        ),
        in_specs=[whole(), lane, lane, column],
        out_specs=(column, column, lane),
        compiler_params=params(2 * width * total + 8 * MIB),
        cost_estimate=cost(4 * width * total * edges),
        name="gather_edges",
    )(rows, spos, dpos, operator)


def split(x):
    high = x.astype(BF16)
    return high, (x - high.astype(F32)).astype(BF16)


def score_kernel(groups, *refs):
    negs = refs[:groups]
    src_ref, dst_ref, op_ref, gpos_ref, gs_ref, gd_ref = refs[groups : groups + 6]
    outs = refs[groups + 6 : 2 * groups + 6]
    each = negs[0].shape[1]
    count = groups * each
    wide = jnp.concatenate([n[...] for n in negs], axis=1)
    tall = jnp.concatenate([n[...].T for n in negs], axis=0)
    operator = op_ref[...]
    u = src_ref[...].astype(F32) * operator
    u_half = u.astype(BF16)
    scores = jnp.dot(tall, u_half, preferred_element_type=F32)
    g_neg = (jax.nn.sigmoid(scores) / count).astype(BF16)
    sums = lax.dot_general(u_half, g_neg, NT, preferred_element_type=F32)
    for g in range(groups):
        outs[g][...] = sums[:, g * each : (g + 1) * each].astype(BF16)
    g_pos = gpos_ref[...]
    grad_u = g_pos * dst_ref[...].astype(F32) + jnp.dot(wide, g_neg, preferred_element_type=F32)
    gs_ref[0], gs_ref[1] = split(grad_u * operator)
    gd_ref[0], gd_ref[1] = split(g_pos * u)


def score(negs, source, target, operator, g_pos):
    groups = len(negs)
    width, each = negs[0].shape
    edges = source.shape[1]
    out = pl.pallas_call(
        functools.partial(score_kernel, groups),
        out_shape=(
            jax.ShapeDtypeStruct((2, width, edges), BF16),
            jax.ShapeDtypeStruct((2, width, edges), BF16),
            *[jax.ShapeDtypeStruct((width, each), BF16)] * groups,
        ),
        in_specs=[whole()] * (groups + 4),
        out_specs=(whole(),) * (groups + 2),
        compiler_params=params(20 * MIB),
        cost_estimate=cost(6 * width * edges * groups * each),
        name="score",
    )(*negs, source, target, operator, g_pos)
    return out[0], out[1], out[2:]


def scatter_kernel(base_ref, gs_ref, gd_ref, spos, dpos, out_ref):
    width, edges = gs_ref.shape[1:]
    first = base_ref[0] * BLK

    def tile(t, _):
        index = lax.broadcasted_iota(jnp.int32, (TILE, edges), 0) + (first + t * TILE)
        both = None
        for grads, pos in ((gs_ref, spos), (gd_ref, dpos)):
            hot = jnp.where(index == pos[...], 1.0, 0.0).astype(BF16)
            part = lax.dot_general(
                grads[...].reshape(2 * width, edges), hot, NT, preferred_element_type=F32
            )
            both = part if both is None else both + part
        out_ref[:, pl.ds(pl.multiple_of(t * TILE, TILE), TILE)] = both[:width] + both[width:]
        return 0

    blocks = base_ref[1] - base_ref[0]
    lax.fori_loop(0, (blocks * BLK + TILE - 1) // TILE, tile, 0)


def scatter(bases, grads_src, grads_dst, spos, dpos, blocks):
    width, edges = grads_src.shape[1:]
    rows = -(-blocks * BLK // TILE) * TILE
    return pl.pallas_call(
        scatter_kernel,
        out_shape=jax.ShapeDtypeStruct((width, rows), F32),
        in_specs=[smem(), whole(), whole(), whole(), whole()],
        out_specs=whole(),
        compiler_params=params(4 * width * rows),
        cost_estimate=cost(4 * width * rows * edges),
        name="scatter",
    )(bases, grads_src, grads_dst, spos, dpos)


def encode(x, out_ref):
    width = x.shape[0]
    top = jnp.max(jnp.abs(x), axis=0, keepdims=True)
    power = jnp.ceil(jnp.log2(jnp.maximum(top, 1e-30)))
    code = jnp.clip(jnp.round(x * jnp.exp2(15.0 - power)), -32767.0, 32767.0)
    out_ref[:width, :] = code.astype(jnp.int32).astype(jnp.int16)
    tail = jnp.broadcast_to(power, (TAIL, x.shape[1]))
    out_ref[width:, :] = tail.astype(jnp.int32).astype(jnp.int16)


def decode(code, width):
    power = code[width:, :].astype(jnp.int32).astype(F32)[:1]
    return code[:width, :].astype(jnp.int32).astype(F32) * jnp.exp2(power - 15.0)


def pack_kernel(first, rank_ref, live_ref, slots_ref, npos, *refs):
    count = len(refs) - 1
    peers = 0
    while refs[peers].shape[0] == slots_ref.shape[0]:
        peers += 1
    grads, outs, total = refs[:peers], refs[peers:count], refs[count]
    width = slots_ref.shape[0]
    total[:width], total[width:] = split(sum(g[...].astype(F32) for g in grads))
    base = rank_ref[first]
    for k, out_ref in enumerate(outs):
        alive = live_ref[first + k] > 0

        @pl.when(alive)
        def _():
            rank = rank_ref[first + k]
            index = lax.broadcasted_iota(jnp.int32, (BLK, npos.shape[1]), 0) + rank * BLK
            hot = jnp.where(index == npos[...], 1.0, 0.0).astype(BF16)
            both = lax.dot_general(total[...], hot, NT, preferred_element_type=F32)
            lanes = pl.ds(pl.multiple_of((rank - base) * BLK, BLK), BLK)
            encode(slots_ref[:, lanes] + (both[:width] + both[width:]), out_ref)

        @pl.when(jnp.logical_not(alive))
        def _():
            out_ref[...] = jnp.zeros(out_ref.shape, jnp.int16)


def pack(first, group, rank, live, slots, grad_negs, npos):
    width = slots.shape[0]
    return pl.pallas_call(
        functools.partial(pack_kernel, first),
        out_shape=(jax.ShapeDtypeStruct((width + TAIL, BLK), jnp.int16),) * group,
        in_specs=[smem(), smem(), whole(), whole()] + [whole()] * len(grad_negs),
        out_specs=(whole(),) * group,
        scratch_shapes=[pltpu.VMEM((2 * width, npos.shape[1]), BF16)],
        compiler_params=params(0),
        cost_estimate=cost(4 * width * BLK * BLK * group),
        name="pack",
    )(rank, live, slots, npos, *grad_negs)


def add_kernel(first, fresh, asked_ref, *refs):
    grad = refs[-1]
    backs = refs[: -1 if fresh else -2]
    width = grad.shape[0]
    if fresh:
        grad[...] = jnp.zeros_like(grad)
    for k, back in enumerate(backs):
        lanes = pl.ds(pl.multiple_of(asked_ref[first + k] * BLK, BLK), BLK)
        grad[:, lanes] += decode(back, width)


def add(first, asked, backs, grad, width, rows):
    fresh = grad is None
    extra = [] if fresh else [grad]
    return pl.pallas_call(
        functools.partial(add_kernel, first, fresh),
        out_shape=jax.ShapeDtypeStruct((width, rows), F32),
        in_specs=[smem()] + [whole()] * (len(backs) + len(extra)),
        out_specs=whole(),
        input_output_aliases={} if fresh else {len(backs) + 1: 0},
        compiler_params=params(0),
        cost_estimate=cost(width * BLK * len(backs) * 64),
        name="add",
    )(asked, *backs, *extra)


def update_kernel(first, asked_ref, *refs):
    backs = refs[:-7]
    grad, table_ref, state_ref, table_out, state_out, fresh, sems = refs[-7:]
    width, rows = grad.shape
    for k, back in enumerate(backs):
        lanes = pl.ds(pl.multiple_of(asked_ref[first + k] * BLK, BLK), BLK)
        grad[:, lanes] += decode(back, width)
    span = fresh.shape[1] // sems.shape[0]

    def copy(b):
        lanes = pl.ds(pl.multiple_of(b * span, span), span)
        return pltpu.make_async_copy(fresh.at[:, lanes], table_out.at[:, lanes], sems.at[b])

    for b in range(sems.shape[0]):
        for c in range(b * span, (b + 1) * span, BLK):
            lanes = slice(c, c + BLK)
            g = grad[:, lanes]
            new_state = state_ref[:, lanes] + jnp.sum(g * g, axis=0, keepdims=True) / width
            state_out[:, lanes] = new_state
            fresh[:, lanes] = table_ref[:, lanes] - 0.1 * g / (jnp.sqrt(new_state) + 1e-10)
        copy(b).start()
    for b in range(sems.shape[0]):
        copy(b).wait()


def update(first, asked, backs, grad, table, state, parts=4):
    width, rows = table.shape
    return pl.pallas_call(
        functools.partial(update_kernel, first),
        out_shape=(
            jax.ShapeDtypeStruct((width, rows), F32),
            jax.ShapeDtypeStruct((1, rows), F32),
        ),
        in_specs=[smem()] + [whole()] * (len(backs) + 3),
        out_specs=(anywhere(), whole()),
        scratch_shapes=[pltpu.VMEM((width, rows), F32), pltpu.SemaphoreType.DMA((parts,))],
        compiler_params=params(4 * width * rows),
        cost_estimate=cost(width * rows * 64),
        name="update",
    )(asked, *backs, grad, table, state)


def per_device(table, state, relations, rel_ids, block_list, src_pos, dst_pos, neg_pos):
    devices = lax.axis_size(AXES)
    named = devices // 2
    rows_dev, width = table.shape
    blocks = rows_dev // BLK
    wanted = lax.all_to_all(
        block_list.reshape(devices, 1), AXES, split_axis=0, concat_axis=0, tiled=True
    )
    asked = wanted.reshape(devices)
    outgoing = table.reshape(blocks, BLK, width).astype(BF16)[asked]
    fetched = lax.all_to_all(
        outgoing.transpose(0, 2, 1), AXES, split_axis=0, concat_axis=0, tiled=True
    )
    operator = relations[rel_ids].T

    half = devices // 2
    order = [k for pair in zip(range(devices - 1, half - 1, -1), range(half - 1, -1, -1)) for k in pair]
    partners = lax.axis_index(AXES) ^ jnp.array(order, jnp.int32)
    ids = jnp.arange(devices, dtype=jnp.int32)
    seat = partners[:, None] == ids[None, :]
    named_by = jnp.max((src_pos // BLK)[:, None] == ids[None, :], axis=0).astype(jnp.int32)
    alive = jnp.sum(jnp.where(seat, named_by[None, :], 0), axis=1)
    rank = jnp.sum(jnp.where(ids[None, :] < ids[:, None], alive[None, :], 0), axis=1)
    place = jnp.sum(jnp.where(seat, rank[:, None], 0), axis=0)
    slot = jnp.arange(named, dtype=jnp.int32)
    live = jnp.sum(
        jnp.where((rank[None, :] == slot[:, None]) & (alive[None, :] > 0), partners[None, :], 0), axis=1
    )
    asked = jnp.sum(jnp.where(seat, asked[None, :], 0), axis=1)
    group = devices // GROUPS
    starts = jnp.concatenate([rank[::group], jnp.full((1,), named, jnp.int32)])

    def compact(pos):
        where = jnp.sum(jnp.where((pos // BLK)[:, None] == ids[None, :], place[None, :], 0), axis=1)
        return (where * BLK + pos % BLK).reshape(1, -1)

    spos, dpos, npos = compact(src_pos), compact(dst_pos), compact(neg_pos)
    bases = [starts[g : g + 2] for g in range(GROUPS)]
    fetched, operator, live, rank, alive, asked, spos, dpos, npos, bases = lax.optimization_barrier(
        (fetched, operator, live, rank, alive, asked, spos, dpos, npos, bases)
    )

    def swap(x, shift, axis):
        count = lax.axis_size(axis)
        return lax.ppermute(x, axis, [(i, i ^ shift) for i in range(count)])

    peers = lax.axis_size("dst")
    own_negs, rows = gather_negs(live, fetched, npos)
    negs = [own_negs] + [swap(own_negs, shift, "dst") for shift in range(1, peers)]
    source, target, g_pos = gather_edges(rows, spos, dpos, operator)
    grads_src, grads_dst, part_negs = score(negs, source, target, operator, g_pos)
    own_grad = [part_negs[0]] + [swap(part_negs[shift], shift, "dst") for shift in range(1, peers)]
    grad = None
    for g in range(GROUPS):
        first = g * group
        slots = scatter(bases[g], grads_src, grads_dst, spos, dpos, min(group, named))
        packed = pack(first, group, rank, alive, slots, own_grad, npos)
        backs = [
            swap(x, shift, AXES) if shift else x
            for x, shift in zip(packed, order[first : first + group])
        ]
        if g < GROUPS - 1:
            grad = add(first, asked, backs, grad, width, rows_dev)
        else:
            new_table, new_state = update(
                first, asked, backs, grad, table.T, state.reshape(1, rows_dev)
            )
    return (new_table.T, new_state.reshape(rows_dev))


def solution(mesh):
    in_specs = (
        P(AXES, None),
        P(AXES),
        P(),
        P(AXES),
        P(AXES, None),
        P(AXES),
        P(AXES),
        P(AXES),
    )
    out_specs = (P(AXES, None), P(AXES))
    return jax.shard_map(
        per_device, mesh=mesh, in_specs=in_specs, out_specs=out_specs, check_vma=False
    )
```

time: 248 us -> 234 us (0.944)
  blocking collectives: 81 us -> 0 us
  starting transfers between devices: 23.3 us -> 80.8 us
  waiting for transfers between devices: 54.7 us -> 65.3 us
  Pallas kernels: 54.6 us -> 50.4 us
    all_to_all x1 -> x0, blocking collectives: 81 us -> none  [per_device(): lax.all_to_all(packed, AXES, split_axis=0, concat_axis=0, tiled=True)]
    ppermute x14 -> x45, starting transfers between devices: 12.5 us -> 70.8 us  [swap(): return lax.ppermute(x, axis, [(i, i ^ shift) for i in range(count)])]
    ppermute x14 -> x45, waiting for transfers between devices: 1.51 us -> 14.3 us  [swap(): return lax.ppermute(x, axis, [(i, i ^ shift) for i in range(count)])]
    pallas_call x1, Pallas kernels: 11.1 us -> 8.04 us  [gather_edges(): pl.pallas_call(edge_kernel, grid=(edges // tile,), out_shape=(jax.ShapeDt...]
    pallas_call x5 -> x14, Pallas kernels: 43.4 us -> 42.4 us  [the longest x4 19.4 us: scatter(): pl.pallas_call(scatter_kernel, out_shape=jax.ShapeDtypeStruct((width, row...]
    unnamed x13 -> x17, local copies, waits for them, and re-layouts: 8.57 us -> 8.64 us
  transfers between devices with their start and end apart: 16 -> 47, of which waited for: 4 -> 12; matrix products, arithmetic and copies ran while one was open for 11% -> 13% of each run, Pallas kernels for 11% -> 16%
where the time goes in v3:
time: 234 us; the launch traced here: 233 us
  starting transfers between devices  80.8 us (35%)
  waiting for transfers between devices  65.3 us (28%)
  Pallas kernels  50.4 us (22%)
  local copies, waits for them, and re-layouts  31.1 us (13%)
  other arithmetic  3.94 us (2%)
    ppermute x45, starting transfers between devices, swap(): return lax.ppermute(x, axis, [(i, i ^ shift) for i in range(count)])  70.8 us
    all_to_all x1, waiting for transfers between devices, per_device(): lax.all_to_all(outgoing.transpose(0, 2, 1), AXES, split_axis=0, concat_ax...  46 us
    pallas_call x4, Pallas kernels, scatter(): pl.pallas_call(scatter_kernel, out_shape=jax.ShapeDtypeStruct((width, row...  19.4 us
    gather x2, local copies, waits for them, and re-layouts, per_device(): operator = relations[rel_ids].T  18.2 us
    ppermute x45, waiting for transfers between devices, swap(): return lax.ppermute(x, axis, [(i, i ^ shift) for i in range(count)])  14.3 us
    unnamed x17, local copies, waits for them, and re-layouts  8.64 us
    pallas_call x1, Pallas kernels, gather_edges(): pl.pallas_call(edge_kernel, grid=(edges // tile,), out_shape=(jax.ShapeDt...  8.04 us
    pallas_call x4, Pallas kernels, pack(): pl.pallas_call(functools.partial(pack_kernel, first), out_shape=(jax.Shap...  7.97 us
  transfers between devices with their start and end apart: 47, of which 12 were waited for; matrix products, arithmetic and copies ran while one was open for 13% of the time, Pallas kernels for 16%

profile of v3, /device:TPU:0, one launch (start us, length us, event | category | flops | bytes accessed | tf_op | source)
XLA Modules:
  0.0 232.7 jit_solution(17598429118909905447)
XLA Ops:
  0.6 1.3 copy.28
  2.0 7.3 %all-to-all-start = ((s32[32,1,1]{2,1,0:T(1,128)}), s32[32,1,1]{2,1,0:T(1,128)S(1)}, u32[]{:S(2)}, u32[]{:S(2)}) async-start(s32[32,1,1]{2,1,0:T(1,128)} %copy.28), calls=%async_computation | async-start | bytes 32768 | tf_op jit(solution)/shard_map/all_to_all | solution.py:336
  9.3 2.1 copy_bitcast_fusion
  11.4 4.9 %all-to-all-done = s32[32,1,1]{2,1,0:T(1,128)S(1)} async-done(((s32[32,1,1]{2,1,0:T(1,128)}), s32[32,1,1]{2,1,0:T(1,128)S(1)}, u32[]{:S(2)}, u32[]{:S(2)}) %all-to-all-start) | async-done | bytes 160 | tf_op jit(solution)/shard_map/all_to_all | solution.py:336
  16.3 0.7 reduce
  17.0 2.7 %gather_fusion = bf16[32,128,400]{1,2,0:T(8,128)(2,1)} fusion(bf16[16,128,400]{1,2,0:T(8,128)(2,1)S(1)} %copy_bitcast_fusion, s32[1024]{0:T(1024)S(1)} %pad_clamp_fusion), kind=kCustom, calls=%fused_computation | custom fusion | bytes 6553728 | tf_op jit(solution)/shard_map/gather | solution.py:340
  19.7 2.8 %all-to-all-start.1 = ((bf16[32,400,128]{2,1,0:T(8,128)(2,1)}), bf16[32,400,128]{2,1,0:T(8,128)(2,1)S(1)}, u32[]{:S(2)}, u32[]{:S(2)}) async-start(bf16[32,400,128]{2,1,0:T(8,128)(2,1)} %bitcast.34), calls=%async_computation.1 | async-start | bytes 6553600 | tf_op jit(solution)/shard_map/all_to_all | solution.py:341
  22.5 8.6 %copy.30 = f32[4096,400]{1,0:T(8,128)} copy(f32[4096,400]{0,1:T(8,128)} %param.11) | data formatting | bytes 13107200 | tf_op args[2]
  31.1 12.9 %gather_fusion.1 = f32[2048,400]{1,0:T(8,128)} fusion(f32[4096,400]{1,0:T(8,128)} %copy.30, s32[2048]{0:T(1024)S(1)} %fusion.3), kind=kCustom, calls=%fused_computation.1 | custom fusion | bytes 6561792 | tf_op jit(solution)/shard_map/gather | solution.py:344
  44.1 5.2 %copy.31 = f32[2048,400]{0,1:T(8,128)} copy(f32[2048,400]{1,0:T(8,128)} %gather_fusion.1) | data formatting | bytes 6553600 | tf_op jit(solution)/shard_map/gather | solution.py:344
  50.8 46.0 %all-to-all-done.1.fetched = bf16[32,400,128]{2,1,0:T(8,128)(2,1)S(1)} async-done(((bf16[32,400,128]{2,1,0:T(8,128)(2,1)}), bf16[32,400,128]{2,1,0:T(8,128)(2,1)S(1)}, u32[]{:S(2)}, u32[]{:S(2)}) %all-to-all-start.1) | async-done | bytes 3276832 | tf_op jit(solution)/shard_map/all_to_all | solution.py:341
  96.8 1.7 gather_negs.1
  98.6 1.3 collective-permute-start.1
  99.9 0.6 collective-permute-start.2
  100.5 1.2 collective-permute-start.3
  102.2 2.1 collective-permute-start.5
  104.3 0.9 collective-permute-start.6
  105.3 8.0 %gather_edges.1 = (bf16[400,2048]{1,0:T(8,128)(2,1)S(1)}, bf16[400,2048]{1,0:T(8,128)(2,1)S(1)}, f32[1,2048]{1,0:T(1,128)S(1)}) custom-call(bf16[400,2048]{1,0:T(8,128)(2,1)S(1)} %get-tuple-element.72.rows, s32[1,2048]{1,0:T(1,128)S(1)} %bitcast.24, s32[1,2048]{1,0:T(1,128)S(1)} %bitcast.29, f32[400,2048]{1,0:T(8,128)S(1)} %bitcast.21), custom_call_target="tpu_custom_call" | custom-call | flops 6710886400 | bytes 13107200 | tf_op jit(solution)/shard_map/gather_edges/pallas_call | solution.py:111
  113.4 6.2 %score.1 = (bf16[2,400,2048]{2,1,0:T(8,128)(2,1)S(1)}, bf16[2,400,2048]{2,1,0:T(8,128)(2,1)S(1)}, bf16[400,128]{1,0:T(8,128)(2,1)S(1)}, bf16[400,128]{1,0:T(8,12...) custom-call(bf16[400,128]{1,0:T(8,128)(2,1)S(1)} %get-tuple-element., ...), custom_call_target="tpu_custom_call" | custom-call | flops 5033164800 | bytes 9830400 | tf_op jit(solution)/shard_map/score/pallas_call | solution.py:158
  119.6 1.4 collective-permute-start.7
  121.5 0.9 collective-permute-start.9
  123.0 1.5 collective-permute-start.11
  124.5 0.8 collective-permute-start.12
  125.3 1.4 collective-permute-done.8.refs_2_
  126.8 6.4 %scatter.4.slots_ref = f32[400,1024]{1,0:T(8,128)S(1)} custom-call(s32[2]{0:T(128)S(1)} %slice.19.base_ref, bf16[2,400,2048]{2,1,0:T(8,128)(2,1)S(1)} %get-tuple-element.79.gs_ref, bf16[2,400,2048]{2,1,0:T(8,128)(2,1)S(1)} %get-tuple-element.80.gd_ref, s32[1,2048]{1,0:T(1,128)S(1)} %bitcast.25, s32[1,2048]{1,0:T(1,128)S(1)} %bitcast.30), custom_call_target="tpu_custom_call" | custom-call | flops 3355443200 | bytes 6553600 | tf_op jit(solution)/shard_map/scatter/pallas_call | solution.py:197
  133.3 1.0 collective-permute-done.11.refs_5_
  134.3 2.2 pack.4
  136.6 4.3 %scatter.5.slots_ref = f32[400,1024]{1,0:T(8,128)S(1)} custom-call(s32[2]{0:T(128)S(1)} %get-tuple-element.97.base_ref, bf16[2,400,2048]{2,1,0:T(8,128)(2,1)S(1)} %get-tuple-element.79.gs_ref, bf16[2,400,2048]{2,1,0:T(8,128)(2,1)S(1)} %get-tuple-element.80.gd_ref, s32[1,2048]{1,0:T(1,128)S(1)} %bitcast.26, s32[1,2048]{1,0:T(1,128)S(1)} %bitcast.31), custom_call_target="tpu_custom_call" | custom-call | flops 3355443200 | bytes 6553600 | tf_op jit(solution)/shard_map/scatter/pallas_call | solution.py:197
  140.9 0.9 collective-permute-start.15
  141.8 1.9 pack.5
  143.7 4.6 %collective-permute-start.21 = (s16[408,128]{1,0:T(8,128)(2,1)S(1)}, s16[408,128]{1,0:T(8,128)(2,1)S(1)}, u32[]{:S(2)}, u32[]{:S(2)}) collective-permute-start(s16[408,128]{1,0:T(8,128)(2,1)S(1)} %get-tuple-element.98), channel_id=1, source_target_pairs={{0,23},{1,22},{2,21},{3,20},{4,19},{5,18},{6,17},{7,16},{8,31},{9,... | collective-permute-start | bytes 313352 | tf_op jit(solution)/shard_map/ppermute | solution.py:375
  148.3 3.0 %collective-permute-start.22 = (s16[408,128]{1,0:T(8,128)(2,1)S(1)}, s16[408,128]{1,0:T(8,128)(2,1)S(1)}, u32[]{:S(2)}, u32[]{:S(2)}) collective-permute-start(s16[408,128]{1,0:T(8,128)(2,1)S(1)} %get-tuple-element.99), channel_id=1, source_target_pairs={{0,7},{1,6},{2,5},{3,4},{4,3},{5,2},{6,1},{7,0},{8,15},{9,14},{10,... | collective-permute-start | bytes 313352 | tf_op jit(solution)/shard_map/ppermute | solution.py:375
  151.3 0.9 collective-permute-start.24
  152.3 4.3 %scatter.6.slots_ref = f32[400,1024]{1,0:T(8,128)S(1)} custom-call(s32[2]{0:T(128)S(1)} %get-tuple-element.106.base_ref, bf16[2,400,2048]{2,1,0:T(8,128)(2,1)S(1)} %get-tuple-element.79.gs_ref, bf16[2,400,2048]{2,1,0:T(8,128)(2,1)S(1)} %get-tuple-element.80.gd_ref, s32[1,2048]{1,0:T(1,128)S(1)} %bitcast.27, s32[1,2048]{1,0:T(1,128)S(1)} %bitcast.32), custom_call_target="tpu_custom_call" | custom-call | flops 3355443200 | bytes 6553600 | tf_op jit(solution)/shard_map/scatter/pallas_call | solution.py:197
  156.6 1.7 pack.6
  158.3 3.0 %collective-permute-start.25 = (s16[408,128]{1,0:T(8,128)(2,1)S(1)}, s16[408,128]{1,0:T(8,128)(2,1)S(1)}, u32[]{:S(2)}, u32[]{:S(2)}) collective-permute-start(s16[408,128]{1,0:T(8,128)(2,1)S(1)} %get-tuple-element.102), channel_id=1, source_target_pairs={{0,21},{1,20},{2,23},{3,22},{4,17},{5,16},{6,19},{7,18},{8,29},{9,... | collective-permute-start | bytes 313352 | tf_op jit(solution)/shard_map/ppermute | solution.py:375
  161.3 5.1 %collective-permute-start.26 = (s16[408,128]{1,0:T(8,128)(2,1)S(1)}, s16[408,128]{1,0:T(8,128)(2,1)S(1)}, u32[]{:S(2)}, u32[]{:S(2)}) collective-permute-start(s16[408,128]{1,0:T(8,128)(2,1)S(1)} %get-tuple-element.103), channel_id=1, source_target_pairs={{0,5},{1,4},{2,7},{3,6},{4,1},{5,0},{6,3},{7,2},{8,13},{9,12},{10,... | collective-permute-start | bytes 313352 | tf_op jit(solution)/shard_map/ppermute | solution.py:375
  166.8 1.7 collective-permute-start.29
  168.5 3.4 %collective-permute-start.30 = (s16[408,128]{1,0:T(8,128)(2,1)S(1)}, s16[408,128]{1,0:T(8,128)(2,1)S(1)}, u32[]{:S(2)}, u32[]{:S(2)}) collective-permute-start(s16[408,128]{1,0:T(8,128)(2,1)S(1)} %get-tuple-element.108), channel_id=1, source_target_pairs={{0,11},{1,10},{2,9},{3,8},{4,15},{5,14},{6,13},{7,12},{8,3},{9,2},... | collective-permute-start | bytes 313352 | tf_op jit(solution)/shard_map/ppermute | solution.py:375
  171.9 0.7 collective-permute-start.31
  172.9 1.7 collective-permute-start.32
  174.6 2.0 collective-permute-start.33
  176.6 5.2 %collective-permute-start.34 = (s16[408,128]{1,0:T(8,128)(2,1)S(1)}, s16[408,128]{1,0:T(8,128)(2,1)S(1)}, u32[]{:S(2)}, u32[]{:S(2)}) collective-permute-start(s16[408,128]{1,0:T(8,128)(2,1)S(1)} %get-tuple-element.112), channel_id=1, source_target_pairs={{0,9},{1,8},{2,11},{3,10},{4,13},{5,12},{6,15},{7,14},{8,1},{9,0},... | collective-permute-start | bytes 313352 | tf_op jit(solution)/shard_map/ppermute | solution.py:375
  181.8 4.3 %scatter.7.slots_ref = f32[400,1024]{1,0:T(8,128)S(1)} custom-call(s32[2]{0:T(128)S(1)} %get-tuple-element.115.base_ref, bf16[2,400,2048]{2,1,0:T(8,128)(2,1)S(1)} %get-tuple-element.79.gs_ref, bf16[2,400,2048]{2,1,0:T(8,128)(2,1)S(1)} %get-tuple-element.80.gd_ref, s32[1,2048]{1,0:T(1,128)S(1)} %bitcast.28, s32[1,2048]{1,0:T(1,128)S(1)} %bitcast.33), custom_call_target="tpu_custom_call" | custom-call | flops 3355443200 | bytes 6553600 | tf_op jit(solution)/shard_map/scatter/pallas_call | solution.py:197
  186.1 2.2 pack.7
  188.3 1.2 collective-permute-start.35
  189.5 1.1 collective-permute-start.36
  190.6 1.5 collective-permute-start.37
  192.0 2.8 %collective-permute-start.38 = (s16[408,128]{1,0:T(8,128)(2,1)S(1)}, s16[408,128]{1,0:T(8,128)(2,1)S(1)}, u32[]{:S(2)}, u32[]{:S(2)}) collective-permute-start(s16[408,128]{1,0:T(8,128)(2,1)S(1)} %get-tuple-element.117), channel_id=1, source_target_pairs={{0,15},{1,14},{2,13},{3,12},{4,11},{5,10},{6,9},{7,8},{8,7},{9,6},... | collective-permute-start | bytes 313352 | tf_op jit(solution)/shard_map/ppermute | solution.py:375
  194.9 3.8 %collective-permute-start.39 = (s16[408,128]{1,0:T(8,128)(2,1)S(1)}, s16[408,128]{1,0:T(8,128)(2,1)S(1)}, u32[]{:S(2)}, u32[]{:S(2)}) collective-permute-start(s16[408,128]{1,0:T(8,128)(2,1)S(1)} %get-tuple-element.118), channel_id=1, source_target_pairs={{0,30},{1,31},{2,28},{3,29},{4,26},{5,27},{6,24},{7,25},{8,22},{9,... | collective-permute-start | bytes 313352 | tf_op jit(solution)/shard_map/ppermute | solution.py:375
  198.8 3.6 %collective-permute-start.41 = (s16[408,128]{1,0:T(8,128)(2,1)S(1)}, s16[408,128]{1,0:T(8,128)(2,1)S(1)}, u32[]{:S(2)}, u32[]{:S(2)}) collective-permute-start(s16[408,128]{1,0:T(8,128)(2,1)S(1)} %get-tuple-element.120), channel_id=1, source_target_pairs={{0,29},{1,28},{2,31},{3,30},{4,25},{5,24},{6,27},{7,26},{8,21},{9,... | collective-permute-start | bytes 313352 | tf_op jit(solution)/shard_map/ppermute | solution.py:375
  202.6 3.7 %collective-permute-start.43 = (s16[408,128]{1,0:T(8,128)(2,1)S(1)}, s16[408,128]{1,0:T(8,128)(2,1)S(1)}, u32[]{:S(2)}, u32[]{:S(2)}) collective-permute-start(s16[408,128]{1,0:T(8,128)(2,1)S(1)} %get-tuple-element.122), channel_id=1, source_target_pairs={{0,28},{1,29},{2,30},{3,31},{4,24},{5,25},{6,26},{7,27},{8,20},{9,... | collective-permute-start | bytes 313352 | tf_op jit(solution)/shard_map/ppermute | solution.py:375
  207.2 4.6 %collective-permute-start.16 = (s16[408,128]{1,0:T(8,128)(2,1)S(1)}, s16[408,128]{1,0:T(8,128)(2,1)S(1)}, u32[]{:S(2)}, u32[]{:S(2)}) collective-permute-start(s16[408,128]{1,0:T(8,128)(2,1)S(1)} %get-tuple-element.91), channel_id=1, source_target_pairs={{0,18},{1,19},{2,16},{3,17},{4,22},{5,23},{6,20},{7,21},{8,26},{9,... | collective-permute-start | bytes 313352 | tf_op jit(solution)/shard_map/ppermute | solution.py:375
  212.4 0.8 collective-permute-start.18
  213.1 1.8 collective-permute-done.43.refs_6_
  215.2 1.4 collective-permute-done.44.refs_7_
  216.5 1.2 collective-permute-start.20
  217.8 1.2 add.92.refs_8_
  219.0 1.0 add.93.refs_8_
  220.1 1.0 add.94.refs_8_
  221.1 4.3 %collective-permute-done.16.refs_2_ = s16[408,128]{1,0:T(8,128)(2,1)S(1)} collective-permute-done((s16[408,128]{1,0:T(8,128)(2,1)S(1)}, s16[408,128]{1,0:T(8,128)(2,1)S(1)}, u32[]{:S(2)}, u32[]{:S(2)}) %collective-permute-start.16) | collective-permute-done | bytes 104480 | tf_op jit(solution)/shard_map/ppermute | solution.py:375
  225.4 0.7 collective-permute-done.18.refs_4_
  226.1 2.6 %collective-permute-done.20.refs_6_ = s16[408,128]{1,0:T(8,128)(2,1)S(1)} collective-permute-done((s16[408,128]{1,0:T(8,128)(2,1)S(1)}, s16[408,128]{1,0:T(8,128)(2,1)S(1)}, u32[]{:S(2)}, u32[]{:S(2)}) %collective-permute-start.20) | collective-permute-done | bytes 104480 | tf_op jit(solution)/shard_map/ppermute | solution.py:375
  228.8 3.7 %update.1 = (f32[400,2048]{1,0:T(8,128)}, f32[1,2048]{1,0:T(1,128)}) custom-call(s32[32]{0:T(128)S(1)} %get-tuple-element.64.asked_ref, s16[408,128]{1,0:T(8,128)(2,1)S(1)} %collective-permute-done.14.refs_0_, s16[408,128]{1,0:T(8,128)(2,1)S(1)} %collective-permute-done.15.refs_1_, s16[408,128]{1,0:T(8,128)(2,1)S(1)} %collective-permute-done.16.refs_2_, ...), custom_call_target="tpu_custom_call" | custom-call | flops 52428800 | bytes 102400 | tf_op jit(solution)/shard_map/update/pallas_call | solution.py:316
  (90 shorter events, 6.0 us)
Async XLA Ops:
  2.0 14.4 %all-to-all-start = ((s32[32,1,1]{2,1,0:T(1,128)}), s32[32,1,1]{2,1,0:T(1,128)S(1)}, u32[]{:S(2)}, u32[]{:S(2)}) async-start(s32[32,1,1]{2,1,0:T(1,128)} %copy.28), calls=%async_computation | async-start | bytes 32768 | tf_op jit(solution)/shard_map/all_to_all | solution.py:336
  19.7 77.1 %all-to-all-start.1 = ((bf16[32,400,128]{2,1,0:T(8,128)(2,1)}), bf16[32,400,128]{2,1,0:T(8,128)(2,1)S(1)}, u32[]{:S(2)}, u32[]{:S(2)}) async-start(bf16[32,400,128]{2,1,0:T(8,128)(2,1)} %bitcast.34), calls=%async_computation.1 | async-start | bytes 6553600 | tf_op jit(solution)/shard_map/all_to_all | solution.py:341
  22.5 8.6 %copy-start.5 = (s32[2048]{0:T(1024)S(1)}, s32[2048]{0:T(1024)}, u32[]{:S(2)}) copy-start(s32[2048]{0:T(1024)} %param.12) | copy-start | bytes 24580
  44.0 5.3 %copy-start.3 = (s32[2048]{0:T(1024)S(1)}, s32[2048]{0:T(1024)}, u32[]{:S(2)}) copy-start(s32[2048]{0:T(1024)} %param.14) | copy-start | bytes 24580
  44.0 5.4 %copy-start.7 = (s32[32]{0:T(128)S(1)}, s32[32]{0:T(128)}, u32[]{:S(2)}) copy-start(s32[32]{0:T(128)} %constant.85.clone) | copy-start | bytes 388
  44.0 6.1 %copy-start.6 = (s32[128]{0:T(128)S(1)}, s32[128]{0:T(128)}, u32[]{:S(2)}) copy-start(s32[128]{0:T(128)} %param.16) | copy-start | bytes 1540
  44.0 6.2 %copy-start.4 = (s32[2048]{0:T(1024)S(1)}, s32[2048]{0:T(1024)}, u32[]{:S(2)}) copy-start(s32[2048]{0:T(1024)} %param.15) | copy-start | bytes 24580
  96.8 8.5 %copy-start.1 = (f32[2048,400]{0,1:T(8,128)S(1)}, f32[2048,400]{0,1:T(8,128)}, u32[]{:S(2)}) copy-start(f32[2048,400]{0,1:T(8,128)} %copy.31) | copy-start | bytes 9830404
  98.5 3.6 %collective-permute-start = (bf16[400,128]{1,0:T(8,128)(2,1)S(1)}, bf16[400,128]{1,0:T(8,128)(2,1)S(1)}, u32[]{:S(2)}, u32[]{:S(2)}) collective-permute-start(bf16[400,128]{1,0:T(8,128)(2,1)S(1)} %get-tuple-element.71.refs_0_), channel_id=1, source_target_pairs={{0,1},{1,0},{2,3},{3,2},{4,5},{5,4},{6,7},{7,6},{8,9},{9,8},{10,11... | collective-permute-start | bytes 307208 | tf_op jit(solution)/shard_map/ppermute | solution.py:375
  98.6 5.7 %collective-permute-start.1 = (bf16[400,128]{1,0:T(8,128)(2,1)S(1)}, bf16[400,128]{1,0:T(8,128)(2,1)S(1)}, u32[]{:S(2)}, u32[]{:S(2)}) collective-permute-start(bf16[400,128]{1,0:T(8,128)(2,1)S(1)} %get-tuple-element.71.refs_0_), channel_id=1, source_target_pairs={{0,2},{1,3},{2,0},{3,1},{4,6},{5,7},{6,4},{7,5},{8,10},{9,11},{10,... | collective-permute-start | bytes 307208 | tf_op jit(solution)/shard_map/ppermute | solution.py:375
  99.9 13.5 %collective-permute-start.2 = (bf16[400,128]{1,0:T(8,128)(2,1)S(1)}, bf16[400,128]{1,0:T(8,128)(2,1)S(1)}, u32[]{:S(2)}, u32[]{:S(2)}) collective-permute-start(bf16[400,128]{1,0:T(8,128)(2,1)S(1)} %get-tuple-element.71.refs_0_), channel_id=1, source_target_pairs={{0,3},{1,2},{2,1},{3,0},{4,7},{5,6},{6,5},{7,4},{8,11},{9,10},{10,... | collective-permute-start | bytes 307208 | tf_op jit(solution)/shard_map/ppermute | solution.py:375
  100.5 12.9 %collective-permute-start.3 = (bf16[400,128]{1,0:T(8,128)(2,1)S(1)}, bf16[400,128]{1,0:T(8,128)(2,1)S(1)}, u32[]{:S(2)}, u32[]{:S(2)}) collective-permute-start(bf16[400,128]{1,0:T(8,128)(2,1)S(1)} %get-tuple-element.71.refs_0_), channel_id=1, source_target_pairs={{0,4},{1,5},{2,6},{3,7},{4,0},{5,1},{6,2},{7,3},{8,12},{9,13},{10,... | collective-permute-start | bytes 307208 | tf_op jit(solution)/shard_map/ppermute | solution.py:375
  101.6 11.7 %collective-permute-start.4 = (bf16[400,128]{1,0:T(8,128)(2,1)S(1)}, bf16[400,128]{1,0:T(8,128)(2,1)S(1)}, u32[]{:S(2)}, u32[]{:S(2)}) collective-permute-start(bf16[400,128]{1,0:T(8,128)(2,1)S(1)} %get-tuple-element.71.refs_0_), channel_id=1, source_target_pairs={{0,5},{1,4},{2,7},{3,6},{4,1},{5,0},{6,3},{7,2},{8,13},{9,12},{10,... | collective-permute-start | bytes 307208 | tf_op jit(solution)/shard_map/ppermute | solution.py:375
  102.2 11.2 %collective-permute-start.5 = (bf16[400,128]{1,0:T(8,128)(2,1)S(1)}, bf16[400,128]{1,0:T(8,128)(2,1)S(1)}, u32[]{:S(2)}, u32[]{:S(2)}) collective-permute-start(bf16[400,128]{1,0:T(8,128)(2,1)S(1)} %get-tuple-element.71.refs_0_), channel_id=1, source_target_pairs={{0,6},{1,7},{2,4},{3,5},{4,2},{5,3},{6,0},{7,1},{8,14},{9,15},{10,... | collective-permute-start | bytes 307208 | tf_op jit(solution)/shard_map/ppermute | solution.py:375
  104.3 9.0 %collective-permute-start.6 = (bf16[400,128]{1,0:T(8,128)(2,1)S(1)}, bf16[400,128]{1,0:T(8,128)(2,1)S(1)}, u32[]{:S(2)}, u32[]{:S(2)}) collective-permute-start(bf16[400,128]{1,0:T(8,128)(2,1)S(1)} %get-tuple-element.71.refs_0_), channel_id=1, source_target_pairs={{0,7},{1,6},{2,5},{3,4},{4,3},{5,2},{6,1},{7,0},{8,15},{9,14},{10,... | collective-permute-start | bytes 307208 | tf_op jit(solution)/shard_map/ppermute | solution.py:375
  119.6 4.9 %collective-permute-start.7 = (bf16[400,128]{1,0:T(8,128)(2,1)S(1)}, bf16[400,128]{1,0:T(8,128)(2,1)S(1)}, u32[]{:S(2)}, u32[]{:S(2)}) collective-permute-start(bf16[400,128]{1,0:T(8,128)(2,1)S(1)} %get-tuple-element.82), channel_id=1, source_target_pairs={{0,1},{1,0},{2,3},{3,2},{4,5},{5,4},{6,7},{7,6},{8,9},{9,8},{10,11... | collective-permute-start | bytes 307208 | tf_op jit(solution)/shard_map/ppermute | solution.py:375
  121.0 5.7 %collective-permute-start.8 = (bf16[400,128]{1,0:T(8,128)(2,1)S(1)}, bf16[400,128]{1,0:T(8,128)(2,1)S(1)}, u32[]{:S(2)}, u32[]{:S(2)}) collective-permute-start(bf16[400,128]{1,0:T(8,128)(2,1)S(1)} %get-tuple-element.83), channel_id=1, source_target_pairs={{0,2},{1,3},{2,0},{3,1},{4,6},{5,7},{6,4},{7,5},{8,10},{9,11},{10,... | collective-permute-start | bytes 307208 | tf_op jit(solution)/shard_map/ppermute | solution.py:375
  121.5 11.7 %collective-permute-start.9 = (bf16[400,128]{1,0:T(8,128)(2,1)S(1)}, bf16[400,128]{1,0:T(8,128)(2,1)S(1)}, u32[]{:S(2)}, u32[]{:S(2)}) collective-permute-start(bf16[400,128]{1,0:T(8,128)(2,1)S(1)} %get-tuple-element.84), channel_id=1, source_target_pairs={{0,3},{1,2},{2,1},{3,0},{4,7},{5,6},{6,5},{7,4},{8,11},{9,10},{10,... | collective-permute-start | bytes 307208 | tf_op jit(solution)/shard_map/ppermute | solution.py:375
  122.4 10.8 %collective-permute-start.10 = (bf16[400,128]{1,0:T(8,128)(2,1)S(1)}, bf16[400,128]{1,0:T(8,128)(2,1)S(1)}, u32[]{:S(2)}, u32[]{:S(2)}) collective-permute-start(bf16[400,128]{1,0:T(8,128)(2,1)S(1)} %get-tuple-element.85), channel_id=1, source_target_pairs={{0,4},{1,5},{2,6},{3,7},{4,0},{5,1},{6,2},{7,3},{8,12},{9,13},{10,... | collective-permute-start | bytes 307208 | tf_op jit(solution)/shard_map/ppermute | solution.py:375
  123.0 11.3 %collective-permute-start.11 = (bf16[400,128]{1,0:T(8,128)(2,1)S(1)}, bf16[400,128]{1,0:T(8,128)(2,1)S(1)}, u32[]{:S(2)}, u32[]{:S(2)}) collective-permute-start(bf16[400,128]{1,0:T(8,128)(2,1)S(1)} %get-tuple-element.86), channel_id=1, source_target_pairs={{0,5},{1,4},{2,7},{3,6},{4,1},{5,0},{6,3},{7,2},{8,13},{9,12},{10,... | collective-permute-start | bytes 307208 | tf_op jit(solution)/shard_map/ppermute | solution.py:375
  124.5 9.7 %collective-permute-start.12 = (bf16[400,128]{1,0:T(8,128)(2,1)S(1)}, bf16[400,128]{1,0:T(8,128)(2,1)S(1)}, u32[]{:S(2)}, u32[]{:S(2)}) collective-permute-start(bf16[400,128]{1,0:T(8,128)(2,1)S(1)} %get-tuple-element.87), channel_id=1, source_target_pairs={{0,6},{1,7},{2,4},{3,5},{4,2},{5,3},{6,0},{7,1},{8,14},{9,15},{10,... | collective-permute-start | bytes 307208 | tf_op jit(solution)/shard_map/ppermute | solution.py:375
  126.7 7.5 %collective-permute-start.13 = (bf16[400,128]{1,0:T(8,128)(2,1)S(1)}, bf16[400,128]{1,0:T(8,128)(2,1)S(1)}, u32[]{:S(2)}, u32[]{:S(2)}) collective-permute-start(bf16[400,128]{1,0:T(8,128)(2,1)S(1)} %get-tuple-element.88), channel_id=1, source_target_pairs={{0,7},{1,6},{2,5},{3,4},{4,3},{5,2},{6,1},{7,0},{8,15},{9,14},{10,... | collective-permute-start | bytes 307208 | tf_op jit(solution)/shard_map/ppermute | solution.py:375
  136.5 14.8 %collective-permute-start.14 = (s16[408,128]{1,0:T(8,128)(2,1)S(1)}, s16[408,128]{1,0:T(8,128)(2,1)S(1)}, u32[]{:S(2)}, u32[]{:S(2)}) collective-permute-start(s16[408,128]{1,0:T(8,128)(2,1)S(1)} %get-tuple-element.89), channel_id=1, source_target_pairs={{0,19},{1,18},{2,17},{3,16},{4,23},{5,22},{6,21},{7,20},{8,27},{9,... | collective-permute-start | bytes 313352 | tf_op jit(solution)/shard_map/ppermute | solution.py:375
  140.9 17.4 %collective-permute-start.15 = (s16[408,128]{1,0:T(8,128)(2,1)S(1)}, s16[408,128]{1,0:T(8,128)(2,1)S(1)}, u32[]{:S(2)}, u32[]{:S(2)}) collective-permute-start(s16[408,128]{1,0:T(8,128)(2,1)S(1)} %get-tuple-element.90), channel_id=1, source_target_pairs={{0,3},{1,2},{2,1},{3,0},{4,7},{5,6},{6,5},{7,4},{8,11},{9,10},{10,... | collective-permute-start | bytes 313352 | tf_op jit(solution)/shard_map/ppermute | solution.py:375
  143.7 17.6 %collective-permute-start.21 = (s16[408,128]{1,0:T(8,128)(2,1)S(1)}, s16[408,128]{1,0:T(8,128)(2,1)S(1)}, u32[]{:S(2)}, u32[]{:S(2)}) collective-permute-start(s16[408,128]{1,0:T(8,128)(2,1)S(1)} %get-tuple-element.98), channel_id=1, source_target_pairs={{0,23},{1,22},{2,21},{3,20},{4,19},{5,18},{6,17},{7,16},{8,31},{9,... | collective-permute-start | bytes 313352 | tf_op jit(solution)/shard_map/ppermute | solution.py:375
  148.3 18.0 %collective-permute-start.22 = (s16[408,128]{1,0:T(8,128)(2,1)S(1)}, s16[408,128]{1,0:T(8,128)(2,1)S(1)}, u32[]{:S(2)}, u32[]{:S(2)}) collective-permute-start(s16[408,128]{1,0:T(8,128)(2,1)S(1)} %get-tuple-element.99), channel_id=1, source_target_pairs={{0,7},{1,6},{2,5},{3,4},{4,3},{5,2},{6,1},{7,0},{8,15},{9,14},{10,... | collective-permute-start | bytes 313352 | tf_op jit(solution)/shard_map/ppermute | solution.py:375
  151.3 15.0 %collective-permute-start.23 = (s16[408,128]{1,0:T(8,128)(2,1)S(1)}, s16[408,128]{1,0:T(8,128)(2,1)S(1)}, u32[]{:S(2)}, u32[]{:S(2)}) collective-permute-start(s16[408,128]{1,0:T(8,128)(2,1)S(1)} %get-tuple-element.100), channel_id=1, source_target_pairs={{0,22},{1,23},{2,20},{3,21},{4,18},{5,19},{6,16},{7,17},{8,30},{9,... | collective-permute-start | bytes 313352 | tf_op jit(solution)/shard_map/ppermute | solution.py:375
  151.3 15.5 %collective-permute-start.24 = (s16[408,128]{1,0:T(8,128)(2,1)S(1)}, s16[408,128]{1,0:T(8,128)(2,1)S(1)}, u32[]{:S(2)}, u32[]{:S(2)}) collective-permute-start(s16[408,128]{1,0:T(8,128)(2,1)S(1)} %get-tuple-element.101), channel_id=1, source_target_pairs={{0,6},{1,7},{2,4},{3,5},{4,2},{5,3},{6,0},{7,1},{8,14},{9,15},{10,... | collective-permute-start | bytes 313352 | tf_op jit(solution)/shard_map/ppermute | solution.py:375
  158.3 10.2 %collective-permute-start.25 = (s16[408,128]{1,0:T(8,128)(2,1)S(1)}, s16[408,128]{1,0:T(8,128)(2,1)S(1)}, u32[]{:S(2)}, u32[]{:S(2)}) collective-permute-start(s16[408,128]{1,0:T(8,128)(2,1)S(1)} %get-tuple-element.102), channel_id=1, source_target_pairs={{0,21},{1,20},{2,23},{3,22},{4,17},{5,16},{6,19},{7,18},{8,29},{9,... | collective-permute-start | bytes 313352 | tf_op jit(solution)/shard_map/ppermute | solution.py:375
  161.3 10.6 %collective-permute-start.26 = (s16[408,128]{1,0:T(8,128)(2,1)S(1)}, s16[408,128]{1,0:T(8,128)(2,1)S(1)}, u32[]{:S(2)}, u32[]{:S(2)}) collective-permute-start(s16[408,128]{1,0:T(8,128)(2,1)S(1)} %get-tuple-element.103), channel_id=1, source_target_pairs={{0,5},{1,4},{2,7},{3,6},{4,1},{5,0},{6,3},{7,2},{8,13},{9,12},{10,... | collective-permute-start | bytes 313352 | tf_op jit(solution)/shard_map/ppermute | solution.py:375
  166.3 6.6 %collective-permute-start.27 = (s16[408,128]{1,0:T(8,128)(2,1)S(1)}, s16[408,128]{1,0:T(8,128)(2,1)S(1)}, u32[]{:S(2)}, u32[]{:S(2)}) collective-permute-start(s16[408,128]{1,0:T(8,128)(2,1)S(1)} %get-tuple-element.104), channel_id=1, source_target_pairs={{0,20},{1,21},{2,22},{3,23},{4,16},{5,17},{6,18},{7,19},{8,28},{9,... | collective-permute-start | bytes 313352 | tf_op jit(solution)/shard_map/ppermute | solution.py:375
  166.3 8.3 %collective-permute-start.28 = (s16[408,128]{1,0:T(8,128)(2,1)S(1)}, s16[408,128]{1,0:T(8,128)(2,1)S(1)}, u32[]{:S(2)}, u32[]{:S(2)}) collective-permute-start(s16[408,128]{1,0:T(8,128)(2,1)S(1)} %get-tuple-element.105), channel_id=1, source_target_pairs={{0,4},{1,5},{2,6},{3,7},{4,0},{5,1},{6,2},{7,3},{8,12},{9,13},{10,... | collective-permute-start | bytes 313352 | tf_op jit(solution)/shard_map/ppermute | solution.py:375
  166.8 9.8 %collective-permute-start.29 = (s16[408,128]{1,0:T(8,128)(2,1)S(1)}, s16[408,128]{1,0:T(8,128)(2,1)S(1)}, u32[]{:S(2)}, u32[]{:S(2)}) collective-permute-start(s16[408,128]{1,0:T(8,128)(2,1)S(1)} %get-tuple-element.107), channel_id=1, source_target_pairs={{0,27},{1,26},{2,25},{3,24},{4,31},{5,30},{6,29},{7,28},{8,19},{9,... | collective-permute-start | bytes 313352 | tf_op jit(solution)/shard_map/ppermute | solution.py:375
  168.5 19.8 %collective-permute-start.30 = (s16[408,128]{1,0:T(8,128)(2,1)S(1)}, s16[408,128]{1,0:T(8,128)(2,1)S(1)}, u32[]{:S(2)}, u32[]{:S(2)}) collective-permute-start(s16[408,128]{1,0:T(8,128)(2,1)S(1)} %get-tuple-element.108), channel_id=1, source_target_pairs={{0,11},{1,10},{2,9},{3,8},{4,15},{5,14},{6,13},{7,12},{8,3},{9,2},... | collective-permute-start | bytes 313352 | tf_op jit(solution)/shard_map/ppermute | solution.py:375
  171.9 17.6 %collective-permute-start.31 = (s16[408,128]{1,0:T(8,128)(2,1)S(1)}, s16[408,128]{1,0:T(8,128)(2,1)S(1)}, u32[]{:S(2)}, u32[]{:S(2)}) collective-permute-start(s16[408,128]{1,0:T(8,128)(2,1)S(1)} %get-tuple-element.109), channel_id=1, source_target_pairs={{0,26},{1,27},{2,24},{3,25},{4,30},{5,31},{6,28},{7,29},{8,18},{9,... | collective-permute-start | bytes 313352 | tf_op jit(solution)/shard_map/ppermute | solution.py:375
  172.9 17.6 %collective-permute-start.32 = (s16[408,128]{1,0:T(8,128)(2,1)S(1)}, s16[408,128]{1,0:T(8,128)(2,1)S(1)}, u32[]{:S(2)}, u32[]{:S(2)}) collective-permute-start(s16[408,128]{1,0:T(8,128)(2,1)S(1)} %get-tuple-element.110), channel_id=1, source_target_pairs={{0,10},{1,11},{2,8},{3,9},{4,14},{5,15},{6,12},{7,13},{8,2},{9,3},... | collective-permute-start | bytes 313352 | tf_op jit(solution)/shard_map/ppermute | solution.py:375
  174.6 17.4 %collective-permute-start.33 = (s16[408,128]{1,0:T(8,128)(2,1)S(1)}, s16[408,128]{1,0:T(8,128)(2,1)S(1)}, u32[]{:S(2)}, u32[]{:S(2)}) collective-permute-start(s16[408,128]{1,0:T(8,128)(2,1)S(1)} %get-tuple-element.111), channel_id=1, source_target_pairs={{0,25},{1,24},{2,27},{3,26},{4,29},{5,28},{6,31},{7,30},{8,17},{9,... | collective-permute-start | bytes 313352 | tf_op jit(solution)/shard_map/ppermute | solution.py:375
  176.6 18.3 %collective-permute-start.34 = (s16[408,128]{1,0:T(8,128)(2,1)S(1)}, s16[408,128]{1,0:T(8,128)(2,1)S(1)}, u32[]{:S(2)}, u32[]{:S(2)}) collective-permute-start(s16[408,128]{1,0:T(8,128)(2,1)S(1)} %get-tuple-element.112), channel_id=1, source_target_pairs={{0,9},{1,8},{2,11},{3,10},{4,13},{5,12},{6,15},{7,14},{8,1},{9,0},... | collective-permute-start | bytes 313352 | tf_op jit(solution)/shard_map/ppermute | solution.py:375
  188.3 10.4 %collective-permute-start.35 = (s16[408,128]{1,0:T(8,128)(2,1)S(1)}, s16[408,128]{1,0:T(8,128)(2,1)S(1)}, u32[]{:S(2)}, u32[]{:S(2)}) collective-permute-start(s16[408,128]{1,0:T(8,128)(2,1)S(1)} %get-tuple-element.113), channel_id=1, source_target_pairs={{0,24},{1,25},{2,26},{3,27},{4,28},{5,29},{6,30},{7,31},{8,16},{9,... | collective-permute-start | bytes 313352 | tf_op jit(solution)/shard_map/ppermute | solution.py:375
  189.5 9.4 %collective-permute-start.36 = (s16[408,128]{1,0:T(8,128)(2,1)S(1)}, s16[408,128]{1,0:T(8,128)(2,1)S(1)}, u32[]{:S(2)}, u32[]{:S(2)}) collective-permute-start(s16[408,128]{1,0:T(8,128)(2,1)S(1)} %get-tuple-element.114), channel_id=1, source_target_pairs={{0,8},{1,9},{2,10},{3,11},{4,12},{5,13},{6,14},{7,15},{8,0},{9,1},... | collective-permute-start | bytes 313352 | tf_op jit(solution)/shard_map/ppermute | solution.py:375
  190.6 11.9 %collective-permute-start.37 = (s16[408,128]{1,0:T(8,128)(2,1)S(1)}, s16[408,128]{1,0:T(8,128)(2,1)S(1)}, u32[]{:S(2)}, u32[]{:S(2)}) collective-permute-start(s16[408,128]{1,0:T(8,128)(2,1)S(1)} %get-tuple-element.116), channel_id=1, source_target_pairs={{0,31},{1,30},{2,29},{3,28},{4,27},{5,26},{6,25},{7,24},{8,23},{9,... | collective-permute-start | bytes 313352 | tf_op jit(solution)/shard_map/ppermute | solution.py:375
  192.0 10.5 %collective-permute-start.38 = (s16[408,128]{1,0:T(8,128)(2,1)S(1)}, s16[408,128]{1,0:T(8,128)(2,1)S(1)}, u32[]{:S(2)}, u32[]{:S(2)}) collective-permute-start(s16[408,128]{1,0:T(8,128)(2,1)S(1)} %get-tuple-element.117), channel_id=1, source_target_pairs={{0,15},{1,14},{2,13},{3,12},{4,11},{5,10},{6,9},{7,8},{8,7},{9,6},... | collective-permute-start | bytes 313352 | tf_op jit(solution)/shard_map/ppermute | solution.py:375
  194.9 11.4 %collective-permute-start.39 = (s16[408,128]{1,0:T(8,128)(2,1)S(1)}, s16[408,128]{1,0:T(8,128)(2,1)S(1)}, u32[]{:S(2)}, u32[]{:S(2)}) collective-permute-start(s16[408,128]{1,0:T(8,128)(2,1)S(1)} %get-tuple-element.118), channel_id=1, source_target_pairs={{0,30},{1,31},{2,28},{3,29},{4,26},{5,27},{6,24},{7,25},{8,22},{9,... | collective-permute-start | bytes 313352 | tf_op jit(solution)/shard_map/ppermute | solution.py:375
  198.7 8.5 %collective-permute-start.40 = (s16[408,128]{1,0:T(8,128)(2,1)S(1)}, s16[408,128]{1,0:T(8,128)(2,1)S(1)}, u32[]{:S(2)}, u32[]{:S(2)}) collective-permute-start(s16[408,128]{1,0:T(8,128)(2,1)S(1)} %get-tuple-element.119), channel_id=1, source_target_pairs={{0,14},{1,15},{2,12},{3,13},{4,10},{5,11},{6,8},{7,9},{8,6},{9,7},... | collective-permute-start | bytes 313352 | tf_op jit(solution)/shard_map/ppermute | solution.py:375
  198.8 13.0 %collective-permute-start.41 = (s16[408,128]{1,0:T(8,128)(2,1)S(1)}, s16[408,128]{1,0:T(8,128)(2,1)S(1)}, u32[]{:S(2)}, u32[]{:S(2)}) collective-permute-start(s16[408,128]{1,0:T(8,128)(2,1)S(1)} %get-tuple-element.120), channel_id=1, source_target_pairs={{0,29},{1,28},{2,31},{3,30},{4,25},{5,24},{6,27},{7,26},{8,21},{9,... | collective-permute-start | bytes 313352 | tf_op jit(solution)/shard_map/ppermute | solution.py:375
  202.5 9.9 %collective-permute-start.42 = (s16[408,128]{1,0:T(8,128)(2,1)S(1)}, s16[408,128]{1,0:T(8,128)(2,1)S(1)}, u32[]{:S(2)}, u32[]{:S(2)}) collective-permute-start(s16[408,128]{1,0:T(8,128)(2,1)S(1)} %get-tuple-element.121), channel_id=1, source_target_pairs={{0,13},{1,12},{2,15},{3,14},{4,9},{5,8},{6,11},{7,10},{8,5},{9,4},... | collective-permute-start | bytes 313352 | tf_op jit(solution)/shard_map/ppermute | solution.py:375
  202.6 12.4 %collective-permute-start.43 = (s16[408,128]{1,0:T(8,128)(2,1)S(1)}, s16[408,128]{1,0:T(8,128)(2,1)S(1)}, u32[]{:S(2)}, u32[]{:S(2)}) collective-permute-start(s16[408,128]{1,0:T(8,128)(2,1)S(1)} %get-tuple-element.122), channel_id=1, source_target_pairs={{0,28},{1,29},{2,30},{3,31},{4,24},{5,25},{6,26},{7,27},{8,20},{9,... | collective-permute-start | bytes 313352 | tf_op jit(solution)/shard_map/ppermute | solution.py:375
  206.3 10.3 %collective-permute-start.44 = (s16[408,128]{1,0:T(8,128)(2,1)S(1)}, s16[408,128]{1,0:T(8,128)(2,1)S(1)}, u32[]{:S(2)}, u32[]{:S(2)}) collective-permute-start(s16[408,128]{1,0:T(8,128)(2,1)S(1)} %get-tuple-element.123), channel_id=1, source_target_pairs={{0,12},{1,13},{2,14},{3,15},{4,8},{5,9},{6,10},{7,11},{8,4},{9,5},... | collective-permute-start | bytes 313352 | tf_op jit(solution)/shard_map/ppermute | solution.py:375
  207.2 18.2 %collective-permute-start.16 = (s16[408,128]{1,0:T(8,128)(2,1)S(1)}, s16[408,128]{1,0:T(8,128)(2,1)S(1)}, u32[]{:S(2)}, u32[]{:S(2)}) collective-permute-start(s16[408,128]{1,0:T(8,128)(2,1)S(1)} %get-tuple-element.91), channel_id=1, source_target_pairs={{0,18},{1,19},{2,16},{3,17},{4,22},{5,23},{6,20},{7,21},{8,26},{9,... | collective-permute-start | bytes 313352 | tf_op jit(solution)/shard_map/ppermute | solution.py:375
  211.8 13.6 %collective-permute-start.17 = (s16[408,128]{1,0:T(8,128)(2,1)S(1)}, s16[408,128]{1,0:T(8,128)(2,1)S(1)}, u32[]{:S(2)}, u32[]{:S(2)}) collective-permute-start(s16[408,128]{1,0:T(8,128)(2,1)S(1)} %get-tuple-element.92), channel_id=1, source_target_pairs={{0,2},{1,3},{2,0},{3,1},{4,6},{5,7},{6,4},{7,5},{8,10},{9,11},{10,... | collective-permute-start | bytes 313352 | tf_op jit(solution)/shard_map/ppermute | solution.py:375
  212.4 13.8 %collective-permute-start.18 = (s16[408,128]{1,0:T(8,128)(2,1)S(1)}, s16[408,128]{1,0:T(8,128)(2,1)S(1)}, u32[]{:S(2)}, u32[]{:S(2)}) collective-permute-start(s16[408,128]{1,0:T(8,128)(2,1)S(1)} %get-tuple-element.93), channel_id=1, source_target_pairs={{0,17},{1,16},{2,19},{3,18},{4,21},{5,20},{6,23},{7,22},{8,25},{9,... | collective-permute-start | bytes 313352 | tf_op jit(solution)/shard_map/ppermute | solution.py:375
  215.0 11.2 %collective-permute-start.19 = (s16[408,128]{1,0:T(8,128)(2,1)S(1)}, s16[408,128]{1,0:T(8,128)(2,1)S(1)}, u32[]{:S(2)}, u32[]{:S(2)}) collective-permute-start(s16[408,128]{1,0:T(8,128)(2,1)S(1)} %get-tuple-element.94), channel_id=1, source_target_pairs={{0,1},{1,0},{2,3},{3,2},{4,5},{5,4},{6,7},{7,6},{8,9},{9,8},{10,11... | collective-permute-start | bytes 313352 | tf_op jit(solution)/shard_map/ppermute | solution.py:375
  216.5 12.3 %collective-permute-start.20 = (s16[408,128]{1,0:T(8,128)(2,1)S(1)}, s16[408,128]{1,0:T(8,128)(2,1)S(1)}, u32[]{:S(2)}, u32[]{:S(2)}) collective-permute-start(s16[408,128]{1,0:T(8,128)(2,1)S(1)} %get-tuple-element.95), channel_id=1, source_target_pairs={{0,16},{1,17},{2,18},{3,19},{4,20},{5,21},{6,22},{7,23},{8,24},{9,... | collective-permute-start | bytes 313352 | tf_op jit(solution)/shard_map/ppermute | solution.py:375
  220.1 8.7 %copy-start = (f32[2048,400]{0,1:T(8,128)S(1)}, f32[2048,400]{0,1:T(8,128)}, u32[]{:S(2)}) copy-start(f32[2048,400]{0,1:T(8,128)} %param.9) | copy-start | bytes 9830404
  220.1 8.7 %copy-start.2 = (f32[2048]{0:T(1024)S(1)}, f32[2048]{0:T(1024)}, u32[]{:S(2)}) copy-start(f32[2048]{0:T(1024)} %param.10) | copy-start | bytes 24580

commit v4 on v3

--- a/solution.py
+++ b/solution.py
@@ -9,7 +9,7 @@
 
 BLK = 128
 TAIL = 8
-GROUPS = 4
+CUTS = (1, 1, 2, 2, 2)
 TILE = 256
 AXES = ("src", "dst")
 F32 = jnp.float32
@@ -357,15 +357,16 @@
         jnp.where((rank[None, :] == slot[:, None]) & (alive[None, :] > 0), partners[None, :], 0), axis=1
     )
     asked = jnp.sum(jnp.where(seat, asked[None, :], 0), axis=1)
-    group = devices // GROUPS
-    starts = jnp.concatenate([rank[::group], jnp.full((1,), named, jnp.int32)])
+    sizes = [cut * devices // sum(CUTS) for cut in CUTS]
+    firsts = [sum(sizes[:g]) for g in range(len(sizes))]
+    starts = [rank[first] for first in firsts] + [jnp.int32(named)]
 
     def compact(pos):
         where = jnp.sum(jnp.where((pos // BLK)[:, None] == ids[None, :], place[None, :], 0), axis=1)
         return (where * BLK + pos % BLK).reshape(1, -1)
 
     spos, dpos, npos = compact(src_pos), compact(dst_pos), compact(neg_pos)
-    bases = [starts[g : g + 2] for g in range(GROUPS)]
+    bases = [jnp.stack(starts[g : g + 2]) for g in range(len(sizes))]
     fetched, operator, live, rank, alive, asked, spos, dpos, npos, bases = lax.optimization_barrier(
         (fetched, operator, live, rank, alive, asked, spos, dpos, npos, bases)
     )
@@ -381,20 +382,25 @@
     grads_src, grads_dst, part_negs = score(negs, source, target, operator, g_pos)
     own_grad = [part_negs[0]] + [swap(part_negs[shift], shift, "dst") for shift in range(1, peers)]
     grad = None
-    for g in range(GROUPS):
-        first = g * group
-        slots = scatter(bases[g], grads_src, grads_dst, spos, dpos, min(group, named))
+    backs = []
+    for g, (first, group) in enumerate(zip(firsts, sizes)):
+        base = bases[g]
+        if g:
+            ahead = len(backs) // 2
+            base, backs[:ahead] = lax.optimization_barrier((base, backs[:ahead]))
+        if g > 1:
+            base, grad = lax.optimization_barrier((base, grad))
+        slots = scatter(base, grads_src, grads_dst, spos, dpos, min(group, named))
         packed = pack(first, group, rank, alive, slots, own_grad, npos)
+        if g:
+            grad = add(firsts[g - 1], asked, backs, grad, width, rows_dev)
         backs = [
             swap(x, shift, AXES) if shift else x
             for x, shift in zip(packed, order[first : first + group])
         ]
-        if g < GROUPS - 1:
-            grad = add(first, asked, backs, grad, width, rows_dev)
-        else:
-            new_table, new_state = update(
-                first, asked, backs, grad, table.T, state.reshape(1, rows_dev)
-            )
+    new_table, new_state = update(
+        firsts[-1], asked, backs, grad, table.T, state.reshape(1, rows_dev)
+    )
     return (new_table.T, new_state.reshape(rows_dev))
 
 

time: 234 us -> 243 us (1.038)
  waiting for transfers between devices: 65.3 us -> 72.1 us
  other arithmetic: 3.94 us -> 8.4 us
    ppermute x45, waiting for transfers between devices: 14.3 us -> 26.1 us  [swap(): return lax.ppermute(x, axis, [(i, i ^ shift) for i in range(count)])]
    all_to_all x1, waiting for transfers between devices: 46 us -> 41.1 us  [per_device(): lax.all_to_all(outgoing.transpose(0, 2, 1), AXES, split_axis=0, concat_ax...]
    another operation x0 -> x3, other arithmetic: none -> 4.54 us  [per_device(): bases = [jnp.stack(starts[g:g + 2]) for g in range(len(sizes))]]
    ppermute x45, starting transfers between devices: 70.8 us -> 68.3 us  [swap(): return lax.ppermute(x, axis, [(i, i ^ shift) for i in range(count)])]
    pallas_call x4 -> x5, Pallas kernels: 7.97 us -> 8.65 us  [pack(): pl.pallas_call(functools.partial(pack_kernel, first), out_shape=(jax.Shap...]
    pallas_call x4 -> x5, Pallas kernels: 19.4 us -> 19.9 us  [scatter(): pl.pallas_call(scatter_kernel, out_shape=jax.ShapeDtypeStruct((width, row...]
  transfers between devices with their start and end apart: 47 -> 47, of which waited for: 12 -> 14; matrix products, arithmetic and copies ran while one was open for 13% -> 14% of each run, Pallas kernels for 16% -> 16%
where the time goes in v4:
time: 243 us; the launch traced here: 244 us
  starting transfers between devices  78.4 us (32%)
  waiting for transfers between devices  72.1 us (30%)
  Pallas kernels  52.4 us (22%)
  local copies, waits for them, and re-layouts  31.5 us (13%)
  other arithmetic  8.4 us (3%)
    ppermute x45, starting transfers between devices, swap(): return lax.ppermute(x, axis, [(i, i ^ shift) for i in range(count)])  68.3 us
    all_to_all x1, waiting for transfers between devices, per_device(): lax.all_to_all(outgoing.transpose(0, 2, 1), AXES, split_axis=0, concat_ax...  41.1 us
    ppermute x45, waiting for transfers between devices, swap(): return lax.ppermute(x, axis, [(i, i ^ shift) for i in range(count)])  26.1 us
    pallas_call x5, Pallas kernels, scatter(): pl.pallas_call(scatter_kernel, out_shape=jax.ShapeDtypeStruct((width, row...  19.9 us
    gather x2, local copies, waits for them, and re-layouts, per_device(): operator = relations[rel_ids].T  18.2 us
    pallas_call x5, Pallas kernels, pack(): pl.pallas_call(functools.partial(pack_kernel, first), out_shape=(jax.Shap...  8.65 us
    unnamed x17, local copies, waits for them, and re-layouts  8.64 us
    pallas_call x1, Pallas kernels, gather_edges(): pl.pallas_call(edge_kernel, grid=(edges // tile,), out_shape=(jax.ShapeDt...  8.04 us
  transfers between devices with their start and end apart: 47, of which 14 were waited for; matrix products, arithmetic and copies ran while one was open for 14% of the time, Pallas kernels for 16%

profile of v4, /device:TPU:0, one launch (start us, length us, event | category | flops | bytes accessed | tf_op | source)
XLA Modules:
  0.0 244.1 jit_solution(115202681148038638)
XLA Ops:
  0.6 1.3 copy.29
  2.0 7.3 %all-to-all-start = ((s32[32,1,1]{2,1,0:T(1,128)}), s32[32,1,1]{2,1,0:T(1,128)S(1)}, u32[]{:S(2)}, u32[]{:S(2)}) async-start(s32[32,1,1]{2,1,0:T(1,128)} %copy.29), calls=%async_computation | async-start | bytes 32768 | tf_op jit(solution)/shard_map/all_to_all | solution.py:336
  9.3 2.1 copy_bitcast_fusion
  11.4 4.9 %all-to-all-done = s32[32,1,1]{2,1,0:T(1,128)S(1)} async-done(((s32[32,1,1]{2,1,0:T(1,128)}), s32[32,1,1]{2,1,0:T(1,128)S(1)}, u32[]{:S(2)}, u32[]{:S(2)}) %all-to-all-start) | async-done | bytes 160 | tf_op jit(solution)/shard_map/all_to_all | solution.py:336
  17.0 2.7 %gather_fusion = bf16[32,128,400]{1,2,0:T(8,128)(2,1)} fusion(bf16[16,128,400]{1,2,0:T(8,128)(2,1)S(1)} %copy_bitcast_fusion, s32[1024]{0:T(1024)S(1)} %pad_clamp_fusion), kind=kCustom, calls=%fused_computation | custom fusion | bytes 6553728 | tf_op jit(solution)/shard_map/gather | solution.py:340
  19.7 2.8 %all-to-all-start.1 = ((bf16[32,400,128]{2,1,0:T(8,128)(2,1)}), bf16[32,400,128]{2,1,0:T(8,128)(2,1)S(1)}, u32[]{:S(2)}, u32[]{:S(2)}) async-start(bf16[32,400,128]{2,1,0:T(8,128)(2,1)} %bitcast.36), calls=%async_computation.1 | async-start | bytes 6553600 | tf_op jit(solution)/shard_map/all_to_all | solution.py:341
  22.5 8.6 %copy.31 = f32[4096,400]{1,0:T(8,128)} copy(f32[4096,400]{0,1:T(8,128)} %param.11) | data formatting | bytes 13107200 | tf_op args[2]
  31.1 12.9 %gather_fusion.1 = f32[2048,400]{1,0:T(8,128)} fusion(f32[4096,400]{1,0:T(8,128)} %copy.31, s32[2048]{0:T(1024)S(1)} %fusion.3), kind=kCustom, calls=%fused_computation.1 | custom fusion | bytes 6561792 | tf_op jit(solution)/shard_map/gather | solution.py:344
  44.1 5.3 %copy.32 = f32[2048,400]{0,1:T(8,128)} copy(f32[2048,400]{1,0:T(8,128)} %gather_fusion.1) | data formatting | bytes 6553600 | tf_op jit(solution)/shard_map/gather | solution.py:344
  51.2 1.9 pad_add_fusion.2
  53.1 1.9 pad_add_fusion
  55.7 41.1 %all-to-all-done.1.fetched = bf16[32,400,128]{2,1,0:T(8,128)(2,1)S(1)} async-done(((bf16[32,400,128]{2,1,0:T(8,128)(2,1)}), bf16[32,400,128]{2,1,0:T(8,128)(2,1)S(1)}, u32[]{:S(2)}, u32[]{:S(2)}) %all-to-all-start.1) | async-done | bytes 3276832 | tf_op jit(solution)/shard_map/all_to_all | solution.py:341
  96.8 1.7 gather_negs.1
  98.6 1.3 collective-permute-start.1
  100.5 1.2 collective-permute-start.3
  102.2 2.1 collective-permute-start.5
  104.3 0.9 collective-permute-start.6
  105.3 8.0 %gather_edges.1 = (bf16[400,2048]{1,0:T(8,128)(2,1)S(1)}, bf16[400,2048]{1,0:T(8,128)(2,1)S(1)}, f32[1,2048]{1,0:T(1,128)S(1)}) custom-call(bf16[400,2048]{1,0:T(8,128)(2,1)S(1)} %get-tuple-element.99.rows, s32[1,2048]{1,0:T(1,128)S(1)} %bitcast.23, s32[1,2048]{1,0:T(1,128)S(1)} %bitcast.29, f32[400,2048]{1,0:T(8,128)S(1)} %bitcast.21), custom_call_target="tpu_custom_call" | custom-call | flops 6710886400 | bytes 13107200 | tf_op jit(solution)/shard_map/gather_edges/pallas_call | solution.py:111
  113.4 6.2 %score.1 = (bf16[2,400,2048]{2,1,0:T(8,128)(2,1)S(1)}, bf16[2,400,2048]{2,1,0:T(8,128)(2,1)S(1)}, bf16[400,128]{1,0:T(8,128)(2,1)S(1)}, bf16[400,128]{1,0:T(8,12...) custom-call(bf16[400,128]{1,0:T(8,128)(2,1)S(1)} %get-tuple-element., ...), custom_call_target="tpu_custom_call" | custom-call | flops 5033164800 | bytes 9830400 | tf_op jit(solution)/shard_map/score/pallas_call | solution.py:158
  119.6 1.4 collective-permute-start.7
  121.5 0.9 collective-permute-start.9
  123.0 1.6 collective-permute-start.11
  124.5 0.8 collective-permute-start.12
  125.3 1.4 collective-permute-done.8.refs_2_
  126.8 2.6 %scatter.5.slots_ref = f32[400,512]{1,0:T(8,128)S(1)} custom-call(s32[2]{0:T(128)S(1)} %get-tuple-element.94.base_ref, bf16[2,400,2048]{2,1,0:T(8,128)(2,1)S(1)} %get-tuple-element.106.gs_ref, bf16[2,400,2048]{2,1,0:T(8,128)(2,1)S(1)} %get-tuple-element.107.gd_ref, s32[1,2048]{1,0:T(1,128)S(1)} %bitcast.24, s32[1,2048]{1,0:T(1,128)S(1)} %bitcast.30), custom_call_target="tpu_custom_call" | custom-call | flops 1677721600 | bytes 3276800 | tf_op jit(solution)/shard_map/scatter/pallas_call | solution.py:197
  129.5 3.1 %collective-permute-done.10.refs_4_ = bf16[400,128]{1,0:T(8,128)(2,1)S(1)} collective-permute-done((bf16[400,128]{1,0:T(8,128)(2,1)S(1)}, bf16[400,128]{1,0:T(8,128)(2,1)S(1)}, u32[]{:S(2)}, u32[]{:S(2)}) %collective-permute-start.10) | collective-permute-done | bytes 102432 | tf_op jit(solution)/shard_map/ppermute | solution.py:376
  132.6 1.7 collective-permute-done.11.refs_5_
  134.3 1.0 pack.5
  135.3 2.4 collective-permute-start.14
  137.7 3.2 %collective-permute-start.18 = (s16[408,128]{1,0:T(8,128)(2,1)S(1)}, s16[408,128]{1,0:T(8,128)(2,1)S(1)}, u32[]{:S(2)}, u32[]{:S(2)}) collective-permute-start(s16[408,128]{1,0:T(8,128)(2,1)S(1)} %get-tuple-element.124), channel_id=1, source_target_pairs={{0,30},{1,31},{2,28},{3,29},{4,26},{5,27},{6,24},{7,25},{8,22},{9,... | collective-permute-start | bytes 313352 | tf_op jit(solution)/shard_map/ppermute | solution.py:376
  141.0 2.7 %collective-permute-start.19 = (s16[408,128]{1,0:T(8,128)(2,1)S(1)}, s16[408,128]{1,0:T(8,128)(2,1)S(1)}, u32[]{:S(2)}, u32[]{:S(2)}) collective-permute-start(s16[408,128]{1,0:T(8,128)(2,1)S(1)} %get-tuple-element.125), channel_id=1, source_target_pairs={{0,14},{1,15},{2,12},{3,13},{4,10},{5,11},{6,8},{7,9},{8,6},{9,7},... | collective-permute-start | bytes 313352 | tf_op jit(solution)/shard_map/ppermute | solution.py:376
  143.8 3.0 %collective-permute-done.15.refs_1_ = s16[408,128]{1,0:T(8,128)(2,1)S(1)} collective-permute-done((s16[408,128]{1,0:T(8,128)(2,1)S(1)}, s16[408,128]{1,0:T(8,128)(2,1)S(1)}, u32[]{:S(2)}, u32[]{:S(2)}) %collective-permute-start.15) | collective-permute-done | bytes 104480 | tf_op jit(solution)/shard_map/ppermute | solution.py:376
  146.8 4.3 %scatter.6.slots_ref = f32[400,512]{1,0:T(8,128)S(1)} custom-call(s32[2]{0:T(128)S(1)} %get-tuple-element.118.base_ref, bf16[2,400,2048]{2,1,0:T(8,128)(2,1)S(1)} %get-tuple-element.106.gs_ref, bf16[2,400,2048]{2,1,0:T(8,128)(2,1)S(1)} %get-tuple-element.107.gd_ref, s32[1,2048]{1,0:T(1,128)S(1)} %bitcast.25, s32[1,2048]{1,0:T(1,128)S(1)} %bitcast.31), custom_call_target="tpu_custom_call" | custom-call | flops 1677721600 | bytes 3276800 | tf_op jit(solution)/shard_map/scatter/pallas_call | solution.py:197
  151.2 1.9 pack.6
  153.2 4.2 %collective-permute-start.24 = (s16[408,128]{1,0:T(8,128)(2,1)S(1)}, s16[408,128]{1,0:T(8,128)(2,1)S(1)}, u32[]{:S(2)}, u32[]{:S(2)}) collective-permute-start(s16[408,128]{1,0:T(8,128)(2,1)S(1)} %get-tuple-element.134), channel_id=1, source_target_pairs={{0,28},{1,29},{2,30},{3,31},{4,24},{5,25},{6,26},{7,27},{8,20},{9,... | collective-permute-start | bytes 313352 | tf_op jit(solution)/shard_map/ppermute | solution.py:376
  157.4 2.2 collective-permute-start.25
  159.6 1.0 add.101.refs_4_
  161.0 4.3 %scatter.7.slots_ref = f32[400,1024]{1,0:T(8,128)S(1)} custom-call(s32[2]{0:T(128)S(1)} %get-tuple-element.126.base_ref, bf16[2,400,2048]{2,1,0:T(8,128)(2,1)S(1)} %get-tuple-element.106.gs_ref, bf16[2,400,2048]{2,1,0:T(8,128)(2,1)S(1)} %get-tuple-element.107.gd_ref, s32[1,2048]{1,0:T(1,128)S(1)} %bitcast.26, s32[1,2048]{1,0:T(1,128)S(1)} %bitcast.32), custom_call_target="tpu_custom_call" | custom-call | flops 3355443200 | bytes 6553600 | tf_op jit(solution)/shard_map/scatter/pallas_call | solution.py:197
  165.4 1.9 pack.7
  167.3 1.2 collective-permute-start.20
  168.6 5.1 %collective-permute-start.21 = (s16[408,128]{1,0:T(8,128)(2,1)S(1)}, s16[408,128]{1,0:T(8,128)(2,1)S(1)}, u32[]{:S(2)}, u32[]{:S(2)}) collective-permute-start(s16[408,128]{1,0:T(8,128)(2,1)S(1)} %get-tuple-element.128), channel_id=1, source_target_pairs={{0,11},{1,10},{2,9},{3,8},{4,15},{5,14},{6,13},{7,12},{8,3},{9,2},... | collective-permute-start | bytes 313352 | tf_op jit(solution)/shard_map/ppermute | solution.py:376
  173.7 1.0 collective-permute-start.22
  174.7 3.4 %collective-permute-start.30 = (s16[408,128]{1,0:T(8,128)(2,1)S(1)}, s16[408,128]{1,0:T(8,128)(2,1)S(1)}, u32[]{:S(2)}, u32[]{:S(2)}) collective-permute-start(s16[408,128]{1,0:T(8,128)(2,1)S(1)} %get-tuple-element.147), channel_id=1, source_target_pairs={{0,25},{1,24},{2,27},{3,26},{4,29},{5,28},{6,31},{7,30},{8,17},{9,... | collective-permute-start | bytes 313352 | tf_op jit(solution)/shard_map/ppermute | solution.py:376
  178.1 0.8 add.102.refs_8_
  178.9 1.2 collective-permute-start.31
  180.1 4.1 %collective-permute-start.32 = (s16[408,128]{1,0:T(8,128)(2,1)S(1)}, s16[408,128]{1,0:T(8,128)(2,1)S(1)}, u32[]{:S(2)}, u32[]{:S(2)}) collective-permute-start(s16[408,128]{1,0:T(8,128)(2,1)S(1)} %get-tuple-element.149), channel_id=1, source_target_pairs={{0,24},{1,25},{2,26},{3,27},{4,28},{5,29},{6,30},{7,31},{8,16},{9,... | collective-permute-start | bytes 313352 | tf_op jit(solution)/shard_map/ppermute | solution.py:376
  184.2 4.3 %scatter.8.slots_ref = f32[400,1024]{1,0:T(8,128)S(1)} custom-call(s32[2]{0:T(128)S(1)} %get-tuple-element.137.base_ref, bf16[2,400,2048]{2,1,0:T(8,128)(2,1)S(1)} %get-tuple-element.106.gs_ref, bf16[2,400,2048]{2,1,0:T(8,128)(2,1)S(1)} %get-tuple-element.107.gd_ref, s32[1,2048]{1,0:T(1,128)S(1)} %bitcast.27, s32[1,2048]{1,0:T(1,128)S(1)} %bitcast.33), custom_call_target="tpu_custom_call" | custom-call | flops 3355443200 | bytes 6553600 | tf_op jit(solution)/shard_map/scatter/pallas_call | solution.py:197
  188.6 1.9 pack.8
  190.4 4.2 %collective-permute-start.26 = (s16[408,128]{1,0:T(8,128)(2,1)S(1)}, s16[408,128]{1,0:T(8,128)(2,1)S(1)}, u32[]{:S(2)}, u32[]{:S(2)}) collective-permute-start(s16[408,128]{1,0:T(8,128)(2,1)S(1)} %get-tuple-element.138), channel_id=1, source_target_pairs={{0,23},{1,22},{2,21},{3,20},{4,19},{5,18},{6,17},{7,16},{8,31},{9,... | collective-permute-start | bytes 313352 | tf_op jit(solution)/shard_map/ppermute | solution.py:376
  194.6 4.2 %collective-permute-start.27 = (s16[408,128]{1,0:T(8,128)(2,1)S(1)}, s16[408,128]{1,0:T(8,128)(2,1)S(1)}, u32[]{:S(2)}, u32[]{:S(2)}) collective-permute-start(s16[408,128]{1,0:T(8,128)(2,1)S(1)} %get-tuple-element.139), channel_id=1, source_target_pairs={{0,7},{1,6},{2,5},{3,4},{4,3},{5,2},{6,1},{7,0},{8,15},{9,14},{10,... | collective-permute-start | bytes 313352 | tf_op jit(solution)/shard_map/ppermute | solution.py:376
  199.3 1.6 collective-permute-start.41
  200.9 1.0 add.103.refs_8_
  202.0 4.5 %collective-permute-start.42 = (s16[408,128]{1,0:T(8,128)(2,1)S(1)}, s16[408,128]{1,0:T(8,128)(2,1)S(1)}, u32[]{:S(2)}, u32[]{:S(2)}) collective-permute-start(s16[408,128]{1,0:T(8,128)(2,1)S(1)} %get-tuple-element.166), channel_id=1, source_target_pairs={{0,5},{1,4},{2,7},{3,6},{4,1},{5,0},{6,3},{7,2},{8,13},{9,12},{10,... | collective-permute-start | bytes 313352 | tf_op jit(solution)/shard_map/ppermute | solution.py:376
  206.5 5.9 %collective-permute-done.28.refs_2_ = s16[408,128]{1,0:T(8,128)(2,1)S(1)} collective-permute-done((s16[408,128]{1,0:T(8,128)(2,1)S(1)}, s16[408,128]{1,0:T(8,128)(2,1)S(1)}, u32[]{:S(2)}, u32[]{:S(2)}) %collective-permute-start.28) | collective-permute-done | bytes 104480 | tf_op jit(solution)/shard_map/ppermute | solution.py:376
  212.4 4.3 %scatter.9.slots_ref = f32[400,1024]{1,0:T(8,128)S(1)} custom-call(s32[2]{0:T(128)S(1)} %pad_add_fusion.4.base_ref, bf16[2,400,2048]{2,1,0:T(8,128)(2,1)S(1)} %get-tuple-element.106.gs_ref, bf16[2,400,2048]{2,1,0:T(8,128)(2,1)S(1)} %get-tuple-element.107.gd_ref, s32[1,2048]{1,0:T(1,128)S(1)} %bitcast.28, s32[1,2048]{1,0:T(1,128)S(1)} %bitcast.34), custom_call_target="tpu_custom_call" | custom-call | flops 3355443200 | bytes 6553600 | tf_op jit(solution)/shard_map/scatter/pallas_call | solution.py:197
  216.7 1.9 pack.9
  218.8 1.7 collective-permute-start.35
  220.5 3.8 %collective-permute-start.36 = (s16[408,128]{1,0:T(8,128)(2,1)S(1)}, s16[408,128]{1,0:T(8,128)(2,1)S(1)}, u32[]{:S(2)}, u32[]{:S(2)}) collective-permute-start(s16[408,128]{1,0:T(8,128)(2,1)S(1)} %get-tuple-element.155), channel_id=1, source_target_pairs={{0,18},{1,19},{2,16},{3,17},{4,22},{5,23},{6,20},{7,21},{8,26},{9,... | collective-permute-start | bytes 313352 | tf_op jit(solution)/shard_map/ppermute | solution.py:376
  224.7 3.9 %collective-permute-start.39 = (s16[408,128]{1,0:T(8,128)(2,1)S(1)}, s16[408,128]{1,0:T(8,128)(2,1)S(1)}, u32[]{:S(2)}, u32[]{:S(2)}) collective-permute-start(s16[408,128]{1,0:T(8,128)(2,1)S(1)} %get-tuple-element.158), channel_id=1, source_target_pairs={{0,1},{1,0},{2,3},{3,2},{4,5},{5,4},{6,7},{7,6},{8,9},{9,8},{10,11... | collective-permute-start | bytes 313352 | tf_op jit(solution)/shard_map/ppermute | solution.py:376
  228.7 1.0 add.104.refs_8_
  230.0 1.3 collective-permute-done.37.refs_3_
  231.4 3.7 %collective-permute-done.38.refs_4_ = s16[408,128]{1,0:T(8,128)(2,1)S(1)} collective-permute-done((s16[408,128]{1,0:T(8,128)(2,1)S(1)}, s16[408,128]{1,0:T(8,128)(2,1)S(1)}, u32[]{:S(2)}, u32[]{:S(2)}) %collective-permute-start.38) | collective-permute-done | bytes 104480 | tf_op jit(solution)/shard_map/ppermute | solution.py:376
  235.1 4.9 %collective-permute-done.40.refs_6_ = s16[408,128]{1,0:T(8,128)(2,1)S(1)} collective-permute-done((s16[408,128]{1,0:T(8,128)(2,1)S(1)}, s16[408,128]{1,0:T(8,128)(2,1)S(1)}, u32[]{:S(2)}, u32[]{:S(2)}) %collective-permute-start.40) | collective-permute-done | bytes 104480 | tf_op jit(solution)/shard_map/ppermute | solution.py:376
  240.0 3.9 %update.1 = (f32[400,2048]{1,0:T(8,128)}, f32[1,2048]{1,0:T(1,128)}) custom-call(s32[32]{0:T(128)S(1)} %get-tuple-element.87.asked_ref, s16[408,128]{1,0:T(8,128)(2,1)S(1)} %collective-permute-done.34.refs_0_, s16[408,128]{1,0:T(8,128)(2,1)S(1)} %collective-permute-done.35.refs_1_, s16[408,128]{1,0:T(8,128)(2,1)S(1)} %collective-permute-done.36.refs_2_, ...), custom_call_target="tpu_custom_call" | custom-call | flops 52428800 | bytes 102400 | tf_op jit(solution)/shard_map/update/pallas_call | solution.py:316
  (93 shorter events, 7.6 us)
Async XLA Ops:
  2.0 14.4 %all-to-all-start = ((s32[32,1,1]{2,1,0:T(1,128)}), s32[32,1,1]{2,1,0:T(1,128)S(1)}, u32[]{:S(2)}, u32[]{:S(2)}) async-start(s32[32,1,1]{2,1,0:T(1,128)} %copy.29), calls=%async_computation | async-start | bytes 32768 | tf_op jit(solution)/shard_map/all_to_all | solution.py:336
  19.7 77.1 %all-to-all-start.1 = ((bf16[32,400,128]{2,1,0:T(8,128)(2,1)}), bf16[32,400,128]{2,1,0:T(8,128)(2,1)S(1)}, u32[]{:S(2)}, u32[]{:S(2)}) async-start(bf16[32,400,128]{2,1,0:T(8,128)(2,1)} %bitcast.36), calls=%async_computation.1 | async-start | bytes 6553600 | tf_op jit(solution)/shard_map/all_to_all | solution.py:341
  22.5 8.6 %copy-start.5 = (s32[2048]{0:T(1024)S(1)}, s32[2048]{0:T(1024)}, u32[]{:S(2)}) copy-start(s32[2048]{0:T(1024)} %param.12) | copy-start | bytes 24580
  44.1 5.3 %copy-start.3 = (s32[2048]{0:T(1024)S(1)}, s32[2048]{0:T(1024)}, u32[]{:S(2)}) copy-start(s32[2048]{0:T(1024)} %param.14) | copy-start | bytes 24580
  44.1 5.4 %copy-start.7 = (s32[32]{0:T(128)S(1)}, s32[32]{0:T(128)}, u32[]{:S(2)}) copy-start(s32[32]{0:T(128)} %constant.85.clone) | copy-start | bytes 388
  44.1 11.1 %copy-start.6 = (s32[128]{0:T(128)S(1)}, s32[128]{0:T(128)}, u32[]{:S(2)}) copy-start(s32[128]{0:T(128)} %param.16) | copy-start | bytes 1540
  44.1 11.1 %copy-start.4 = (s32[2048]{0:T(1024)S(1)}, s32[2048]{0:T(1024)}, u32[]{:S(2)}) copy-start(s32[2048]{0:T(1024)} %param.15) | copy-start | bytes 24580
  96.8 8.5 %copy-start.1 = (f32[2048,400]{0,1:T(8,128)S(1)}, f32[2048,400]{0,1:T(8,128)}, u32[]{:S(2)}) copy-start(f32[2048,400]{0,1:T(8,128)} %copy.32) | copy-start | bytes 9830404
  98.5 3.6 %collective-permute-start = (bf16[400,128]{1,0:T(8,128)(2,1)S(1)}, bf16[400,128]{1,0:T(8,128)(2,1)S(1)}, u32[]{:S(2)}, u32[]{:S(2)}) collective-permute-start(bf16[400,128]{1,0:T(8,128)(2,1)S(1)} %get-tuple-element.98.refs_0_), channel_id=1, source_target_pairs={{0,1},{1,0},{2,3},{3,2},{4,5},{5,4},{6,7},{7,6},{8,9},{9,8},{10,11... | collective-permute-start | bytes 307208 | tf_op jit(solution)/shard_map/ppermute | solution.py:376
  98.6 5.7 %collective-permute-start.1 = (bf16[400,128]{1,0:T(8,128)(2,1)S(1)}, bf16[400,128]{1,0:T(8,128)(2,1)S(1)}, u32[]{:S(2)}, u32[]{:S(2)}) collective-permute-start(bf16[400,128]{1,0:T(8,128)(2,1)S(1)} %get-tuple-element.98.refs_0_), channel_id=1, source_target_pairs={{0,2},{1,3},{2,0},{3,1},{4,6},{5,7},{6,4},{7,5},{8,10},{9,11},{10,... | collective-permute-start | bytes 307208 | tf_op jit(solution)/shard_map/ppermute | solution.py:376
  99.9 13.5 %collective-permute-start.2 = (bf16[400,128]{1,0:T(8,128)(2,1)S(1)}, bf16[400,128]{1,0:T(8,128)(2,1)S(1)}, u32[]{:S(2)}, u32[]{:S(2)}) collective-permute-start(bf16[400,128]{1,0:T(8,128)(2,1)S(1)} %get-tuple-element.98.refs_0_), channel_id=1, source_target_pairs={{0,3},{1,2},{2,1},{3,0},{4,7},{5,6},{6,5},{7,4},{8,11},{9,10},{10,... | collective-permute-start | bytes 307208 | tf_op jit(solution)/shard_map/ppermute | solution.py:376
  100.5 12.9 %collective-permute-start.3 = (bf16[400,128]{1,0:T(8,128)(2,1)S(1)}, bf16[400,128]{1,0:T(8,128)(2,1)S(1)}, u32[]{:S(2)}, u32[]{:S(2)}) collective-permute-start(bf16[400,128]{1,0:T(8,128)(2,1)S(1)} %get-tuple-element.98.refs_0_), channel_id=1, source_target_pairs={{0,4},{1,5},{2,6},{3,7},{4,0},{5,1},{6,2},{7,3},{8,12},{9,13},{10,... | collective-permute-start | bytes 307208 | tf_op jit(solution)/shard_map/ppermute | solution.py:376
  101.6 11.7 %collective-permute-start.4 = (bf16[400,128]{1,0:T(8,128)(2,1)S(1)}, bf16[400,128]{1,0:T(8,128)(2,1)S(1)}, u32[]{:S(2)}, u32[]{:S(2)}) collective-permute-start(bf16[400,128]{1,0:T(8,128)(2,1)S(1)} %get-tuple-element.98.refs_0_), channel_id=1, source_target_pairs={{0,5},{1,4},{2,7},{3,6},{4,1},{5,0},{6,3},{7,2},{8,13},{9,12},{10,... | collective-permute-start | bytes 307208 | tf_op jit(solution)/shard_map/ppermute | solution.py:376
  102.2 11.2 %collective-permute-start.5 = (bf16[400,128]{1,0:T(8,128)(2,1)S(1)}, bf16[400,128]{1,0:T(8,128)(2,1)S(1)}, u32[]{:S(2)}, u32[]{:S(2)}) collective-permute-start(bf16[400,128]{1,0:T(8,128)(2,1)S(1)} %get-tuple-element.98.refs_0_), channel_id=1, source_target_pairs={{0,6},{1,7},{2,4},{3,5},{4,2},{5,3},{6,0},{7,1},{8,14},{9,15},{10,... | collective-permute-start | bytes 307208 | tf_op jit(solution)/shard_map/ppermute | solution.py:376
  104.3 9.0 %collective-permute-start.6 = (bf16[400,128]{1,0:T(8,128)(2,1)S(1)}, bf16[400,128]{1,0:T(8,128)(2,1)S(1)}, u32[]{:S(2)}, u32[]{:S(2)}) collective-permute-start(bf16[400,128]{1,0:T(8,128)(2,1)S(1)} %get-tuple-element.98.refs_0_), channel_id=1, source_target_pairs={{0,7},{1,6},{2,5},{3,4},{4,3},{5,2},{6,1},{7,0},{8,15},{9,14},{10,... | collective-permute-start | bytes 307208 | tf_op jit(solution)/shard_map/ppermute | solution.py:376
  119.6 4.9 %collective-permute-start.7 = (bf16[400,128]{1,0:T(8,128)(2,1)S(1)}, bf16[400,128]{1,0:T(8,128)(2,1)S(1)}, u32[]{:S(2)}, u32[]{:S(2)}) collective-permute-start(bf16[400,128]{1,0:T(8,128)(2,1)S(1)} %get-tuple-element.109), channel_id=1, source_target_pairs={{0,1},{1,0},{2,3},{3,2},{4,5},{5,4},{6,7},{7,6},{8,9},{9,8},{10,11... | collective-permute-start | bytes 307208 | tf_op jit(solution)/shard_map/ppermute | solution.py:376
  121.0 5.7 %collective-permute-start.8 = (bf16[400,128]{1,0:T(8,128)(2,1)S(1)}, bf16[400,128]{1,0:T(8,128)(2,1)S(1)}, u32[]{:S(2)}, u32[]{:S(2)}) collective-permute-start(bf16[400,128]{1,0:T(8,128)(2,1)S(1)} %get-tuple-element.110), channel_id=1, source_target_pairs={{0,2},{1,3},{2,0},{3,1},{4,6},{5,7},{6,4},{7,5},{8,10},{9,11},{10,... | collective-permute-start | bytes 307208 | tf_op jit(solution)/shard_map/ppermute | solution.py:376
  121.5 8.0 %collective-permute-start.9 = (bf16[400,128]{1,0:T(8,128)(2,1)S(1)}, bf16[400,128]{1,0:T(8,128)(2,1)S(1)}, u32[]{:S(2)}, u32[]{:S(2)}) collective-permute-start(bf16[400,128]{1,0:T(8,128)(2,1)S(1)} %get-tuple-element.111), channel_id=1, source_target_pairs={{0,3},{1,2},{2,1},{3,0},{4,7},{5,6},{6,5},{7,4},{8,11},{9,10},{10,... | collective-permute-start | bytes 307208 | tf_op jit(solution)/shard_map/ppermute | solution.py:376
  122.4 10.1 %collective-permute-start.10 = (bf16[400,128]{1,0:T(8,128)(2,1)S(1)}, bf16[400,128]{1,0:T(8,128)(2,1)S(1)}, u32[]{:S(2)}, u32[]{:S(2)}) collective-permute-start(bf16[400,128]{1,0:T(8,128)(2,1)S(1)} %get-tuple-element.112), channel_id=1, source_target_pairs={{0,4},{1,5},{2,6},{3,7},{4,0},{5,1},{6,2},{7,3},{8,12},{9,13},{10,... | collective-permute-start | bytes 307208 | tf_op jit(solution)/shard_map/ppermute | solution.py:376
  123.0 11.3 %collective-permute-start.11 = (bf16[400,128]{1,0:T(8,128)(2,1)S(1)}, bf16[400,128]{1,0:T(8,128)(2,1)S(1)}, u32[]{:S(2)}, u32[]{:S(2)}) collective-permute-start(bf16[400,128]{1,0:T(8,128)(2,1)S(1)} %get-tuple-element.113), channel_id=1, source_target_pairs={{0,5},{1,4},{2,7},{3,6},{4,1},{5,0},{6,3},{7,2},{8,13},{9,12},{10,... | collective-permute-start | bytes 307208 | tf_op jit(solution)/shard_map/ppermute | solution.py:376
  124.5 9.7 %collective-permute-start.12 = (bf16[400,128]{1,0:T(8,128)(2,1)S(1)}, bf16[400,128]{1,0:T(8,128)(2,1)S(1)}, u32[]{:S(2)}, u32[]{:S(2)}) collective-permute-start(bf16[400,128]{1,0:T(8,128)(2,1)S(1)} %get-tuple-element.114), channel_id=1, source_target_pairs={{0,6},{1,7},{2,4},{3,5},{4,2},{5,3},{6,0},{7,1},{8,14},{9,15},{10,... | collective-permute-start | bytes 307208 | tf_op jit(solution)/shard_map/ppermute | solution.py:376
  126.7 7.5 %collective-permute-start.13 = (bf16[400,128]{1,0:T(8,128)(2,1)S(1)}, bf16[400,128]{1,0:T(8,128)(2,1)S(1)}, u32[]{:S(2)}, u32[]{:S(2)}) collective-permute-start(bf16[400,128]{1,0:T(8,128)(2,1)S(1)} %get-tuple-element.115), channel_id=1, source_target_pairs={{0,7},{1,6},{2,5},{3,4},{4,3},{5,2},{6,1},{7,0},{8,15},{9,14},{10,... | collective-permute-start | bytes 307208 | tf_op jit(solution)/shard_map/ppermute | solution.py:376
  135.3 8.5 %collective-permute-start.14 = (s16[408,128]{1,0:T(8,128)(2,1)S(1)}, s16[408,128]{1,0:T(8,128)(2,1)S(1)}, u32[]{:S(2)}, u32[]{:S(2)}) collective-permute-start(s16[408,128]{1,0:T(8,128)(2,1)S(1)} %get-tuple-element.116), channel_id=1, source_target_pairs={{0,31},{1,30},{2,29},{3,28},{4,27},{5,26},{6,25},{7,24},{8,23},{9,... | collective-permute-start | bytes 313352 | tf_op jit(solution)/shard_map/ppermute | solution.py:376
  137.7 9.1 %collective-permute-start.15 = (s16[408,128]{1,0:T(8,128)(2,1)S(1)}, s16[408,128]{1,0:T(8,128)(2,1)S(1)}, u32[]{:S(2)}, u32[]{:S(2)}) collective-permute-start(s16[408,128]{1,0:T(8,128)(2,1)S(1)} %get-tuple-element.117), channel_id=1, source_target_pairs={{0,15},{1,14},{2,13},{3,12},{4,11},{5,10},{6,9},{7,8},{8,7},{9,6},... | collective-permute-start | bytes 313352 | tf_op jit(solution)/shard_map/ppermute | solution.py:376
  137.7 19.7 %collective-permute-start.18 = (s16[408,128]{1,0:T(8,128)(2,1)S(1)}, s16[408,128]{1,0:T(8,128)(2,1)S(1)}, u32[]{:S(2)}, u32[]{:S(2)}) collective-permute-start(s16[408,128]{1,0:T(8,128)(2,1)S(1)} %get-tuple-element.124), channel_id=1, source_target_pairs={{0,30},{1,31},{2,28},{3,29},{4,26},{5,27},{6,24},{7,25},{8,22},{9,... | collective-permute-start | bytes 313352 | tf_op jit(solution)/shard_map/ppermute | solution.py:376
  141.0 18.6 %collective-permute-start.19 = (s16[408,128]{1,0:T(8,128)(2,1)S(1)}, s16[408,128]{1,0:T(8,128)(2,1)S(1)}, u32[]{:S(2)}, u32[]{:S(2)}) collective-permute-start(s16[408,128]{1,0:T(8,128)(2,1)S(1)} %get-tuple-element.125), channel_id=1, source_target_pairs={{0,14},{1,15},{2,12},{3,13},{4,10},{5,11},{6,8},{7,9},{8,6},{9,7},... | collective-permute-start | bytes 313352 | tf_op jit(solution)/shard_map/ppermute | solution.py:376
  153.1 8.0 %collective-permute-start.16 = (s16[408,128]{1,0:T(8,128)(2,1)S(1)}, s16[408,128]{1,0:T(8,128)(2,1)S(1)}, u32[]{:S(2)}, u32[]{:S(2)}) collective-permute-start(s16[408,128]{1,0:T(8,128)(2,1)S(1)} %get-tuple-element.119), channel_id=1, source_target_pairs={{0,29},{1,28},{2,31},{3,30},{4,25},{5,24},{6,27},{7,26},{8,21},{9,... | collective-permute-start | bytes 313352 | tf_op jit(solution)/shard_map/ppermute | solution.py:376
  153.1 7.9 %collective-permute-start.17 = (s16[408,128]{1,0:T(8,128)(2,1)S(1)}, s16[408,128]{1,0:T(8,128)(2,1)S(1)}, u32[]{:S(2)}, u32[]{:S(2)}) collective-permute-start(s16[408,128]{1,0:T(8,128)(2,1)S(1)} %get-tuple-element.120), channel_id=1, source_target_pairs={{0,13},{1,12},{2,15},{3,14},{4,9},{5,8},{6,11},{7,10},{8,5},{9,4},... | collective-permute-start | bytes 313352 | tf_op jit(solution)/shard_map/ppermute | solution.py:376
  153.2 21.5 %collective-permute-start.24 = (s16[408,128]{1,0:T(8,128)(2,1)S(1)}, s16[408,128]{1,0:T(8,128)(2,1)S(1)}, u32[]{:S(2)}, u32[]{:S(2)}) collective-permute-start(s16[408,128]{1,0:T(8,128)(2,1)S(1)} %get-tuple-element.134), channel_id=1, source_target_pairs={{0,28},{1,29},{2,30},{3,31},{4,24},{5,25},{6,26},{7,27},{8,20},{9,... | collective-permute-start | bytes 313352 | tf_op jit(solution)/shard_map/ppermute | solution.py:376
  157.4 17.3 %collective-permute-start.25 = (s16[408,128]{1,0:T(8,128)(2,1)S(1)}, s16[408,128]{1,0:T(8,128)(2,1)S(1)}, u32[]{:S(2)}, u32[]{:S(2)}) collective-permute-start(s16[408,128]{1,0:T(8,128)(2,1)S(1)} %get-tuple-element.135), channel_id=1, source_target_pairs={{0,12},{1,13},{2,14},{3,15},{4,8},{5,9},{6,10},{7,11},{8,4},{9,5},... | collective-permute-start | bytes 313352 | tf_op jit(solution)/shard_map/ppermute | solution.py:376
  167.3 11.6 %collective-permute-start.20 = (s16[408,128]{1,0:T(8,128)(2,1)S(1)}, s16[408,128]{1,0:T(8,128)(2,1)S(1)}, u32[]{:S(2)}, u32[]{:S(2)}) collective-permute-start(s16[408,128]{1,0:T(8,128)(2,1)S(1)} %get-tuple-element.127), channel_id=1, source_target_pairs={{0,27},{1,26},{2,25},{3,24},{4,31},{5,30},{6,29},{7,28},{8,19},{9,... | collective-permute-start | bytes 313352 | tf_op jit(solution)/shard_map/ppermute | solution.py:376
  168.6 11.5 %collective-permute-start.21 = (s16[408,128]{1,0:T(8,128)(2,1)S(1)}, s16[408,128]{1,0:T(8,128)(2,1)S(1)}, u32[]{:S(2)}, u32[]{:S(2)}) collective-permute-start(s16[408,128]{1,0:T(8,128)(2,1)S(1)} %get-tuple-element.128), channel_id=1, source_target_pairs={{0,11},{1,10},{2,9},{3,8},{4,15},{5,14},{6,13},{7,12},{8,3},{9,2},... | collective-permute-start | bytes 313352 | tf_op jit(solution)/shard_map/ppermute | solution.py:376
  173.7 10.5 %collective-permute-start.22 = (s16[408,128]{1,0:T(8,128)(2,1)S(1)}, s16[408,128]{1,0:T(8,128)(2,1)S(1)}, u32[]{:S(2)}, u32[]{:S(2)}) collective-permute-start(s16[408,128]{1,0:T(8,128)(2,1)S(1)} %get-tuple-element.129), channel_id=1, source_target_pairs={{0,26},{1,27},{2,24},{3,25},{4,30},{5,31},{6,28},{7,29},{8,18},{9,... | collective-permute-start | bytes 313352 | tf_op jit(solution)/shard_map/ppermute | solution.py:376
  174.7 9.5 %collective-permute-start.23 = (s16[408,128]{1,0:T(8,128)(2,1)S(1)}, s16[408,128]{1,0:T(8,128)(2,1)S(1)}, u32[]{:S(2)}, u32[]{:S(2)}) collective-permute-start(s16[408,128]{1,0:T(8,128)(2,1)S(1)} %get-tuple-element.130), channel_id=1, source_target_pairs={{0,10},{1,11},{2,8},{3,9},{4,14},{5,15},{6,12},{7,13},{8,2},{9,3},... | collective-permute-start | bytes 313352 | tf_op jit(solution)/shard_map/ppermute | solution.py:376
  174.7 19.9 %collective-permute-start.30 = (s16[408,128]{1,0:T(8,128)(2,1)S(1)}, s16[408,128]{1,0:T(8,128)(2,1)S(1)}, u32[]{:S(2)}, u32[]{:S(2)}) collective-permute-start(s16[408,128]{1,0:T(8,128)(2,1)S(1)} %get-tuple-element.147), channel_id=1, source_target_pairs={{0,25},{1,24},{2,27},{3,26},{4,29},{5,28},{6,31},{7,30},{8,17},{9,... | collective-permute-start | bytes 313352 | tf_op jit(solution)/shard_map/ppermute | solution.py:376
  178.9 19.9 %collective-permute-start.31 = (s16[408,128]{1,0:T(8,128)(2,1)S(1)}, s16[408,128]{1,0:T(8,128)(2,1)S(1)}, u32[]{:S(2)}, u32[]{:S(2)}) collective-permute-start(s16[408,128]{1,0:T(8,128)(2,1)S(1)} %get-tuple-element.148), channel_id=1, source_target_pairs={{0,9},{1,8},{2,11},{3,10},{4,13},{5,12},{6,15},{7,14},{8,1},{9,0},... | collective-permute-start | bytes 313352 | tf_op jit(solution)/shard_map/ppermute | solution.py:376
  180.1 19.0 %collective-permute-start.32 = (s16[408,128]{1,0:T(8,128)(2,1)S(1)}, s16[408,128]{1,0:T(8,128)(2,1)S(1)}, u32[]{:S(2)}, u32[]{:S(2)}) collective-permute-start(s16[408,128]{1,0:T(8,128)(2,1)S(1)} %get-tuple-element.149), channel_id=1, source_target_pairs={{0,24},{1,25},{2,26},{3,27},{4,28},{5,29},{6,30},{7,31},{8,16},{9,... | collective-permute-start | bytes 313352 | tf_op jit(solution)/shard_map/ppermute | solution.py:376
  184.2 15.1 %collective-permute-start.33 = (s16[408,128]{1,0:T(8,128)(2,1)S(1)}, s16[408,128]{1,0:T(8,128)(2,1)S(1)}, u32[]{:S(2)}, u32[]{:S(2)}) collective-permute-start(s16[408,128]{1,0:T(8,128)(2,1)S(1)} %get-tuple-element.150), channel_id=1, source_target_pairs={{0,8},{1,9},{2,10},{3,11},{4,12},{5,13},{6,14},{7,15},{8,0},{9,1},... | collective-permute-start | bytes 313352 | tf_op jit(solution)/shard_map/ppermute | solution.py:376
  190.4 11.5 %collective-permute-start.26 = (s16[408,128]{1,0:T(8,128)(2,1)S(1)}, s16[408,128]{1,0:T(8,128)(2,1)S(1)}, u32[]{:S(2)}, u32[]{:S(2)}) collective-permute-start(s16[408,128]{1,0:T(8,128)(2,1)S(1)} %get-tuple-element.138), channel_id=1, source_target_pairs={{0,23},{1,22},{2,21},{3,20},{4,19},{5,18},{6,17},{7,16},{8,31},{9,... | collective-permute-start | bytes 313352 | tf_op jit(solution)/shard_map/ppermute | solution.py:376
  194.6 11.8 %collective-permute-start.27 = (s16[408,128]{1,0:T(8,128)(2,1)S(1)}, s16[408,128]{1,0:T(8,128)(2,1)S(1)}, u32[]{:S(2)}, u32[]{:S(2)}) collective-permute-start(s16[408,128]{1,0:T(8,128)(2,1)S(1)} %get-tuple-element.139), channel_id=1, source_target_pairs={{0,7},{1,6},{2,5},{3,4},{4,3},{5,2},{6,1},{7,0},{8,15},{9,14},{10,... | collective-permute-start | bytes 313352 | tf_op jit(solution)/shard_map/ppermute | solution.py:376
  198.9 13.5 %collective-permute-start.28 = (s16[408,128]{1,0:T(8,128)(2,1)S(1)}, s16[408,128]{1,0:T(8,128)(2,1)S(1)}, u32[]{:S(2)}, u32[]{:S(2)}) collective-permute-start(s16[408,128]{1,0:T(8,128)(2,1)S(1)} %get-tuple-element.140), channel_id=1, source_target_pairs={{0,22},{1,23},{2,20},{3,21},{4,18},{5,19},{6,16},{7,17},{8,30},{9,... | collective-permute-start | bytes 313352 | tf_op jit(solution)/shard_map/ppermute | solution.py:376
  199.1 13.3 %collective-permute-start.29 = (s16[408,128]{1,0:T(8,128)(2,1)S(1)}, s16[408,128]{1,0:T(8,128)(2,1)S(1)}, u32[]{:S(2)}, u32[]{:S(2)}) collective-permute-start(s16[408,128]{1,0:T(8,128)(2,1)S(1)} %get-tuple-element.141), channel_id=1, source_target_pairs={{0,6},{1,7},{2,4},{3,5},{4,2},{5,3},{6,0},{7,1},{8,14},{9,15},{10,... | collective-permute-start | bytes 313352 | tf_op jit(solution)/shard_map/ppermute | solution.py:376
  199.3 19.4 %collective-permute-start.41 = (s16[408,128]{1,0:T(8,128)(2,1)S(1)}, s16[408,128]{1,0:T(8,128)(2,1)S(1)}, u32[]{:S(2)}, u32[]{:S(2)}) collective-permute-start(s16[408,128]{1,0:T(8,128)(2,1)S(1)} %get-tuple-element.165), channel_id=1, source_target_pairs={{0,21},{1,20},{2,23},{3,22},{4,17},{5,16},{6,19},{7,18},{8,29},{9,... | collective-permute-start | bytes 313352 | tf_op jit(solution)/shard_map/ppermute | solution.py:376
  202.0 18.5 %collective-permute-start.42 = (s16[408,128]{1,0:T(8,128)(2,1)S(1)}, s16[408,128]{1,0:T(8,128)(2,1)S(1)}, u32[]{:S(2)}, u32[]{:S(2)}) collective-permute-start(s16[408,128]{1,0:T(8,128)(2,1)S(1)} %get-tuple-element.166), channel_id=1, source_target_pairs={{0,5},{1,4},{2,7},{3,6},{4,1},{5,0},{6,3},{7,2},{8,13},{9,12},{10,... | collective-permute-start | bytes 313352 | tf_op jit(solution)/shard_map/ppermute | solution.py:376
  206.5 17.8 %collective-permute-start.43 = (s16[408,128]{1,0:T(8,128)(2,1)S(1)}, s16[408,128]{1,0:T(8,128)(2,1)S(1)}, u32[]{:S(2)}, u32[]{:S(2)}) collective-permute-start(s16[408,128]{1,0:T(8,128)(2,1)S(1)} %get-tuple-element.167), channel_id=1, source_target_pairs={{0,20},{1,21},{2,22},{3,23},{4,16},{5,17},{6,18},{7,19},{8,28},{9,... | collective-permute-start | bytes 313352 | tf_op jit(solution)/shard_map/ppermute | solution.py:376
  212.4 12.0 %collective-permute-start.44 = (s16[408,128]{1,0:T(8,128)(2,1)S(1)}, s16[408,128]{1,0:T(8,128)(2,1)S(1)}, u32[]{:S(2)}, u32[]{:S(2)}) collective-permute-start(s16[408,128]{1,0:T(8,128)(2,1)S(1)} %get-tuple-element.168), channel_id=1, source_target_pairs={{0,4},{1,5},{2,6},{3,7},{4,0},{5,1},{6,2},{7,3},{8,12},{9,13},{10,... | collective-permute-start | bytes 313352 | tf_op jit(solution)/shard_map/ppermute | solution.py:376
  218.7 6.0 %collective-permute-start.34 = (s16[408,128]{1,0:T(8,128)(2,1)S(1)}, s16[408,128]{1,0:T(8,128)(2,1)S(1)}, u32[]{:S(2)}, u32[]{:S(2)}) collective-permute-start(s16[408,128]{1,0:T(8,128)(2,1)S(1)} %get-tuple-element.153), channel_id=1, source_target_pairs={{0,19},{1,18},{2,17},{3,16},{4,23},{5,22},{6,21},{7,20},{8,27},{9,... | collective-permute-start | bytes 313352 | tf_op jit(solution)/shard_map/ppermute | solution.py:376
  218.8 9.9 %collective-permute-start.35 = (s16[408,128]{1,0:T(8,128)(2,1)S(1)}, s16[408,128]{1,0:T(8,128)(2,1)S(1)}, u32[]{:S(2)}, u32[]{:S(2)}) collective-permute-start(s16[408,128]{1,0:T(8,128)(2,1)S(1)} %get-tuple-element.154), channel_id=1, source_target_pairs={{0,3},{1,2},{2,1},{3,0},{4,7},{5,6},{6,5},{7,4},{8,11},{9,10},{10,... | collective-permute-start | bytes 313352 | tf_op jit(solution)/shard_map/ppermute | solution.py:376
  220.5 9.5 %collective-permute-start.36 = (s16[408,128]{1,0:T(8,128)(2,1)S(1)}, s16[408,128]{1,0:T(8,128)(2,1)S(1)}, u32[]{:S(2)}, u32[]{:S(2)}) collective-permute-start(s16[408,128]{1,0:T(8,128)(2,1)S(1)} %get-tuple-element.155), channel_id=1, source_target_pairs={{0,18},{1,19},{2,16},{3,17},{4,22},{5,23},{6,20},{7,21},{8,26},{9,... | collective-permute-start | bytes 313352 | tf_op jit(solution)/shard_map/ppermute | solution.py:376
  224.3 7.1 %collective-permute-start.37 = (s16[408,128]{1,0:T(8,128)(2,1)S(1)}, s16[408,128]{1,0:T(8,128)(2,1)S(1)}, u32[]{:S(2)}, u32[]{:S(2)}) collective-permute-start(s16[408,128]{1,0:T(8,128)(2,1)S(1)} %get-tuple-element.156), channel_id=1, source_target_pairs={{0,2},{1,3},{2,0},{3,1},{4,6},{5,7},{6,4},{7,5},{8,10},{9,11},{10,... | collective-permute-start | bytes 313352 | tf_op jit(solution)/shard_map/ppermute | solution.py:376
  224.3 10.8 %collective-permute-start.38 = (s16[408,128]{1,0:T(8,128)(2,1)S(1)}, s16[408,128]{1,0:T(8,128)(2,1)S(1)}, u32[]{:S(2)}, u32[]{:S(2)}) collective-permute-start(s16[408,128]{1,0:T(8,128)(2,1)S(1)} %get-tuple-element.157), channel_id=1, source_target_pairs={{0,17},{1,16},{2,19},{3,18},{4,21},{5,20},{6,23},{7,22},{8,25},{9,... | collective-permute-start | bytes 313352 | tf_op jit(solution)/shard_map/ppermute | solution.py:376
  224.7 10.4 %collective-permute-start.39 = (s16[408,128]{1,0:T(8,128)(2,1)S(1)}, s16[408,128]{1,0:T(8,128)(2,1)S(1)}, u32[]{:S(2)}, u32[]{:S(2)}) collective-permute-start(s16[408,128]{1,0:T(8,128)(2,1)S(1)} %get-tuple-element.158), channel_id=1, source_target_pairs={{0,1},{1,0},{2,3},{3,2},{4,5},{5,4},{6,7},{7,6},{8,9},{9,8},{10,11... | collective-permute-start | bytes 313352 | tf_op jit(solution)/shard_map/ppermute | solution.py:376
  228.7 11.3 %copy-start = (f32[2048,400]{0,1:T(8,128)S(1)}, f32[2048,400]{0,1:T(8,128)}, u32[]{:S(2)}) copy-start(f32[2048,400]{0,1:T(8,128)} %param.9) | copy-start | bytes 9830404
  228.7 11.3 %copy-start.2 = (f32[2048]{0:T(1024)S(1)}, f32[2048]{0:T(1024)}, u32[]{:S(2)}) copy-start(f32[2048]{0:T(1024)} %param.10) | copy-start | bytes 24580
  228.7 11.3 %collective-permute-start.40 = (s16[408,128]{1,0:T(8,128)(2,1)S(1)}, s16[408,128]{1,0:T(8,128)(2,1)S(1)}, u32[]{:S(2)}, u32[]{:S(2)}) collective-permute-start(s16[408,128]{1,0:T(8,128)(2,1)S(1)} %get-tuple-element.159), channel_id=1, source_target_pairs={{0,16},{1,17},{2,18},{3,19},{4,20},{5,21},{6,22},{7,23},{8,24},{9,... | collective-permute-start | bytes 313352 | tf_op jit(solution)/shard_map/ppermute | solution.py:376

commit v5 on v4

--- a/solution.py
+++ b/solution.py
@@ -9,7 +9,8 @@
 
 BLK = 128
 TAIL = 8
-CUTS = (1, 1, 2, 2, 2)
+CUTS = (1, 2, 2, 2, 1)
+STEPS = (1, 3, 4)
 TILE = 256
 AXES = ("src", "dst")
 F32 = jnp.float32
@@ -171,9 +172,8 @@
     return out[0], out[1], out[2:]
 
 
-def scatter_kernel(base_ref, gs_ref, gd_ref, spos, dpos, out_ref):
+def scatter_kernel(first, gs_ref, gd_ref, spos, dpos, out_ref):
     width, edges = gs_ref.shape[1:]
-    first = base_ref[0] * BLK
 
     def tile(t, _):
         index = lax.broadcasted_iota(jnp.int32, (TILE, edges), 0) + (first + t * TILE)
@@ -187,22 +187,21 @@
         out_ref[:, pl.ds(pl.multiple_of(t * TILE, TILE), TILE)] = both[:width] + both[width:]
         return 0
 
-    blocks = base_ref[1] - base_ref[0]
-    lax.fori_loop(0, (blocks * BLK + TILE - 1) // TILE, tile, 0)
-
-
-def scatter(bases, grads_src, grads_dst, spos, dpos, blocks):
+    lax.fori_loop(0, out_ref.shape[1] // TILE, tile, 0)
+
+
+def scatter(first, after, grads_src, grads_dst, spos, dpos):
     width, edges = grads_src.shape[1:]
-    rows = -(-blocks * BLK // TILE) * TILE
-    return pl.pallas_call(
-        scatter_kernel,
+    rows = (after - first) * BLK
+    return pl.pallas_call(
+        functools.partial(scatter_kernel, first * BLK),
         out_shape=jax.ShapeDtypeStruct((width, rows), F32),
-        in_specs=[smem(), whole(), whole(), whole(), whole()],
+        in_specs=[whole(), whole(), whole(), whole()],
         out_specs=whole(),
         compiler_params=params(4 * width * rows),
         cost_estimate=cost(4 * width * rows * edges),
         name="scatter",
-    )(bases, grads_src, grads_dst, spos, dpos)
+    )(grads_src, grads_dst, spos, dpos)
 
 
 def encode(x, out_ref):
@@ -220,44 +219,49 @@
     return code[:width, :].astype(jnp.int32).astype(F32) * jnp.exp2(power - 15.0)
 
 
-def pack_kernel(first, rank_ref, live_ref, slots_ref, npos, *refs):
-    count = len(refs) - 1
-    peers = 0
-    while refs[peers].shape[0] == slots_ref.shape[0]:
-        peers += 1
-    grads, outs, total = refs[:peers], refs[peers:count], refs[count]
-    width = slots_ref.shape[0]
+def pack_kernel(first, bounds, peers, rank_ref, live_ref, npos, *refs):
+    chunks, grads = refs[: len(bounds)], refs[len(bounds) : len(bounds) + peers]
+    outs, total, slot = refs[len(bounds) + peers : -2], refs[-2], refs[-1]
+    width = slot.shape[0]
     total[:width], total[width:] = split(sum(g[...].astype(F32) for g in grads))
-    base = rank_ref[first]
     for k, out_ref in enumerate(outs):
         alive = live_ref[first + k] > 0
+        rank = rank_ref[first + k]
+
+        for chunk, (low, high) in zip(chunks, bounds):
+
+            @pl.when(alive & (rank >= low) & (rank < high))
+            def _():
+                lanes = pl.ds(pl.multiple_of((rank - low) * BLK, BLK), BLK)
+                slot[...] = chunk[:, lanes]
 
         @pl.when(alive)
         def _():
-            rank = rank_ref[first + k]
             index = lax.broadcasted_iota(jnp.int32, (BLK, npos.shape[1]), 0) + rank * BLK
             hot = jnp.where(index == npos[...], 1.0, 0.0).astype(BF16)
             both = lax.dot_general(total[...], hot, NT, preferred_element_type=F32)
-            lanes = pl.ds(pl.multiple_of((rank - base) * BLK, BLK), BLK)
-            encode(slots_ref[:, lanes] + (both[:width] + both[width:]), out_ref)
+            encode(slot[...] + (both[:width] + both[width:]), out_ref)
 
         @pl.when(jnp.logical_not(alive))
         def _():
             out_ref[...] = jnp.zeros(out_ref.shape, jnp.int16)
 
 
-def pack(first, group, rank, live, slots, grad_negs, npos):
-    width = slots.shape[0]
-    return pl.pallas_call(
-        functools.partial(pack_kernel, first),
+def pack(first, group, rank, live, chunks, bounds, grad_negs, npos):
+    width = chunks[0].shape[0]
+    return pl.pallas_call(
+        functools.partial(pack_kernel, first, tuple(bounds), len(grad_negs)),
         out_shape=(jax.ShapeDtypeStruct((width + TAIL, BLK), jnp.int16),) * group,
-        in_specs=[smem(), smem(), whole(), whole()] + [whole()] * len(grad_negs),
+        in_specs=[smem(), smem()] + [whole()] * (1 + len(chunks) + len(grad_negs)),
         out_specs=(whole(),) * group,
-        scratch_shapes=[pltpu.VMEM((2 * width, npos.shape[1]), BF16)],
+        scratch_shapes=[
+            pltpu.VMEM((2 * width, npos.shape[1]), BF16),
+            pltpu.VMEM((width, BLK), F32),
+        ],
         compiler_params=params(0),
         cost_estimate=cost(4 * width * BLK * BLK * group),
         name="pack",
-    )(rank, live, slots, npos, *grad_negs)
+    )(rank, live, npos, *chunks, *grad_negs)
 
 
 def add_kernel(first, fresh, asked_ref, *refs):
@@ -359,16 +363,16 @@
     asked = jnp.sum(jnp.where(seat, asked[None, :], 0), axis=1)
     sizes = [cut * devices // sum(CUTS) for cut in CUTS]
     firsts = [sum(sizes[:g]) for g in range(len(sizes))]
-    starts = [rank[first] for first in firsts] + [jnp.int32(named)]
+    steps = [0] + [named * step // STEPS[-1] for step in STEPS]
+    bounds = list(zip(steps[:-1], steps[1:]))
 
     def compact(pos):
         where = jnp.sum(jnp.where((pos // BLK)[:, None] == ids[None, :], place[None, :], 0), axis=1)
         return (where * BLK + pos % BLK).reshape(1, -1)
 
     spos, dpos, npos = compact(src_pos), compact(dst_pos), compact(neg_pos)
-    bases = [jnp.stack(starts[g : g + 2]) for g in range(len(sizes))]
-    fetched, operator, live, rank, alive, asked, spos, dpos, npos, bases = lax.optimization_barrier(
-        (fetched, operator, live, rank, alive, asked, spos, dpos, npos, bases)
+    fetched, operator, live, rank, alive, asked, spos, dpos, npos = lax.optimization_barrier(
+        (fetched, operator, live, rank, alive, asked, spos, dpos, npos)
     )
 
     def swap(x, shift, axis):
@@ -382,17 +386,20 @@
     grads_src, grads_dst, part_negs = score(negs, source, target, operator, g_pos)
     own_grad = [part_negs[0]] + [swap(part_negs[shift], shift, "dst") for shift in range(1, peers)]
     grad = None
-    backs = []
+    backs, chunks = [], []
     for g, (first, group) in enumerate(zip(firsts, sizes)):
-        base = bases[g]
+        if g < len(bounds):
+            edges_at = (spos, dpos)
+            if g:
+                edges_at, backs[:1] = lax.optimization_barrier((edges_at, backs[:1]))
+            chunks.append(scatter(*bounds[g], grads_src, grads_dst, *edges_at))
+        packed = list(pack(first, group, rank, alive, chunks, bounds[: len(chunks)], own_grad, npos))
         if g:
             ahead = len(backs) // 2
-            base, backs[:ahead] = lax.optimization_barrier((base, backs[:ahead]))
-        if g > 1:
-            base, grad = lax.optimization_barrier((base, grad))
-        slots = scatter(base, grads_src, grads_dst, spos, dpos, min(group, named))
-        packed = pack(first, group, rank, alive, slots, own_grad, npos)
-        if g:
+            if grad is None:
+                packed, backs[:ahead] = lax.optimization_barrier((packed, backs[:ahead]))
+            else:
+                packed, backs[:ahead], grad = lax.optimization_barrier((packed, backs[:ahead], grad))
             grad = add(firsts[g - 1], asked, backs, grad, width, rows_dev)
         backs = [
             swap(x, shift, AXES) if shift else x

time: 243 us -> 227 us (0.934)
  starting transfers between devices: 78.4 us -> 62.8 us
  waiting for transfers between devices: 72.1 us -> 79.8 us
  other arithmetic: 8.4 us -> 3.86 us
  Pallas kernels: 52.4 us -> 48.4 us
    ppermute x45, starting transfers between devices: 68.3 us -> 52.8 us  [swap(): return lax.ppermute(x, axis, [(i, i ^ shift) for i in range(count)])]
    all_to_all x1, waiting for transfers between devices: 41.1 us -> 46.4 us  [per_device(): lax.all_to_all(outgoing.transpose(0, 2, 1), AXES, split_axis=0, concat_ax...]
    another operation x3 -> x0, other arithmetic: 4.54 us -> none  [per_device(): bases = [jnp.stack(starts[g:g + 2]) for g in range(len(sizes))]]
    pallas_call x10 -> x8, Pallas kernels: 28.6 us -> 24.8 us  [the longest x3 15.1 us: scatter(): pl.pallas_call(functools.partial(scatter_kernel, first * BLK), out_shape=...]
    ppermute x45, waiting for transfers between devices: 26.1 us -> 28.5 us  [swap(): return lax.ppermute(x, axis, [(i, i ^ shift) for i in range(count)])]
  transfers between devices with their start and end apart: 47 -> 47, of which waited for: 14 -> 15; matrix products, arithmetic and copies ran while one was open for 14% -> 13% of each run, Pallas kernels for 16% -> 15%
where the time goes in v5:
time: 227 us
  waiting for transfers between devices  79.8 us (35%)
  starting transfers between devices  62.8 us (28%)
  Pallas kernels  48.4 us (21%)
  local copies, waits for them, and re-layouts  30.8 us (14%)
  other arithmetic  3.86 us (2%)
    ppermute x45, starting transfers between devices, swap(): return lax.ppermute(x, axis, [(i, i ^ shift) for i in range(count)])  52.8 us
    all_to_all x1, waiting for transfers between devices, per_device(): lax.all_to_all(outgoing.transpose(0, 2, 1), AXES, split_axis=0, concat_ax...  46.4 us
    ppermute x45, waiting for transfers between devices, swap(): return lax.ppermute(x, axis, [(i, i ^ shift) for i in range(count)])  28.5 us
    gather x2, local copies, waits for them, and re-layouts, per_device(): operator = relations[rel_ids].T  18.2 us
    pallas_call x3, Pallas kernels, scatter(): pl.pallas_call(functools.partial(scatter_kernel, first * BLK), out_shape=...  15.1 us
    pallas_call x5, Pallas kernels, pack(): pl.pallas_call(functools.partial(pack_kernel, first, tuple(bounds), len(g...  9.73 us
    unnamed x17, local copies, waits for them, and re-layouts  8.64 us
    pallas_call x1, Pallas kernels, gather_edges(): pl.pallas_call(edge_kernel, grid=(edges // tile,), out_shape=(jax.ShapeDt...  8.04 us
  transfers between devices with their start and end apart: 47, of which 15 were waited for; matrix products, arithmetic and copies ran while one was open for 13% of the time, Pallas kernels for 15%

profile of v5, /device:TPU:0, one launch (start us, length us, event | category | flops | bytes accessed | tf_op | source)
XLA Modules:
  0.0 227.0 jit_solution(4716707185933468107)
XLA Ops:
  0.6 1.3 copy.29
  2.0 7.3 %all-to-all-start = ((s32[32,1,1]{2,1,0:T(1,128)}), s32[32,1,1]{2,1,0:T(1,128)S(1)}, u32[]{:S(2)}, u32[]{:S(2)}) async-start(s32[32,1,1]{2,1,0:T(1,128)} %copy.29), calls=%async_computation | async-start | bytes 32768 | tf_op jit(solution)/shard_map/all_to_all | solution.py:340
  9.3 2.1 copy_bitcast_fusion
  11.4 4.9 %all-to-all-done = s32[32,1,1]{2,1,0:T(1,128)S(1)} async-done(((s32[32,1,1]{2,1,0:T(1,128)}), s32[32,1,1]{2,1,0:T(1,128)S(1)}, u32[]{:S(2)}, u32[]{:S(2)}) %all-to-all-start) | async-done | bytes 160 | tf_op jit(solution)/shard_map/all_to_all | solution.py:340
  17.0 2.7 %gather_fusion = bf16[32,128,400]{1,2,0:T(8,128)(2,1)} fusion(bf16[16,128,400]{1,2,0:T(8,128)(2,1)S(1)} %copy_bitcast_fusion, s32[1024]{0:T(1024)S(1)} %pad_clamp_fusion), kind=kCustom, calls=%fused_computation | custom fusion | bytes 6553728 | tf_op jit(solution)/shard_map/gather | solution.py:344
  19.7 2.8 %all-to-all-start.1 = ((bf16[32,400,128]{2,1,0:T(8,128)(2,1)}), bf16[32,400,128]{2,1,0:T(8,128)(2,1)S(1)}, u32[]{:S(2)}, u32[]{:S(2)}) async-start(bf16[32,400,128]{2,1,0:T(8,128)(2,1)} %bitcast.32), calls=%async_computation.1 | async-start | bytes 6553600 | tf_op jit(solution)/shard_map/all_to_all | solution.py:345
  22.5 8.6 %copy.31 = f32[4096,400]{1,0:T(8,128)} copy(f32[4096,400]{0,1:T(8,128)} %param.11) | data formatting | bytes 13107200 | tf_op args[2]
  31.1 12.9 %gather_fusion.1 = f32[2048,400]{1,0:T(8,128)} fusion(f32[4096,400]{1,0:T(8,128)} %copy.31, s32[2048]{0:T(1024)S(1)} %fusion.3), kind=kCustom, calls=%fused_computation.1 | custom fusion | bytes 6561792 | tf_op jit(solution)/shard_map/gather | solution.py:348
  44.1 5.2 %copy.32 = f32[2048,400]{0,1:T(8,128)} copy(f32[2048,400]{1,0:T(8,128)} %gather_fusion.1) | data formatting | bytes 6553600 | tf_op jit(solution)/shard_map/gather | solution.py:348
  50.4 46.4 %all-to-all-done.1.fetched = bf16[32,400,128]{2,1,0:T(8,128)(2,1)S(1)} async-done(((bf16[32,400,128]{2,1,0:T(8,128)(2,1)}), bf16[32,400,128]{2,1,0:T(8,128)(2,1)S(1)}, u32[]{:S(2)}, u32[]{:S(2)}) %all-to-all-start.1) | async-done | bytes 3276832 | tf_op jit(solution)/shard_map/all_to_all | solution.py:345
  96.8 1.7 gather_negs.1
  98.6 1.3 collective-permute-start.1
  100.5 1.2 collective-permute-start.3
  102.2 2.1 collective-permute-start.5
  104.3 0.9 collective-permute-start.6
  105.3 8.0 %gather_edges.1 = (bf16[400,2048]{1,0:T(8,128)(2,1)S(1)}, bf16[400,2048]{1,0:T(8,128)(2,1)S(1)}, f32[1,2048]{1,0:T(1,128)S(1)}) custom-call(bf16[400,2048]{1,0:T(8,128)(2,1)S(1)} %get-tuple-element.118.rows, s32[1,2048]{1,0:T(1,128)S(1)} %bitcast.23, s32[1,2048]{1,0:T(1,128)S(1)} %bitcast.27, f32[400,2048]{1,0:T(8,128)S(1)} %bitcast.21), custom_call_target="tpu_custom_call" | custom-call | flops 6710886400 | bytes 13107200 | tf_op jit(solution)/shard_map/gather_edges/pallas_call | solution.py:112
  113.4 6.2 %score.1 = (bf16[2,400,2048]{2,1,0:T(8,128)(2,1)S(1)}, bf16[2,400,2048]{2,1,0:T(8,128)(2,1)S(1)}, bf16[400,128]{1,0:T(8,128)(2,1)S(1)}, bf16[400,128]{1,0:T(8,12...) custom-call(bf16[400,128]{1,0:T(8,128)(2,1)S(1)} %get-tuple-element., ...), custom_call_target="tpu_custom_call" | custom-call | flops 5033164800 | bytes 9830400 | tf_op jit(solution)/shard_map/score/pallas_call | solution.py:159
  119.6 1.4 collective-permute-start.7
  121.5 0.9 collective-permute-start.9
  123.0 1.5 collective-permute-start.11
  125.3 1.4 collective-permute-done.8.refs_3_.refs_4_.refs_5_
  126.8 3.8 %scatter.3.refs_0_ = f32[400,512]{1,0:T(8,128)S(1)} custom-call(bf16[2,400,2048]{2,1,0:T(8,128)(2,1)S(1)} %get-tuple-element.125.gs_ref, bf16[2,400,2048]{2,1,0:T(8,128)(2,1)S(1)} %get-tuple-element.126.gd_ref, s32[1,2048]{1,0:T(1,128)S(1)} %bitcast.24, s32[1,2048]{1,0:T(1,128)S(1)} %bitcast.28), custom_call_target="tpu_custom_call" | custom-call | flops 1677721600 | bytes 3276800 | tf_op jit(solution)/shard_map/scatter/pallas_call | solution.py:196
  130.6 2.0 collective-permute-done.10.refs_5_.refs_6_.refs_7_
  132.6 1.7 collective-permute-done.11.refs_6_.refs_7_.refs_8_
  134.3 2.1 pack.5
  136.4 1.6 collective-permute-start.14
  138.0 3.2 %collective-permute-start.20 = (s16[408,128]{1,0:T(8,128)(2,1)S(1)}, s16[408,128]{1,0:T(8,128)(2,1)S(1)}, u32[]{:S(2)}, u32[]{:S(2)}) collective-permute-start(s16[408,128]{1,0:T(8,128)(2,1)S(1)} %get-tuple-element.177), channel_id=1, source_target_pairs={{0,30},{1,31},{2,28},{3,29},{4,26},{5,27},{6,24},{7,25},{8,22},{9,... | collective-permute-start | bytes 313352 | tf_op jit(solution)/shard_map/ppermute | solution.py:380
  141.2 3.5 %collective-permute-start.21 = (s16[408,128]{1,0:T(8,128)(2,1)S(1)}, s16[408,128]{1,0:T(8,128)(2,1)S(1)}, u32[]{:S(2)}, u32[]{:S(2)}) collective-permute-start(s16[408,128]{1,0:T(8,128)(2,1)S(1)} %get-tuple-element.178), channel_id=1, source_target_pairs={{0,14},{1,15},{2,12},{3,13},{4,10},{5,11},{6,8},{7,9},{8,6},{9,7},... | collective-permute-start | bytes 313352 | tf_op jit(solution)/shard_map/ppermute | solution.py:380
  145.3 7.6 %scatter.4.refs_1_ = f32[400,1024]{1,0:T(8,128)S(1)} custom-call(bf16[2,400,2048]{2,1,0:T(8,128)(2,1)S(1)} %get-tuple-element.125.gs_ref, bf16[2,400,2048]{2,1,0:T(8,128)(2,1)S(1)} %get-tuple-element.126.gd_ref, s32[1,2048]{1,0:T(1,128)S(1)} %bitcast.25, s32[1,2048]{1,0:T(1,128)S(1)} %bitcast.29), custom_call_target="tpu_custom_call" | custom-call | flops 3355443200 | bytes 6553600 | tf_op jit(solution)/shard_map/scatter/pallas_call | solution.py:196
  152.8 1.6 pack.6
  154.4 2.1 collective-permute-start.16
  156.5 2.4 %collective-permute-start.18 = (s16[408,128]{1,0:T(8,128)(2,1)S(1)}, s16[408,128]{1,0:T(8,128)(2,1)S(1)}, u32[]{:S(2)}, u32[]{:S(2)}) collective-permute-start(s16[408,128]{1,0:T(8,128)(2,1)S(1)} %get-tuple-element.173), channel_id=1, source_target_pairs={{0,28},{1,29},{2,30},{3,31},{4,24},{5,25},{6,26},{7,27},{8,20},{9,... | collective-permute-start | bytes 313352 | tf_op jit(solution)/shard_map/ppermute | solution.py:380
  159.0 2.0 collective-permute-start.19
  161.6 1.0 add.91.refs_8_
  162.6 1.5 collective-permute-start.27
  164.1 0.9 collective-permute-done.17.refs_1_
  164.9 1.9 collective-permute-start.28
  166.8 3.8 %scatter.5.refs_2_ = f32[400,512]{1,0:T(8,128)S(1)} custom-call(bf16[2,400,2048]{2,1,0:T(8,128)(2,1)S(1)} %get-tuple-element.125.gs_ref, bf16[2,400,2048]{2,1,0:T(8,128)(2,1)S(1)} %get-tuple-element.126.gd_ref, s32[1,2048]{1,0:T(1,128)S(1)} %bitcast.26, s32[1,2048]{1,0:T(1,128)S(1)} %bitcast.30), custom_call_target="tpu_custom_call" | custom-call | flops 1677721600 | bytes 3276800 | tf_op jit(solution)/shard_map/scatter/pallas_call | solution.py:196
  170.6 2.5 %pack.9 = (s16[408,128]{1,0:T(8,128)(2,1)S(1)}, s16[408,128]{1,0:T(8,128)(2,1)S(1)}, s16[408,128]{1,0:T(8,128)(2,1)S(1)}, s16[408,128]{1,0:T(8,128)(2,1)S(1)}, s...) custom-call(s32[32]{0:T(128)S(1)} %select_reduce_fusion.5.rank_ref, ...), custom_call_target="tpu_custom_call" | custom-call | flops 209715200 | bytes 409600 | tf_op jit(solution)/shard_map/pack/pallas_call | solution.py:252
  173.1 0.9 collective-permute-start.29
  174.0 1.6 collective-permute-start.22
  175.6 1.3 collective-permute-start.23
  177.8 0.9 collective-permute-start.25
  178.7 1.9 pack.8
  180.6 1.2 collective-permute-done.29.refs_7_
  181.8 1.6 collective-permute-start.34
  183.4 2.3 %collective-permute-start.35 = (s16[408,128]{1,0:T(8,128)(2,1)S(1)}, s16[408,128]{1,0:T(8,128)(2,1)S(1)}, u32[]{:S(2)}, u32[]{:S(2)}) collective-permute-start(s16[408,128]{1,0:T(8,128)(2,1)S(1)} %get-tuple-element.201), channel_id=1, source_target_pairs={{0,7},{1,6},{2,5},{3,4},{4,3},{5,2},{6,1},{7,0},{8,15},{9,14},{10,... | collective-permute-start | bytes 313352 | tf_op jit(solution)/shard_map/ppermute | solution.py:380
  185.7 1.0 add.92.refs_8_
  186.7 2.0 collective-permute-start.36
  188.7 1.6 collective-permute-start.37
  190.6 1.4 collective-permute-done.34.refs_4_
  192.0 1.3 collective-permute-start.31
  193.3 1.0 collective-permute-start.32
  194.3 4.2 %collective-permute-done.36.refs_6_ = s16[408,128]{1,0:T(8,128)(2,1)S(1)} collective-permute-done((s16[408,128]{1,0:T(8,128)(2,1)S(1)}, s16[408,128]{1,0:T(8,128)(2,1)S(1)}, u32[]{:S(2)}, u32[]{:S(2)}) %collective-permute-start.36) | collective-permute-done | bytes 104480 | tf_op jit(solution)/shard_map/ppermute | solution.py:380
  198.6 1.3 collective-permute-start.41
  199.9 5.7 %collective-permute-done.30.refs_0_ = s16[408,128]{1,0:T(8,128)(2,1)S(1)} collective-permute-done((s16[408,128]{1,0:T(8,128)(2,1)S(1)}, s16[408,128]{1,0:T(8,128)(2,1)S(1)}, u32[]{:S(2)}, u32[]{:S(2)}) %collective-permute-start.30) | collective-permute-done | bytes 104480 | tf_op jit(solution)/shard_map/ppermute | solution.py:380
  205.7 1.6 pack.7
  207.7 1.3 collective-permute-start.44
  209.1 1.0 add.93.refs_8_
  210.1 2.4 %collective-permute-start.38 = (s16[408,128]{1,0:T(8,128)(2,1)S(1)}, s16[408,128]{1,0:T(8,128)(2,1)S(1)}, u32[]{:S(2)}, u32[]{:S(2)}) collective-permute-start(s16[408,128]{1,0:T(8,128)(2,1)S(1)} %get-tuple-element.205), channel_id=1, source_target_pairs={{0,17},{1,16},{2,19},{3,18},{4,21},{5,20},{6,23},{7,22},{8,25},{9,... | collective-permute-start | bytes 313352 | tf_op jit(solution)/shard_map/ppermute | solution.py:380
  213.3 6.2 %collective-permute-done.43.refs_6_ = s16[408,128]{1,0:T(8,128)(2,1)S(1)} collective-permute-done((s16[408,128]{1,0:T(8,128)(2,1)S(1)}, s16[408,128]{1,0:T(8,128)(2,1)S(1)}, u32[]{:S(2)}, u32[]{:S(2)}) %collective-permute-start.43) | collective-permute-done | bytes 104480 | tf_op jit(solution)/shard_map/ppermute | solution.py:380
  219.5 1.0 add.94.refs_4_
  220.5 2.8 %collective-permute-done.40.refs_2_ = s16[408,128]{1,0:T(8,128)(2,1)S(1)} collective-permute-done((s16[408,128]{1,0:T(8,128)(2,1)S(1)}, s16[408,128]{1,0:T(8,128)(2,1)S(1)}, u32[]{:S(2)}, u32[]{:S(2)}) %collective-permute-start.40) | collective-permute-done | bytes 104480 | tf_op jit(solution)/shard_map/ppermute | solution.py:380
  223.3 3.5 %update.1 = (f32[400,2048]{1,0:T(8,128)}, f32[1,2048]{1,0:T(1,128)}) custom-call(s32[32]{0:T(128)S(1)} %get-tuple-element.111.asked_ref, s16[408,128]{1,0:T(8,128)(2,1)S(1)} %collective-permute-done.38.refs_0_, s16[408,128]{1,0:T(8,128)(2,1)S(1)} %collective-permute-done.39.refs_1_, s16[408,128]{1,0:T(8,128)(2,1)S(1)} %collective-permute-done.40.refs_2_, ...), custom_call_target="tpu_custom_call" | custom-call | flops 52428800 | bytes 102400 | tf_op jit(solution)/shard_map/update/pallas_call | solution.py:320
  (87 shorter events, 8.5 us)
Async XLA Ops:
  2.0 14.4 %all-to-all-start = ((s32[32,1,1]{2,1,0:T(1,128)}), s32[32,1,1]{2,1,0:T(1,128)S(1)}, u32[]{:S(2)}, u32[]{:S(2)}) async-start(s32[32,1,1]{2,1,0:T(1,128)} %copy.29), calls=%async_computation | async-start | bytes 32768 | tf_op jit(solution)/shard_map/all_to_all | solution.py:340
  19.7 77.1 %all-to-all-start.1 = ((bf16[32,400,128]{2,1,0:T(8,128)(2,1)}), bf16[32,400,128]{2,1,0:T(8,128)(2,1)S(1)}, u32[]{:S(2)}, u32[]{:S(2)}) async-start(bf16[32,400,128]{2,1,0:T(8,128)(2,1)} %bitcast.32), calls=%async_computation.1 | async-start | bytes 6553600 | tf_op jit(solution)/shard_map/all_to_all | solution.py:345
  22.5 8.6 %copy-start.5 = (s32[2048]{0:T(1024)S(1)}, s32[2048]{0:T(1024)}, u32[]{:S(2)}) copy-start(s32[2048]{0:T(1024)} %param.12) | copy-start | bytes 24580
  44.0 5.3 %copy-start.3 = (s32[2048]{0:T(1024)S(1)}, s32[2048]{0:T(1024)}, u32[]{:S(2)}) copy-start(s32[2048]{0:T(1024)} %param.14) | copy-start | bytes 24580
  44.0 5.4 %copy-start.7 = (s32[32]{0:T(128)S(1)}, s32[32]{0:T(128)}, u32[]{:S(2)}) copy-start(s32[32]{0:T(128)} %constant.83.clone) | copy-start | bytes 388
  44.0 5.9 %copy-start.6 = (s32[128]{0:T(128)S(1)}, s32[128]{0:T(128)}, u32[]{:S(2)}) copy-start(s32[128]{0:T(128)} %param.16) | copy-start | bytes 1540
  44.0 5.9 %copy-start.4 = (s32[2048]{0:T(1024)S(1)}, s32[2048]{0:T(1024)}, u32[]{:S(2)}) copy-start(s32[2048]{0:T(1024)} %param.15) | copy-start | bytes 24580
  96.8 8.5 %copy-start.1 = (f32[2048,400]{0,1:T(8,128)S(1)}, f32[2048,400]{0,1:T(8,128)}, u32[]{:S(2)}) copy-start(f32[2048,400]{0,1:T(8,128)} %copy.32) | copy-start | bytes 9830404
  98.5 3.6 %collective-permute-start = (bf16[400,128]{1,0:T(8,128)(2,1)S(1)}, bf16[400,128]{1,0:T(8,128)(2,1)S(1)}, u32[]{:S(2)}, u32[]{:S(2)}) collective-permute-start(bf16[400,128]{1,0:T(8,128)(2,1)S(1)} %get-tuple-element.117.refs_0_), channel_id=1, source_target_pairs={{0,1},{1,0},{2,3},{3,2},{4,5},{5,4},{6,7},{7,6},{8,9},{9,8},{10,11... | collective-permute-start | bytes 307208 | tf_op jit(solution)/shard_map/ppermute | solution.py:380
  98.6 5.7 %collective-permute-start.1 = (bf16[400,128]{1,0:T(8,128)(2,1)S(1)}, bf16[400,128]{1,0:T(8,128)(2,1)S(1)}, u32[]{:S(2)}, u32[]{:S(2)}) collective-permute-start(bf16[400,128]{1,0:T(8,128)(2,1)S(1)} %get-tuple-element.117.refs_0_), channel_id=1, source_target_pairs={{0,2},{1,3},{2,0},{3,1},{4,6},{5,7},{6,4},{7,5},{8,10},{9,11},{10,... | collective-permute-start | bytes 307208 | tf_op jit(solution)/shard_map/ppermute | solution.py:380
  99.9 13.5 %collective-permute-start.2 = (bf16[400,128]{1,0:T(8,128)(2,1)S(1)}, bf16[400,128]{1,0:T(8,128)(2,1)S(1)}, u32[]{:S(2)}, u32[]{:S(2)}) collective-permute-start(bf16[400,128]{1,0:T(8,128)(2,1)S(1)} %get-tuple-element.117.refs_0_), channel_id=1, source_target_pairs={{0,3},{1,2},{2,1},{3,0},{4,7},{5,6},{6,5},{7,4},{8,11},{9,10},{10,... | collective-permute-start | bytes 307208 | tf_op jit(solution)/shard_map/ppermute | solution.py:380
  100.5 12.9 %collective-permute-start.3 = (bf16[400,128]{1,0:T(8,128)(2,1)S(1)}, bf16[400,128]{1,0:T(8,128)(2,1)S(1)}, u32[]{:S(2)}, u32[]{:S(2)}) collective-permute-start(bf16[400,128]{1,0:T(8,128)(2,1)S(1)} %get-tuple-element.117.refs_0_), channel_id=1, source_target_pairs={{0,4},{1,5},{2,6},{3,7},{4,0},{5,1},{6,2},{7,3},{8,12},{9,13},{10,... | collective-permute-start | bytes 307208 | tf_op jit(solution)/shard_map/ppermute | solution.py:380
  101.6 11.7 %collective-permute-start.4 = (bf16[400,128]{1,0:T(8,128)(2,1)S(1)}, bf16[400,128]{1,0:T(8,128)(2,1)S(1)}, u32[]{:S(2)}, u32[]{:S(2)}) collective-permute-start(bf16[400,128]{1,0:T(8,128)(2,1)S(1)} %get-tuple-element.117.refs_0_), channel_id=1, source_target_pairs={{0,5},{1,4},{2,7},{3,6},{4,1},{5,0},{6,3},{7,2},{8,13},{9,12},{10,... | collective-permute-start | bytes 307208 | tf_op jit(solution)/shard_map/ppermute | solution.py:380
  102.2 11.2 %collective-permute-start.5 = (bf16[400,128]{1,0:T(8,128)(2,1)S(1)}, bf16[400,128]{1,0:T(8,128)(2,1)S(1)}, u32[]{:S(2)}, u32[]{:S(2)}) collective-permute-start(bf16[400,128]{1,0:T(8,128)(2,1)S(1)} %get-tuple-element.117.refs_0_), channel_id=1, source_target_pairs={{0,6},{1,7},{2,4},{3,5},{4,2},{5,3},{6,0},{7,1},{8,14},{9,15},{10,... | collective-permute-start | bytes 307208 | tf_op jit(solution)/shard_map/ppermute | solution.py:380
  104.3 9.0 %collective-permute-start.6 = (bf16[400,128]{1,0:T(8,128)(2,1)S(1)}, bf16[400,128]{1,0:T(8,128)(2,1)S(1)}, u32[]{:S(2)}, u32[]{:S(2)}) collective-permute-start(bf16[400,128]{1,0:T(8,128)(2,1)S(1)} %get-tuple-element.117.refs_0_), channel_id=1, source_target_pairs={{0,7},{1,6},{2,5},{3,4},{4,3},{5,2},{6,1},{7,0},{8,15},{9,14},{10,... | collective-permute-start | bytes 307208 | tf_op jit(solution)/shard_map/ppermute | solution.py:380
  119.6 4.9 %collective-permute-start.7 = (bf16[400,128]{1,0:T(8,128)(2,1)S(1)}, bf16[400,128]{1,0:T(8,128)(2,1)S(1)}, u32[]{:S(2)}, u32[]{:S(2)}) collective-permute-start(bf16[400,128]{1,0:T(8,128)(2,1)S(1)} %get-tuple-element.128), channel_id=1, source_target_pairs={{0,1},{1,0},{2,3},{3,2},{4,5},{5,4},{6,7},{7,6},{8,9},{9,8},{10,11... | collective-permute-start | bytes 307208 | tf_op jit(solution)/shard_map/ppermute | solution.py:380
  121.0 5.7 %collective-permute-start.8 = (bf16[400,128]{1,0:T(8,128)(2,1)S(1)}, bf16[400,128]{1,0:T(8,128)(2,1)S(1)}, u32[]{:S(2)}, u32[]{:S(2)}) collective-permute-start(bf16[400,128]{1,0:T(8,128)(2,1)S(1)} %get-tuple-element.129), channel_id=1, source_target_pairs={{0,2},{1,3},{2,0},{3,1},{4,6},{5,7},{6,4},{7,5},{8,10},{9,11},{10,... | collective-permute-start | bytes 307208 | tf_op jit(solution)/shard_map/ppermute | solution.py:380
  121.5 9.1 %collective-permute-start.9 = (bf16[400,128]{1,0:T(8,128)(2,1)S(1)}, bf16[400,128]{1,0:T(8,128)(2,1)S(1)}, u32[]{:S(2)}, u32[]{:S(2)}) collective-permute-start(bf16[400,128]{1,0:T(8,128)(2,1)S(1)} %get-tuple-element.130), channel_id=1, source_target_pairs={{0,3},{1,2},{2,1},{3,0},{4,7},{5,6},{6,5},{7,4},{8,11},{9,10},{10,... | collective-permute-start | bytes 307208 | tf_op jit(solution)/shard_map/ppermute | solution.py:380
  122.4 10.1 %collective-permute-start.10 = (bf16[400,128]{1,0:T(8,128)(2,1)S(1)}, bf16[400,128]{1,0:T(8,128)(2,1)S(1)}, u32[]{:S(2)}, u32[]{:S(2)}) collective-permute-start(bf16[400,128]{1,0:T(8,128)(2,1)S(1)} %get-tuple-element.131), channel_id=1, source_target_pairs={{0,4},{1,5},{2,6},{3,7},{4,0},{5,1},{6,2},{7,3},{8,12},{9,13},{10,... | collective-permute-start | bytes 307208 | tf_op jit(solution)/shard_map/ppermute | solution.py:380
  123.0 11.3 %collective-permute-start.11 = (bf16[400,128]{1,0:T(8,128)(2,1)S(1)}, bf16[400,128]{1,0:T(8,128)(2,1)S(1)}, u32[]{:S(2)}, u32[]{:S(2)}) collective-permute-start(bf16[400,128]{1,0:T(8,128)(2,1)S(1)} %get-tuple-element.132), channel_id=1, source_target_pairs={{0,5},{1,4},{2,7},{3,6},{4,1},{5,0},{6,3},{7,2},{8,13},{9,12},{10,... | collective-permute-start | bytes 307208 | tf_op jit(solution)/shard_map/ppermute | solution.py:380
  124.5 9.7 %collective-permute-start.12 = (bf16[400,128]{1,0:T(8,128)(2,1)S(1)}, bf16[400,128]{1,0:T(8,128)(2,1)S(1)}, u32[]{:S(2)}, u32[]{:S(2)}) collective-permute-start(bf16[400,128]{1,0:T(8,128)(2,1)S(1)} %get-tuple-element.133), channel_id=1, source_target_pairs={{0,6},{1,7},{2,4},{3,5},{4,2},{5,3},{6,0},{7,1},{8,14},{9,15},{10,... | collective-permute-start | bytes 307208 | tf_op jit(solution)/shard_map/ppermute | solution.py:380
  126.7 7.5 %collective-permute-start.13 = (bf16[400,128]{1,0:T(8,128)(2,1)S(1)}, bf16[400,128]{1,0:T(8,128)(2,1)S(1)}, u32[]{:S(2)}, u32[]{:S(2)}) collective-permute-start(bf16[400,128]{1,0:T(8,128)(2,1)S(1)} %get-tuple-element.134), channel_id=1, source_target_pairs={{0,7},{1,6},{2,5},{3,4},{4,3},{5,2},{6,1},{7,0},{8,15},{9,14},{10,... | collective-permute-start | bytes 307208 | tf_op jit(solution)/shard_map/ppermute | solution.py:380
  136.4 8.9 %collective-permute-start.14 = (s16[408,128]{1,0:T(8,128)(2,1)S(1)}, s16[408,128]{1,0:T(8,128)(2,1)S(1)}, u32[]{:S(2)}, u32[]{:S(2)}) collective-permute-start(s16[408,128]{1,0:T(8,128)(2,1)S(1)} %get-tuple-element.135), channel_id=1, source_target_pairs={{0,31},{1,30},{2,29},{3,28},{4,27},{5,26},{6,25},{7,24},{8,23},{9,... | collective-permute-start | bytes 313352 | tf_op jit(solution)/shard_map/ppermute | solution.py:380
  138.0 16.4 %collective-permute-start.15 = (s16[408,128]{1,0:T(8,128)(2,1)S(1)}, s16[408,128]{1,0:T(8,128)(2,1)S(1)}, u32[]{:S(2)}, u32[]{:S(2)}) collective-permute-start(s16[408,128]{1,0:T(8,128)(2,1)S(1)} %get-tuple-element.147), channel_id=1, source_target_pairs={{0,15},{1,14},{2,13},{3,12},{4,11},{5,10},{6,9},{7,8},{8,7},{9,6},... | collective-permute-start | bytes 313352 | tf_op jit(solution)/shard_map/ppermute | solution.py:380
  138.0 21.0 %collective-permute-start.20 = (s16[408,128]{1,0:T(8,128)(2,1)S(1)}, s16[408,128]{1,0:T(8,128)(2,1)S(1)}, u32[]{:S(2)}, u32[]{:S(2)}) collective-permute-start(s16[408,128]{1,0:T(8,128)(2,1)S(1)} %get-tuple-element.177), channel_id=1, source_target_pairs={{0,30},{1,31},{2,28},{3,29},{4,26},{5,27},{6,24},{7,25},{8,22},{9,... | collective-permute-start | bytes 313352 | tf_op jit(solution)/shard_map/ppermute | solution.py:380
  141.2 19.7 %collective-permute-start.21 = (s16[408,128]{1,0:T(8,128)(2,1)S(1)}, s16[408,128]{1,0:T(8,128)(2,1)S(1)}, u32[]{:S(2)}, u32[]{:S(2)}) collective-permute-start(s16[408,128]{1,0:T(8,128)(2,1)S(1)} %get-tuple-element.178), channel_id=1, source_target_pairs={{0,14},{1,15},{2,12},{3,13},{4,10},{5,11},{6,8},{7,9},{8,6},{9,7},... | collective-permute-start | bytes 313352 | tf_op jit(solution)/shard_map/ppermute | solution.py:380
  154.4 8.1 %collective-permute-start.16 = (s16[408,128]{1,0:T(8,128)(2,1)S(1)}, s16[408,128]{1,0:T(8,128)(2,1)S(1)}, u32[]{:S(2)}, u32[]{:S(2)}) collective-permute-start(s16[408,128]{1,0:T(8,128)(2,1)S(1)} %get-tuple-element.148), channel_id=1, source_target_pairs={{0,29},{1,28},{2,31},{3,30},{4,25},{5,24},{6,27},{7,26},{8,21},{9,... | collective-permute-start | bytes 313352 | tf_op jit(solution)/shard_map/ppermute | solution.py:380
  156.5 8.4 %collective-permute-start.17 = (s16[408,128]{1,0:T(8,128)(2,1)S(1)}, s16[408,128]{1,0:T(8,128)(2,1)S(1)}, u32[]{:S(2)}, u32[]{:S(2)}) collective-permute-start(s16[408,128]{1,0:T(8,128)(2,1)S(1)} %get-tuple-element.172), channel_id=1, source_target_pairs={{0,13},{1,12},{2,15},{3,14},{4,9},{5,8},{6,11},{7,10},{8,5},{9,4},... | collective-permute-start | bytes 313352 | tf_op jit(solution)/shard_map/ppermute | solution.py:380
  156.5 16.6 %collective-permute-start.18 = (s16[408,128]{1,0:T(8,128)(2,1)S(1)}, s16[408,128]{1,0:T(8,128)(2,1)S(1)}, u32[]{:S(2)}, u32[]{:S(2)}) collective-permute-start(s16[408,128]{1,0:T(8,128)(2,1)S(1)} %get-tuple-element.173), channel_id=1, source_target_pairs={{0,28},{1,29},{2,30},{3,31},{4,24},{5,25},{6,26},{7,27},{8,20},{9,... | collective-permute-start | bytes 313352 | tf_op jit(solution)/shard_map/ppermute | solution.py:380
  159.0 15.0 %collective-permute-start.19 = (s16[408,128]{1,0:T(8,128)(2,1)S(1)}, s16[408,128]{1,0:T(8,128)(2,1)S(1)}, u32[]{:S(2)}, u32[]{:S(2)}) collective-permute-start(s16[408,128]{1,0:T(8,128)(2,1)S(1)} %get-tuple-element.174), channel_id=1, source_target_pairs={{0,12},{1,13},{2,14},{3,15},{4,8},{5,9},{6,10},{7,11},{8,4},{9,5},... | collective-permute-start | bytes 313352 | tf_op jit(solution)/shard_map/ppermute | solution.py:380
  161.0 14.6 %collective-permute-start.26 = (s16[408,128]{1,0:T(8,128)(2,1)S(1)}, s16[408,128]{1,0:T(8,128)(2,1)S(1)}, u32[]{:S(2)}, u32[]{:S(2)}) collective-permute-start(s16[408,128]{1,0:T(8,128)(2,1)S(1)} %get-tuple-element.187), channel_id=1, source_target_pairs={{0,27},{1,26},{2,25},{3,24},{4,31},{5,30},{6,29},{7,28},{8,19},{9,... | collective-permute-start | bytes 313352 | tf_op jit(solution)/shard_map/ppermute | solution.py:380
  162.6 14.4 %collective-permute-start.27 = (s16[408,128]{1,0:T(8,128)(2,1)S(1)}, s16[408,128]{1,0:T(8,128)(2,1)S(1)}, u32[]{:S(2)}, u32[]{:S(2)}) collective-permute-start(s16[408,128]{1,0:T(8,128)(2,1)S(1)} %get-tuple-element.188), channel_id=1, source_target_pairs={{0,11},{1,10},{2,9},{3,8},{4,15},{5,14},{6,13},{7,12},{8,3},{9,2},... | collective-permute-start | bytes 313352 | tf_op jit(solution)/shard_map/ppermute | solution.py:380
  164.9 12.8 %collective-permute-start.28 = (s16[408,128]{1,0:T(8,128)(2,1)S(1)}, s16[408,128]{1,0:T(8,128)(2,1)S(1)}, u32[]{:S(2)}, u32[]{:S(2)}) collective-permute-start(s16[408,128]{1,0:T(8,128)(2,1)S(1)} %get-tuple-element.189), channel_id=1, source_target_pairs={{0,26},{1,27},{2,24},{3,25},{4,30},{5,31},{6,28},{7,29},{8,18},{9,... | collective-permute-start | bytes 313352 | tf_op jit(solution)/shard_map/ppermute | solution.py:380
  173.1 8.7 %collective-permute-start.29 = (s16[408,128]{1,0:T(8,128)(2,1)S(1)}, s16[408,128]{1,0:T(8,128)(2,1)S(1)}, u32[]{:S(2)}, u32[]{:S(2)}) collective-permute-start(s16[408,128]{1,0:T(8,128)(2,1)S(1)} %get-tuple-element.190), channel_id=1, source_target_pairs={{0,10},{1,11},{2,8},{3,9},{4,14},{5,15},{6,12},{7,13},{8,2},{9,3},... | collective-permute-start | bytes 313352 | tf_op jit(solution)/shard_map/ppermute | solution.py:380
  174.0 9.4 %collective-permute-start.22 = (s16[408,128]{1,0:T(8,128)(2,1)S(1)}, s16[408,128]{1,0:T(8,128)(2,1)S(1)}, u32[]{:S(2)}, u32[]{:S(2)}) collective-permute-start(s16[408,128]{1,0:T(8,128)(2,1)S(1)} %get-tuple-element.179), channel_id=1, source_target_pairs={{0,25},{1,24},{2,27},{3,26},{4,29},{5,28},{6,31},{7,30},{8,17},{9,... | collective-permute-start | bytes 313352 | tf_op jit(solution)/shard_map/ppermute | solution.py:380
  175.6 11.2 %collective-permute-start.23 = (s16[408,128]{1,0:T(8,128)(2,1)S(1)}, s16[408,128]{1,0:T(8,128)(2,1)S(1)}, u32[]{:S(2)}, u32[]{:S(2)}) collective-permute-start(s16[408,128]{1,0:T(8,128)(2,1)S(1)} %get-tuple-element.180), channel_id=1, source_target_pairs={{0,9},{1,8},{2,11},{3,10},{4,13},{5,12},{6,15},{7,14},{8,1},{9,0},... | collective-permute-start | bytes 313352 | tf_op jit(solution)/shard_map/ppermute | solution.py:380
  176.9 11.8 %collective-permute-start.24 = (s16[408,128]{1,0:T(8,128)(2,1)S(1)}, s16[408,128]{1,0:T(8,128)(2,1)S(1)}, u32[]{:S(2)}, u32[]{:S(2)}) collective-permute-start(s16[408,128]{1,0:T(8,128)(2,1)S(1)} %get-tuple-element.181), channel_id=1, source_target_pairs={{0,24},{1,25},{2,26},{3,27},{4,28},{5,29},{6,30},{7,31},{8,16},{9,... | collective-permute-start | bytes 313352 | tf_op jit(solution)/shard_map/ppermute | solution.py:380
  177.8 12.6 %collective-permute-start.25 = (s16[408,128]{1,0:T(8,128)(2,1)S(1)}, s16[408,128]{1,0:T(8,128)(2,1)S(1)}, u32[]{:S(2)}, u32[]{:S(2)}) collective-permute-start(s16[408,128]{1,0:T(8,128)(2,1)S(1)} %get-tuple-element.182), channel_id=1, source_target_pairs={{0,8},{1,9},{2,10},{3,11},{4,12},{5,13},{6,14},{7,15},{8,0},{9,1},... | collective-permute-start | bytes 313352 | tf_op jit(solution)/shard_map/ppermute | solution.py:380
  181.8 10.2 %collective-permute-start.34 = (s16[408,128]{1,0:T(8,128)(2,1)S(1)}, s16[408,128]{1,0:T(8,128)(2,1)S(1)}, u32[]{:S(2)}, u32[]{:S(2)}) collective-permute-start(s16[408,128]{1,0:T(8,128)(2,1)S(1)} %get-tuple-element.200), channel_id=1, source_target_pairs={{0,23},{1,22},{2,21},{3,20},{4,19},{5,18},{6,17},{7,16},{8,31},{9,... | collective-permute-start | bytes 313352 | tf_op jit(solution)/shard_map/ppermute | solution.py:380
  183.4 9.9 %collective-permute-start.35 = (s16[408,128]{1,0:T(8,128)(2,1)S(1)}, s16[408,128]{1,0:T(8,128)(2,1)S(1)}, u32[]{:S(2)}, u32[]{:S(2)}) collective-permute-start(s16[408,128]{1,0:T(8,128)(2,1)S(1)} %get-tuple-element.201), channel_id=1, source_target_pairs={{0,7},{1,6},{2,5},{3,4},{4,3},{5,2},{6,1},{7,0},{8,15},{9,14},{10,... | collective-permute-start | bytes 313352 | tf_op jit(solution)/shard_map/ppermute | solution.py:380
  186.7 11.8 %collective-permute-start.36 = (s16[408,128]{1,0:T(8,128)(2,1)S(1)}, s16[408,128]{1,0:T(8,128)(2,1)S(1)}, u32[]{:S(2)}, u32[]{:S(2)}) collective-permute-start(s16[408,128]{1,0:T(8,128)(2,1)S(1)} %get-tuple-element.202), channel_id=1, source_target_pairs={{0,22},{1,23},{2,20},{3,21},{4,18},{5,19},{6,16},{7,17},{8,30},{9,... | collective-permute-start | bytes 313352 | tf_op jit(solution)/shard_map/ppermute | solution.py:380
  188.7 9.9 %collective-permute-start.37 = (s16[408,128]{1,0:T(8,128)(2,1)S(1)}, s16[408,128]{1,0:T(8,128)(2,1)S(1)}, u32[]{:S(2)}, u32[]{:S(2)}) collective-permute-start(s16[408,128]{1,0:T(8,128)(2,1)S(1)} %get-tuple-element.203), channel_id=1, source_target_pairs={{0,6},{1,7},{2,4},{3,5},{4,2},{5,3},{6,0},{7,1},{8,14},{9,15},{10,... | collective-permute-start | bytes 313352 | tf_op jit(solution)/shard_map/ppermute | solution.py:380
  190.3 15.3 %collective-permute-start.30 = (s16[408,128]{1,0:T(8,128)(2,1)S(1)}, s16[408,128]{1,0:T(8,128)(2,1)S(1)}, u32[]{:S(2)}, u32[]{:S(2)}) collective-permute-start(s16[408,128]{1,0:T(8,128)(2,1)S(1)} %get-tuple-element.192), channel_id=1, source_target_pairs={{0,21},{1,20},{2,23},{3,22},{4,17},{5,16},{6,19},{7,18},{8,29},{9,... | collective-permute-start | bytes 313352 | tf_op jit(solution)/shard_map/ppermute | solution.py:380
  192.0 15.3 %collective-permute-start.31 = (s16[408,128]{1,0:T(8,128)(2,1)S(1)}, s16[408,128]{1,0:T(8,128)(2,1)S(1)}, u32[]{:S(2)}, u32[]{:S(2)}) collective-permute-start(s16[408,128]{1,0:T(8,128)(2,1)S(1)} %get-tuple-element.193), channel_id=1, source_target_pairs={{0,5},{1,4},{2,7},{3,6},{4,1},{5,0},{6,3},{7,2},{8,13},{9,12},{10,... | collective-permute-start | bytes 313352 | tf_op jit(solution)/shard_map/ppermute | solution.py:380
  193.3 14.5 %collective-permute-start.32 = (s16[408,128]{1,0:T(8,128)(2,1)S(1)}, s16[408,128]{1,0:T(8,128)(2,1)S(1)}, u32[]{:S(2)}, u32[]{:S(2)}) collective-permute-start(s16[408,128]{1,0:T(8,128)(2,1)S(1)} %get-tuple-element.194), channel_id=1, source_target_pairs={{0,20},{1,21},{2,22},{3,23},{4,16},{5,17},{6,18},{7,19},{8,28},{9,... | collective-permute-start | bytes 313352 | tf_op jit(solution)/shard_map/ppermute | solution.py:380
  198.6 11.5 %collective-permute-start.33 = (s16[408,128]{1,0:T(8,128)(2,1)S(1)}, s16[408,128]{1,0:T(8,128)(2,1)S(1)}, u32[]{:S(2)}, u32[]{:S(2)}) collective-permute-start(s16[408,128]{1,0:T(8,128)(2,1)S(1)} %get-tuple-element.195), channel_id=1, source_target_pairs={{0,4},{1,5},{2,6},{3,7},{4,0},{5,1},{6,2},{7,3},{8,12},{9,13},{10,... | collective-permute-start | bytes 313352 | tf_op jit(solution)/shard_map/ppermute | solution.py:380
  198.6 13.9 %collective-permute-start.41 = (s16[408,128]{1,0:T(8,128)(2,1)S(1)}, s16[408,128]{1,0:T(8,128)(2,1)S(1)}, u32[]{:S(2)}, u32[]{:S(2)}) collective-permute-start(s16[408,128]{1,0:T(8,128)(2,1)S(1)} %get-tuple-element.213), channel_id=1, source_target_pairs={{0,19},{1,18},{2,17},{3,16},{4,23},{5,22},{6,21},{7,20},{8,27},{9,... | collective-permute-start | bytes 313352 | tf_op jit(solution)/shard_map/ppermute | solution.py:380
  205.6 7.4 %collective-permute-start.42 = (s16[408,128]{1,0:T(8,128)(2,1)S(1)}, s16[408,128]{1,0:T(8,128)(2,1)S(1)}, u32[]{:S(2)}, u32[]{:S(2)}) collective-permute-start(s16[408,128]{1,0:T(8,128)(2,1)S(1)} %get-tuple-element.214), channel_id=1, source_target_pairs={{0,3},{1,2},{2,1},{3,0},{4,7},{5,6},{6,5},{7,4},{8,11},{9,10},{10,... | collective-permute-start | bytes 313352 | tf_op jit(solution)/shard_map/ppermute | solution.py:380
  207.3 12.1 %collective-permute-start.43 = (s16[408,128]{1,0:T(8,128)(2,1)S(1)}, s16[408,128]{1,0:T(8,128)(2,1)S(1)}, u32[]{:S(2)}, u32[]{:S(2)}) collective-permute-start(s16[408,128]{1,0:T(8,128)(2,1)S(1)} %get-tuple-element.215), channel_id=1, source_target_pairs={{0,18},{1,19},{2,16},{3,17},{4,22},{5,23},{6,20},{7,21},{8,26},{9,... | collective-permute-start | bytes 313352 | tf_op jit(solution)/shard_map/ppermute | solution.py:380
  207.7 11.7 %collective-permute-start.44 = (s16[408,128]{1,0:T(8,128)(2,1)S(1)}, s16[408,128]{1,0:T(8,128)(2,1)S(1)}, u32[]{:S(2)}, u32[]{:S(2)}) collective-permute-start(s16[408,128]{1,0:T(8,128)(2,1)S(1)} %get-tuple-element.216), channel_id=1, source_target_pairs={{0,2},{1,3},{2,0},{3,1},{4,6},{5,7},{6,4},{7,5},{8,10},{9,11},{10,... | collective-permute-start | bytes 313352 | tf_op jit(solution)/shard_map/ppermute | solution.py:380
  210.1 13.2 %copy-start = (f32[2048,400]{0,1:T(8,128)S(1)}, f32[2048,400]{0,1:T(8,128)}, u32[]{:S(2)}) copy-start(f32[2048,400]{0,1:T(8,128)} %param.9) | copy-start | bytes 9830404
  210.1 13.2 %copy-start.2 = (f32[2048]{0:T(1024)S(1)}, f32[2048]{0:T(1024)}, u32[]{:S(2)}) copy-start(f32[2048]{0:T(1024)} %param.10) | copy-start | bytes 24580
  210.1 10.3 %collective-permute-start.38 = (s16[408,128]{1,0:T(8,128)(2,1)S(1)}, s16[408,128]{1,0:T(8,128)(2,1)S(1)}, u32[]{:S(2)}, u32[]{:S(2)}) collective-permute-start(s16[408,128]{1,0:T(8,128)(2,1)S(1)} %get-tuple-element.205), channel_id=1, source_target_pairs={{0,17},{1,16},{2,19},{3,18},{4,21},{5,20},{6,23},{7,22},{8,25},{9,... | collective-permute-start | bytes 313352 | tf_op jit(solution)/shard_map/ppermute | solution.py:380
  212.5 8.0 %collective-permute-start.39 = (s16[408,128]{1,0:T(8,128)(2,1)S(1)}, s16[408,128]{1,0:T(8,128)(2,1)S(1)}, u32[]{:S(2)}, u32[]{:S(2)}) collective-permute-start(s16[408,128]{1,0:T(8,128)(2,1)S(1)} %get-tuple-element.206), channel_id=1, source_target_pairs={{0,1},{1,0},{2,3},{3,2},{4,5},{5,4},{6,7},{7,6},{8,9},{9,8},{10,11... | collective-permute-start | bytes 313352 | tf_op jit(solution)/shard_map/ppermute | solution.py:380
  213.0 10.3 %collective-permute-start.40 = (s16[408,128]{1,0:T(8,128)(2,1)S(1)}, s16[408,128]{1,0:T(8,128)(2,1)S(1)}, u32[]{:S(2)}, u32[]{:S(2)}) collective-permute-start(s16[408,128]{1,0:T(8,128)(2,1)S(1)} %get-tuple-element.207), channel_id=1, source_target_pairs={{0,16},{1,17},{2,18},{3,19},{4,20},{5,21},{6,22},{7,23},{8,24},{9,... | collective-permute-start | bytes 313352 | tf_op jit(solution)/shard_map/ppermute | solution.py:380

commit v6 on v5

--- a/solution.py
+++ b/solution.py
@@ -10,7 +10,7 @@
 BLK = 128
 TAIL = 8
 CUTS = (1, 2, 2, 2, 1)
-STEPS = (1, 3, 4)
+STEPS = (2, 3, 6, 8)
 TILE = 256
 AXES = ("src", "dst")
 F32 = jnp.float32
@@ -133,7 +133,7 @@
 def score_kernel(groups, *refs):
     negs = refs[:groups]
     src_ref, dst_ref, op_ref, gpos_ref, gs_ref, gd_ref = refs[groups : groups + 6]
-    outs = refs[groups + 6 : 2 * groups + 6]
+    outs = refs[groups + 6 :]
     each = negs[0].shape[1]
     count = groups * each
     wide = jnp.concatenate([n[...] for n in negs], axis=1)
@@ -145,7 +145,7 @@
     g_neg = (jax.nn.sigmoid(scores) / count).astype(BF16)
     sums = lax.dot_general(u_half, g_neg, NT, preferred_element_type=F32)
     for g in range(groups):
-        outs[g][...] = sums[:, g * each : (g + 1) * each].astype(BF16)
+        outs[g // 2][g % 2] = sums[:, g * each : (g + 1) * each].astype(BF16)
     g_pos = gpos_ref[...]
     grad_u = g_pos * dst_ref[...].astype(F32) + jnp.dot(wide, g_neg, preferred_element_type=F32)
     gs_ref[0], gs_ref[1] = split(grad_u * operator)
@@ -161,15 +161,34 @@
         out_shape=(
             jax.ShapeDtypeStruct((2, width, edges), BF16),
             jax.ShapeDtypeStruct((2, width, edges), BF16),
-            *[jax.ShapeDtypeStruct((width, each), BF16)] * groups,
+            *[jax.ShapeDtypeStruct((2, width, each), BF16)] * (groups // 2),
         ),
         in_specs=[whole()] * (groups + 4),
-        out_specs=(whole(),) * (groups + 2),
+        out_specs=(whole(),) * (groups // 2 + 2),
         compiler_params=params(20 * MIB),
         cost_estimate=cost(6 * width * edges * groups * each),
         name="score",
     )(*negs, source, target, operator, g_pos)
     return out[0], out[1], out[2:]
+
+
+def mix_kernel(*refs):
+    parts, own_ref, other_ref = refs[:-2], refs[-2], refs[-1]
+    own_ref[...] = sum(p[0].astype(F32) for p in parts)
+    other_ref[...] = sum(p[1].astype(F32) for p in parts).astype(BF16)
+
+
+def mix(parts):
+    shape = parts[0].shape[1:]
+    return pl.pallas_call(
+        mix_kernel,
+        out_shape=(jax.ShapeDtypeStruct(shape, F32), jax.ShapeDtypeStruct(shape, BF16)),
+        in_specs=[whole()] * len(parts),
+        out_specs=(whole(), whole()),
+        compiler_params=params(0),
+        cost_estimate=cost(MIB),
+        name="mix",
+    )(*parts)
 
 
 def scatter_kernel(first, gs_ref, gd_ref, spos, dpos, out_ref):
@@ -224,7 +243,10 @@
     outs, total, slot = refs[len(bounds) + peers : -2], refs[-2], refs[-1]
     width = slot.shape[0]
     total[:width], total[width:] = split(sum(g[...].astype(F32) for g in grads))
-    for k, out_ref in enumerate(outs):
+    seats = []
+    for out in outs:
+        seats += [out.at[0], out.at[1]] if len(out.shape) == 3 else [out]
+    for k, out_ref in enumerate(seats):
         alive = live_ref[first + k] > 0
         rank = rank_ref[first + k]
 
@@ -247,13 +269,15 @@
             out_ref[...] = jnp.zeros(out_ref.shape, jnp.int16)
 
 
-def pack(first, group, rank, live, chunks, bounds, grad_negs, npos):
+def pack(first, group, paired, rank, live, chunks, bounds, grad_negs, npos):
     width = chunks[0].shape[0]
+    block = (width + TAIL, BLK)
+    shape, outs = ((2,) + block, group // 2) if paired else (block, group)
     return pl.pallas_call(
         functools.partial(pack_kernel, first, tuple(bounds), len(grad_negs)),
-        out_shape=(jax.ShapeDtypeStruct((width + TAIL, BLK), jnp.int16),) * group,
+        out_shape=(jax.ShapeDtypeStruct(shape, jnp.int16),) * outs,
         in_specs=[smem(), smem()] + [whole()] * (1 + len(chunks) + len(grad_negs)),
-        out_specs=(whole(),) * group,
+        out_specs=(whole(),) * outs,
         scratch_shapes=[
             pltpu.VMEM((2 * width, npos.shape[1]), BF16),
             pltpu.VMEM((width, BLK), F32),
@@ -264,39 +288,56 @@
     )(rank, live, npos, *chunks, *grad_negs)
 
 
-def add_kernel(first, fresh, asked_ref, *refs):
-    grad = refs[-1]
-    backs = refs[: -1 if fresh else -2]
-    width = grad.shape[0]
+def add_blocks(grad, asked_ref, places, blocks):
+    for place, block in zip(places, blocks):
+        lanes = pl.ds(pl.multiple_of(asked_ref[place] * BLK, BLK), BLK)
+        grad[:, lanes] += decode(block[...], grad.shape[0])
+
+
+def add_kernel(first, count, before, fresh, asked_ref, *refs):
+    backs, grad, on_ref = refs[:count], refs[-2], refs[-1]
     if fresh:
         grad[...] = jnp.zeros_like(grad)
     for k, back in enumerate(backs):
-        lanes = pl.ds(pl.multiple_of(asked_ref[first + k] * BLK, BLK), BLK)
-        grad[:, lanes] += decode(back, width)
-
-
-def add(first, asked, backs, grad, width, rows):
+        on_ref[k] = back[1]
+    add_blocks(grad, asked_ref, range(first, first + 2 * count, 2), [b.at[0] for b in backs])
+    if before:
+        handed = refs[count]
+        add_blocks(
+            grad,
+            asked_ref,
+            range(before[0] + 1, before[0] + 2 * before[1], 2),
+            [handed.at[k] for k in range(before[1])],
+        )
+
+
+def add(first, asked, backs, before, handed, grad, width, rows):
     fresh = grad is None
-    extra = [] if fresh else [grad]
-    return pl.pallas_call(
-        functools.partial(add_kernel, first, fresh),
-        out_shape=jax.ShapeDtypeStruct((width, rows), F32),
-        in_specs=[smem()] + [whole()] * (len(backs) + len(extra)),
-        out_specs=whole(),
-        input_output_aliases={} if fresh else {len(backs) + 1: 0},
+    more = [] if handed is None else [handed]
+    if not fresh:
+        more.append(grad)
+    return pl.pallas_call(
+        functools.partial(add_kernel, first, len(backs), before, fresh),
+        out_shape=(
+            jax.ShapeDtypeStruct((width, rows), F32),
+            jax.ShapeDtypeStruct((len(backs),) + backs[0].shape[1:], backs[0].dtype),
+        ),
+        in_specs=[smem()] + [whole()] * (len(backs) + len(more)),
+        out_specs=(whole(), whole()),
+        input_output_aliases={} if fresh else {len(backs) + len(more): 0},
         compiler_params=params(0),
         cost_estimate=cost(width * BLK * len(backs) * 64),
         name="add",
-    )(asked, *backs, *extra)
-
-
-def update_kernel(first, asked_ref, *refs):
-    backs = refs[:-7]
+    )(asked, *backs, *more)
+
+
+def update_kernel(first, before, asked_ref, *refs):
+    backs, handed = refs[:-8], refs[-8]
     grad, table_ref, state_ref, table_out, state_out, fresh, sems = refs[-7:]
     width, rows = grad.shape
-    for k, back in enumerate(backs):
-        lanes = pl.ds(pl.multiple_of(asked_ref[first + k] * BLK, BLK), BLK)
-        grad[:, lanes] += decode(back, width)
+    places = range(before[0] + 1, before[0] + 2 * before[1], 2)
+    add_blocks(grad, asked_ref, places, [handed.at[k] for k in range(before[1])])
+    add_blocks(grad, asked_ref, range(first, first + len(backs)), backs)
     span = fresh.shape[1] // sems.shape[0]
 
     def copy(b):
@@ -315,21 +356,21 @@
         copy(b).wait()
 
 
-def update(first, asked, backs, grad, table, state, parts=4):
+def update(first, asked, backs, before, handed, grad, table, state, parts=4):
     width, rows = table.shape
     return pl.pallas_call(
-        functools.partial(update_kernel, first),
+        functools.partial(update_kernel, first, before),
         out_shape=(
             jax.ShapeDtypeStruct((width, rows), F32),
             jax.ShapeDtypeStruct((1, rows), F32),
         ),
-        in_specs=[smem()] + [whole()] * (len(backs) + 3),
+        in_specs=[smem()] + [whole()] * (len(backs) + 4),
         out_specs=(anywhere(), whole()),
         scratch_shapes=[pltpu.VMEM((width, rows), F32), pltpu.SemaphoreType.DMA((parts,))],
         compiler_params=params(4 * width * rows),
         cost_estimate=cost(width * rows * 64),
         name="update",
-    )(asked, *backs, grad, table, state)
+    )(asked, *backs, handed, grad, table, state)
 
 
 def per_device(table, state, relations, rel_ids, block_list, src_pos, dst_pos, neg_pos):
@@ -347,8 +388,14 @@
     )
     operator = relations[rel_ids].T
 
-    half = devices // 2
-    order = [k for pair in zip(range(devices - 1, half - 1, -1), range(half - 1, -1, -1)) for k in pair]
+    pairs = devices // 2
+    far, near = list(range(pairs - 1, pairs // 2 - 1, -1)), list(range(pairs // 2 - 1, -1, -1))
+    lead = pairs // sum(CUTS)
+    chips = far[:lead]
+    for f, n in zip(far[lead:], near):
+        chips += [f, n]
+    chips += near[len(far) - lead :]
+    order = [2 * chip + side for chip in chips for side in range(2)]
     partners = lax.axis_index(AXES) ^ jnp.array(order, jnp.int32)
     ids = jnp.arange(devices, dtype=jnp.int32)
     seat = partners[:, None] == ids[None, :]
@@ -384,29 +431,36 @@
     negs = [own_negs] + [swap(own_negs, shift, "dst") for shift in range(1, peers)]
     source, target, g_pos = gather_edges(rows, spos, dpos, operator)
     grads_src, grads_dst, part_negs = score(negs, source, target, operator, g_pos)
-    own_grad = [part_negs[0]] + [swap(part_negs[shift], shift, "dst") for shift in range(1, peers)]
-    grad = None
-    backs, chunks = [], []
+    parts = [part_negs[0]]
+    parts += [swap(part_negs[pair], 2 * pair, "dst") for pair in range(1, peers // 2)]
+    chunks = [scatter(*bounds[0], grads_src, grads_dst, spos, dpos)]
+    parts, chunks = lax.optimization_barrier((parts, chunks))
+    mine, other = mix(parts)
+    own_grad = [mine, swap(other, 1, "dst")]
+    grad, handed, before, backs = None, None, None, []
     for g, (first, group) in enumerate(zip(firsts, sizes)):
-        if g < len(bounds):
+        last = g == len(sizes) - 1
+        if len(chunks) < len(bounds):
             edges_at = (spos, dpos)
-            if g:
+            if g > 1:
                 edges_at, backs[:1] = lax.optimization_barrier((edges_at, backs[:1]))
-            chunks.append(scatter(*bounds[g], grads_src, grads_dst, *edges_at))
-        packed = list(pack(first, group, rank, alive, chunks, bounds[: len(chunks)], own_grad, npos))
+            chunks.append(scatter(*bounds[len(chunks)], grads_src, grads_dst, *edges_at))
+        packed = list(
+            pack(first, group, not last, rank, alive, chunks, bounds[: len(chunks)], own_grad, npos)
+        )
         if g:
             ahead = len(backs) // 2
-            if grad is None:
-                packed, backs[:ahead] = lax.optimization_barrier((packed, backs[:ahead]))
-            else:
-                packed, backs[:ahead], grad = lax.optimization_barrier((packed, backs[:ahead], grad))
-            grad = add(firsts[g - 1], asked, backs, grad, width, rows_dev)
-        backs = [
-            swap(x, shift, AXES) if shift else x
-            for x, shift in zip(packed, order[first : first + group])
-        ]
+            packed, backs[:ahead], grad = lax.optimization_barrier((packed, backs[:ahead], grad))
+        shifts = order[first : first + group : 1 if last else 2]
+        sent = [swap(x, shift, AXES) if shift else x for x, shift in zip(packed, shifts)]
+        if g:
+            backs, sent[:1] = lax.optimization_barrier((backs, sent[:1]))
+            now = (firsts[g - 1], len(backs))
+            grad, hand = add(now[0], asked, backs, before, handed, grad, width, rows_dev)
+            before, handed = now, swap(hand, 1, AXES)
+        backs = sent
     new_table, new_state = update(
-        firsts[-1], asked, backs, grad, table.T, state.reshape(1, rows_dev)
+        firsts[-1], asked, backs, before, handed, grad, table.T, state.reshape(1, rows_dev)
     )
     return (new_table.T, new_state.reshape(rows_dev))
 

time: 227 us -> 238 us (1.048)
  waiting for transfers between devices: 79.8 us -> 92.6 us
    ppermute x45 -> x32, waiting for transfers between devices: 28.5 us -> 41.3 us  [swap(): return lax.ppermute(x, axis, [(i, i ^ shift) for i in range(count)])]
    ppermute x45 -> x32, starting transfers between devices: 52.8 us -> 50.4 us  [swap(): return lax.ppermute(x, axis, [(i, i ^ shift) for i in range(count)])]
    pallas_call x3 -> x4, Pallas kernels: 15.1 us -> 15.3 us  [scatter(): pl.pallas_call(functools.partial(scatter_kernel, first * BLK), out_shape=...]
    pallas_call x5 -> x6, Pallas kernels: 7.61 us -> 7.76 us  [the longest x4 3.96 us: add(): pl.pallas_call(functools.partial(add_kernel, first, len(backs), before, f...]
  transfers between devices with their start and end apart: 47 -> 34, of which waited for: 15 -> 13; matrix products, arithmetic and copies ran while one was open for 13% -> 13% of each run, Pallas kernels for 15% -> 14%
where the time goes in v6:
time: 238 us; the launch traced here: 237 us
  waiting for transfers between devices  92.6 us (39%)
  starting transfers between devices  60.5 us (25%)
  Pallas kernels  48.2 us (20%)
  local copies, waits for them, and re-layouts  30.8 us (13%)
  other arithmetic  3.86 us (2%)
    ppermute x32, starting transfers between devices, swap(): return lax.ppermute(x, axis, [(i, i ^ shift) for i in range(count)])  50.4 us
    all_to_all x1, waiting for transfers between devices, per_device(): lax.all_to_all(outgoing.transpose(0, 2, 1), AXES, split_axis=0, concat_ax...  46.3 us
    ppermute x32, waiting for transfers between devices, swap(): return lax.ppermute(x, axis, [(i, i ^ shift) for i in range(count)])  41.3 us
    gather x2, local copies, waits for them, and re-layouts, per_device(): operator = relations[rel_ids].T  18.2 us
    pallas_call x4, Pallas kernels, scatter(): pl.pallas_call(functools.partial(scatter_kernel, first * BLK), out_shape=...  15.3 us
    pallas_call x5, Pallas kernels, pack(): pl.pallas_call(functools.partial(pack_kernel, first, tuple(bounds), len(g...  9.22 us
    unnamed x17, local copies, waits for them, and re-layouts  8.62 us
    pallas_call x1, Pallas kernels, gather_edges(): pl.pallas_call(edge_kernel, grid=(edges // tile,), out_shape=(jax.ShapeDt...  8.04 us
  transfers between devices with their start and end apart: 34, of which 13 were waited for; matrix products, arithmetic and copies ran while one was open for 13% of the time, Pallas kernels for 14%

profile of v6, /device:TPU:0, one launch (start us, length us, event | category | flops | bytes accessed | tf_op | source)
XLA Modules:
  0.0 237.2 jit_solution(10186103903443042726)
XLA Ops:
  0.6 1.3 copy.29
  2.0 7.3 %all-to-all-start = ((s32[32,1,1]{2,1,0:T(1,128)}), s32[32,1,1]{2,1,0:T(1,128)S(1)}, u32[]{:S(2)}, u32[]{:S(2)}) async-start(s32[32,1,1]{2,1,0:T(1,128)} %copy.29), calls=%async_computation | async-start | bytes 32768 | tf_op jit(solution)/shard_map/all_to_all | solution.py:381
  9.3 2.1 copy_bitcast_fusion
  11.4 4.9 %all-to-all-done = s32[32,1,1]{2,1,0:T(1,128)S(1)} async-done(((s32[32,1,1]{2,1,0:T(1,128)}), s32[32,1,1]{2,1,0:T(1,128)S(1)}, u32[]{:S(2)}, u32[]{:S(2)}) %all-to-all-start) | async-done | bytes 160 | tf_op jit(solution)/shard_map/all_to_all | solution.py:381
  16.3 0.7 reduce
  17.0 2.7 %gather_fusion = bf16[32,128,400]{1,2,0:T(8,128)(2,1)} fusion(bf16[16,128,400]{1,2,0:T(8,128)(2,1)S(1)} %copy_bitcast_fusion, s32[1024]{0:T(1024)S(1)} %pad_clamp_fusion), kind=kCustom, calls=%fused_computation | custom fusion | bytes 6553728 | tf_op jit(solution)/shard_map/gather | solution.py:385
  19.7 2.8 %all-to-all-start.1 = ((bf16[32,400,128]{2,1,0:T(8,128)(2,1)}), bf16[32,400,128]{2,1,0:T(8,128)(2,1)S(1)}, u32[]{:S(2)}, u32[]{:S(2)}) async-start(bf16[32,400,128]{2,1,0:T(8,128)(2,1)} %bitcast.34), calls=%async_computation.1 | async-start | bytes 6553600 | tf_op jit(solution)/shard_map/all_to_all | solution.py:386
  22.5 8.6 %copy.31 = f32[4096,400]{1,0:T(8,128)} copy(f32[4096,400]{0,1:T(8,128)} %param.11) | data formatting | bytes 13107200 | tf_op args[2]
  31.1 12.9 %gather_fusion.1 = f32[2048,400]{1,0:T(8,128)} fusion(f32[4096,400]{1,0:T(8,128)} %copy.31, s32[2048]{0:T(1024)S(1)} %fusion.3), kind=kCustom, calls=%fused_computation.1 | custom fusion | bytes 6561792 | tf_op jit(solution)/shard_map/gather | solution.py:389
  44.1 5.2 %copy.32 = f32[2048,400]{0,1:T(8,128)} copy(f32[2048,400]{1,0:T(8,128)} %gather_fusion.1) | data formatting | bytes 6553600 | tf_op jit(solution)/shard_map/gather | solution.py:389
  49.5 0.2 select_reduce_fusion.6.live_ref
  50.0 0.2 select_reduce_fusion.3
  50.2 0.2 select_reduce_fusion
  50.4 46.3 %all-to-all-done.1.fetched = bf16[32,400,128]{2,1,0:T(8,128)(2,1)S(1)} async-done(((bf16[32,400,128]{2,1,0:T(8,128)(2,1)}), bf16[32,400,128]{2,1,0:T(8,128)(2,1)S(1)}, u32[]{:S(2)}, u32[]{:S(2)}) %all-to-all-start.1) | async-done | bytes 3276832 | tf_op jit(solution)/shard_map/all_to_all | solution.py:386
  96.8 1.7 gather_negs.1
  98.6 1.3 collective-permute-start.1
  99.9 0.6 collective-permute-start.2
  100.5 1.2 collective-permute-start.3
  101.6 0.5 collective-permute-start.4
  102.2 2.1 collective-permute-start.5
  104.3 0.9 collective-permute-start.6
  105.3 8.0 %gather_edges.1 = (bf16[400,2048]{1,0:T(8,128)(2,1)S(1)}, bf16[400,2048]{1,0:T(8,128)(2,1)S(1)}, f32[1,2048]{1,0:T(1,128)S(1)}) custom-call(bf16[400,2048]{1,0:T(8,128)(2,1)S(1)} %get-tuple-element.111.rows, s32[1,2048]{1,0:T(1,128)S(1)} %bitcast.23, s32[1,2048]{1,0:T(1,128)S(1)} %bitcast.28, f32[400,2048]{1,0:T(8,128)S(1)} %bitcast.21), custom_call_target="tpu_custom_call" | custom-call | flops 6710886400 | bytes 13107200 | tf_op jit(solution)/shard_map/gather_edges/pallas_call | solution.py:112
  113.4 6.1 %score.1 = (bf16[2,400,2048]{2,1,0:T(8,128)(2,1)S(1)}, bf16[2,400,2048]{2,1,0:T(8,128)(2,1)S(1)}, bf16[2,400,128]{2,1,0:T(8,128)(2,1)S(1)}, bf16[2,400,128]{2,1,...) custom-call(bf16[400,128]{1,0:T(8,128)(2,1)S(1)} %get-tuple-element.110.refs_0_, ...), custom_call_target="tpu_custom_call" | custom-call | flops 5033164800 | bytes 9830400 | tf_op jit(solution)/shard_map/score/pallas_call | solution.py:159
  119.5 0.8 collective-permute-start.7
  120.4 1.5 collective-permute-start.8
  121.8 1.2 collective-permute-start.9
  123.1 4.0 %scatter.4.refs_0_ = f32[400,512]{1,0:T(8,128)S(1)} custom-call(bf16[2,400,2048]{2,1,0:T(8,128)(2,1)S(1)} %get-tuple-element.122.gs_ref, bf16[2,400,2048]{2,1,0:T(8,128)(2,1)S(1)} %get-tuple-element.123.gd_ref, s32[1,2048]{1,0:T(1,128)S(1)} %bitcast.24, s32[1,2048]{1,0:T(1,128)S(1)} %bitcast.29), custom_call_target="tpu_custom_call" | custom-call | flops 1677721600 | bytes 3276800 | tf_op jit(solution)/shard_map/scatter/pallas_call | solution.py:215
  127.1 0.2 collective-permute-done.7.refs_1_
  127.2 5.3 %collective-permute-done.8.refs_2_ = bf16[2,400,128]{2,1,0:T(8,128)(2,1)S(1)} collective-permute-done((bf16[2,400,128]{2,1,0:T(8,128)(2,1)S(1)}, bf16[2,400,128]{2,1,0:T(8,128)(2,1)S(1)}, u32[]{:S(2)}, u32[]{:S(2)}) %collective-permute-start.8) | collective-permute-done | bytes 204832 | tf_op jit(solution)/shard_map/ppermute | solution.py:427
  132.7 1.9 scatter.5.refs_1_
  134.6 0.7 pack.6
  135.3 2.7 %collective-permute-start.11 = (s16[2,408,128]{2,1,0:T(8,128)(2,1)S(1)}, s16[2,408,128]{2,1,0:T(8,128)(2,1)S(1)}, u32[]{:S(2)}, u32[]{:S(2)}) collective-permute-start(s16[2,408,128]{2,1,0:T(8,128)(2,1)S(1)} %get-tuple-element.135), channel_id=1, source_target_pairs={{0,30},{1,31},{2,28},{3,29},{4,26},{5,27},{6,24},{7,25},{8,22},{9,... | collective-permute-start | bytes 626696 | tf_op jit(solution)/shard_map/ppermute | solution.py:427
  138.0 5.7 %scatter.6.refs_2_ = f32[400,768]{1,0:T(8,128)S(1)} custom-call(bf16[2,400,2048]{2,1,0:T(8,128)(2,1)S(1)} %get-tuple-element.122.gs_ref, bf16[2,400,2048]{2,1,0:T(8,128)(2,1)S(1)} %get-tuple-element.123.gd_ref, s32[1,2048]{1,0:T(1,128)S(1)} %bitcast.26, s32[1,2048]{1,0:T(1,128)S(1)} %bitcast.31), custom_call_target="tpu_custom_call" | custom-call | flops 2516582400 | bytes 4915200 | tf_op jit(solution)/shard_map/scatter/pallas_call | solution.py:215
  143.7 4.0 %collective-permute-start.12 = (s16[2,408,128]{2,1,0:T(8,128)(2,1)S(1)}, s16[2,408,128]{2,1,0:T(8,128)(2,1)S(1)}, u32[]{:S(2)}, u32[]{:S(2)}) collective-permute-start(s16[2,408,128]{2,1,0:T(8,128)(2,1)S(1)} %get-tuple-element.137), channel_id=1, source_target_pairs={{0,28},{1,29},{2,30},{3,31},{4,24},{5,25},{6,26},{7,27},{8,20},{9,... | collective-permute-start | bytes 626696 | tf_op jit(solution)/shard_map/ppermute | solution.py:427
  147.7 1.8 pack.5
  149.5 2.1 collective-permute-start.13
  151.6 1.2 collective-permute-start.14
  152.7 0.4 collective-permute-start.15
  153.1 3.2 %collective-permute-start.16 = (s16[2,408,128]{2,1,0:T(8,128)(2,1)S(1)}, s16[2,408,128]{2,1,0:T(8,128)(2,1)S(1)}, u32[]{:S(2)}, u32[]{:S(2)}) collective-permute-start(s16[2,408,128]{2,1,0:T(8,128)(2,1)S(1)} %get-tuple-element.162), channel_id=1, source_target_pairs={{0,12},{1,13},{2,14},{3,15},{4,8},{5,9},{6,10},{7,11},{8,4},{9,5},... | collective-permute-start | bytes 626696 | tf_op jit(solution)/shard_map/ppermute | solution.py:427
  156.3 4.1 %collective-permute-done.13.refs_0_ = s16[2,408,128]{2,1,0:T(8,128)(2,1)S(1)} collective-permute-done((s16[2,408,128]{2,1,0:T(8,128)(2,1)S(1)}, s16[2,408,128]{2,1,0:T(8,128)(2,1)S(1)}, u32[]{:S(2)}, u32[]{:S(2)}) %collective-permute-start.13) | collective-permute-done | bytes 208928 | tf_op jit(solution)/shard_map/ppermute | solution.py:427
  160.4 0.9 add.91
  161.3 3.8 %scatter.7.refs_3_ = f32[400,512]{1,0:T(8,128)S(1)} custom-call(bf16[2,400,2048]{2,1,0:T(8,128)(2,1)S(1)} %get-tuple-element.122.gs_ref, bf16[2,400,2048]{2,1,0:T(8,128)(2,1)S(1)} %get-tuple-element.123.gd_ref, s32[1,2048]{1,0:T(1,128)S(1)} %bitcast.27, s32[1,2048]{1,0:T(1,128)S(1)} %bitcast.32), custom_call_target="tpu_custom_call" | custom-call | flops 1677721600 | bytes 3276800 | tf_op jit(solution)/shard_map/scatter/pallas_call | solution.py:215
  165.1 2.4 %pack.9 = (s16[2,408,128]{2,1,0:T(8,128)(2,1)S(1)}, s16[2,408,128]{2,1,0:T(8,128)(2,1)S(1)}, s16[2,408,128]{2,1,0:T(8,128)(2,1)S(1)}, s16[2,408,128]{2,1,0:T(8,128)(2,1)S(1)}) custom-call(s32[32]{0:T(128)S(1)} %select_reduce_fusion.5.rank_ref, s32[32]{0:T(128)S(1)} %select_reduce_fusion.6.live_ref, s32[1,128]{1,0:T(1,128)S(1)} %fusion.11.pos_ref.npos, ...), custom_call_target="tpu_custom_call" | custom-call | flops 209715200 | bytes 409600 | tf_op jit(solution)/shard_map/pack/pallas_call | solution.py:276
  167.5 12.5 %collective-permute-start.17 = (s16[2,408,128]{2,1,0:T(8,128)(2,1)S(1)}, s16[2,408,128]{2,1,0:T(8,128)(2,1)S(1)}, u32[]{:S(2)}, u32[]{:S(2)}) collective-permute-start(s16[2,408,128]{2,1,0:T(8,128)(2,1)S(1)} %get-tuple-element.163), channel_id=1, source_target_pairs={{0,22},{1,23},{2,20},{3,21},{4,18},{5,19},{6,16},{7,17},{8,30},{9,... | collective-permute-start | bytes 626696 | tf_op jit(solution)/shard_map/ppermute | solution.py:427
  180.0 9.5 %collective-permute-done.17.refs_0_ = s16[2,408,128]{2,1,0:T(8,128)(2,1)S(1)} collective-permute-done((s16[2,408,128]{2,1,0:T(8,128)(2,1)S(1)}, s16[2,408,128]{2,1,0:T(8,128)(2,1)S(1)}, u32[]{:S(2)}, u32[]{:S(2)}) %collective-permute-start.17) | collective-permute-done | bytes 208928 | tf_op jit(solution)/shard_map/ppermute | solution.py:427
  189.5 0.9 add.92
  190.5 5.3 %collective-permute-start.20 = (s16[2,408,128]{2,1,0:T(8,128)(2,1)S(1)}, s16[2,408,128]{2,1,0:T(8,128)(2,1)S(1)}, u32[]{:S(2)}, u32[]{:S(2)}) collective-permute-start(s16[2,408,128]{2,1,0:T(8,128)(2,1)S(1)} %get-tuple-element.175), channel_id=1, source_target_pairs={{0,20},{1,21},{2,22},{3,23},{4,16},{5,17},{6,18},{7,19},{8,28},{9,... | collective-permute-start | bytes 626696 | tf_op jit(solution)/shard_map/ppermute | solution.py:427
  195.9 2.9 %pack.8 = (s16[2,408,128]{2,1,0:T(8,128)(2,1)S(1)}, s16[2,408,128]{2,1,0:T(8,128)(2,1)S(1)}, s16[2,408,128]{2,1,0:T(8,128)(2,1)S(1)}, s16[2,408,128]{2,1,0:T(8,128)(2,1)S(1)}) custom-call(s32[32]{0:T(128)S(1)} %select_reduce_fusion.5.rank_ref, s32[32]{0:T(128)S(1)} %select_reduce_fusion.6.live_ref, s32[1,128]{1,0:T(1,128)S(1)} %fusion.11.pos_ref.npos, ...), custom_call_target="tpu_custom_call" | custom-call | flops 209715200 | bytes 409600 | tf_op jit(solution)/shard_map/pack/pallas_call | solution.py:276
  198.8 0.6 collective-permute-start.22
  199.4 4.1 %collective-permute-done.20.refs_2_ = s16[2,408,128]{2,1,0:T(8,128)(2,1)S(1)} collective-permute-done((s16[2,408,128]{2,1,0:T(8,128)(2,1)S(1)}, s16[2,408,128]{2,1,0:T(8,128)(2,1)S(1)}, u32[]{:S(2)}, u32[]{:S(2)}) %collective-permute-start.20) | collective-permute-done | bytes 208928 | tf_op jit(solution)/shard_map/ppermute | solution.py:427
  203.5 4.1 %collective-permute-done.21.refs_3_ = s16[2,408,128]{2,1,0:T(8,128)(2,1)S(1)} collective-permute-done((s16[2,408,128]{2,1,0:T(8,128)(2,1)S(1)}, s16[2,408,128]{2,1,0:T(8,128)(2,1)S(1)}, u32[]{:S(2)}, u32[]{:S(2)}) %collective-permute-start.21) | collective-permute-done | bytes 208928 | tf_op jit(solution)/shard_map/ppermute | solution.py:427
  207.6 4.2 %collective-permute-done.22.refs_0_ = s16[2,408,128]{2,1,0:T(8,128)(2,1)S(1)} collective-permute-done((s16[2,408,128]{2,1,0:T(8,128)(2,1)S(1)}, s16[2,408,128]{2,1,0:T(8,128)(2,1)S(1)}, u32[]{:S(2)}, u32[]{:S(2)}) %collective-permute-start.22) | collective-permute-done | bytes 208928 | tf_op jit(solution)/shard_map/ppermute | solution.py:427
  211.8 1.1 add.93
  213.0 1.9 collective-permute-start.23
  214.8 1.2 collective-permute-start.25
  216.1 1.3 collective-permute-start.26
  217.4 1.4 pack.7
  218.8 2.8 %collective-permute-done.23.refs_1_ = s16[2,408,128]{2,1,0:T(8,128)(2,1)S(1)} collective-permute-done((s16[2,408,128]{2,1,0:T(8,128)(2,1)S(1)}, s16[2,408,128]{2,1,0:T(8,128)(2,1)S(1)}, u32[]{:S(2)}, u32[]{:S(2)}) %collective-permute-start.23) | collective-permute-done | bytes 208928 | tf_op jit(solution)/shard_map/ppermute | solution.py:427
  221.6 2.3 collective-permute-start.27
  223.8 3.6 %collective-permute-done.25.refs_2_ = s16[2,408,128]{2,1,0:T(8,128)(2,1)S(1)} collective-permute-done((s16[2,408,128]{2,1,0:T(8,128)(2,1)S(1)}, s16[2,408,128]{2,1,0:T(8,128)(2,1)S(1)}, u32[]{:S(2)}, u32[]{:S(2)}) %collective-permute-start.25) | collective-permute-done | bytes 208928 | tf_op jit(solution)/shard_map/ppermute | solution.py:427
  227.4 1.1 add.94
  228.6 1.2 collective-permute-start.28
  229.9 3.4 %collective-permute-done.28.refs_1_ = s16[408,128]{1,0:T(8,128)(2,1)S(1)} collective-permute-done((s16[408,128]{1,0:T(8,128)(2,1)S(1)}, s16[408,128]{1,0:T(8,128)(2,1)S(1)}, u32[]{:S(2)}, u32[]{:S(2)}) %collective-permute-start.28) | collective-permute-done | bytes 104480 | tf_op jit(solution)/shard_map/ppermute | solution.py:427
  233.3 3.7 %update.1 = (f32[400,2048]{1,0:T(8,128)}, f32[1,2048]{1,0:T(1,128)}) custom-call(s32[32]{0:T(128)S(1)} %get-tuple-element.104.asked_ref, s16[408,128]{1,0:T(8,128)(2,1)S(1)} %collective-permute-done.27.refs_0_, s16[408,128]{1,0:T(8,128)(2,1)S(1)} %collective-permute-done.28.refs_1_, s16[408,128]{1,0:T(8,128)(2,1)S(1)} %get-tuple-element.194.refs_2_, ...), custom_call_target="tpu_custom_call" | custom-call | flops 52428800 | bytes 102400 | tf_op jit(solution)/shard_map/update/pallas_call | solution.py:361
  (63 shorter events, 1.2 us)
Async XLA Ops:
  2.0 14.4 %all-to-all-start = ((s32[32,1,1]{2,1,0:T(1,128)}), s32[32,1,1]{2,1,0:T(1,128)S(1)}, u32[]{:S(2)}, u32[]{:S(2)}) async-start(s32[32,1,1]{2,1,0:T(1,128)} %copy.29), calls=%async_computation | async-start | bytes 32768 | tf_op jit(solution)/shard_map/all_to_all | solution.py:381
  19.7 77.1 %all-to-all-start.1 = ((bf16[32,400,128]{2,1,0:T(8,128)(2,1)}), bf16[32,400,128]{2,1,0:T(8,128)(2,1)S(1)}, u32[]{:S(2)}, u32[]{:S(2)}) async-start(bf16[32,400,128]{2,1,0:T(8,128)(2,1)} %bitcast.34), calls=%async_computation.1 | async-start | bytes 6553600 | tf_op jit(solution)/shard_map/all_to_all | solution.py:386
  22.5 8.6 %copy-start.5 = (s32[2048]{0:T(1024)S(1)}, s32[2048]{0:T(1024)}, u32[]{:S(2)}) copy-start(s32[2048]{0:T(1024)} %param.12) | copy-start | bytes 24580
  44.1 5.3 %copy-start.3 = (s32[2048]{0:T(1024)S(1)}, s32[2048]{0:T(1024)}, u32[]{:S(2)}) copy-start(s32[2048]{0:T(1024)} %param.14) | copy-start | bytes 24580
  44.1 5.4 %copy-start.7 = (s32[32]{0:T(128)S(1)}, s32[32]{0:T(128)}, u32[]{:S(2)}) copy-start(s32[32]{0:T(128)} %constant.83.clone) | copy-start | bytes 388
  44.1 5.9 %copy-start.6 = (s32[128]{0:T(128)S(1)}, s32[128]{0:T(128)}, u32[]{:S(2)}) copy-start(s32[128]{0:T(128)} %param.16) | copy-start | bytes 1540
  44.1 5.9 %copy-start.4 = (s32[2048]{0:T(1024)S(1)}, s32[2048]{0:T(1024)}, u32[]{:S(2)}) copy-start(s32[2048]{0:T(1024)} %param.15) | copy-start | bytes 24580
  96.8 8.5 %copy-start.1 = (f32[2048,400]{0,1:T(8,128)S(1)}, f32[2048,400]{0,1:T(8,128)}, u32[]{:S(2)}) copy-start(f32[2048,400]{0,1:T(8,128)} %copy.32) | copy-start | bytes 9830404
  98.5 3.6 %collective-permute-start = (bf16[400,128]{1,0:T(8,128)(2,1)S(1)}, bf16[400,128]{1,0:T(8,128)(2,1)S(1)}, u32[]{:S(2)}, u32[]{:S(2)}) collective-permute-start(bf16[400,128]{1,0:T(8,128)(2,1)S(1)} %get-tuple-element.110.refs_0_), channel_id=1, source_target_pairs={{0,1},{1,0},{2,3},{3,2},{4,5},{5,4},{6,7},{7,6},{8,9},{9,8},{10,11... | collective-permute-start | bytes 307208 | tf_op jit(solution)/shard_map/ppermute | solution.py:427
  98.6 5.7 %collective-permute-start.1 = (bf16[400,128]{1,0:T(8,128)(2,1)S(1)}, bf16[400,128]{1,0:T(8,128)(2,1)S(1)}, u32[]{:S(2)}, u32[]{:S(2)}) collective-permute-start(bf16[400,128]{1,0:T(8,128)(2,1)S(1)} %get-tuple-element.110.refs_0_), channel_id=1, source_target_pairs={{0,2},{1,3},{2,0},{3,1},{4,6},{5,7},{6,4},{7,5},{8,10},{9,11},{10,... | collective-permute-start | bytes 307208 | tf_op jit(solution)/shard_map/ppermute | solution.py:427
  99.9 13.5 %collective-permute-start.2 = (bf16[400,128]{1,0:T(8,128)(2,1)S(1)}, bf16[400,128]{1,0:T(8,128)(2,1)S(1)}, u32[]{:S(2)}, u32[]{:S(2)}) collective-permute-start(bf16[400,128]{1,0:T(8,128)(2,1)S(1)} %get-tuple-element.110.refs_0_), channel_id=1, source_target_pairs={{0,3},{1,2},{2,1},{3,0},{4,7},{5,6},{6,5},{7,4},{8,11},{9,10},{10,... | collective-permute-start | bytes 307208 | tf_op jit(solution)/shard_map/ppermute | solution.py:427
  100.5 12.9 %collective-permute-start.3 = (bf16[400,128]{1,0:T(8,128)(2,1)S(1)}, bf16[400,128]{1,0:T(8,128)(2,1)S(1)}, u32[]{:S(2)}, u32[]{:S(2)}) collective-permute-start(bf16[400,128]{1,0:T(8,128)(2,1)S(1)} %get-tuple-element.110.refs_0_), channel_id=1, source_target_pairs={{0,4},{1,5},{2,6},{3,7},{4,0},{5,1},{6,2},{7,3},{8,12},{9,13},{10,... | collective-permute-start | bytes 307208 | tf_op jit(solution)/shard_map/ppermute | solution.py:427
  101.6 11.7 %collective-permute-start.4 = (bf16[400,128]{1,0:T(8,128)(2,1)S(1)}, bf16[400,128]{1,0:T(8,128)(2,1)S(1)}, u32[]{:S(2)}, u32[]{:S(2)}) collective-permute-start(bf16[400,128]{1,0:T(8,128)(2,1)S(1)} %get-tuple-element.110.refs_0_), channel_id=1, source_target_pairs={{0,5},{1,4},{2,7},{3,6},{4,1},{5,0},{6,3},{7,2},{8,13},{9,12},{10,... | collective-permute-start | bytes 307208 | tf_op jit(solution)/shard_map/ppermute | solution.py:427
  102.2 11.2 %collective-permute-start.5 = (bf16[400,128]{1,0:T(8,128)(2,1)S(1)}, bf16[400,128]{1,0:T(8,128)(2,1)S(1)}, u32[]{:S(2)}, u32[]{:S(2)}) collective-permute-start(bf16[400,128]{1,0:T(8,128)(2,1)S(1)} %get-tuple-element.110.refs_0_), channel_id=1, source_target_pairs={{0,6},{1,7},{2,4},{3,5},{4,2},{5,3},{6,0},{7,1},{8,14},{9,15},{10,... | collective-permute-start | bytes 307208 | tf_op jit(solution)/shard_map/ppermute | solution.py:427
  104.3 9.0 %collective-permute-start.6 = (bf16[400,128]{1,0:T(8,128)(2,1)S(1)}, bf16[400,128]{1,0:T(8,128)(2,1)S(1)}, u32[]{:S(2)}, u32[]{:S(2)}) collective-permute-start(bf16[400,128]{1,0:T(8,128)(2,1)S(1)} %get-tuple-element.110.refs_0_), channel_id=1, source_target_pairs={{0,7},{1,6},{2,5},{3,4},{4,3},{5,2},{6,1},{7,0},{8,15},{9,14},{10,... | collective-permute-start | bytes 307208 | tf_op jit(solution)/shard_map/ppermute | solution.py:427
  119.5 7.7 %collective-permute-start.7 = (bf16[2,400,128]{2,1,0:T(8,128)(2,1)S(1)}, bf16[2,400,128]{2,1,0:T(8,128)(2,1)S(1)}, u32[]{:S(2)}, u32[]{:S(2)}) collective-permute-start(bf16[2,400,128]{2,1,0:T(8,128)(2,1)S(1)} %get-tuple-element.119), channel_id=1, source_target_pairs={{0,2},{1,3},{2,0},{3,1},{4,6},{5,7},{6,4},{7,5},{8,10},{9,11},{10,... | collective-permute-start | bytes 614408 | tf_op jit(solution)/shard_map/ppermute | solution.py:427
  120.4 12.1 %collective-permute-start.8 = (bf16[2,400,128]{2,1,0:T(8,128)(2,1)S(1)}, bf16[2,400,128]{2,1,0:T(8,128)(2,1)S(1)}, u32[]{:S(2)}, u32[]{:S(2)}) collective-permute-start(bf16[2,400,128]{2,1,0:T(8,128)(2,1)S(1)} %get-tuple-element.120), channel_id=1, source_target_pairs={{0,4},{1,5},{2,6},{3,7},{4,0},{5,1},{6,2},{7,3},{8,12},{9,13},{10,... | collective-permute-start | bytes 614408 | tf_op jit(solution)/shard_map/ppermute | solution.py:427
  121.8 10.6 %collective-permute-start.9 = (bf16[2,400,128]{2,1,0:T(8,128)(2,1)S(1)}, bf16[2,400,128]{2,1,0:T(8,128)(2,1)S(1)}, u32[]{:S(2)}, u32[]{:S(2)}) collective-permute-start(bf16[2,400,128]{2,1,0:T(8,128)(2,1)S(1)} %get-tuple-element.121), channel_id=1, source_target_pairs={{0,6},{1,7},{2,4},{3,5},{4,2},{5,3},{6,0},{7,1},{8,14},{9,15},{10,... | collective-permute-start | bytes 614408 | tf_op jit(solution)/shard_map/ppermute | solution.py:427
  132.6 2.0 collective-permute-start.10
  135.3 14.2 %collective-permute-start.11 = (s16[2,408,128]{2,1,0:T(8,128)(2,1)S(1)}, s16[2,408,128]{2,1,0:T(8,128)(2,1)S(1)}, u32[]{:S(2)}, u32[]{:S(2)}) collective-permute-start(s16[2,408,128]{2,1,0:T(8,128)(2,1)S(1)} %get-tuple-element.135), channel_id=1, source_target_pairs={{0,30},{1,31},{2,28},{3,29},{4,26},{5,27},{6,24},{7,25},{8,22},{9,... | collective-permute-start | bytes 626696 | tf_op jit(solution)/shard_map/ppermute | solution.py:427
  143.7 12.7 %collective-permute-start.12 = (s16[2,408,128]{2,1,0:T(8,128)(2,1)S(1)}, s16[2,408,128]{2,1,0:T(8,128)(2,1)S(1)}, u32[]{:S(2)}, u32[]{:S(2)}) collective-permute-start(s16[2,408,128]{2,1,0:T(8,128)(2,1)S(1)} %get-tuple-element.137), channel_id=1, source_target_pairs={{0,28},{1,29},{2,30},{3,31},{4,24},{5,25},{6,26},{7,27},{8,20},{9,... | collective-permute-start | bytes 626696 | tf_op jit(solution)/shard_map/ppermute | solution.py:427
  149.5 10.9 %collective-permute-start.13 = (s16[2,408,128]{2,1,0:T(8,128)(2,1)S(1)}, s16[2,408,128]{2,1,0:T(8,128)(2,1)S(1)}, u32[]{:S(2)}, u32[]{:S(2)}) collective-permute-start(s16[2,408,128]{2,1,0:T(8,128)(2,1)S(1)} %get-tuple-element.138), channel_id=1, source_target_pairs={{0,26},{1,27},{2,24},{3,25},{4,30},{5,31},{6,28},{7,29},{8,18},{9,... | collective-permute-start | bytes 626696 | tf_op jit(solution)/shard_map/ppermute | solution.py:427
  151.6 15.9 %collective-permute-start.14 = (s16[2,408,128]{2,1,0:T(8,128)(2,1)S(1)}, s16[2,408,128]{2,1,0:T(8,128)(2,1)S(1)}, u32[]{:S(2)}, u32[]{:S(2)}) collective-permute-start(s16[2,408,128]{2,1,0:T(8,128)(2,1)S(1)} %get-tuple-element.155), channel_id=1, source_target_pairs={{0,14},{1,15},{2,12},{3,13},{4,10},{5,11},{6,8},{7,9},{8,6},{9,7},... | collective-permute-start | bytes 626696 | tf_op jit(solution)/shard_map/ppermute | solution.py:427
  152.7 27.3 %collective-permute-start.15 = (s16[2,408,128]{2,1,0:T(8,128)(2,1)S(1)}, s16[2,408,128]{2,1,0:T(8,128)(2,1)S(1)}, u32[]{:S(2)}, u32[]{:S(2)}) collective-permute-start(s16[2,408,128]{2,1,0:T(8,128)(2,1)S(1)} %get-tuple-element.161), channel_id=1, source_target_pairs={{0,24},{1,25},{2,26},{3,27},{4,28},{5,29},{6,30},{7,31},{8,16},{9,... | collective-permute-start | bytes 626696 | tf_op jit(solution)/shard_map/ppermute | solution.py:427
  153.1 26.9 %collective-permute-start.16 = (s16[2,408,128]{2,1,0:T(8,128)(2,1)S(1)}, s16[2,408,128]{2,1,0:T(8,128)(2,1)S(1)}, u32[]{:S(2)}, u32[]{:S(2)}) collective-permute-start(s16[2,408,128]{2,1,0:T(8,128)(2,1)S(1)} %get-tuple-element.162), channel_id=1, source_target_pairs={{0,12},{1,13},{2,14},{3,15},{4,8},{5,9},{6,10},{7,11},{8,4},{9,5},... | collective-permute-start | bytes 626696 | tf_op jit(solution)/shard_map/ppermute | solution.py:427
  167.5 22.0 %collective-permute-start.17 = (s16[2,408,128]{2,1,0:T(8,128)(2,1)S(1)}, s16[2,408,128]{2,1,0:T(8,128)(2,1)S(1)}, u32[]{:S(2)}, u32[]{:S(2)}) collective-permute-start(s16[2,408,128]{2,1,0:T(8,128)(2,1)S(1)} %get-tuple-element.163), channel_id=1, source_target_pairs={{0,22},{1,23},{2,20},{3,21},{4,18},{5,19},{6,16},{7,17},{8,30},{9,... | collective-permute-start | bytes 626696 | tf_op jit(solution)/shard_map/ppermute | solution.py:427
  180.0 9.5 %collective-permute-start.19 = (s16[2,408,128]{2,1,0:T(8,128)(2,1)S(1)}, s16[2,408,128]{2,1,0:T(8,128)(2,1)S(1)}, u32[]{:S(2)}, u32[]{:S(2)}) collective-permute-start(s16[2,408,128]{2,1,0:T(8,128)(2,1)S(1)} %get-tuple-element.170), channel_id=1, source_target_pairs={{0,1},{1,0},{2,3},{3,2},{4,5},{5,4},{6,7},{7,6},{8,9},{9,8},{10,11... | collective-permute-start | bytes 626696 | tf_op jit(solution)/shard_map/ppermute | solution.py:427
  180.0 18.8 %collective-permute-start.18 = (s16[2,408,128]{2,1,0:T(8,128)(2,1)S(1)}, s16[2,408,128]{2,1,0:T(8,128)(2,1)S(1)}, u32[]{:S(2)}, u32[]{:S(2)}) collective-permute-start(s16[2,408,128]{2,1,0:T(8,128)(2,1)S(1)} %get-tuple-element.165), channel_id=1, source_target_pairs={{0,10},{1,11},{2,8},{3,9},{4,14},{5,15},{6,12},{7,13},{8,2},{9,3},... | collective-permute-start | bytes 626696 | tf_op jit(solution)/shard_map/ppermute | solution.py:427
  190.5 21.3 %collective-permute-start.24 = (s16[4,408,128]{2,1,0:T(8,128)(2,1)S(1)}, s16[4,408,128]{2,1,0:T(8,128)(2,1)S(1)}, u32[]{:S(2)}, u32[]{:S(2)}) collective-permute-start(s16[4,408,128]{2,1,0:T(8,128)(2,1)S(1)} %get-tuple-element.184), channel_id=1, source_target_pairs={{0,1},{1,0},{2,3},{3,2},{4,5},{5,4},{6,7},{7,6},{8,9},{9,8},{10,11... | collective-permute-start | bytes 1253384 | tf_op jit(solution)/shard_map/ppermute | solution.py:427
  190.5 12.9 %collective-permute-start.20 = (s16[2,408,128]{2,1,0:T(8,128)(2,1)S(1)}, s16[2,408,128]{2,1,0:T(8,128)(2,1)S(1)}, u32[]{:S(2)}, u32[]{:S(2)}) collective-permute-start(s16[2,408,128]{2,1,0:T(8,128)(2,1)S(1)} %get-tuple-element.175), channel_id=1, source_target_pairs={{0,20},{1,21},{2,22},{3,23},{4,16},{5,17},{6,18},{7,19},{8,28},{9,... | collective-permute-start | bytes 626696 | tf_op jit(solution)/shard_map/ppermute | solution.py:427
  195.9 11.7 %collective-permute-start.21 = (s16[2,408,128]{2,1,0:T(8,128)(2,1)S(1)}, s16[2,408,128]{2,1,0:T(8,128)(2,1)S(1)}, u32[]{:S(2)}, u32[]{:S(2)}) collective-permute-start(s16[2,408,128]{2,1,0:T(8,128)(2,1)S(1)} %get-tuple-element.176), channel_id=1, source_target_pairs={{0,8},{1,9},{2,10},{3,11},{4,12},{5,13},{6,14},{7,15},{8,0},{9,1},... | collective-permute-start | bytes 626696 | tf_op jit(solution)/shard_map/ppermute | solution.py:427
  198.8 13.0 %collective-permute-start.22 = (s16[2,408,128]{2,1,0:T(8,128)(2,1)S(1)}, s16[2,408,128]{2,1,0:T(8,128)(2,1)S(1)}, u32[]{:S(2)}, u32[]{:S(2)}) collective-permute-start(s16[2,408,128]{2,1,0:T(8,128)(2,1)S(1)} %get-tuple-element.177), channel_id=1, source_target_pairs={{0,18},{1,19},{2,16},{3,17},{4,22},{5,23},{6,20},{7,21},{8,26},{9,... | collective-permute-start | bytes 626696 | tf_op jit(solution)/shard_map/ppermute | solution.py:427
  212.9 20.5 %copy-start = (f32[2048,400]{0,1:T(8,128)S(1)}, f32[2048,400]{0,1:T(8,128)}, u32[]{:S(2)}) copy-start(f32[2048,400]{0,1:T(8,128)} %param.9) | copy-start | bytes 9830404
  212.9 20.4 %copy-start.2 = (f32[2048]{0:T(1024)S(1)}, f32[2048]{0:T(1024)}, u32[]{:S(2)}) copy-start(f32[2048]{0:T(1024)} %param.10) | copy-start | bytes 24580
  212.9 14.5 %collective-permute-start.30 = (s16[4,408,128]{2,1,0:T(8,128)(2,1)S(1)}, s16[4,408,128]{2,1,0:T(8,128)(2,1)S(1)}, u32[]{:S(2)}, u32[]{:S(2)}) collective-permute-start(s16[4,408,128]{2,1,0:T(8,128)(2,1)S(1)} %get-tuple-element.200), channel_id=1, source_target_pairs={{0,1},{1,0},{2,3},{3,2},{4,5},{5,4},{6,7},{7,6},{8,9},{9,8},{10,11... | collective-permute-start | bytes 1253384 | tf_op jit(solution)/shard_map/ppermute | solution.py:427
  213.0 8.6 %collective-permute-start.23 = (s16[2,408,128]{2,1,0:T(8,128)(2,1)S(1)}, s16[2,408,128]{2,1,0:T(8,128)(2,1)S(1)}, u32[]{:S(2)}, u32[]{:S(2)}) collective-permute-start(s16[2,408,128]{2,1,0:T(8,128)(2,1)S(1)} %get-tuple-element.179), channel_id=1, source_target_pairs={{0,6},{1,7},{2,4},{3,5},{4,2},{5,3},{6,0},{7,1},{8,14},{9,15},{10,... | collective-permute-start | bytes 626696 | tf_op jit(solution)/shard_map/ppermute | solution.py:427
  214.8 12.6 %collective-permute-start.25 = (s16[2,408,128]{2,1,0:T(8,128)(2,1)S(1)}, s16[2,408,128]{2,1,0:T(8,128)(2,1)S(1)}, u32[]{:S(2)}, u32[]{:S(2)}) collective-permute-start(s16[2,408,128]{2,1,0:T(8,128)(2,1)S(1)} %get-tuple-element.189), channel_id=1, source_target_pairs={{0,16},{1,17},{2,18},{3,19},{4,20},{5,21},{6,22},{7,23},{8,24},{9,... | collective-permute-start | bytes 626696 | tf_op jit(solution)/shard_map/ppermute | solution.py:427
  216.1 11.4 %collective-permute-start.26 = (s16[2,408,128]{2,1,0:T(8,128)(2,1)S(1)}, s16[2,408,128]{2,1,0:T(8,128)(2,1)S(1)}, u32[]{:S(2)}, u32[]{:S(2)}) collective-permute-start(s16[2,408,128]{2,1,0:T(8,128)(2,1)S(1)} %get-tuple-element.190), channel_id=1, source_target_pairs={{0,4},{1,5},{2,6},{3,7},{4,0},{5,1},{6,2},{7,3},{8,12},{9,13},{10,... | collective-permute-start | bytes 626696 | tf_op jit(solution)/shard_map/ppermute | solution.py:427
  221.6 5.9 %collective-permute-start.27 = (s16[408,128]{1,0:T(8,128)(2,1)S(1)}, s16[408,128]{1,0:T(8,128)(2,1)S(1)}, u32[]{:S(2)}, u32[]{:S(2)}) collective-permute-start(s16[408,128]{1,0:T(8,128)(2,1)S(1)} %get-tuple-element.191), channel_id=1, source_target_pairs={{0,2},{1,3},{2,0},{3,1},{4,6},{5,7},{6,4},{7,5},{8,10},{9,11},{10,... | collective-permute-start | bytes 313352 | tf_op jit(solution)/shard_map/ppermute | solution.py:427
  228.5 4.8 %collective-permute-start.31 = (s16[4,408,128]{2,1,0:T(8,128)(2,1)S(1)}, s16[4,408,128]{2,1,0:T(8,128)(2,1)S(1)}, u32[]{:S(2)}, u32[]{:S(2)}) collective-permute-start(s16[4,408,128]{2,1,0:T(8,128)(2,1)S(1)} %get-tuple-element.202), channel_id=1, source_target_pairs={{0,1},{1,0},{2,3},{3,2},{4,5},{5,4},{6,7},{7,6},{8,9},{9,8},{10,11... | collective-permute-start | bytes 1253384 | tf_op jit(solution)/shard_map/ppermute | solution.py:427
  228.6 4.7 %collective-permute-start.28 = (s16[408,128]{1,0:T(8,128)(2,1)S(1)}, s16[408,128]{1,0:T(8,128)(2,1)S(1)}, u32[]{:S(2)}, u32[]{:S(2)}) collective-permute-start(s16[408,128]{1,0:T(8,128)(2,1)S(1)} %get-tuple-element.193), channel_id=1, source_target_pairs={{0,3},{1,2},{2,1},{3,0},{4,7},{5,6},{6,5},{7,4},{8,11},{9,10},{10,... | collective-permute-start | bytes 313352 | tf_op jit(solution)/shard_map/ppermute | solution.py:427
  229.8 3.5 %collective-permute-start.29 = (s16[408,128]{1,0:T(8,128)(2,1)S(1)}, s16[408,128]{1,0:T(8,128)(2,1)S(1)}, u32[]{:S(2)}, u32[]{:S(2)}) collective-permute-start(s16[408,128]{1,0:T(8,128)(2,1)S(1)} %get-tuple-element.195), channel_id=1, source_target_pairs={{0,1},{1,0},{2,3},{3,2},{4,5},{5,4},{6,7},{7,6},{8,9},{9,8},{10,11... | collective-permute-start | bytes 313352 | tf_op jit(solution)/shard_map/ppermute | solution.py:427

commit v7 on v5

--- a/solution.py
+++ b/solution.py
@@ -10,7 +10,8 @@
 BLK = 128
 TAIL = 8
 CUTS = (1, 2, 2, 2, 1)
-STEPS = (1, 3, 4)
+STEPS = (3, 6, 8)
+WINDOW = 5
 TILE = 256
 AXES = ("src", "dst")
 F32 = jnp.float32
@@ -26,7 +27,7 @@
 
 
 def cost(flops):
-    return pl.CostEstimate(flops=flops, bytes_accessed=flops // 512, transcendentals=0)
+    return pl.CostEstimate(flops=flops // 64, bytes_accessed=flops // 32768, transcendentals=0)
 
 
 def whole():
@@ -348,7 +349,12 @@
     operator = relations[rel_ids].T
 
     half = devices // 2
-    order = [k for pair in zip(range(devices - 1, half - 1, -1), range(half - 1, -1, -1)) for k in pair]
+    far, near = list(range(devices - 1, half - 1, -1)), list(range(half - 1, -1, -1))
+    lead = devices // 8
+    order = far[:lead]
+    for f, n in zip(far[lead:], near):
+        order += [f, n]
+    order += near[half - lead :]
     partners = lax.axis_index(AXES) ^ jnp.array(order, jnp.int32)
     ids = jnp.arange(devices, dtype=jnp.int32)
     seat = partners[:, None] == ids[None, :]
@@ -385,26 +391,25 @@
     source, target, g_pos = gather_edges(rows, spos, dpos, operator)
     grads_src, grads_dst, part_negs = score(negs, source, target, operator, g_pos)
     own_grad = [part_negs[0]] + [swap(part_negs[shift], shift, "dst") for shift in range(1, peers)]
-    grad = None
-    backs, chunks = [], []
+    grad, chunks, flight, queue = None, [], [], []
     for g, (first, group) in enumerate(zip(firsts, sizes)):
         if g < len(bounds):
             edges_at = (spos, dpos)
-            if g:
-                edges_at, backs[:1] = lax.optimization_barrier((edges_at, backs[:1]))
+            if g > 1:
+                edges_at, flight[-group] = lax.optimization_barrier((edges_at, flight[-group]))
             chunks.append(scatter(*bounds[g], grads_src, grads_dst, *edges_at))
-        packed = list(pack(first, group, rank, alive, chunks, bounds[: len(chunks)], own_grad, npos))
+        packed = pack(first, group, rank, alive, chunks, bounds[: len(chunks)], own_grad, npos)
+        for k, (x, shift) in enumerate(zip(packed, order[first : first + group])):
+            i = first + k
+            if i >= WINDOW:
+                x, flight[i - WINDOW] = lax.optimization_barrier((x, flight[i - WINDOW]))
+            if k == WINDOW and g > 1:
+                x, grad = lax.optimization_barrier((x, grad))
+            flight.append(swap(x, shift, AXES) if shift else x)
         if g:
-            ahead = len(backs) // 2
-            if grad is None:
-                packed, backs[:ahead] = lax.optimization_barrier((packed, backs[:ahead]))
-            else:
-                packed, backs[:ahead], grad = lax.optimization_barrier((packed, backs[:ahead], grad))
-            grad = add(firsts[g - 1], asked, backs, grad, width, rows_dev)
-        backs = [
-            swap(x, shift, AXES) if shift else x
-            for x, shift in zip(packed, order[first : first + group])
-        ]
+            before = firsts[g - 1]
+            grad = add(before, asked, flight[before:first], grad, width, rows_dev)
+    backs = flight[firsts[-1] :]
     new_table, new_state = update(
         firsts[-1], asked, backs, grad, table.T, state.reshape(1, rows_dev)
     )

time: 227 us -> 226 us (level)
  waiting for transfers between devices: 79.8 us -> 70.1 us
  starting transfers between devices: 62.8 us -> 71.7 us
    ppermute x45, waiting for transfers between devices: 28.5 us -> 17.4 us  [swap(): return lax.ppermute(x, axis, [(i, i ^ shift) for i in range(count)])]
    ppermute x45, starting transfers between devices: 52.8 us -> 60.8 us  [swap(): return lax.ppermute(x, axis, [(i, i ^ shift) for i in range(count)])]
    unnamed x17 -> x15, local copies, waits for them, and re-layouts: 8.64 us -> 8.62 us
  transfers between devices with their start and end apart: 47 -> 47, of which waited for: 15 -> 14; matrix products, arithmetic and copies ran while one was open for 13% -> 13% of each run, Pallas kernels for 15% -> 15%
where the time goes in v7:
time: 226 us; the launch traced here: 225 us
  starting transfers between devices  71.7 us (32%)
  waiting for transfers between devices  70.1 us (31%)
  Pallas kernels  48.8 us (22%)
  local copies, waits for them, and re-layouts  29.3 us (13%)
  other arithmetic  3.86 us (2%)
    ppermute x45, starting transfers between devices, swap(): return lax.ppermute(x, axis, [(i, i ^ shift) for i in range(count)])  60.8 us
    all_to_all x1, waiting for transfers between devices, per_device(): lax.all_to_all(outgoing.transpose(0, 2, 1), AXES, split_axis=0, concat_ax...  47.8 us
    ppermute x45, waiting for transfers between devices, swap(): return lax.ppermute(x, axis, [(i, i ^ shift) for i in range(count)])  17.4 us
    gather x2, local copies, waits for them, and re-layouts, per_device(): operator = relations[rel_ids].T  16.7 us
    pallas_call x3, Pallas kernels, scatter(): pl.pallas_call(functools.partial(scatter_kernel, first * BLK), out_shape=...  15.1 us
    pallas_call x5, Pallas kernels, pack(): pl.pallas_call(functools.partial(pack_kernel, first, tuple(bounds), len(g...  9.38 us
    unnamed x15, local copies, waits for them, and re-layouts  8.62 us
    pallas_call x1, Pallas kernels, gather_edges(): pl.pallas_call(edge_kernel, grid=(edges // tile,), out_shape=(jax.ShapeDt...  8.04 us
  transfers between devices with their start and end apart: 47, of which 14 were waited for; matrix products, arithmetic and copies ran while one was open for 13% of the time, Pallas kernels for 15%

profile of v7, /device:TPU:0, one launch (start us, length us, event | category | flops | bytes accessed | tf_op | source)
XLA Modules:
  0.0 225.0 jit_solution(8239954493361873145)
XLA Ops:
  0.6 1.3 copy.29
  2.0 7.3 %all-to-all-start = ((s32[32,1,1]{2,1,0:T(1,128)}), s32[32,1,1]{2,1,0:T(1,128)S(1)}, u32[]{:S(2)}, u32[]{:S(2)}) async-start(s32[32,1,1]{2,1,0:T(1,128)} %copy.29), calls=%async_computation | async-start | bytes 32768 | tf_op jit(solution)/shard_map/all_to_all | solution.py:341
  9.3 2.1 copy_bitcast_fusion
  11.4 4.9 %all-to-all-done = s32[32,1,1]{2,1,0:T(1,128)S(1)} async-done(((s32[32,1,1]{2,1,0:T(1,128)}), s32[32,1,1]{2,1,0:T(1,128)S(1)}, u32[]{:S(2)}, u32[]{:S(2)}) %all-to-all-start) | async-done | bytes 160 | tf_op jit(solution)/shard_map/all_to_all | solution.py:341
  17.0 2.7 %gather_fusion = bf16[32,128,400]{1,2,0:T(8,128)(2,1)} fusion(bf16[16,128,400]{1,2,0:T(8,128)(2,1)S(1)} %copy_bitcast_fusion, s32[1024]{0:T(1024)S(1)} %pad_clamp_fusion), kind=kCustom, calls=%fused_computation | custom fusion | bytes 6553728 | tf_op jit(solution)/shard_map/gather | solution.py:345
  19.7 3.5 %all-to-all-start.1 = ((bf16[32,400,128]{2,1,0:T(8,128)(2,1)}), bf16[32,400,128]{2,1,0:T(8,128)(2,1)}, u32[]{:S(2)}, u32[]{:S(2)}) async-start(bf16[32,400,128]{2,1,0:T(8,128)(2,1)} %bitcast.32), calls=%async_computation.1 | async-start | bytes 6553600 | tf_op jit(solution)/shard_map/all_to_all | solution.py:346
  23.3 8.6 %copy.31 = f32[4096,400]{1,0:T(8,128)} copy(f32[4096,400]{0,1:T(8,128)} %param.11) | data formatting | bytes 13107200 | tf_op args[2]
  31.9 12.9 %gather_fusion.1 = f32[2048,400]{1,0:T(8,128)} fusion(f32[4096,400]{1,0:T(8,128)} %copy.31, s32[2048]{0:T(1024)S(1)} %fusion.3), kind=kCustom, calls=%fused_computation.1 | custom fusion | bytes 6561792 | tf_op jit(solution)/shard_map/gather | solution.py:349
  44.8 3.8 %copy.32 = f32[2048,400]{0,1:T(8,128)S(1)} copy(f32[2048,400]{1,0:T(8,128)} %gather_fusion.1) | data formatting | bytes 6553600 | tf_op jit(solution)/shard_map/gather | solution.py:349
  49.8 47.8 %all-to-all-done.1.fetched = bf16[32,400,128]{2,1,0:T(8,128)(2,1)} async-done(((bf16[32,400,128]{2,1,0:T(8,128)(2,1)}), bf16[32,400,128]{2,1,0:T(8,128)(2,1)}, u32[]{:S(2)}, u32[]{:S(2)}) %all-to-all-start.1) | async-done | bytes 3276832 | tf_op jit(solution)/shard_map/all_to_all | solution.py:346
  97.6 2.6 %gather_negs.1 = (bf16[400,128]{1,0:T(8,128)(2,1)S(1)}, bf16[400,2048]{1,0:T(8,128)(2,1)S(1)}) custom-call(s32[16]{0:T(128)S(1)} %select_reduce_fusion.7.live_ref, bf16[32,400,128]{2,1,0:T(8,128)(2,1)} %all-to-all-done.1.fetched, s32[1,128]{1,0:T(1,128)S(1)} %fusion.11.pos_ref.npos), custom_call_target="tpu_custom_call" | custom-call | tf_op jit(solution)/shard_map/gather_negs/pallas_call | solution.py:84
  100.3 1.3 collective-permute-start.1
  102.1 1.2 collective-permute-start.3
  103.8 2.1 collective-permute-start.5
  106.0 0.9 collective-permute-start.6
  107.0 8.0 %gather_edges.1 = (bf16[400,2048]{1,0:T(8,128)(2,1)S(1)}, bf16[400,2048]{1,0:T(8,128)(2,1)S(1)}, f32[1,2048]{1,0:T(1,128)S(1)}) custom-call(bf16[400,2048]{1,0:T(8,128)(2,1)S(1)} %get-tuple-element.128.rows, s32[1,2048]{1,0:T(1,128)S(1)} %bitcast.23, s32[1,2048]{1,0:T(1,128)S(1)} %bitcast.27, f32[400,2048]{1,0:T(8,128)S(1)} %bitcast.20), custom_call_target="tpu_custom_call" | custom-call | flops 104857600 | bytes 204800 | tf_op jit(solution)/shard_map/gather_edges/pallas_call | solution.py:113
  115.1 6.1 %score.1 = (bf16[2,400,2048]{2,1,0:T(8,128)(2,1)S(1)}, bf16[2,400,2048]{2,1,0:T(8,128)(2,1)S(1)}, bf16[400,128]{1,0:T(8,128)(2,1)S(1)}, bf16[400,128]{1,0:T(8,12...) custom-call(bf16[400,128]{1,0:T(8,128)(2,1)S(1)} %get-tuple-element., ...), custom_call_target="tpu_custom_call" | custom-call | flops 78643200 | bytes 153600 | tf_op jit(solution)/shard_map/score/pallas_call | solution.py:160
  121.1 1.4 collective-permute-start.7
  123.0 0.9 collective-permute-start.9
  124.5 1.5 collective-permute-start.11
  126.8 1.4 collective-permute-done.8.refs_4_.refs_5_.refs_3_
  128.3 5.7 %scatter.3.refs_0_ = f32[400,768]{1,0:T(8,128)S(1)} custom-call(bf16[2,400,2048]{2,1,0:T(8,128)(2,1)S(1)} %get-tuple-element.135.gs_ref, bf16[2,400,2048]{2,1,0:T(8,128)(2,1)S(1)} %get-tuple-element.136.gd_ref, s32[1,2048]{1,0:T(1,128)S(1)} %bitcast.24, s32[1,2048]{1,0:T(1,128)S(1)} %bitcast.28), custom_call_target="tpu_custom_call" | custom-call | flops 39321600 | bytes 76800 | tf_op jit(solution)/shard_map/scatter/pallas_call | solution.py:197
  134.1 1.7 collective-permute-done.11.refs_7_.refs_8_.refs_6_
  135.8 1.8 pack.9
  137.6 2.0 collective-permute-start.26
  139.6 2.4 %collective-permute-start.15 = (s16[408,128]{1,0:T(8,128)(2,1)S(1)}, s16[408,128]{1,0:T(8,128)(2,1)S(1)}, u32[]{:S(2)}, u32[]{:S(2)}) collective-permute-start(s16[408,128]{1,0:T(8,128)(2,1)S(1)} %get-tuple-element.155), channel_id=1, source_target_pairs={{0,28},{1,29},{2,30},{3,31},{4,24},{5,25},{6,26},{7,27},{8,20},{9,... | collective-permute-start | bytes 313352 | tf_op jit(solution)/shard_map/ppermute | solution.py:386
  142.0 2.1 collective-permute-start.31
  144.1 3.0 %collective-permute-start.33 = (s16[408,128]{1,0:T(8,128)(2,1)S(1)}, s16[408,128]{1,0:T(8,128)(2,1)S(1)}, u32[]{:S(2)}, u32[]{:S(2)}) collective-permute-start(s16[408,128]{1,0:T(8,128)(2,1)S(1)} %get-tuple-element.191), channel_id=1, source_target_pairs={{0,29},{1,28},{2,31},{3,30},{4,25},{5,24},{6,27},{7,26},{8,21},{9,... | collective-permute-start | bytes 313352 | tf_op jit(solution)/shard_map/ppermute | solution.py:386
  147.2 5.7 %scatter.4.refs_1_ = f32[400,768]{1,0:T(8,128)S(1)} custom-call(bf16[2,400,2048]{2,1,0:T(8,128)(2,1)S(1)} %get-tuple-element.135.gs_ref, bf16[2,400,2048]{2,1,0:T(8,128)(2,1)S(1)} %get-tuple-element.136.gd_ref, s32[1,2048]{1,0:T(1,128)S(1)} %bitcast.25, s32[1,2048]{1,0:T(1,128)S(1)} %bitcast.29), custom_call_target="tpu_custom_call" | custom-call | flops 39321600 | bytes 76800 | tf_op jit(solution)/shard_map/scatter/pallas_call | solution.py:197
  152.8 1.8 pack.5
  154.7 2.6 %collective-permute-start.14 = (s16[408,128]{1,0:T(8,128)(2,1)S(1)}, s16[408,128]{1,0:T(8,128)(2,1)S(1)}, u32[]{:S(2)}, u32[]{:S(2)}) collective-permute-start(s16[408,128]{1,0:T(8,128)(2,1)S(1)} %get-tuple-element.146), channel_id=1, source_target_pairs={{0,27},{1,26},{2,25},{3,24},{4,31},{5,30},{6,29},{7,28},{8,19},{9,... | collective-permute-start | bytes 313352 | tf_op jit(solution)/shard_map/ppermute | solution.py:386
  157.7 2.6 %collective-permute-start.32 = (s16[408,128]{1,0:T(8,128)(2,1)S(1)}, s16[408,128]{1,0:T(8,128)(2,1)S(1)}, u32[]{:S(2)}, u32[]{:S(2)}) collective-permute-start(s16[408,128]{1,0:T(8,128)(2,1)S(1)} %get-tuple-element.187), channel_id=1, source_target_pairs={{0,26},{1,27},{2,24},{3,25},{4,30},{5,31},{6,28},{7,29},{8,18},{9,... | collective-permute-start | bytes 313352 | tf_op jit(solution)/shard_map/ppermute | solution.py:386
  160.3 2.8 %collective-permute-start.34 = (s16[408,128]{1,0:T(8,128)(2,1)S(1)}, s16[408,128]{1,0:T(8,128)(2,1)S(1)}, u32[]{:S(2)}, u32[]{:S(2)}) collective-permute-start(s16[408,128]{1,0:T(8,128)(2,1)S(1)} %get-tuple-element.192), channel_id=1, source_target_pairs={{0,14},{1,15},{2,12},{3,13},{4,10},{5,11},{6,8},{7,9},{8,6},{9,7},... | collective-permute-start | bytes 313352 | tf_op jit(solution)/shard_map/ppermute | solution.py:386
  163.1 1.0 collective-permute-start.21
  164.1 1.4 collective-permute-done.27.refs_1_
  165.5 2.0 collective-permute-start.28
  167.5 3.8 %scatter.5.refs_2_ = f32[400,512]{1,0:T(8,128)S(1)} custom-call(bf16[2,400,2048]{2,1,0:T(8,128)(2,1)S(1)} %get-tuple-element.135.gs_ref, bf16[2,400,2048]{2,1,0:T(8,128)(2,1)S(1)} %get-tuple-element.136.gd_ref, s32[1,2048]{1,0:T(1,128)S(1)} %bitcast.26, s32[1,2048]{1,0:T(1,128)S(1)} %bitcast.30), custom_call_target="tpu_custom_call" | custom-call | flops 26214400 | bytes 51200 | tf_op jit(solution)/shard_map/scatter/pallas_call | solution.py:197
  171.3 1.9 pack.8
  173.3 6.2 %collective-permute-start.35 = (s16[408,128]{1,0:T(8,128)(2,1)S(1)}, s16[408,128]{1,0:T(8,128)(2,1)S(1)}, u32[]{:S(2)}, u32[]{:S(2)}) collective-permute-start(s16[408,128]{1,0:T(8,128)(2,1)S(1)} %get-tuple-element.198), channel_id=1, source_target_pairs={{0,12},{1,13},{2,14},{3,15},{4,8},{5,9},{6,10},{7,11},{8,4},{9,5},... | collective-permute-start | bytes 313352 | tf_op jit(solution)/shard_map/ppermute | solution.py:386
  179.5 1.5 collective-permute-start.22
  181.0 3.0 %collective-permute-start.29 = (s16[408,128]{1,0:T(8,128)(2,1)S(1)}, s16[408,128]{1,0:T(8,128)(2,1)S(1)}, u32[]{:S(2)}, u32[]{:S(2)}) collective-permute-start(s16[408,128]{1,0:T(8,128)(2,1)S(1)} %get-tuple-element.179), channel_id=1, source_target_pairs={{0,10},{1,11},{2,8},{3,9},{4,14},{5,15},{6,12},{7,13},{8,2},{9,3},... | collective-permute-start | bytes 313352 | tf_op jit(solution)/shard_map/ppermute | solution.py:386
  184.0 1.0 add.91.refs_8_
  185.0 2.2 pack.7
  187.3 3.4 %collective-permute-start.39 = (s16[408,128]{1,0:T(8,128)(2,1)S(1)}, s16[408,128]{1,0:T(8,128)(2,1)S(1)}, u32[]{:S(2)}, u32[]{:S(2)}) collective-permute-start(s16[408,128]{1,0:T(8,128)(2,1)S(1)} %get-tuple-element.213), channel_id=1, source_target_pairs={{0,21},{1,20},{2,23},{3,22},{4,17},{5,16},{6,19},{7,18},{8,29},{9,... | collective-permute-start | bytes 313352 | tf_op jit(solution)/shard_map/ppermute | solution.py:386
  190.8 1.0 collective-permute-start.42
  191.7 1.1 collective-permute-start.23
  192.8 1.0 collective-permute-start.30
  193.9 1.0 add.92.refs_8_
  194.9 4.5 %collective-permute-done.18.refs_6_ = s16[408,128]{1,0:T(8,128)(2,1)S(1)} collective-permute-done((s16[408,128]{1,0:T(8,128)(2,1)S(1)}, s16[408,128]{1,0:T(8,128)(2,1)S(1)}, u32[]{:S(2)}, u32[]{:S(2)}) %collective-permute-start.18) | collective-permute-done | bytes 104480 | tf_op jit(solution)/shard_map/ppermute | solution.py:386
  199.4 1.1 collective-permute-done.39.refs_4_
  200.5 1.2 collective-permute-start.40
  201.6 3.0 %collective-permute-done.23.refs_7_ = s16[408,128]{1,0:T(8,128)(2,1)S(1)} collective-permute-done((s16[408,128]{1,0:T(8,128)(2,1)S(1)}, s16[408,128]{1,0:T(8,128)(2,1)S(1)}, u32[]{:S(2)}, u32[]{:S(2)}) %collective-permute-start.23) | collective-permute-done | bytes 104480 | tf_op jit(solution)/shard_map/ppermute | solution.py:386
  204.6 1.3 collective-permute-start.24
  205.9 1.0 collective-permute-start.37
  206.9 1.7 pack.6
  208.7 2.8 %collective-permute-start.41 = (s16[408,128]{1,0:T(8,128)(2,1)S(1)}, s16[408,128]{1,0:T(8,128)(2,1)S(1)}, u32[]{:S(2)}, u32[]{:S(2)}) collective-permute-start(s16[408,128]{1,0:T(8,128)(2,1)S(1)} %get-tuple-element.215), channel_id=1, source_target_pairs={{0,16},{1,17},{2,18},{3,19},{4,20},{5,21},{6,22},{7,23},{8,24},{9,... | collective-permute-start | bytes 313352 | tf_op jit(solution)/shard_map/ppermute | solution.py:386
  211.5 0.9 collective-permute-done.43.refs_2_
  212.4 2.5 %collective-permute-start.44 = (s16[408,128]{1,0:T(8,128)(2,1)S(1)}, s16[408,128]{1,0:T(8,128)(2,1)S(1)}, u32[]{:S(2)}, u32[]{:S(2)}) collective-permute-start(s16[408,128]{1,0:T(8,128)(2,1)S(1)} %get-tuple-element.228), channel_id=1, source_target_pairs={{0,4},{1,5},{2,6},{3,7},{4,0},{5,1},{6,2},{7,3},{8,12},{9,13},{10,... | collective-permute-start | bytes 313352 | tf_op jit(solution)/shard_map/ppermute | solution.py:386
  215.0 1.4 collective-permute-done.24.refs_4_
  216.4 1.0 collective-permute-start.25
  217.4 1.0 add.93.refs_8_
  218.6 1.0 add.94.refs_4_
  219.7 1.6 collective-permute-done.25.refs_1_
  221.4 3.5 %update.1 = (f32[400,2048]{1,0:T(8,128)}, f32[1,2048]{1,0:T(1,128)}) custom-call(s32[32]{0:T(128)S(1)} %get-tuple-element.121.asked_ref, s16[408,128]{1,0:T(8,128)(2,1)S(1)} %collective-permute-done.20.refs_0_, s16[408,128]{1,0:T(8,128)(2,1)S(1)} %collective-permute-done.25.refs_1_, s16[408,128]{1,0:T(8,128)(2,1)S(1)} %collective-permute-done.38.refs_2_, ...), custom_call_target="tpu_custom_call" | custom-call | flops 819200 | bytes 1600 | tf_op jit(solution)/shard_map/update/pallas_call | solution.py:321
  (85 shorter events, 6.0 us)
Async XLA Ops:
  2.0 14.4 %all-to-all-start = ((s32[32,1,1]{2,1,0:T(1,128)}), s32[32,1,1]{2,1,0:T(1,128)S(1)}, u32[]{:S(2)}, u32[]{:S(2)}) async-start(s32[32,1,1]{2,1,0:T(1,128)} %copy.29), calls=%async_computation | async-start | bytes 32768 | tf_op jit(solution)/shard_map/all_to_all | solution.py:341
  19.7 77.8 %all-to-all-start.1 = ((bf16[32,400,128]{2,1,0:T(8,128)(2,1)}), bf16[32,400,128]{2,1,0:T(8,128)(2,1)}, u32[]{:S(2)}, u32[]{:S(2)}) async-start(bf16[32,400,128]{2,1,0:T(8,128)(2,1)} %bitcast.32), calls=%async_computation.1 | async-start | bytes 6553600 | tf_op jit(solution)/shard_map/all_to_all | solution.py:346
  23.3 8.6 %copy-start.4 = (s32[2048]{0:T(1024)S(1)}, s32[2048]{0:T(1024)}, u32[]{:S(2)}) copy-start(s32[2048]{0:T(1024)} %param.12) | copy-start | bytes 24580
  44.8 3.8 %copy-start.2 = (s32[2048]{0:T(1024)S(1)}, s32[2048]{0:T(1024)}, u32[]{:S(2)}) copy-start(s32[2048]{0:T(1024)} %param.14) | copy-start | bytes 24580
  44.8 4.0 %copy-start.6 = (s32[32]{0:T(128)S(1)}, s32[32]{0:T(128)}, u32[]{:S(2)}) copy-start(s32[32]{0:T(128)} %constant.83.clone) | copy-start | bytes 388
  44.8 4.4 %copy-start.5 = (s32[128]{0:T(128)S(1)}, s32[128]{0:T(128)}, u32[]{:S(2)}) copy-start(s32[128]{0:T(128)} %param.16) | copy-start | bytes 1540
  44.8 4.4 %copy-start.3 = (s32[2048]{0:T(1024)S(1)}, s32[2048]{0:T(1024)}, u32[]{:S(2)}) copy-start(s32[2048]{0:T(1024)} %param.15) | copy-start | bytes 24580
  100.2 3.6 %collective-permute-start = (bf16[400,128]{1,0:T(8,128)(2,1)S(1)}, bf16[400,128]{1,0:T(8,128)(2,1)S(1)}, u32[]{:S(2)}, u32[]{:S(2)}) collective-permute-start(bf16[400,128]{1,0:T(8,128)(2,1)S(1)} %get-tuple-element.127.refs_0_), channel_id=1, source_target_pairs={{0,1},{1,0},{2,3},{3,2},{4,5},{5,4},{6,7},{7,6},{8,9},{9,8},{10,11... | collective-permute-start | bytes 307208 | tf_op jit(solution)/shard_map/ppermute | solution.py:386
  100.3 5.7 %collective-permute-start.1 = (bf16[400,128]{1,0:T(8,128)(2,1)S(1)}, bf16[400,128]{1,0:T(8,128)(2,1)S(1)}, u32[]{:S(2)}, u32[]{:S(2)}) collective-permute-start(bf16[400,128]{1,0:T(8,128)(2,1)S(1)} %get-tuple-element.127.refs_0_), channel_id=1, source_target_pairs={{0,2},{1,3},{2,0},{3,1},{4,6},{5,7},{6,4},{7,5},{8,10},{9,11},{10,... | collective-permute-start | bytes 307208 | tf_op jit(solution)/shard_map/ppermute | solution.py:386
  101.5 13.5 %collective-permute-start.2 = (bf16[400,128]{1,0:T(8,128)(2,1)S(1)}, bf16[400,128]{1,0:T(8,128)(2,1)S(1)}, u32[]{:S(2)}, u32[]{:S(2)}) collective-permute-start(bf16[400,128]{1,0:T(8,128)(2,1)S(1)} %get-tuple-element.127.refs_0_), channel_id=1, source_target_pairs={{0,3},{1,2},{2,1},{3,0},{4,7},{5,6},{6,5},{7,4},{8,11},{9,10},{10,... | collective-permute-start | bytes 307208 | tf_op jit(solution)/shard_map/ppermute | solution.py:386
  102.1 12.9 %collective-permute-start.3 = (bf16[400,128]{1,0:T(8,128)(2,1)S(1)}, bf16[400,128]{1,0:T(8,128)(2,1)S(1)}, u32[]{:S(2)}, u32[]{:S(2)}) collective-permute-start(bf16[400,128]{1,0:T(8,128)(2,1)S(1)} %get-tuple-element.127.refs_0_), channel_id=1, source_target_pairs={{0,4},{1,5},{2,6},{3,7},{4,0},{5,1},{6,2},{7,3},{8,12},{9,13},{10,... | collective-permute-start | bytes 307208 | tf_op jit(solution)/shard_map/ppermute | solution.py:386
  103.3 11.7 %collective-permute-start.4 = (bf16[400,128]{1,0:T(8,128)(2,1)S(1)}, bf16[400,128]{1,0:T(8,128)(2,1)S(1)}, u32[]{:S(2)}, u32[]{:S(2)}) collective-permute-start(bf16[400,128]{1,0:T(8,128)(2,1)S(1)} %get-tuple-element.127.refs_0_), channel_id=1, source_target_pairs={{0,5},{1,4},{2,7},{3,6},{4,1},{5,0},{6,3},{7,2},{8,13},{9,12},{10,... | collective-permute-start | bytes 307208 | tf_op jit(solution)/shard_map/ppermute | solution.py:386
  103.8 11.2 %collective-permute-start.5 = (bf16[400,128]{1,0:T(8,128)(2,1)S(1)}, bf16[400,128]{1,0:T(8,128)(2,1)S(1)}, u32[]{:S(2)}, u32[]{:S(2)}) collective-permute-start(bf16[400,128]{1,0:T(8,128)(2,1)S(1)} %get-tuple-element.127.refs_0_), channel_id=1, source_target_pairs={{0,6},{1,7},{2,4},{3,5},{4,2},{5,3},{6,0},{7,1},{8,14},{9,15},{10,... | collective-permute-start | bytes 307208 | tf_op jit(solution)/shard_map/ppermute | solution.py:386
  106.0 9.0 %collective-permute-start.6 = (bf16[400,128]{1,0:T(8,128)(2,1)S(1)}, bf16[400,128]{1,0:T(8,128)(2,1)S(1)}, u32[]{:S(2)}, u32[]{:S(2)}) collective-permute-start(bf16[400,128]{1,0:T(8,128)(2,1)S(1)} %get-tuple-element.127.refs_0_), channel_id=1, source_target_pairs={{0,7},{1,6},{2,5},{3,4},{4,3},{5,2},{6,1},{7,0},{8,15},{9,14},{10,... | collective-permute-start | bytes 307208 | tf_op jit(solution)/shard_map/ppermute | solution.py:386
  121.1 4.9 %collective-permute-start.7 = (bf16[400,128]{1,0:T(8,128)(2,1)S(1)}, bf16[400,128]{1,0:T(8,128)(2,1)S(1)}, u32[]{:S(2)}, u32[]{:S(2)}) collective-permute-start(bf16[400,128]{1,0:T(8,128)(2,1)S(1)} %get-tuple-element.138), channel_id=1, source_target_pairs={{0,1},{1,0},{2,3},{3,2},{4,5},{5,4},{6,7},{7,6},{8,9},{9,8},{10,11... | collective-permute-start | bytes 307208 | tf_op jit(solution)/shard_map/ppermute | solution.py:386
  122.5 5.7 %collective-permute-start.8 = (bf16[400,128]{1,0:T(8,128)(2,1)S(1)}, bf16[400,128]{1,0:T(8,128)(2,1)S(1)}, u32[]{:S(2)}, u32[]{:S(2)}) collective-permute-start(bf16[400,128]{1,0:T(8,128)(2,1)S(1)} %get-tuple-element.139), channel_id=1, source_target_pairs={{0,2},{1,3},{2,0},{3,1},{4,6},{5,7},{6,4},{7,5},{8,10},{9,11},{10,... | collective-permute-start | bytes 307208 | tf_op jit(solution)/shard_map/ppermute | solution.py:386
  123.0 11.0 %collective-permute-start.9 = (bf16[400,128]{1,0:T(8,128)(2,1)S(1)}, bf16[400,128]{1,0:T(8,128)(2,1)S(1)}, u32[]{:S(2)}, u32[]{:S(2)}) collective-permute-start(bf16[400,128]{1,0:T(8,128)(2,1)S(1)} %get-tuple-element.140), channel_id=1, source_target_pairs={{0,3},{1,2},{2,1},{3,0},{4,7},{5,6},{6,5},{7,4},{8,11},{9,10},{10,... | collective-permute-start | bytes 307208 | tf_op jit(solution)/shard_map/ppermute | solution.py:386
  123.9 10.1 %collective-permute-start.10 = (bf16[400,128]{1,0:T(8,128)(2,1)S(1)}, bf16[400,128]{1,0:T(8,128)(2,1)S(1)}, u32[]{:S(2)}, u32[]{:S(2)}) collective-permute-start(bf16[400,128]{1,0:T(8,128)(2,1)S(1)} %get-tuple-element.141), channel_id=1, source_target_pairs={{0,4},{1,5},{2,6},{3,7},{4,0},{5,1},{6,2},{7,3},{8,12},{9,13},{10,... | collective-permute-start | bytes 307208 | tf_op jit(solution)/shard_map/ppermute | solution.py:386
  124.5 11.3 %collective-permute-start.11 = (bf16[400,128]{1,0:T(8,128)(2,1)S(1)}, bf16[400,128]{1,0:T(8,128)(2,1)S(1)}, u32[]{:S(2)}, u32[]{:S(2)}) collective-permute-start(bf16[400,128]{1,0:T(8,128)(2,1)S(1)} %get-tuple-element.142), channel_id=1, source_target_pairs={{0,5},{1,4},{2,7},{3,6},{4,1},{5,0},{6,3},{7,2},{8,13},{9,12},{10,... | collective-permute-start | bytes 307208 | tf_op jit(solution)/shard_map/ppermute | solution.py:386
  126.0 9.7 %collective-permute-start.12 = (bf16[400,128]{1,0:T(8,128)(2,1)S(1)}, bf16[400,128]{1,0:T(8,128)(2,1)S(1)}, u32[]{:S(2)}, u32[]{:S(2)}) collective-permute-start(bf16[400,128]{1,0:T(8,128)(2,1)S(1)} %get-tuple-element.143), channel_id=1, source_target_pairs={{0,6},{1,7},{2,4},{3,5},{4,2},{5,3},{6,0},{7,1},{8,14},{9,15},{10,... | collective-permute-start | bytes 307208 | tf_op jit(solution)/shard_map/ppermute | solution.py:386
  128.2 7.5 %collective-permute-start.13 = (bf16[400,128]{1,0:T(8,128)(2,1)S(1)}, bf16[400,128]{1,0:T(8,128)(2,1)S(1)}, u32[]{:S(2)}, u32[]{:S(2)}) collective-permute-start(bf16[400,128]{1,0:T(8,128)(2,1)S(1)} %get-tuple-element.144), channel_id=1, source_target_pairs={{0,7},{1,6},{2,5},{3,4},{4,3},{5,2},{6,1},{7,0},{8,15},{9,14},{10,... | collective-permute-start | bytes 307208 | tf_op jit(solution)/shard_map/ppermute | solution.py:386
  137.6 19.7 %collective-permute-start.26 = (s16[408,128]{1,0:T(8,128)(2,1)S(1)}, s16[408,128]{1,0:T(8,128)(2,1)S(1)}, u32[]{:S(2)}, u32[]{:S(2)}) collective-permute-start(s16[408,128]{1,0:T(8,128)(2,1)S(1)} %get-tuple-element.176), channel_id=1, source_target_pairs={{0,31},{1,30},{2,29},{3,28},{4,27},{5,26},{6,25},{7,24},{8,23},{9,... | collective-permute-start | bytes 313352 | tf_op jit(solution)/shard_map/ppermute | solution.py:386
  139.6 17.7 %collective-permute-start.15 = (s16[408,128]{1,0:T(8,128)(2,1)S(1)}, s16[408,128]{1,0:T(8,128)(2,1)S(1)}, u32[]{:S(2)}, u32[]{:S(2)}) collective-permute-start(s16[408,128]{1,0:T(8,128)(2,1)S(1)} %get-tuple-element.155), channel_id=1, source_target_pairs={{0,28},{1,29},{2,30},{3,31},{4,24},{5,25},{6,26},{7,27},{8,20},{9,... | collective-permute-start | bytes 313352 | tf_op jit(solution)/shard_map/ppermute | solution.py:386
  142.0 15.7 %collective-permute-start.31 = (s16[408,128]{1,0:T(8,128)(2,1)S(1)}, s16[408,128]{1,0:T(8,128)(2,1)S(1)}, u32[]{:S(2)}, u32[]{:S(2)}) collective-permute-start(s16[408,128]{1,0:T(8,128)(2,1)S(1)} %get-tuple-element.186), channel_id=1, source_target_pairs={{0,30},{1,31},{2,28},{3,29},{4,26},{5,27},{6,24},{7,25},{8,22},{9,... | collective-permute-start | bytes 313352 | tf_op jit(solution)/shard_map/ppermute | solution.py:386
  144.1 16.2 %collective-permute-start.33 = (s16[408,128]{1,0:T(8,128)(2,1)S(1)}, s16[408,128]{1,0:T(8,128)(2,1)S(1)}, u32[]{:S(2)}, u32[]{:S(2)}) collective-permute-start(s16[408,128]{1,0:T(8,128)(2,1)S(1)} %get-tuple-element.191), channel_id=1, source_target_pairs={{0,29},{1,28},{2,31},{3,30},{4,25},{5,24},{6,27},{7,26},{8,21},{9,... | collective-permute-start | bytes 313352 | tf_op jit(solution)/shard_map/ppermute | solution.py:386
  154.7 8.5 %collective-permute-start.14 = (s16[408,128]{1,0:T(8,128)(2,1)S(1)}, s16[408,128]{1,0:T(8,128)(2,1)S(1)}, u32[]{:S(2)}, u32[]{:S(2)}) collective-permute-start(s16[408,128]{1,0:T(8,128)(2,1)S(1)} %get-tuple-element.146), channel_id=1, source_target_pairs={{0,27},{1,26},{2,25},{3,24},{4,31},{5,30},{6,29},{7,28},{8,19},{9,... | collective-permute-start | bytes 313352 | tf_op jit(solution)/shard_map/ppermute | solution.py:386
  157.2 8.3 %collective-permute-start.27 = (s16[408,128]{1,0:T(8,128)(2,1)S(1)}, s16[408,128]{1,0:T(8,128)(2,1)S(1)}, u32[]{:S(2)}, u32[]{:S(2)}) collective-permute-start(s16[408,128]{1,0:T(8,128)(2,1)S(1)} %get-tuple-element.177), channel_id=1, source_target_pairs={{0,15},{1,14},{2,13},{3,12},{4,11},{5,10},{6,9},{7,8},{8,7},{9,6},... | collective-permute-start | bytes 313352 | tf_op jit(solution)/shard_map/ppermute | solution.py:386
  157.3 15.9 %collective-permute-start.16 = (s16[408,128]{1,0:T(8,128)(2,1)S(1)}, s16[408,128]{1,0:T(8,128)(2,1)S(1)}, u32[]{:S(2)}, u32[]{:S(2)}) collective-permute-start(s16[408,128]{1,0:T(8,128)(2,1)S(1)} %get-tuple-element.156), channel_id=1, source_target_pairs={{0,25},{1,24},{2,27},{3,26},{4,29},{5,28},{6,31},{7,30},{8,17},{9,... | collective-permute-start | bytes 313352 | tf_op jit(solution)/shard_map/ppermute | solution.py:386
  157.7 15.6 %collective-permute-start.32 = (s16[408,128]{1,0:T(8,128)(2,1)S(1)}, s16[408,128]{1,0:T(8,128)(2,1)S(1)}, u32[]{:S(2)}, u32[]{:S(2)}) collective-permute-start(s16[408,128]{1,0:T(8,128)(2,1)S(1)} %get-tuple-element.187), channel_id=1, source_target_pairs={{0,26},{1,27},{2,24},{3,25},{4,30},{5,31},{6,28},{7,29},{8,18},{9,... | collective-permute-start | bytes 313352 | tf_op jit(solution)/shard_map/ppermute | solution.py:386
  160.3 19.2 %collective-permute-start.34 = (s16[408,128]{1,0:T(8,128)(2,1)S(1)}, s16[408,128]{1,0:T(8,128)(2,1)S(1)}, u32[]{:S(2)}, u32[]{:S(2)}) collective-permute-start(s16[408,128]{1,0:T(8,128)(2,1)S(1)} %get-tuple-element.192), channel_id=1, source_target_pairs={{0,14},{1,15},{2,12},{3,13},{4,10},{5,11},{6,8},{7,9},{8,6},{9,7},... | collective-permute-start | bytes 313352 | tf_op jit(solution)/shard_map/ppermute | solution.py:386
  163.1 16.3 %collective-permute-start.21 = (s16[408,128]{1,0:T(8,128)(2,1)S(1)}, s16[408,128]{1,0:T(8,128)(2,1)S(1)}, u32[]{:S(2)}, u32[]{:S(2)}) collective-permute-start(s16[408,128]{1,0:T(8,128)(2,1)S(1)} %get-tuple-element.165), channel_id=1, source_target_pairs={{0,13},{1,12},{2,15},{3,14},{4,9},{5,8},{6,11},{7,10},{8,5},{9,4},... | collective-permute-start | bytes 313352 | tf_op jit(solution)/shard_map/ppermute | solution.py:386
  165.5 15.5 %collective-permute-start.28 = (s16[408,128]{1,0:T(8,128)(2,1)S(1)}, s16[408,128]{1,0:T(8,128)(2,1)S(1)}, u32[]{:S(2)}, u32[]{:S(2)}) collective-permute-start(s16[408,128]{1,0:T(8,128)(2,1)S(1)} %get-tuple-element.178), channel_id=1, source_target_pairs={{0,24},{1,25},{2,26},{3,27},{4,28},{5,29},{6,30},{7,31},{8,16},{9,... | collective-permute-start | bytes 313352 | tf_op jit(solution)/shard_map/ppermute | solution.py:386
  173.2 14.0 %collective-permute-start.17 = (s16[408,128]{1,0:T(8,128)(2,1)S(1)}, s16[408,128]{1,0:T(8,128)(2,1)S(1)}, u32[]{:S(2)}, u32[]{:S(2)}) collective-permute-start(s16[408,128]{1,0:T(8,128)(2,1)S(1)} %get-tuple-element.157), channel_id=1, source_target_pairs={{0,11},{1,10},{2,9},{3,8},{4,15},{5,14},{6,13},{7,12},{8,3},{9,2},... | collective-permute-start | bytes 313352 | tf_op jit(solution)/shard_map/ppermute | solution.py:386
  173.3 14.0 %collective-permute-start.35 = (s16[408,128]{1,0:T(8,128)(2,1)S(1)}, s16[408,128]{1,0:T(8,128)(2,1)S(1)}, u32[]{:S(2)}, u32[]{:S(2)}) collective-permute-start(s16[408,128]{1,0:T(8,128)(2,1)S(1)} %get-tuple-element.198), channel_id=1, source_target_pairs={{0,12},{1,13},{2,14},{3,15},{4,8},{5,9},{6,10},{7,11},{8,4},{9,5},... | collective-permute-start | bytes 313352 | tf_op jit(solution)/shard_map/ppermute | solution.py:386
  179.5 11.3 %collective-permute-start.36 = (s16[408,128]{1,0:T(8,128)(2,1)S(1)}, s16[408,128]{1,0:T(8,128)(2,1)S(1)}, u32[]{:S(2)}, u32[]{:S(2)}) collective-permute-start(s16[408,128]{1,0:T(8,128)(2,1)S(1)} %get-tuple-element.201), channel_id=1, source_target_pairs={{0,23},{1,22},{2,21},{3,20},{4,19},{5,18},{6,17},{7,16},{8,31},{9,... | collective-permute-start | bytes 313352 | tf_op jit(solution)/shard_map/ppermute | solution.py:386
  179.5 12.2 %collective-permute-start.22 = (s16[408,128]{1,0:T(8,128)(2,1)S(1)}, s16[408,128]{1,0:T(8,128)(2,1)S(1)}, u32[]{:S(2)}, u32[]{:S(2)}) collective-permute-start(s16[408,128]{1,0:T(8,128)(2,1)S(1)} %get-tuple-element.166), channel_id=1, source_target_pairs={{0,22},{1,23},{2,20},{3,21},{4,18},{5,19},{6,16},{7,17},{8,30},{9,... | collective-permute-start | bytes 313352 | tf_op jit(solution)/shard_map/ppermute | solution.py:386
  181.0 11.9 %collective-permute-start.29 = (s16[408,128]{1,0:T(8,128)(2,1)S(1)}, s16[408,128]{1,0:T(8,128)(2,1)S(1)}, u32[]{:S(2)}, u32[]{:S(2)}) collective-permute-start(s16[408,128]{1,0:T(8,128)(2,1)S(1)} %get-tuple-element.179), channel_id=1, source_target_pairs={{0,10},{1,11},{2,8},{3,9},{4,14},{5,15},{6,12},{7,13},{8,2},{9,3},... | collective-permute-start | bytes 313352 | tf_op jit(solution)/shard_map/ppermute | solution.py:386
  187.2 12.2 %collective-permute-start.18 = (s16[408,128]{1,0:T(8,128)(2,1)S(1)}, s16[408,128]{1,0:T(8,128)(2,1)S(1)}, u32[]{:S(2)}, u32[]{:S(2)}) collective-permute-start(s16[408,128]{1,0:T(8,128)(2,1)S(1)} %get-tuple-element.158), channel_id=1, source_target_pairs={{0,20},{1,21},{2,22},{3,23},{4,16},{5,17},{6,18},{7,19},{8,28},{9,... | collective-permute-start | bytes 313352 | tf_op jit(solution)/shard_map/ppermute | solution.py:386
  187.3 13.1 %collective-permute-start.39 = (s16[408,128]{1,0:T(8,128)(2,1)S(1)}, s16[408,128]{1,0:T(8,128)(2,1)S(1)}, u32[]{:S(2)}, u32[]{:S(2)}) collective-permute-start(s16[408,128]{1,0:T(8,128)(2,1)S(1)} %get-tuple-element.213), channel_id=1, source_target_pairs={{0,21},{1,20},{2,23},{3,22},{4,17},{5,16},{6,19},{7,18},{8,29},{9,... | collective-permute-start | bytes 313352 | tf_op jit(solution)/shard_map/ppermute | solution.py:386
  190.8 10.9 %collective-permute-start.42 = (s16[408,128]{1,0:T(8,128)(2,1)S(1)}, s16[408,128]{1,0:T(8,128)(2,1)S(1)}, u32[]{:S(2)}, u32[]{:S(2)}) collective-permute-start(s16[408,128]{1,0:T(8,128)(2,1)S(1)} %get-tuple-element.221), channel_id=1, source_target_pairs={{0,9},{1,8},{2,11},{3,10},{4,13},{5,12},{6,15},{7,14},{8,1},{9,0},... | collective-permute-start | bytes 313352 | tf_op jit(solution)/shard_map/ppermute | solution.py:386
  191.7 12.9 %collective-permute-start.23 = (s16[408,128]{1,0:T(8,128)(2,1)S(1)}, s16[408,128]{1,0:T(8,128)(2,1)S(1)}, u32[]{:S(2)}, u32[]{:S(2)}) collective-permute-start(s16[408,128]{1,0:T(8,128)(2,1)S(1)} %get-tuple-element.167), channel_id=1, source_target_pairs={{0,8},{1,9},{2,10},{3,11},{4,12},{5,13},{6,14},{7,15},{8,0},{9,1},... | collective-permute-start | bytes 313352 | tf_op jit(solution)/shard_map/ppermute | solution.py:386
  192.8 13.0 %collective-permute-start.30 = (s16[408,128]{1,0:T(8,128)(2,1)S(1)}, s16[408,128]{1,0:T(8,128)(2,1)S(1)}, u32[]{:S(2)}, u32[]{:S(2)}) collective-permute-start(s16[408,128]{1,0:T(8,128)(2,1)S(1)} %get-tuple-element.180), channel_id=1, source_target_pairs={{0,19},{1,18},{2,17},{3,16},{4,23},{5,22},{6,21},{7,20},{8,27},{9,... | collective-permute-start | bytes 313352 | tf_op jit(solution)/shard_map/ppermute | solution.py:386
  199.4 9.2 %collective-permute-start.19 = (s16[408,128]{1,0:T(8,128)(2,1)S(1)}, s16[408,128]{1,0:T(8,128)(2,1)S(1)}, u32[]{:S(2)}, u32[]{:S(2)}) collective-permute-start(s16[408,128]{1,0:T(8,128)(2,1)S(1)} %get-tuple-element.159), channel_id=1, source_target_pairs={{0,6},{1,7},{2,4},{3,5},{4,2},{5,3},{6,0},{7,1},{8,14},{9,15},{10,... | collective-permute-start | bytes 313352 | tf_op jit(solution)/shard_map/ppermute | solution.py:386
  200.5 8.2 %collective-permute-start.40 = (s16[408,128]{1,0:T(8,128)(2,1)S(1)}, s16[408,128]{1,0:T(8,128)(2,1)S(1)}, u32[]{:S(2)}, u32[]{:S(2)}) collective-permute-start(s16[408,128]{1,0:T(8,128)(2,1)S(1)} %get-tuple-element.214), channel_id=1, source_target_pairs={{0,7},{1,6},{2,5},{3,4},{4,3},{5,2},{6,1},{7,0},{8,15},{9,14},{10,... | collective-permute-start | bytes 313352 | tf_op jit(solution)/shard_map/ppermute | solution.py:386
  201.6 10.8 %collective-permute-start.43 = (s16[408,128]{1,0:T(8,128)(2,1)S(1)}, s16[408,128]{1,0:T(8,128)(2,1)S(1)}, u32[]{:S(2)}, u32[]{:S(2)}) collective-permute-start(s16[408,128]{1,0:T(8,128)(2,1)S(1)} %get-tuple-element.222), channel_id=1, source_target_pairs={{0,18},{1,19},{2,16},{3,17},{4,22},{5,23},{6,20},{7,21},{8,26},{9,... | collective-permute-start | bytes 313352 | tf_op jit(solution)/shard_map/ppermute | solution.py:386
  204.6 11.8 %collective-permute-start.24 = (s16[408,128]{1,0:T(8,128)(2,1)S(1)}, s16[408,128]{1,0:T(8,128)(2,1)S(1)}, u32[]{:S(2)}, u32[]{:S(2)}) collective-permute-start(s16[408,128]{1,0:T(8,128)(2,1)S(1)} %get-tuple-element.168), channel_id=1, source_target_pairs={{0,17},{1,16},{2,19},{3,18},{4,21},{5,20},{6,23},{7,22},{8,25},{9,... | collective-permute-start | bytes 313352 | tf_op jit(solution)/shard_map/ppermute | solution.py:386
  205.9 11.5 %collective-permute-start.37 = (s16[408,128]{1,0:T(8,128)(2,1)S(1)}, s16[408,128]{1,0:T(8,128)(2,1)S(1)}, u32[]{:S(2)}, u32[]{:S(2)}) collective-permute-start(s16[408,128]{1,0:T(8,128)(2,1)S(1)} %get-tuple-element.208), channel_id=1, source_target_pairs={{0,5},{1,4},{2,7},{3,6},{4,1},{5,0},{6,3},{7,2},{8,13},{9,12},{10,... | collective-permute-start | bytes 313352 | tf_op jit(solution)/shard_map/ppermute | solution.py:386
  208.6 11.1 %collective-permute-start.20 = (s16[408,128]{1,0:T(8,128)(2,1)S(1)}, s16[408,128]{1,0:T(8,128)(2,1)S(1)}, u32[]{:S(2)}, u32[]{:S(2)}) collective-permute-start(s16[408,128]{1,0:T(8,128)(2,1)S(1)} %get-tuple-element.160), channel_id=1, source_target_pairs={{0,3},{1,2},{2,1},{3,0},{4,7},{5,6},{6,5},{7,4},{8,11},{9,10},{10,... | collective-permute-start | bytes 313352 | tf_op jit(solution)/shard_map/ppermute | solution.py:386
  208.7 9.9 %collective-permute-start.41 = (s16[408,128]{1,0:T(8,128)(2,1)S(1)}, s16[408,128]{1,0:T(8,128)(2,1)S(1)}, u32[]{:S(2)}, u32[]{:S(2)}) collective-permute-start(s16[408,128]{1,0:T(8,128)(2,1)S(1)} %get-tuple-element.215), channel_id=1, source_target_pairs={{0,16},{1,17},{2,18},{3,19},{4,20},{5,21},{6,22},{7,23},{8,24},{9,... | collective-permute-start | bytes 313352 | tf_op jit(solution)/shard_map/ppermute | solution.py:386
  212.4 6.2 %collective-permute-start.44 = (s16[408,128]{1,0:T(8,128)(2,1)S(1)}, s16[408,128]{1,0:T(8,128)(2,1)S(1)}, u32[]{:S(2)}, u32[]{:S(2)}) collective-permute-start(s16[408,128]{1,0:T(8,128)(2,1)S(1)} %get-tuple-element.228), channel_id=1, source_target_pairs={{0,4},{1,5},{2,6},{3,7},{4,0},{5,1},{6,2},{7,3},{8,12},{9,13},{10,... | collective-permute-start | bytes 313352 | tf_op jit(solution)/shard_map/ppermute | solution.py:386
  216.4 4.9 %collective-permute-start.25 = (s16[408,128]{1,0:T(8,128)(2,1)S(1)}, s16[408,128]{1,0:T(8,128)(2,1)S(1)}, u32[]{:S(2)}, u32[]{:S(2)}) collective-permute-start(s16[408,128]{1,0:T(8,128)(2,1)S(1)} %get-tuple-element.169), channel_id=1, source_target_pairs={{0,2},{1,3},{2,0},{3,1},{4,6},{5,7},{6,4},{7,5},{8,10},{9,11},{10,... | collective-permute-start | bytes 313352 | tf_op jit(solution)/shard_map/ppermute | solution.py:386
  217.4 3.9 %collective-permute-start.38 = (s16[408,128]{1,0:T(8,128)(2,1)S(1)}, s16[408,128]{1,0:T(8,128)(2,1)S(1)}, u32[]{:S(2)}, u32[]{:S(2)}) collective-permute-start(s16[408,128]{1,0:T(8,128)(2,1)S(1)} %get-tuple-element.209), channel_id=1, source_target_pairs={{0,1},{1,0},{2,3},{3,2},{4,5},{5,4},{6,7},{7,6},{8,9},{9,8},{10,11... | collective-permute-start | bytes 313352 | tf_op jit(solution)/shard_map/ppermute | solution.py:386
  218.6 2.7 %copy-start = (f32[2048,400]{0,1:T(8,128)S(1)}, f32[2048,400]{0,1:T(8,128)}, u32[]{:S(2)}) copy-start(f32[2048,400]{0,1:T(8,128)} %param.9) | copy-start | bytes 9830404
  218.6 2.7 %copy-start.1 = (f32[2048]{0:T(1024)S(1)}, f32[2048]{0:T(1024)}, u32[]{:S(2)}) copy-start(f32[2048]{0:T(1024)} %param.10) | copy-start | bytes 24580

commit v8 on v5

--- a/solution.py
+++ b/solution.py
@@ -9,10 +9,10 @@
 
 BLK = 128
 TAIL = 8
-CUTS = (1, 2, 2, 2, 1)
-STEPS = (1, 3, 4)
+STEPS = (3, 8)
+WINDOW = 5
 TILE = 256
-AXES = ("src", "dst")
+AXES = ("far", "near", "dst")
 F32 = jnp.float32
 BF16 = jnp.bfloat16
 NT = (((1,), (1,)), ((), ()))
@@ -26,7 +26,7 @@
 
 
 def cost(flops):
-    return pl.CostEstimate(flops=flops, bytes_accessed=flops // 512, transcendentals=0)
+    return pl.CostEstimate(flops=flops // 64, bytes_accessed=flops // 32768, transcendentals=0)
 
 
 def whole():
@@ -224,7 +224,8 @@
     outs, total, slot = refs[len(bounds) + peers : -2], refs[-2], refs[-1]
     width = slot.shape[0]
     total[:width], total[width:] = split(sum(g[...].astype(F32) for g in grads))
-    for k, out_ref in enumerate(outs):
+    seats = outs if len(outs[0].shape) == 2 else [outs[0].at[k] for k in range(outs[0].shape[0])]
+    for k, out_ref in enumerate(seats):
         alive = live_ref[first + k] > 0
         rank = rank_ref[first + k]
 
@@ -247,13 +248,15 @@
             out_ref[...] = jnp.zeros(out_ref.shape, jnp.int16)
 
 
-def pack(first, group, rank, live, chunks, bounds, grad_negs, npos):
+def pack(first, group, joined, rank, live, chunks, bounds, grad_negs, npos):
     width = chunks[0].shape[0]
+    block = (width + TAIL, BLK)
+    shape, outs = ((group,) + block, 1) if joined else (block, group)
     return pl.pallas_call(
         functools.partial(pack_kernel, first, tuple(bounds), len(grad_negs)),
-        out_shape=(jax.ShapeDtypeStruct((width + TAIL, BLK), jnp.int16),) * group,
+        out_shape=(pltpu.HBM(shape, jnp.int16),) * outs,
         in_specs=[smem(), smem()] + [whole()] * (1 + len(chunks) + len(grad_negs)),
-        out_specs=(whole(),) * group,
+        out_specs=(pl.BlockSpec(shape, lambda: (0,) * len(shape)),) * outs,
         scratch_shapes=[
             pltpu.VMEM((2 * width, npos.shape[1]), BF16),
             pltpu.VMEM((width, BLK), F32),
@@ -267,12 +270,14 @@
 def add_kernel(first, fresh, asked_ref, *refs):
     grad = refs[-1]
     backs = refs[: -1 if fresh else -2]
+    if len(backs[0].shape) == 3:
+        backs = [backs[0].at[k] for k in range(backs[0].shape[0])]
     width = grad.shape[0]
     if fresh:
         grad[...] = jnp.zeros_like(grad)
     for k, back in enumerate(backs):
         lanes = pl.ds(pl.multiple_of(asked_ref[first + k] * BLK, BLK), BLK)
-        grad[:, lanes] += decode(back, width)
+        grad[:, lanes] += decode(back[...], width)
 
 
 def add(first, asked, backs, grad, width, rows):
@@ -296,7 +301,7 @@
     width, rows = grad.shape
     for k, back in enumerate(backs):
         lanes = pl.ds(pl.multiple_of(asked_ref[first + k] * BLK, BLK), BLK)
-        grad[:, lanes] += decode(back, width)
+        grad[:, lanes] += decode(back[...], width)
     span = fresh.shape[1] // sems.shape[0]
 
     def copy(b):
@@ -348,8 +353,11 @@
     operator = relations[rel_ids].T
 
     half = devices // 2
-    order = [k for pair in zip(range(devices - 1, half - 1, -1), range(half - 1, -1, -1)) for k in pair]
-    partners = lax.axis_index(AXES) ^ jnp.array(order, jnp.int32)
+    order = list(range(devices - 1, half - 1, -1))
+    me = lax.axis_index(AXES)
+    partners = jnp.concatenate(
+        [me ^ jnp.array(order, jnp.int32), me // half * half + jnp.arange(half, dtype=jnp.int32)]
+    )
     ids = jnp.arange(devices, dtype=jnp.int32)
     seat = partners[:, None] == ids[None, :]
     named_by = jnp.max((src_pos // BLK)[:, None] == ids[None, :], axis=0).astype(jnp.int32)
@@ -361,8 +369,6 @@
         jnp.where((rank[None, :] == slot[:, None]) & (alive[None, :] > 0), partners[None, :], 0), axis=1
     )
     asked = jnp.sum(jnp.where(seat, asked[None, :], 0), axis=1)
-    sizes = [cut * devices // sum(CUTS) for cut in CUTS]
-    firsts = [sum(sizes[:g]) for g in range(len(sizes))]
     steps = [0] + [named * step // STEPS[-1] for step in STEPS]
     bounds = list(zip(steps[:-1], steps[1:]))
 
@@ -385,26 +391,31 @@
     source, target, g_pos = gather_edges(rows, spos, dpos, operator)
     grads_src, grads_dst, part_negs = score(negs, source, target, operator, g_pos)
     own_grad = [part_negs[0]] + [swap(part_negs[shift], shift, "dst") for shift in range(1, peers)]
-    grad = None
-    backs, chunks = [], []
-    for g, (first, group) in enumerate(zip(firsts, sizes)):
-        if g < len(bounds):
-            edges_at = (spos, dpos)
-            if g:
-                edges_at, backs[:1] = lax.optimization_barrier((edges_at, backs[:1]))
-            chunks.append(scatter(*bounds[g], grads_src, grads_dst, *edges_at))
-        packed = list(pack(first, group, rank, alive, chunks, bounds[: len(chunks)], own_grad, npos))
-        if g:
-            ahead = len(backs) // 2
-            if grad is None:
-                packed, backs[:ahead] = lax.optimization_barrier((packed, backs[:ahead]))
-            else:
-                packed, backs[:ahead], grad = lax.optimization_barrier((packed, backs[:ahead], grad))
-            grad = add(firsts[g - 1], asked, backs, grad, width, rows_dev)
-        backs = [
-            swap(x, shift, AXES) if shift else x
-            for x, shift in zip(packed, order[first : first + group])
-        ]
+    def packs(first, group, joined, chunks):
+        return pack(
+            first, group, joined, rank, alive, chunks, bounds[: len(chunks)], own_grad, npos
+        )
+
+    lead = steps[1]
+    chunks = [scatter(*bounds[0], grads_src, grads_dst, spos, dpos)]
+    leaving = list(packs(0, lead, False, chunks))
+    flight = [swap(x, shift, AXES) for x, shift in zip(leaving, order)]
+    chunks.append(scatter(*bounds[1], grads_src, grads_dst, spos, dpos))
+    leaving += packs(lead, half - lead, False, chunks)
+    near = packs(half, half, True, chunks)[0]
+    near, leaving, flight = lax.optimization_barrier((near, leaving, flight))
+    near = lax.all_to_all(near, AXES[1:], split_axis=0, concat_axis=0, tiled=True)
+    part = half // 2
+    for i in range(lead, half):
+        x = leaving[i]
+        if i >= WINDOW:
+            x, flight[i - WINDOW] = lax.optimization_barrier((x, flight[i - WINDOW]))
+        if i == part + WINDOW:
+            grad = add(0, asked, flight[:part], None, width, rows_dev)
+            x, grad = lax.optimization_barrier((x, grad))
+        flight.append(swap(x, order[i], AXES))
+    grad = add(half, asked, [near], grad, width, rows_dev)
+    firsts, backs = [part], flight[part:]
     new_table, new_state = update(
         firsts[-1], asked, backs, grad, table.T, state.reshape(1, rows_dev)
     )
@@ -412,6 +423,8 @@
 
 
 def solution(mesh):
+    across, along = mesh.devices.shape
+    mesh = jax.sharding.Mesh(mesh.devices.reshape(2, across // 2, along), AXES)
     in_specs = (
         P(AXES, None),
         P(AXES),

time: 227 us -> 242 us (1.066)
  waiting for transfers between devices: 79.8 us -> 90.2 us
  local copies, waits for them, and re-layouts: 30.8 us -> 38.5 us
  starting transfers between devices: 62.8 us -> 56.5 us
  Pallas kernels: 48.4 us -> 51.1 us
    ppermute x45 -> x30, starting transfers between devices: 52.8 us -> 41.3 us  [swap(): return lax.ppermute(x, axis, [(i, i ^ shift) for i in range(count)])]
    unnamed x17 -> x51, local copies, waits for them, and re-layouts: 8.64 us -> 17.9 us
    ppermute x45 -> x30, waiting for transfers between devices: 28.5 us -> 37.6 us  [swap(): return lax.ppermute(x, axis, [(i, i ^ shift) for i in range(count)])]
    all_to_all x0 -> x1, starting transfers between devices: none -> 4.41 us  [per_device(): lax.all_to_all(near, AXES[1:], split_axis=0, concat_axis=0, tiled=True)]
    pallas_call x5 -> x3, Pallas kernels: 9.73 us -> 10.8 us  [pack(): pl.pallas_call(functools.partial(pack_kernel, first, tuple(bounds), len(g...]
    pallas_call x3 -> x2, Pallas kernels: 15.1 us -> 15.1 us  [scatter(): pl.pallas_call(functools.partial(scatter_kernel, first * BLK), out_shape=...]
  transfers between devices with their start and end apart: 47 -> 33, of which waited for: 15 -> 13; matrix products, arithmetic and copies ran while one was open for 13% -> 12% of each run, Pallas kernels for 15% -> 15%
where the time goes in v8:
time: 242 us
  waiting for transfers between devices  90.2 us (37%)
  starting transfers between devices  56.5 us (23%)
  Pallas kernels  51.1 us (21%)
  local copies, waits for them, and re-layouts  38.5 us (16%)
  other arithmetic  3.95 us (2%)
    all_to_all x1, waiting for transfers between devices, per_device(): lax.all_to_all(outgoing.transpose(0, 2, 1), AXES, split_axis=0, concat_ax...  47.7 us
    ppermute x30, starting transfers between devices, swap(): return lax.ppermute(x, axis, [(i, i ^ shift) for i in range(count)])  41.3 us
    ppermute x30, waiting for transfers between devices, swap(): return lax.ppermute(x, axis, [(i, i ^ shift) for i in range(count)])  37.6 us
    unnamed x51, local copies, waits for them, and re-layouts  17.9 us
    gather x2, local copies, waits for them, and re-layouts, per_device(): operator = relations[rel_ids].T  16.7 us
    pallas_call x2, Pallas kernels, scatter(): pl.pallas_call(functools.partial(scatter_kernel, first * BLK), out_shape=...  15.1 us
    pallas_call x3, Pallas kernels, pack(): pl.pallas_call(functools.partial(pack_kernel, first, tuple(bounds), len(g...  10.8 us
    pallas_call x1, Pallas kernels, gather_edges(): pl.pallas_call(edge_kernel, grid=(edges // tile,), out_shape=(jax.ShapeDt...  8.04 us
  transfers between devices with their start and end apart: 33, of which 13 were waited for; matrix products, arithmetic and copies ran while one was open for 12% of the time, Pallas kernels for 15%

profile of v8, /device:TPU:0, one launch (start us, length us, event | category | flops | bytes accessed | tf_op | source)
XLA Modules:
  0.0 241.6 jit_solution(16719805003904156172)
XLA Ops:
  0.6 1.3 copy.27
  2.0 7.3 %all-to-all-start = ((s32[32,1,1]{2,1,0:T(1,128)}), s32[32,1,1]{2,1,0:T(1,128)S(1)}, u32[]{:S(2)}, u32[]{:S(2)}) async-start(s32[32,1,1]{2,1,0:T(1,128)} %copy.27), calls=%async_computation | async-start | bytes 32768 | tf_op jit(solution)/shard_map/all_to_all | solution.py:345
  9.3 2.1 copy_bitcast_fusion
  11.4 4.9 %all-to-all-done = s32[32,1,1]{2,1,0:T(1,128)S(1)} async-done(((s32[32,1,1]{2,1,0:T(1,128)}), s32[32,1,1]{2,1,0:T(1,128)S(1)}, u32[]{:S(2)}, u32[]{:S(2)}) %all-to-all-start) | async-done | bytes 160 | tf_op jit(solution)/shard_map/all_to_all | solution.py:345
  16.3 0.7 reduce
  17.0 2.7 %gather_fusion = bf16[32,128,400]{1,2,0:T(8,128)(2,1)} fusion(bf16[16,128,400]{1,2,0:T(8,128)(2,1)S(1)} %copy_bitcast_fusion, s32[1024]{0:T(1024)S(1)} %pad_clamp_fusion), kind=kCustom, calls=%fused_computation | custom fusion | bytes 6553728 | tf_op jit(solution)/shard_map/gather | solution.py:349
  19.7 3.5 %all-to-all-start.1 = ((bf16[32,400,128]{2,1,0:T(8,128)(2,1)}), bf16[32,400,128]{2,1,0:T(8,128)(2,1)}, u32[]{:S(2)}, u32[]{:S(2)}) async-start(bf16[32,400,128]{2,1,0:T(8,128)(2,1)} %bitcast.30), calls=%async_computation.1 | async-start | bytes 6553600 | tf_op jit(solution)/shard_map/all_to_all | solution.py:350
  23.3 8.6 %copy.29 = f32[4096,400]{1,0:T(8,128)} copy(f32[4096,400]{0,1:T(8,128)} %param.11) | data formatting | bytes 13107200 | tf_op args[2]
  31.9 12.9 %gather_fusion.1 = f32[2048,400]{1,0:T(8,128)} fusion(f32[4096,400]{1,0:T(8,128)} %copy.29, s32[2048]{0:T(1024)S(1)} %fusion.3), kind=kCustom, calls=%fused_computation.1 | custom fusion | bytes 6561792 | tf_op jit(solution)/shard_map/gather | solution.py:353
  44.8 3.8 %copy.30 = f32[2048,400]{0,1:T(8,128)S(1)} copy(f32[2048,400]{1,0:T(8,128)} %gather_fusion.1) | data formatting | bytes 6553600 | tf_op jit(solution)/shard_map/gather | solution.py:353
  49.8 47.7 %all-to-all-done.1.fetched = bf16[32,400,128]{2,1,0:T(8,128)(2,1)} async-done(((bf16[32,400,128]{2,1,0:T(8,128)(2,1)}), bf16[32,400,128]{2,1,0:T(8,128)(2,1)}, u32[]{:S(2)}, u32[]{:S(2)}) %all-to-all-start.1) | async-done | bytes 3276832 | tf_op jit(solution)/shard_map/all_to_all | solution.py:350
  97.5 2.6 %gather_negs.1 = (bf16[400,128]{1,0:T(8,128)(2,1)S(1)}, bf16[400,2048]{1,0:T(8,128)(2,1)S(1)}) custom-call(s32[16]{0:T(128)S(1)} %select_reduce_fusion.7.live_ref, bf16[32,400,128]{2,1,0:T(8,128)(2,1)} %all-to-all-done.1.fetched, s32[1,128]{1,0:T(1,128)S(1)} %fusion.11.pos_ref.npos), custom_call_target="tpu_custom_call" | custom-call | tf_op jit(solution)/shard_map/gather_negs/pallas_call | solution.py:83
  100.3 1.3 collective-permute-start.1
  102.1 1.2 collective-permute-start.3
  103.8 2.1 collective-permute-start.5
  106.0 0.9 collective-permute-start.6
  107.0 8.0 %gather_edges.1 = (bf16[400,2048]{1,0:T(8,128)(2,1)S(1)}, bf16[400,2048]{1,0:T(8,128)(2,1)S(1)}, f32[1,2048]{1,0:T(1,128)S(1)}) custom-call(bf16[400,2048]{1,0:T(8,128)(2,1)S(1)} %get-tuple-element.90.rows, s32[1,2048]{1,0:T(1,128)S(1)} %bitcast.23, s32[1,2048]{1,0:T(1,128)S(1)} %bitcast.26, f32[400,2048]{1,0:T(8,128)S(1)} %bitcast.20), custom_call_target="tpu_custom_call" | custom-call | flops 104857600 | bytes 204800 | tf_op jit(solution)/shard_map/gather_edges/pallas_call | solution.py:112
  115.1 6.2 %score.1 = (bf16[2,400,2048]{2,1,0:T(8,128)(2,1)S(1)}, bf16[2,400,2048]{2,1,0:T(8,128)(2,1)S(1)}, bf16[400,128]{1,0:T(8,128)(2,1)S(1)}, bf16[400,128]{1,0:T(8,12...) custom-call(bf16[400,128]{1,0:T(8,128)(2,1)S(1)} %get-tuple-element., ...), custom_call_target="tpu_custom_call" | custom-call | flops 78643200 | bytes 153600 | tf_op jit(solution)/shard_map/score/pallas_call | solution.py:159
  121.2 1.4 collective-permute-start.7
  123.1 0.9 collective-permute-start.9
  124.6 1.5 collective-permute-start.11
  126.1 0.8 collective-permute-start.12
  126.9 1.4 collective-permute-done.8.refs_4_.refs_3_
  128.4 5.7 %scatter.2.refs_0_ = f32[400,768]{1,0:T(8,128)S(1)} custom-call(bf16[2,400,2048]{2,1,0:T(8,128)(2,1)S(1)} %get-tuple-element.97.gs_ref, bf16[2,400,2048]{2,1,0:T(8,128)(2,1)S(1)} %get-tuple-element.98.gd_ref, s32[1,2048]{1,0:T(1,128)S(1)} %bitcast.24, s32[1,2048]{1,0:T(1,128)S(1)} %bitcast.27), custom_call_target="tpu_custom_call" | custom-call | flops 39321600 | bytes 76800 | tf_op jit(solution)/shard_map/scatter/pallas_call | solution.py:196
  134.2 1.7 collective-permute-done.11.refs_7_.refs_6_
  135.8 2.7 %pack.4 = (s16[408,128]{1,0:T(8,128)(2,1)}, s16[408,128]{1,0:T(8,128)(2,1)}, s16[408,128]{1,0:T(8,128)(2,1)}, s16[408,128]{1,0:T(8,128)(2,1)}, s16[408,128]{1,0:T(8,128)(2,1)}, /*index=5*/s16[408,128]{1,0:T(8,128)(2,1)}) custom-call(s32[32]{0:T(128)S(1)} %select_reduce_fusion.5.rank_ref, s32[32]{0:T(128)S(1)} %select_reduce_fusion.6.live_ref, ...), custom_call_target="tpu_custom_call" | custom-call | flops 2457600 | bytes 4800 | tf_op jit(solution)/shard_map/pack/pallas_call | solution.py:255
  138.5 2.5 %collective-permute-start.14 = (s16[408,128]{1,0:T(8,128)(2,1)}, s16[408,128]{1,0:T(8,128)(2,1)S(1)}, u32[]{:S(2)}, u32[]{:S(2)}) collective-permute-start(s16[408,128]{1,0:T(8,128)(2,1)} %get-tuple-element.107), channel_id=1, source_target_pairs={{0,31},{1,30},{2,29},{3,28},{4,27},{5,26},{6,25},{7,24},{8,23},{9,... | collective-permute-start | bytes 313352 | tf_op jit(solution)/shard_map/ppermute | solution.py:386
  141.0 2.5 %collective-permute-start.15 = (s16[408,128]{1,0:T(8,128)(2,1)}, s16[408,128]{1,0:T(8,128)(2,1)S(1)}, u32[]{:S(2)}, u32[]{:S(2)}) collective-permute-start(s16[408,128]{1,0:T(8,128)(2,1)} %get-tuple-element.108), channel_id=1, source_target_pairs={{0,30},{1,31},{2,28},{3,29},{4,26},{5,27},{6,24},{7,25},{8,22},{9,... | collective-permute-start | bytes 313352 | tf_op jit(solution)/shard_map/ppermute | solution.py:386
  143.6 1.5 collective-permute-start.16
  145.0 3.3 %collective-permute-start.17 = (s16[408,128]{1,0:T(8,128)(2,1)}, s16[408,128]{1,0:T(8,128)(2,1)S(1)}, u32[]{:S(2)}, u32[]{:S(2)}) collective-permute-start(s16[408,128]{1,0:T(8,128)(2,1)} %get-tuple-element.110), channel_id=1, source_target_pairs={{0,28},{1,29},{2,30},{3,31},{4,24},{5,25},{6,26},{7,27},{8,20},{9,... | collective-permute-start | bytes 313352 | tf_op jit(solution)/shard_map/ppermute | solution.py:386
  148.3 1.4 collective-permute-start.18
  149.7 2.8 %collective-permute-start.19 = (s16[408,128]{1,0:T(8,128)(2,1)}, s16[408,128]{1,0:T(8,128)(2,1)S(1)}, u32[]{:S(2)}, u32[]{:S(2)}) collective-permute-start(s16[408,128]{1,0:T(8,128)(2,1)} %get-tuple-element.112), channel_id=1, source_target_pairs={{0,26},{1,27},{2,24},{3,25},{4,30},{5,31},{6,28},{7,29},{8,18},{9,... | collective-permute-start | bytes 313352 | tf_op jit(solution)/shard_map/ppermute | solution.py:386
  152.5 9.4 %scatter.3.refs_1_ = f32[400,1280]{1,0:T(8,128)S(1)} custom-call(bf16[2,400,2048]{2,1,0:T(8,128)(2,1)S(1)} %get-tuple-element.97.gs_ref, bf16[2,400,2048]{2,1,0:T(8,128)(2,1)S(1)} %get-tuple-element.98.gd_ref, s32[1,2048]{1,0:T(1,128)S(1)} %bitcast.25, s32[1,2048]{1,0:T(1,128)S(1)} %bitcast.28), custom_call_target="tpu_custom_call" | custom-call | flops 65536000 | bytes 128000 | tf_op jit(solution)/shard_map/scatter/pallas_call | solution.py:196
  162.0 4.0 %pack.5 = (s16[408,128]{1,0:T(8,128)(2,1)}, s16[408,128]{1,0:T(8,128)(2,1)}, s16[408,128]{1,0:T(8,128)(2,1)}, s16[408,128]{1,0:T(8,128)(2,1)}, s16[408,128]{1,0:...) custom-call(s32[32]{0:T(128)S(1)} %select_reduce_fusion.5.rank_ref, ...), custom_call_target="tpu_custom_call" | custom-call | flops 4096000 | bytes 8000 | tf_op jit(solution)/shard_map/pack/pallas_call | solution.py:255
  166.0 4.1 %pack.3 = s16[16,408,128]{2,1,0:T(8,128)(2,1)} custom-call(s32[32]{0:T(128)S(1)} %select_reduce_fusion.5.rank_ref, s32[32]{0:T(128)S(1)} %select_reduce_fusion.6.live_ref, s32[1,128]{1,0:T(1,128)S(1)} %fusion.11.pos_ref.npos, f32[400,768]{1,0:T(8,128)S(1)} %scatter.2.refs_0_, f32[400,1280]{1,0:T(8,128)S(1)} %scatter.3.refs_1_, ...), custom_call_target="tpu_custom_call" | custom-call | flops 6553600 | bytes 12800 | tf_op jit(solution)/shard_map/pack/pallas_call | solution.py:255
  170.1 0.6 copy-done.5
  170.8 0.6 copy-done.7
  171.4 0.6 copy-done.9
  172.1 0.6 copy-done.11
  172.7 0.6 copy-done.13
  173.4 4.4 %all-to-all-start.2 = ((s16[16,408,128]{2,1,0:T(8,128)(2,1)}), s16[16,408,128]{2,1,0:T(8,128)(2,1)}, u32[]{:S(2)}, u32[]{:S(2)}) async-start(s16[16,408,128]{2,1,0:T(8,128)(2,1)} %pack.3), calls=%async_computation.2 | async-start | bytes 3342336 | tf_op jit(solution)/shard_map/all_to_all | solution.py:407
  177.8 3.2 %collective-permute-start.21 = (s16[408,128]{1,0:T(8,128)(2,1)S(1)}, s16[408,128]{1,0:T(8,128)(2,1)S(1)}, u32[]{:S(2)}, u32[]{:S(2)}) collective-permute-start(s16[408,128]{1,0:T(8,128)(2,1)S(1)} %copy-done.23), channel_id=1, source_target_pairs={{0,22},{1,23},{2,20},{3,21},{4,18},{5,19},{6,16},{7,17},{8,30},{9,... | collective-permute-start | bytes 313352 | tf_op jit(solution)/shard_map/ppermute | solution.py:386
  181.0 1.4 collective-permute-start.22
  182.4 2.2 collective-permute-start.23
  184.5 1.9 collective-permute-start.25
  186.4 13.6 %collective-permute-done.21.refs_1_ = s16[408,128]{1,0:T(8,128)(2,1)S(1)} collective-permute-done((s16[408,128]{1,0:T(8,128)(2,1)S(1)}, s16[408,128]{1,0:T(8,128)(2,1)S(1)}, u32[]{:S(2)}, u32[]{:S(2)}) %collective-permute-start.21) | collective-permute-done | bytes 104480 | tf_op jit(solution)/shard_map/ppermute | solution.py:386
  200.0 3.1 %collective-permute-done.22.refs_2_ = s16[408,128]{1,0:T(8,128)(2,1)S(1)} collective-permute-done((s16[408,128]{1,0:T(8,128)(2,1)S(1)}, s16[408,128]{1,0:T(8,128)(2,1)S(1)}, u32[]{:S(2)}, u32[]{:S(2)}) %collective-permute-start.22) | collective-permute-done | bytes 104480 | tf_op jit(solution)/shard_map/ppermute | solution.py:386
  203.1 4.8 %collective-permute-done.23.refs_6_ = s16[408,128]{1,0:T(8,128)(2,1)S(1)} collective-permute-done((s16[408,128]{1,0:T(8,128)(2,1)S(1)}, s16[408,128]{1,0:T(8,128)(2,1)S(1)}, u32[]{:S(2)}, u32[]{:S(2)}) %collective-permute-start.23) | collective-permute-done | bytes 104480 | tf_op jit(solution)/shard_map/ppermute | solution.py:386
  208.0 3.2 %collective-permute-done.25.refs_7_ = s16[408,128]{1,0:T(8,128)(2,1)S(1)} collective-permute-done((s16[408,128]{1,0:T(8,128)(2,1)S(1)}, s16[408,128]{1,0:T(8,128)(2,1)S(1)}, u32[]{:S(2)}, u32[]{:S(2)}) %collective-permute-start.25) | collective-permute-done | bytes 104480 | tf_op jit(solution)/shard_map/ppermute | solution.py:386
  211.2 0.7 collective-permute-start.26
  211.9 0.9 copy-done.4
  212.8 0.9 copy-done.6
  213.7 0.9 copy-done.8
  214.6 0.9 copy-done.10
  215.5 0.9 copy-done.12
  216.4 0.9 copy-done.14
  217.3 1.2 add.106.refs_1_
  219.2 1.8 collective-permute-start.27
  221.0 0.9 collective-permute-start.28
  221.9 2.7 %collective-permute-start.29 = (s16[408,128]{1,0:T(8,128)(2,1)}, s16[408,128]{1,0:T(8,128)(2,1)}, u32[]{:S(2)}, u32[]{:S(2)}) collective-permute-start(s16[408,128]{1,0:T(8,128)(2,1)} %get-tuple-element.159), channel_id=1, source_target_pairs={{0,16},{1,17},{2,18},{3,19},{4,20},{5,21},{6,22},{7,23},{8,24},{9,... | collective-permute-start | bytes 313352 | tf_op jit(solution)/shard_map/ppermute | solution.py:386
  224.6 2.6 %add.107.refs_8_ = f32[400,2048]{1,0:T(8,128)S(1)} custom-call(s32[32]{0:T(128)S(1)} %get-tuple-element.83.asked_ref, s16[16,408,128]{2,1,0:T(8,128)(2,1)} %all-to-all-done.2.refs_0_, f32[400,2048]{1,0:T(8,128)S(1)} %add.106.refs_1_), custom_call_target="tpu_custom_call", output_to_operand_aliasing={{}: (2, {})} | custom-call | flops 51200 | bytes 100 | tf_op jit(solution)/shard_map/add/pallas_call | solution.py:286
  227.3 6.4 %collective-permute-done.27.refs_5_ = s16[408,128]{1,0:T(8,128)(2,1)} collective-permute-done((s16[408,128]{1,0:T(8,128)(2,1)}, s16[408,128]{1,0:T(8,128)(2,1)}, u32[]{:S(2)}, u32[]{:S(2)}) %collective-permute-start.27) | collective-permute-done | bytes 104480 | tf_op jit(solution)/shard_map/ppermute | solution.py:386
  233.7 3.2 %collective-permute-done.29.refs_7_ = s16[408,128]{1,0:T(8,128)(2,1)} collective-permute-done((s16[408,128]{1,0:T(8,128)(2,1)}, s16[408,128]{1,0:T(8,128)(2,1)}, u32[]{:S(2)}, u32[]{:S(2)}) %collective-permute-start.29) | collective-permute-done | bytes 104480 | tf_op jit(solution)/shard_map/ppermute | solution.py:386
  236.9 4.5 %update.1 = (f32[400,2048]{1,0:T(8,128)}, f32[1,2048]{1,0:T(1,128)}) custom-call(s32[32]{0:T(128)S(1)} %get-tuple-element.83.asked_ref, s16[408,128]{1,0:T(8,128)(2,1)S(1)} %copy-done.2, s16[408,128]{1,0:T(8,128)(2,1)S(1)} %collective-permute-done.21.refs_1_, s16[408,128]{1,0:T(8,128)(2,1)S(1)} %collective-permute-done.22.refs_2_, ...), custom_call_target="tpu_custom_call" | custom-call | flops 819200 | bytes 1600 | tf_op jit(solution)/shard_map/update/pallas_call | solution.py:325
  (89 shorter events, 4.4 us)
Async XLA Ops:
  2.0 14.4 %all-to-all-start = ((s32[32,1,1]{2,1,0:T(1,128)}), s32[32,1,1]{2,1,0:T(1,128)S(1)}, u32[]{:S(2)}, u32[]{:S(2)}) async-start(s32[32,1,1]{2,1,0:T(1,128)} %copy.27), calls=%async_computation | async-start | bytes 32768 | tf_op jit(solution)/shard_map/all_to_all | solution.py:345
  19.7 77.8 %all-to-all-start.1 = ((bf16[32,400,128]{2,1,0:T(8,128)(2,1)}), bf16[32,400,128]{2,1,0:T(8,128)(2,1)}, u32[]{:S(2)}, u32[]{:S(2)}) async-start(bf16[32,400,128]{2,1,0:T(8,128)(2,1)} %bitcast.30), calls=%async_computation.1 | async-start | bytes 6553600 | tf_op jit(solution)/shard_map/all_to_all | solution.py:350
  23.3 8.6 %copy-start.18 = (s32[2048]{0:T(1024)S(1)}, s32[2048]{0:T(1024)}, u32[]{:S(2)}) copy-start(s32[2048]{0:T(1024)} %param.12) | copy-start | bytes 24580
  44.8 3.8 %copy-start.16 = (s32[2048]{0:T(1024)S(1)}, s32[2048]{0:T(1024)}, u32[]{:S(2)}) copy-start(s32[2048]{0:T(1024)} %param.14) | copy-start | bytes 24580
  44.8 3.8 %copy-start.17 = (s32[2048]{0:T(1024)S(1)}, s32[2048]{0:T(1024)}, u32[]{:S(2)}) copy-start(s32[2048]{0:T(1024)} %param.15) | copy-start | bytes 24580
  44.8 4.0 %copy-start.19 = (s32[16]{0:T(128)S(1)}, s32[16]{0:T(128)}, u32[]{:S(2)}) copy-start(s32[16]{0:T(128)} %constant.101.clone) | copy-start | bytes 196
  44.8 4.5 %copy-start.24 = (s32[128]{0:T(128)S(1)}, s32[128]{0:T(128)}, u32[]{:S(2)}) copy-start(s32[128]{0:T(128)} %param.16) | copy-start | bytes 1540
  100.2 3.6 %collective-permute-start = (bf16[400,128]{1,0:T(8,128)(2,1)S(1)}, bf16[400,128]{1,0:T(8,128)(2,1)S(1)}, u32[]{:S(2)}, u32[]{:S(2)}) collective-permute-start(bf16[400,128]{1,0:T(8,128)(2,1)S(1)} %get-tuple-element.89.refs_0_), channel_id=1, source_target_pairs={{0,1},{1,0},{2,3},{3,2},{4,5},{5,4},{6,7},{7,6},{8,9},{9,8},{10,11... | collective-permute-start | bytes 307208 | tf_op jit(solution)/shard_map/ppermute | solution.py:386
  100.3 5.7 %collective-permute-start.1 = (bf16[400,128]{1,0:T(8,128)(2,1)S(1)}, bf16[400,128]{1,0:T(8,128)(2,1)S(1)}, u32[]{:S(2)}, u32[]{:S(2)}) collective-permute-start(bf16[400,128]{1,0:T(8,128)(2,1)S(1)} %get-tuple-element.89.refs_0_), channel_id=1, source_target_pairs={{0,2},{1,3},{2,0},{3,1},{4,6},{5,7},{6,4},{7,5},{8,10},{9,11},{10,... | collective-permute-start | bytes 307208 | tf_op jit(solution)/shard_map/ppermute | solution.py:386
  101.5 13.5 %collective-permute-start.2 = (bf16[400,128]{1,0:T(8,128)(2,1)S(1)}, bf16[400,128]{1,0:T(8,128)(2,1)S(1)}, u32[]{:S(2)}, u32[]{:S(2)}) collective-permute-start(bf16[400,128]{1,0:T(8,128)(2,1)S(1)} %get-tuple-element.89.refs_0_), channel_id=1, source_target_pairs={{0,3},{1,2},{2,1},{3,0},{4,7},{5,6},{6,5},{7,4},{8,11},{9,10},{10,... | collective-permute-start | bytes 307208 | tf_op jit(solution)/shard_map/ppermute | solution.py:386
  102.1 12.9 %collective-permute-start.3 = (bf16[400,128]{1,0:T(8,128)(2,1)S(1)}, bf16[400,128]{1,0:T(8,128)(2,1)S(1)}, u32[]{:S(2)}, u32[]{:S(2)}) collective-permute-start(bf16[400,128]{1,0:T(8,128)(2,1)S(1)} %get-tuple-element.89.refs_0_), channel_id=1, source_target_pairs={{0,4},{1,5},{2,6},{3,7},{4,0},{5,1},{6,2},{7,3},{8,12},{9,13},{10,... | collective-permute-start | bytes 307208 | tf_op jit(solution)/shard_map/ppermute | solution.py:386
  103.3 11.7 %collective-permute-start.4 = (bf16[400,128]{1,0:T(8,128)(2,1)S(1)}, bf16[400,128]{1,0:T(8,128)(2,1)S(1)}, u32[]{:S(2)}, u32[]{:S(2)}) collective-permute-start(bf16[400,128]{1,0:T(8,128)(2,1)S(1)} %get-tuple-element.89.refs_0_), channel_id=1, source_target_pairs={{0,5},{1,4},{2,7},{3,6},{4,1},{5,0},{6,3},{7,2},{8,13},{9,12},{10,... | collective-permute-start | bytes 307208 | tf_op jit(solution)/shard_map/ppermute | solution.py:386
  103.8 11.2 %collective-permute-start.5 = (bf16[400,128]{1,0:T(8,128)(2,1)S(1)}, bf16[400,128]{1,0:T(8,128)(2,1)S(1)}, u32[]{:S(2)}, u32[]{:S(2)}) collective-permute-start(bf16[400,128]{1,0:T(8,128)(2,1)S(1)} %get-tuple-element.89.refs_0_), channel_id=1, source_target_pairs={{0,6},{1,7},{2,4},{3,5},{4,2},{5,3},{6,0},{7,1},{8,14},{9,15},{10,... | collective-permute-start | bytes 307208 | tf_op jit(solution)/shard_map/ppermute | solution.py:386
  106.0 9.0 %collective-permute-start.6 = (bf16[400,128]{1,0:T(8,128)(2,1)S(1)}, bf16[400,128]{1,0:T(8,128)(2,1)S(1)}, u32[]{:S(2)}, u32[]{:S(2)}) collective-permute-start(bf16[400,128]{1,0:T(8,128)(2,1)S(1)} %get-tuple-element.89.refs_0_), channel_id=1, source_target_pairs={{0,7},{1,6},{2,5},{3,4},{4,3},{5,2},{6,1},{7,0},{8,15},{9,14},{10,... | collective-permute-start | bytes 307208 | tf_op jit(solution)/shard_map/ppermute | solution.py:386
  121.2 4.9 %collective-permute-start.7 = (bf16[400,128]{1,0:T(8,128)(2,1)S(1)}, bf16[400,128]{1,0:T(8,128)(2,1)S(1)}, u32[]{:S(2)}, u32[]{:S(2)}) collective-permute-start(bf16[400,128]{1,0:T(8,128)(2,1)S(1)} %get-tuple-element.100), channel_id=1, source_target_pairs={{0,1},{1,0},{2,3},{3,2},{4,5},{5,4},{6,7},{7,6},{8,9},{9,8},{10,11... | collective-permute-start | bytes 307208 | tf_op jit(solution)/shard_map/ppermute | solution.py:386
  122.6 5.7 %collective-permute-start.8 = (bf16[400,128]{1,0:T(8,128)(2,1)S(1)}, bf16[400,128]{1,0:T(8,128)(2,1)S(1)}, u32[]{:S(2)}, u32[]{:S(2)}) collective-permute-start(bf16[400,128]{1,0:T(8,128)(2,1)S(1)} %get-tuple-element.101), channel_id=1, source_target_pairs={{0,2},{1,3},{2,0},{3,1},{4,6},{5,7},{6,4},{7,5},{8,10},{9,11},{10,... | collective-permute-start | bytes 307208 | tf_op jit(solution)/shard_map/ppermute | solution.py:386
  123.1 11.0 %collective-permute-start.9 = (bf16[400,128]{1,0:T(8,128)(2,1)S(1)}, bf16[400,128]{1,0:T(8,128)(2,1)S(1)}, u32[]{:S(2)}, u32[]{:S(2)}) collective-permute-start(bf16[400,128]{1,0:T(8,128)(2,1)S(1)} %get-tuple-element.102), channel_id=1, source_target_pairs={{0,3},{1,2},{2,1},{3,0},{4,7},{5,6},{6,5},{7,4},{8,11},{9,10},{10,... | collective-permute-start | bytes 307208 | tf_op jit(solution)/shard_map/ppermute | solution.py:386
  124.0 10.1 %collective-permute-start.10 = (bf16[400,128]{1,0:T(8,128)(2,1)S(1)}, bf16[400,128]{1,0:T(8,128)(2,1)S(1)}, u32[]{:S(2)}, u32[]{:S(2)}) collective-permute-start(bf16[400,128]{1,0:T(8,128)(2,1)S(1)} %get-tuple-element.103), channel_id=1, source_target_pairs={{0,4},{1,5},{2,6},{3,7},{4,0},{5,1},{6,2},{7,3},{8,12},{9,13},{10,... | collective-permute-start | bytes 307208 | tf_op jit(solution)/shard_map/ppermute | solution.py:386
  124.6 11.3 %collective-permute-start.11 = (bf16[400,128]{1,0:T(8,128)(2,1)S(1)}, bf16[400,128]{1,0:T(8,128)(2,1)S(1)}, u32[]{:S(2)}, u32[]{:S(2)}) collective-permute-start(bf16[400,128]{1,0:T(8,128)(2,1)S(1)} %get-tuple-element.104), channel_id=1, source_target_pairs={{0,5},{1,4},{2,7},{3,6},{4,1},{5,0},{6,3},{7,2},{8,13},{9,12},{10,... | collective-permute-start | bytes 307208 | tf_op jit(solution)/shard_map/ppermute | solution.py:386
  126.1 9.7 %collective-permute-start.12 = (bf16[400,128]{1,0:T(8,128)(2,1)S(1)}, bf16[400,128]{1,0:T(8,128)(2,1)S(1)}, u32[]{:S(2)}, u32[]{:S(2)}) collective-permute-start(bf16[400,128]{1,0:T(8,128)(2,1)S(1)} %get-tuple-element.105), channel_id=1, source_target_pairs={{0,6},{1,7},{2,4},{3,5},{4,2},{5,3},{6,0},{7,1},{8,14},{9,15},{10,... | collective-permute-start | bytes 307208 | tf_op jit(solution)/shard_map/ppermute | solution.py:386
  128.3 7.5 %collective-permute-start.13 = (bf16[400,128]{1,0:T(8,128)(2,1)S(1)}, bf16[400,128]{1,0:T(8,128)(2,1)S(1)}, u32[]{:S(2)}, u32[]{:S(2)}) collective-permute-start(bf16[400,128]{1,0:T(8,128)(2,1)S(1)} %get-tuple-element.106), channel_id=1, source_target_pairs={{0,7},{1,6},{2,5},{3,4},{4,3},{5,2},{6,1},{7,0},{8,15},{9,14},{10,... | collective-permute-start | bytes 307208 | tf_op jit(solution)/shard_map/ppermute | solution.py:386
  138.5 11.2 %collective-permute-start.14 = (s16[408,128]{1,0:T(8,128)(2,1)}, s16[408,128]{1,0:T(8,128)(2,1)S(1)}, u32[]{:S(2)}, u32[]{:S(2)}) collective-permute-start(s16[408,128]{1,0:T(8,128)(2,1)} %get-tuple-element.107), channel_id=1, source_target_pairs={{0,31},{1,30},{2,29},{3,28},{4,27},{5,26},{6,25},{7,24},{8,23},{9,... | collective-permute-start | bytes 313352 | tf_op jit(solution)/shard_map/ppermute | solution.py:386
  141.0 29.1 %collective-permute-start.15 = (s16[408,128]{1,0:T(8,128)(2,1)}, s16[408,128]{1,0:T(8,128)(2,1)S(1)}, u32[]{:S(2)}, u32[]{:S(2)}) collective-permute-start(s16[408,128]{1,0:T(8,128)(2,1)} %get-tuple-element.108), channel_id=1, source_target_pairs={{0,30},{1,31},{2,28},{3,29},{4,26},{5,27},{6,24},{7,25},{8,22},{9,... | collective-permute-start | bytes 313352 | tf_op jit(solution)/shard_map/ppermute | solution.py:386
  143.6 27.2 %collective-permute-start.16 = (s16[408,128]{1,0:T(8,128)(2,1)}, s16[408,128]{1,0:T(8,128)(2,1)S(1)}, u32[]{:S(2)}, u32[]{:S(2)}) collective-permute-start(s16[408,128]{1,0:T(8,128)(2,1)} %get-tuple-element.109), channel_id=1, source_target_pairs={{0,29},{1,28},{2,31},{3,30},{4,25},{5,24},{6,27},{7,26},{8,21},{9,... | collective-permute-start | bytes 313352 | tf_op jit(solution)/shard_map/ppermute | solution.py:386
  145.0 26.4 %collective-permute-start.17 = (s16[408,128]{1,0:T(8,128)(2,1)}, s16[408,128]{1,0:T(8,128)(2,1)S(1)}, u32[]{:S(2)}, u32[]{:S(2)}) collective-permute-start(s16[408,128]{1,0:T(8,128)(2,1)} %get-tuple-element.110), channel_id=1, source_target_pairs={{0,28},{1,29},{2,30},{3,31},{4,24},{5,25},{6,26},{7,27},{8,20},{9,... | collective-permute-start | bytes 313352 | tf_op jit(solution)/shard_map/ppermute | solution.py:386
  148.3 23.8 %collective-permute-start.18 = (s16[408,128]{1,0:T(8,128)(2,1)}, s16[408,128]{1,0:T(8,128)(2,1)S(1)}, u32[]{:S(2)}, u32[]{:S(2)}) collective-permute-start(s16[408,128]{1,0:T(8,128)(2,1)} %get-tuple-element.111), channel_id=1, source_target_pairs={{0,27},{1,26},{2,25},{3,24},{4,31},{5,30},{6,29},{7,28},{8,19},{9,... | collective-permute-start | bytes 313352 | tf_op jit(solution)/shard_map/ppermute | solution.py:386
  149.7 12.2 %copy-start.3 = (s16[408,128]{1,0:T(8,128)(2,1)}, s16[408,128]{1,0:T(8,128)(2,1)S(1)}, u32[]{:S(2)}) copy-start(s16[408,128]{1,0:T(8,128)(2,1)S(1)} %collective-permute-done.14.refs_0_) | copy-start | bytes 313348
  149.7 23.0 %collective-permute-start.19 = (s16[408,128]{1,0:T(8,128)(2,1)}, s16[408,128]{1,0:T(8,128)(2,1)S(1)}, u32[]{:S(2)}, u32[]{:S(2)}) collective-permute-start(s16[408,128]{1,0:T(8,128)(2,1)} %get-tuple-element.112), channel_id=1, source_target_pairs={{0,26},{1,27},{2,24},{3,25},{4,30},{5,31},{6,28},{7,29},{8,18},{9,... | collective-permute-start | bytes 313352 | tf_op jit(solution)/shard_map/ppermute | solution.py:386
  166.0 11.8 %copy-start.23 = (s16[408,128]{1,0:T(8,128)(2,1)S(1)}, s16[408,128]{1,0:T(8,128)(2,1)}, u32[]{:S(2)}) copy-start(s16[408,128]{1,0:T(8,128)(2,1)} %get-tuple-element.131) | copy-start | bytes 313348
  166.0 15.0 %copy-start.22 = (s16[408,128]{1,0:T(8,128)(2,1)S(1)}, s16[408,128]{1,0:T(8,128)(2,1)}, u32[]{:S(2)}) copy-start(s16[408,128]{1,0:T(8,128)(2,1)} %get-tuple-element.136) | copy-start | bytes 313348
  166.0 16.4 %copy-start.21 = (s16[408,128]{1,0:T(8,128)(2,1)S(1)}, s16[408,128]{1,0:T(8,128)(2,1)}, u32[]{:S(2)}) copy-start(s16[408,128]{1,0:T(8,128)(2,1)} %get-tuple-element.141) | copy-start | bytes 313348
  166.0 18.5 %copy-start.20 = (s16[408,128]{1,0:T(8,128)(2,1)S(1)}, s16[408,128]{1,0:T(8,128)(2,1)}, u32[]{:S(2)}) copy-start(s16[408,128]{1,0:T(8,128)(2,1)} %get-tuple-element.146) | copy-start | bytes 313348
  170.1 0.6 copy-start.5
  170.8 0.6 copy-start.7
  171.4 0.6 copy-start.9
  172.1 0.6 copy-start.11
  172.7 0.7 copy-start.13
  173.4 51.3 %all-to-all-start.2 = ((s16[16,408,128]{2,1,0:T(8,128)(2,1)}), s16[16,408,128]{2,1,0:T(8,128)(2,1)}, u32[]{:S(2)}, u32[]{:S(2)}) async-start(s16[16,408,128]{2,1,0:T(8,128)(2,1)} %pack.3), calls=%async_computation.2 | async-start | bytes 3342336 | tf_op jit(solution)/shard_map/all_to_all | solution.py:407
  177.8 22.2 %collective-permute-start.21 = (s16[408,128]{1,0:T(8,128)(2,1)S(1)}, s16[408,128]{1,0:T(8,128)(2,1)S(1)}, u32[]{:S(2)}, u32[]{:S(2)}) collective-permute-start(s16[408,128]{1,0:T(8,128)(2,1)S(1)} %copy-done.23), channel_id=1, source_target_pairs={{0,22},{1,23},{2,20},{3,21},{4,18},{5,19},{6,16},{7,17},{8,30},{9,... | collective-permute-start | bytes 313352 | tf_op jit(solution)/shard_map/ppermute | solution.py:386
  181.0 22.2 %collective-permute-start.22 = (s16[408,128]{1,0:T(8,128)(2,1)S(1)}, s16[408,128]{1,0:T(8,128)(2,1)S(1)}, u32[]{:S(2)}, u32[]{:S(2)}) collective-permute-start(s16[408,128]{1,0:T(8,128)(2,1)S(1)} %copy-done.22), channel_id=1, source_target_pairs={{0,21},{1,20},{2,23},{3,22},{4,17},{5,16},{6,19},{7,18},{8,29},{9,... | collective-permute-start | bytes 313352 | tf_op jit(solution)/shard_map/ppermute | solution.py:386
  182.4 25.6 %collective-permute-start.23 = (s16[408,128]{1,0:T(8,128)(2,1)S(1)}, s16[408,128]{1,0:T(8,128)(2,1)S(1)}, u32[]{:S(2)}, u32[]{:S(2)}) collective-permute-start(s16[408,128]{1,0:T(8,128)(2,1)S(1)} %copy-done.21), channel_id=1, source_target_pairs={{0,25},{1,24},{2,27},{3,26},{4,29},{5,28},{6,31},{7,30},{8,17},{9,... | collective-permute-start | bytes 313352 | tf_op jit(solution)/shard_map/ppermute | solution.py:386
  184.5 26.6 %collective-permute-start.25 = (s16[408,128]{1,0:T(8,128)(2,1)S(1)}, s16[408,128]{1,0:T(8,128)(2,1)S(1)}, u32[]{:S(2)}, u32[]{:S(2)}) collective-permute-start(s16[408,128]{1,0:T(8,128)(2,1)S(1)} %copy-done.20), channel_id=1, source_target_pairs={{0,24},{1,25},{2,26},{3,27},{4,28},{5,29},{6,30},{7,31},{8,16},{9,... | collective-permute-start | bytes 313352 | tf_op jit(solution)/shard_map/ppermute | solution.py:386
  186.4 32.1 %collective-permute-start.20 = (s16[408,128]{1,0:T(8,128)(2,1)}, s16[408,128]{1,0:T(8,128)(2,1)S(1)}, u32[]{:S(2)}, u32[]{:S(2)}) collective-permute-start(s16[408,128]{1,0:T(8,128)(2,1)} %get-tuple-element.126), channel_id=1, source_target_pairs={{0,23},{1,22},{2,21},{3,20},{4,19},{5,18},{6,17},{7,16},{8,31},{9,... | collective-permute-start | bytes 313352 | tf_op jit(solution)/shard_map/ppermute | solution.py:386
  208.0 19.3 %collective-permute-start.24 = (s16[408,128]{1,0:T(8,128)(2,1)}, s16[408,128]{1,0:T(8,128)(2,1)}, u32[]{:S(2)}, u32[]{:S(2)}) collective-permute-start(s16[408,128]{1,0:T(8,128)(2,1)} %get-tuple-element.142), channel_id=1, source_target_pairs={{0,20},{1,21},{2,22},{3,23},{4,16},{5,17},{6,18},{7,19},{8,28},{9,... | collective-permute-start | bytes 313352 | tf_op jit(solution)/shard_map/ppermute | solution.py:386
  211.2 16.1 %collective-permute-start.26 = (s16[408,128]{1,0:T(8,128)(2,1)}, s16[408,128]{1,0:T(8,128)(2,1)}, u32[]{:S(2)}, u32[]{:S(2)}) collective-permute-start(s16[408,128]{1,0:T(8,128)(2,1)} %get-tuple-element.147), channel_id=1, source_target_pairs={{0,19},{1,18},{2,17},{3,16},{4,23},{5,22},{6,21},{7,20},{8,27},{9,... | collective-permute-start | bytes 313352 | tf_op jit(solution)/shard_map/ppermute | solution.py:386
  211.9 0.9 copy-start.4
  212.8 0.9 copy-start.6
  213.7 0.9 copy-start.8
  214.6 0.9 copy-start.10
  215.5 0.9 copy-start.12
  216.4 0.9 copy-start.14
  218.5 18.4 %copy-start.15 = (f32[2048]{0:T(1024)S(1)}, f32[2048]{0:T(1024)}, u32[]{:S(2)}) copy-start(f32[2048]{0:T(1024)} %param.10) | copy-start | bytes 24580
  218.5 0.6 copy-start.1
  219.2 14.5 %collective-permute-start.27 = (s16[408,128]{1,0:T(8,128)(2,1)}, s16[408,128]{1,0:T(8,128)(2,1)}, u32[]{:S(2)}, u32[]{:S(2)}) collective-permute-start(s16[408,128]{1,0:T(8,128)(2,1)} %get-tuple-element.157), channel_id=1, source_target_pairs={{0,18},{1,19},{2,16},{3,17},{4,22},{5,23},{6,20},{7,21},{8,26},{9,... | collective-permute-start | bytes 313352 | tf_op jit(solution)/shard_map/ppermute | solution.py:386
  221.0 12.7 %collective-permute-start.28 = (s16[408,128]{1,0:T(8,128)(2,1)}, s16[408,128]{1,0:T(8,128)(2,1)}, u32[]{:S(2)}, u32[]{:S(2)}) collective-permute-start(s16[408,128]{1,0:T(8,128)(2,1)} %get-tuple-element.158), channel_id=1, source_target_pairs={{0,17},{1,16},{2,19},{3,18},{4,21},{5,20},{6,23},{7,22},{8,25},{9,... | collective-permute-start | bytes 313352 | tf_op jit(solution)/shard_map/ppermute | solution.py:386
  221.9 15.0 %collective-permute-start.29 = (s16[408,128]{1,0:T(8,128)(2,1)}, s16[408,128]{1,0:T(8,128)(2,1)}, u32[]{:S(2)}, u32[]{:S(2)}) collective-permute-start(s16[408,128]{1,0:T(8,128)(2,1)} %get-tuple-element.159), channel_id=1, source_target_pairs={{0,16},{1,17},{2,18},{3,19},{4,20},{5,21},{6,22},{7,23},{8,24},{9,... | collective-permute-start | bytes 313352 | tf_op jit(solution)/shard_map/ppermute | solution.py:386
  224.6 12.2 %copy-start = (f32[2048,400]{0,1:T(8,128)S(1)}, f32[2048,400]{0,1:T(8,128)}, u32[]{:S(2)}) copy-start(f32[2048,400]{0,1:T(8,128)} %param.9) | copy-start | bytes 9830404
  224.6 12.2 %copy-start.2 = (s16[408,128]{1,0:T(8,128)(2,1)S(1)}, s16[408,128]{1,0:T(8,128)(2,1)}, u32[]{:S(2)}) copy-start(s16[408,128]{1,0:T(8,128)(2,1)} %copy-done.1) | copy-start | bytes 313348

commit v9 on v7

--- a/solution.py
+++ b/solution.py
@@ -40,6 +40,37 @@
 
 def anywhere():
     return pl.BlockSpec(memory_space=pl.ANY)
+
+
+def select_kernel(asked_ref, blocks_ref, out_ref, sem):
+    count = out_ref.shape[0]
+
+    def copy(k):
+        return pltpu.make_async_copy(blocks_ref.at[asked_ref[k, 0, 0]], out_ref.at[k], sem)
+
+    def start(k, _):
+        copy(k).start()
+        return 0
+
+    def wait(k, _):
+        copy(k).wait()
+        return 0
+
+    lax.fori_loop(0, count, start, 0)
+    lax.fori_loop(0, count, wait, 0)
+
+
+def select(asked, blocks):
+    devices = asked.shape[0]
+    return pl.pallas_call(
+        select_kernel,
+        out_shape=jax.ShapeDtypeStruct((devices,) + blocks.shape[1:], blocks.dtype),
+        in_specs=[smem(), anywhere()],
+        out_specs=anywhere(),
+        scratch_shapes=[pltpu.SemaphoreType.DMA],
+        compiler_params=params(0),
+        name="select",
+    )(asked, blocks)
 
 
 def load_live(live_ref, fetched, rows, sem):
@@ -208,8 +239,8 @@
 def encode(x, out_ref):
     width = x.shape[0]
     top = jnp.max(jnp.abs(x), axis=0, keepdims=True)
-    power = jnp.ceil(jnp.log2(jnp.maximum(top, 1e-30)))
-    code = jnp.clip(jnp.round(x * jnp.exp2(15.0 - power)), -32767.0, 32767.0)
+    power = jnp.ceil(jnp.log2(jnp.maximum(top, 1e-30)) + 1e-3)
+    code = jnp.round(x * (jnp.exp2(-power) * 32767.0))
     out_ref[:width, :] = code.astype(jnp.int32).astype(jnp.int16)
     tail = jnp.broadcast_to(power, (TAIL, x.shape[1]))
     out_ref[width:, :] = tail.astype(jnp.int32).astype(jnp.int16)
@@ -217,7 +248,7 @@
 
 def decode(code, width):
     power = code[width:, :].astype(jnp.int32).astype(F32)[:1]
-    return code[:width, :].astype(jnp.int32).astype(F32) * jnp.exp2(power - 15.0)
+    return code[:width, :].astype(jnp.int32).astype(F32) * (jnp.exp2(power) * (1.0 / 32767.0))
 
 
 def pack_kernel(first, bounds, peers, rank_ref, live_ref, npos, *refs):
@@ -339,13 +370,12 @@
     rows_dev, width = table.shape
     blocks = rows_dev // BLK
     wanted = lax.all_to_all(
-        block_list.reshape(devices, 1), AXES, split_axis=0, concat_axis=0, tiled=True
+        block_list.reshape(devices, 1, 1), AXES, split_axis=0, concat_axis=0, tiled=True
     )
     asked = wanted.reshape(devices)
-    outgoing = table.reshape(blocks, BLK, width).astype(BF16)[asked]
-    fetched = lax.all_to_all(
-        outgoing.transpose(0, 2, 1), AXES, split_axis=0, concat_axis=0, tiled=True
-    )
+    own_blocks = table.reshape(blocks, BLK, width).transpose(0, 2, 1).astype(BF16)
+    outgoing = select(wanted, own_blocks)
+    fetched = lax.all_to_all(outgoing, AXES, split_axis=0, concat_axis=0, tiled=True)
     operator = relations[rel_ids].T
 
     half = devices // 2

time: 226 us -> 224 us (level)
  starting transfers between devices: 71.7 us -> 67.3 us
  Pallas kernels: 48.8 us -> 51.5 us
    ppermute x45, starting transfers between devices: 60.8 us -> 56.5 us  [swap(): return lax.ppermute(x, axis, [(i, i ^ shift) for i in range(count)])]
    gather x1 -> x0, local copies, waits for them, and re-layouts: 2.68 us -> none  [per_device(): outgoing = table.reshape(blocks, BLK, width).astype(BF16)[asked]]
    ppermute x45, waiting for transfers between devices: 17.4 us -> 19.9 us  [swap(): return lax.ppermute(x, axis, [(i, i ^ shift) for i in range(count)])]
    pallas_call x0 -> x1, Pallas kernels: none -> 2.5 us  [select(): pl.pallas_call(select_kernel, out_shape=jax.ShapeDtypeStruct((devices,) +...]
  transfers between devices with their start and end apart: 47 -> 47, of which waited for: 14 -> 15; matrix products, arithmetic and copies ran while one was open for 13% -> 13% of each run, Pallas kernels for 15% -> 16%
where the time goes in v9:
time: 224 us; the launch traced here: 223 us
  waiting for transfers between devices  72 us (32%)
  starting transfers between devices  67.3 us (30%)
  Pallas kernels  51.5 us (23%)
  local copies, waits for them, and re-layouts  27.5 us (12%)
  other arithmetic  3.85 us (2%)
    ppermute x45, starting transfers between devices, swap(): return lax.ppermute(x, axis, [(i, i ^ shift) for i in range(count)])  56.5 us
    all_to_all x1, waiting for transfers between devices, per_device(): lax.all_to_all(outgoing, AXES, split_axis=0, concat_axis=0, tiled=True)  47.1 us
    ppermute x45, waiting for transfers between devices, swap(): return lax.ppermute(x, axis, [(i, i ^ shift) for i in range(count)])  19.9 us
    gather x2, local copies, waits for them, and re-layouts, per_device(): operator = relations[rel_ids].T  16.7 us
    pallas_call x3, Pallas kernels, scatter(): pl.pallas_call(functools.partial(scatter_kernel, first * BLK), out_shape=...  15.1 us
    pallas_call x5, Pallas kernels, pack(): pl.pallas_call(functools.partial(pack_kernel, first, tuple(bounds), len(g...  9.47 us
    unnamed x15, local copies, waits for them, and re-layouts  9.46 us
    pallas_call x1, Pallas kernels, gather_edges(): pl.pallas_call(edge_kernel, grid=(edges // tile,), out_shape=(jax.ShapeDt...  8.04 us
  transfers between devices with their start and end apart: 47, of which 15 were waited for; matrix products, arithmetic and copies ran while one was open for 13% of the time, Pallas kernels for 16%

profile of v9, /device:TPU:0, one launch (start us, length us, event | category | flops | bytes accessed | tf_op | source)
XLA Modules:
  0.0 223.4 jit_solution(478515136024223817)
XLA Ops:
  0.6 1.3 copy.21
  2.0 7.3 %all-to-all-start = ((s32[32,1,1]{2,1,0:T(1,128)}), s32[32,1,1]{2,1,0:T(1,128)S(1)}, u32[]{:S(2)}, u32[]{:S(2)}) async-start(s32[32,1,1]{2,1,0:T(1,128)} %copy.21), calls=%async_computation | async-start | bytes 32768 | tf_op jit(solution)/shard_map/all_to_all | solution.py:372
  9.3 2.1 bitcast_bitcast_fusion.blocks_ref
  11.4 4.9 %all-to-all-done.asked_ref = s32[32,1,1]{2,1,0:T(1,128)S(1)} async-done(((s32[32,1,1]{2,1,0:T(1,128)}), s32[32,1,1]{2,1,0:T(1,128)S(1)}, u32[]{:S(2)}, u32[]{:S(2)}) %all-to-all-start) | async-done | bytes 160 | tf_op jit(solution)/shard_map/all_to_all | solution.py:372
  16.3 2.5 %select.19 = bf16[32,400,128]{2,1,0:T(8,128)(2,1)} custom-call(s32[32,1,1]{2,1,0:T(1,128)S(1)} %all-to-all-done.asked_ref, bf16[16,400,128]{2,1,0:T(8,128)(2,1)S(1)} %bitcast_bitcast_fusion.blocks_ref), custom_call_target="tpu_custom_call" | custom-call | tf_op jit(solution)/shard_map/select/pallas_call | solution.py:65
  18.9 3.6 %all-to-all-start.1 = ((bf16[32,400,128]{2,1,0:T(8,128)(2,1)}), bf16[32,400,128]{2,1,0:T(8,128)(2,1)}, u32[]{:S(2)}, u32[]{:S(2)}) async-start(bf16[32,400,128]{2,1,0:T(8,128)(2,1)} %select.19), calls=%async_computation.1 | async-start | bytes 6553600 | tf_op jit(solution)/shard_map/all_to_all | solution.py:378
  22.4 8.6 %copy.23 = f32[4096,400]{1,0:T(8,128)} copy(f32[4096,400]{0,1:T(8,128)} %param.11) | data formatting | bytes 13107200 | tf_op args[2]
  31.0 12.9 %gather_fusion = f32[2048,400]{1,0:T(8,128)} fusion(f32[4096,400]{1,0:T(8,128)} %copy.23, s32[2048]{0:T(1024)S(1)} %fusion.3), kind=kCustom, calls=%fused_computation | custom fusion | bytes 6561792 | tf_op jit(solution)/shard_map/gather | solution.py:379
  44.0 3.8 %copy.24 = f32[2048,400]{0,1:T(8,128)S(1)} copy(f32[2048,400]{1,0:T(8,128)} %gather_fusion) | data formatting | bytes 6553600 | tf_op jit(solution)/shard_map/gather | solution.py:379
  48.5 0.7 reduce
  49.6 47.1 %all-to-all-done.1.fetched = bf16[32,400,128]{2,1,0:T(8,128)(2,1)} async-done(((bf16[32,400,128]{2,1,0:T(8,128)(2,1)}), bf16[32,400,128]{2,1,0:T(8,128)(2,1)}, u32[]{:S(2)}, u32[]{:S(2)}) %all-to-all-start.1) | async-done | bytes 3276832 | tf_op jit(solution)/shard_map/all_to_all | solution.py:378
  96.7 2.6 %gather_negs.1 = (bf16[400,128]{1,0:T(8,128)(2,1)S(1)}, bf16[400,2048]{1,0:T(8,128)(2,1)S(1)}) custom-call(s32[16]{0:T(128)S(1)} %select_reduce_fusion.7.live_ref, bf16[32,400,128]{2,1,0:T(8,128)(2,1)} %all-to-all-done.1.fetched, s32[1,128]{1,0:T(1,128)S(1)} %fusion.10.pos_ref.npos), custom_call_target="tpu_custom_call" | custom-call | tf_op jit(solution)/shard_map/gather_negs/pallas_call | solution.py:115
  99.5 1.3 collective-permute-start.1
  100.7 0.6 collective-permute-start.2
  101.3 1.2 collective-permute-start.3
  103.0 2.1 collective-permute-start.5
  105.2 0.9 collective-permute-start.6
  106.1 8.0 %gather_edges.1 = (bf16[400,2048]{1,0:T(8,128)(2,1)S(1)}, bf16[400,2048]{1,0:T(8,128)(2,1)S(1)}, f32[1,2048]{1,0:T(1,128)S(1)}) custom-call(bf16[400,2048]{1,0:T(8,128)(2,1)S(1)} %get-tuple-element.128.rows, s32[1,2048]{1,0:T(1,128)S(1)} %bitcast.20, s32[1,2048]{1,0:T(1,128)S(1)} %bitcast.24, f32[400,2048]{1,0:T(8,128)S(1)} %bitcast.17), custom_call_target="tpu_custom_call" | custom-call | flops 104857600 | bytes 204800 | tf_op jit(solution)/shard_map/gather_edges/pallas_call | solution.py:144
  114.2 6.2 %score.1 = (bf16[2,400,2048]{2,1,0:T(8,128)(2,1)S(1)}, bf16[2,400,2048]{2,1,0:T(8,128)(2,1)S(1)}, bf16[400,128]{1,0:T(8,128)(2,1)S(1)}, bf16[400,128]{1,0:T(8,12...) custom-call(bf16[400,128]{1,0:T(8,128)(2,1)S(1)} %get-tuple-element., ...), custom_call_target="tpu_custom_call" | custom-call | flops 78643200 | bytes 153600 | tf_op jit(solution)/shard_map/score/pallas_call | solution.py:191
  120.5 1.4 collective-permute-start.7
  122.3 0.9 collective-permute-start.9
  123.8 1.5 collective-permute-start.11
  125.3 0.8 collective-permute-start.12
  126.1 1.4 collective-permute-done.8.refs_4_.refs_5_.refs_3_
  127.7 5.7 %scatter.3.refs_0_ = f32[400,768]{1,0:T(8,128)S(1)} custom-call(bf16[2,400,2048]{2,1,0:T(8,128)(2,1)S(1)} %get-tuple-element.135.gs_ref, bf16[2,400,2048]{2,1,0:T(8,128)(2,1)S(1)} %get-tuple-element.136.gd_ref, s32[1,2048]{1,0:T(1,128)S(1)} %bitcast.21, s32[1,2048]{1,0:T(1,128)S(1)} %bitcast.25), custom_call_target="tpu_custom_call" | custom-call | flops 39321600 | bytes 76800 | tf_op jit(solution)/shard_map/scatter/pallas_call | solution.py:228
  133.4 1.7 collective-permute-done.11.refs_7_.refs_8_.refs_6_
  135.1 1.0 pack.9
  136.0 3.1 %collective-permute-start.26 = (s16[408,128]{1,0:T(8,128)(2,1)S(1)}, s16[408,128]{1,0:T(8,128)(2,1)S(1)}, u32[]{:S(2)}, u32[]{:S(2)}) collective-permute-start(s16[408,128]{1,0:T(8,128)(2,1)S(1)} %get-tuple-element.176), channel_id=1, source_target_pairs={{0,31},{1,30},{2,29},{3,28},{4,27},{5,26},{6,25},{7,24},{8,23},{9,... | collective-permute-start | bytes 313352 | tf_op jit(solution)/shard_map/ppermute | solution.py:416
  139.2 2.2 collective-permute-start.15
  141.3 2.5 %collective-permute-start.31 = (s16[408,128]{1,0:T(8,128)(2,1)S(1)}, s16[408,128]{1,0:T(8,128)(2,1)S(1)}, u32[]{:S(2)}, u32[]{:S(2)}) collective-permute-start(s16[408,128]{1,0:T(8,128)(2,1)S(1)} %get-tuple-element.186), channel_id=1, source_target_pairs={{0,30},{1,31},{2,28},{3,29},{4,26},{5,27},{6,24},{7,25},{8,22},{9,... | collective-permute-start | bytes 313352 | tf_op jit(solution)/shard_map/ppermute | solution.py:416
  143.8 1.8 collective-permute-start.33
  145.6 5.7 %scatter.4.refs_1_ = f32[400,768]{1,0:T(8,128)S(1)} custom-call(bf16[2,400,2048]{2,1,0:T(8,128)(2,1)S(1)} %get-tuple-element.135.gs_ref, bf16[2,400,2048]{2,1,0:T(8,128)(2,1)S(1)} %get-tuple-element.136.gd_ref, s32[1,2048]{1,0:T(1,128)S(1)} %bitcast.22, s32[1,2048]{1,0:T(1,128)S(1)} %bitcast.26), custom_call_target="tpu_custom_call" | custom-call | flops 39321600 | bytes 76800 | tf_op jit(solution)/shard_map/scatter/pallas_call | solution.py:228
  151.3 2.6 %pack.5 = (s16[408,128]{1,0:T(8,128)(2,1)S(1)}, s16[408,128]{1,0:T(8,128)(2,1)S(1)}, s16[408,128]{1,0:T(8,128)(2,1)S(1)}, s16[408,128]{1,0:T(8,128)(2,1)S(1)}, s...) custom-call(s32[32]{0:T(128)S(1)} %select_reduce_fusion.5.rank_ref, ...), custom_call_target="tpu_custom_call" | custom-call | flops 3276800 | bytes 6400 | tf_op jit(solution)/shard_map/pack/pallas_call | solution.py:284
  153.9 2.0 collective-permute-start.14
  155.9 2.2 collective-permute-start.16
  158.1 2.6 %collective-permute-start.32 = (s16[408,128]{1,0:T(8,128)(2,1)S(1)}, s16[408,128]{1,0:T(8,128)(2,1)S(1)}, u32[]{:S(2)}, u32[]{:S(2)}) collective-permute-start(s16[408,128]{1,0:T(8,128)(2,1)S(1)} %get-tuple-element.187), channel_id=1, source_target_pairs={{0,26},{1,27},{2,24},{3,25},{4,30},{5,31},{6,28},{7,29},{8,18},{9,... | collective-permute-start | bytes 313352 | tf_op jit(solution)/shard_map/ppermute | solution.py:416
  160.7 1.7 collective-permute-start.34
  162.8 4.2 %collective-permute-done.27.refs_1_ = s16[408,128]{1,0:T(8,128)(2,1)S(1)} collective-permute-done((s16[408,128]{1,0:T(8,128)(2,1)S(1)}, s16[408,128]{1,0:T(8,128)(2,1)S(1)}, u32[]{:S(2)}, u32[]{:S(2)}) %collective-permute-start.27) | collective-permute-done | bytes 104480 | tf_op jit(solution)/shard_map/ppermute | solution.py:416
  167.0 3.8 %scatter.5.refs_2_ = f32[400,512]{1,0:T(8,128)S(1)} custom-call(bf16[2,400,2048]{2,1,0:T(8,128)(2,1)S(1)} %get-tuple-element.135.gs_ref, bf16[2,400,2048]{2,1,0:T(8,128)(2,1)S(1)} %get-tuple-element.136.gd_ref, s32[1,2048]{1,0:T(1,128)S(1)} %bitcast.23, s32[1,2048]{1,0:T(1,128)S(1)} %bitcast.27), custom_call_target="tpu_custom_call" | custom-call | flops 26214400 | bytes 51200 | tf_op jit(solution)/shard_map/scatter/pallas_call | solution.py:228
  170.8 2.1 pack.8
  173.0 4.1 %collective-permute-start.35 = (s16[408,128]{1,0:T(8,128)(2,1)S(1)}, s16[408,128]{1,0:T(8,128)(2,1)S(1)}, u32[]{:S(2)}, u32[]{:S(2)}) collective-permute-start(s16[408,128]{1,0:T(8,128)(2,1)S(1)} %get-tuple-element.198), channel_id=1, source_target_pairs={{0,12},{1,13},{2,14},{3,15},{4,8},{5,9},{6,10},{7,11},{8,4},{9,5},... | collective-permute-start | bytes 313352 | tf_op jit(solution)/shard_map/ppermute | solution.py:416
  177.2 2.0 collective-permute-start.36
  179.2 4.3 %collective-permute-start.22 = (s16[408,128]{1,0:T(8,128)(2,1)S(1)}, s16[408,128]{1,0:T(8,128)(2,1)S(1)}, u32[]{:S(2)}, u32[]{:S(2)}) collective-permute-start(s16[408,128]{1,0:T(8,128)(2,1)S(1)} %get-tuple-element.166), channel_id=1, source_target_pairs={{0,22},{1,23},{2,20},{3,21},{4,18},{5,19},{6,16},{7,17},{8,30},{9,... | collective-permute-start | bytes 313352 | tf_op jit(solution)/shard_map/ppermute | solution.py:416
  183.4 1.0 add.71.refs_8_
  184.4 1.6 pack.7
  186.0 2.9 %collective-permute-start.18 = (s16[408,128]{1,0:T(8,128)(2,1)S(1)}, s16[408,128]{1,0:T(8,128)(2,1)S(1)}, u32[]{:S(2)}, u32[]{:S(2)}) collective-permute-start(s16[408,128]{1,0:T(8,128)(2,1)S(1)} %get-tuple-element.158), channel_id=1, source_target_pairs={{0,20},{1,21},{2,22},{3,23},{4,16},{5,17},{6,18},{7,19},{8,28},{9,... | collective-permute-start | bytes 313352 | tf_op jit(solution)/shard_map/ppermute | solution.py:416
  188.9 1.4 collective-permute-start.39
  190.3 2.7 %collective-permute-done.22.refs_2_ = s16[408,128]{1,0:T(8,128)(2,1)S(1)} collective-permute-done((s16[408,128]{1,0:T(8,128)(2,1)S(1)}, s16[408,128]{1,0:T(8,128)(2,1)S(1)}, u32[]{:S(2)}, u32[]{:S(2)}) %collective-permute-start.22) | collective-permute-done | bytes 104480 | tf_op jit(solution)/shard_map/ppermute | solution.py:416
  193.0 1.0 add.72.refs_8_
  194.1 2.9 %collective-permute-done.18.refs_6_ = s16[408,128]{1,0:T(8,128)(2,1)S(1)} collective-permute-done((s16[408,128]{1,0:T(8,128)(2,1)S(1)}, s16[408,128]{1,0:T(8,128)(2,1)S(1)}, u32[]{:S(2)}, u32[]{:S(2)}) %collective-permute-start.18) | collective-permute-done | bytes 104480 | tf_op jit(solution)/shard_map/ppermute | solution.py:416
  197.0 1.5 collective-permute-start.19
  198.6 1.4 collective-permute-done.39.refs_4_
  200.0 1.5 collective-permute-start.40
  201.5 1.7 collective-permute-done.23.refs_7_
  203.8 1.5 collective-permute-start.37
  205.3 2.2 pack.6
  207.9 1.6 collective-permute-start.41
  209.6 2.5 %collective-permute-done.43.refs_2_ = s16[408,128]{1,0:T(8,128)(2,1)S(1)} collective-permute-done((s16[408,128]{1,0:T(8,128)(2,1)S(1)}, s16[408,128]{1,0:T(8,128)(2,1)S(1)}, u32[]{:S(2)}, u32[]{:S(2)}) %collective-permute-start.43) | collective-permute-done | bytes 104480 | tf_op jit(solution)/shard_map/ppermute | solution.py:416
  212.1 1.4 collective-permute-start.44
  213.5 2.9 %collective-permute-start.38 = (s16[408,128]{1,0:T(8,128)(2,1)S(1)}, s16[408,128]{1,0:T(8,128)(2,1)S(1)}, u32[]{:S(2)}, u32[]{:S(2)}) collective-permute-start(s16[408,128]{1,0:T(8,128)(2,1)S(1)} %get-tuple-element.209), channel_id=1, source_target_pairs={{0,1},{1,0},{2,3},{3,2},{4,5},{5,4},{6,7},{7,6},{8,9},{9,8},{10,11... | collective-permute-start | bytes 313352 | tf_op jit(solution)/shard_map/ppermute | solution.py:416
  216.4 1.0 add.73.refs_8_
  217.9 1.0 add.74.refs_4_
  219.0 0.8 copy-done
  219.8 3.4 %update.1 = (f32[400,2048]{1,0:T(8,128)}, f32[1,2048]{1,0:T(1,128)}) custom-call(s32[32]{0:T(128)S(1)} %get-tuple-element.121.asked_ref, s16[408,128]{1,0:T(8,128)(2,1)S(1)} %collective-permute-done.20.refs_0_, s16[408,128]{1,0:T(8,128)(2,1)S(1)} %collective-permute-done.25.refs_1_, s16[408,128]{1,0:T(8,128)(2,1)S(1)} %collective-permute-done.38.refs_2_, ...), custom_call_target="tpu_custom_call" | custom-call | flops 819200 | bytes 1600 | tf_op jit(solution)/shard_map/update/pallas_call | solution.py:352
  (83 shorter events, 4.9 us)
Async XLA Ops:
  2.0 14.4 %all-to-all-start = ((s32[32,1,1]{2,1,0:T(1,128)}), s32[32,1,1]{2,1,0:T(1,128)S(1)}, u32[]{:S(2)}, u32[]{:S(2)}) async-start(s32[32,1,1]{2,1,0:T(1,128)} %copy.21), calls=%async_computation | async-start | bytes 32768 | tf_op jit(solution)/shard_map/all_to_all | solution.py:372
  18.9 77.9 %all-to-all-start.1 = ((bf16[32,400,128]{2,1,0:T(8,128)(2,1)}), bf16[32,400,128]{2,1,0:T(8,128)(2,1)}, u32[]{:S(2)}, u32[]{:S(2)}) async-start(bf16[32,400,128]{2,1,0:T(8,128)(2,1)} %select.19), calls=%async_computation.1 | async-start | bytes 6553600 | tf_op jit(solution)/shard_map/all_to_all | solution.py:378
  22.4 8.6 %copy-start.4 = (s32[2048]{0:T(1024)S(1)}, s32[2048]{0:T(1024)}, u32[]{:S(2)}) copy-start(s32[2048]{0:T(1024)} %param.12) | copy-start | bytes 24580
  44.0 3.8 %copy-start.2 = (s32[2048]{0:T(1024)S(1)}, s32[2048]{0:T(1024)}, u32[]{:S(2)}) copy-start(s32[2048]{0:T(1024)} %param.14) | copy-start | bytes 24580
  44.0 4.0 %copy-start.6 = (s32[32]{0:T(128)S(1)}, s32[32]{0:T(128)}, u32[]{:S(2)}) copy-start(s32[32]{0:T(128)} %constant.80.clone) | copy-start | bytes 388
  44.0 4.4 %copy-start.5 = (s32[128]{0:T(128)S(1)}, s32[128]{0:T(128)}, u32[]{:S(2)}) copy-start(s32[128]{0:T(128)} %param.16) | copy-start | bytes 1540
  44.0 4.4 %copy-start.3 = (s32[2048]{0:T(1024)S(1)}, s32[2048]{0:T(1024)}, u32[]{:S(2)}) copy-start(s32[2048]{0:T(1024)} %param.15) | copy-start | bytes 24580
  99.4 3.6 %collective-permute-start = (bf16[400,128]{1,0:T(8,128)(2,1)S(1)}, bf16[400,128]{1,0:T(8,128)(2,1)S(1)}, u32[]{:S(2)}, u32[]{:S(2)}) collective-permute-start(bf16[400,128]{1,0:T(8,128)(2,1)S(1)} %get-tuple-element.127.refs_0_), channel_id=1, source_target_pairs={{0,1},{1,0},{2,3},{3,2},{4,5},{5,4},{6,7},{7,6},{8,9},{9,8},{10,11... | collective-permute-start | bytes 307208 | tf_op jit(solution)/shard_map/ppermute | solution.py:416
  99.5 5.7 %collective-permute-start.1 = (bf16[400,128]{1,0:T(8,128)(2,1)S(1)}, bf16[400,128]{1,0:T(8,128)(2,1)S(1)}, u32[]{:S(2)}, u32[]{:S(2)}) collective-permute-start(bf16[400,128]{1,0:T(8,128)(2,1)S(1)} %get-tuple-element.127.refs_0_), channel_id=1, source_target_pairs={{0,2},{1,3},{2,0},{3,1},{4,6},{5,7},{6,4},{7,5},{8,10},{9,11},{10,... | collective-permute-start | bytes 307208 | tf_op jit(solution)/shard_map/ppermute | solution.py:416
  100.7 13.5 %collective-permute-start.2 = (bf16[400,128]{1,0:T(8,128)(2,1)S(1)}, bf16[400,128]{1,0:T(8,128)(2,1)S(1)}, u32[]{:S(2)}, u32[]{:S(2)}) collective-permute-start(bf16[400,128]{1,0:T(8,128)(2,1)S(1)} %get-tuple-element.127.refs_0_), channel_id=1, source_target_pairs={{0,3},{1,2},{2,1},{3,0},{4,7},{5,6},{6,5},{7,4},{8,11},{9,10},{10,... | collective-permute-start | bytes 307208 | tf_op jit(solution)/shard_map/ppermute | solution.py:416
  101.3 12.9 %collective-permute-start.3 = (bf16[400,128]{1,0:T(8,128)(2,1)S(1)}, bf16[400,128]{1,0:T(8,128)(2,1)S(1)}, u32[]{:S(2)}, u32[]{:S(2)}) collective-permute-start(bf16[400,128]{1,0:T(8,128)(2,1)S(1)} %get-tuple-element.127.refs_0_), channel_id=1, source_target_pairs={{0,4},{1,5},{2,6},{3,7},{4,0},{5,1},{6,2},{7,3},{8,12},{9,13},{10,... | collective-permute-start | bytes 307208 | tf_op jit(solution)/shard_map/ppermute | solution.py:416
  102.5 11.7 %collective-permute-start.4 = (bf16[400,128]{1,0:T(8,128)(2,1)S(1)}, bf16[400,128]{1,0:T(8,128)(2,1)S(1)}, u32[]{:S(2)}, u32[]{:S(2)}) collective-permute-start(bf16[400,128]{1,0:T(8,128)(2,1)S(1)} %get-tuple-element.127.refs_0_), channel_id=1, source_target_pairs={{0,5},{1,4},{2,7},{3,6},{4,1},{5,0},{6,3},{7,2},{8,13},{9,12},{10,... | collective-permute-start | bytes 307208 | tf_op jit(solution)/shard_map/ppermute | solution.py:416
  103.0 11.2 %collective-permute-start.5 = (bf16[400,128]{1,0:T(8,128)(2,1)S(1)}, bf16[400,128]{1,0:T(8,128)(2,1)S(1)}, u32[]{:S(2)}, u32[]{:S(2)}) collective-permute-start(bf16[400,128]{1,0:T(8,128)(2,1)S(1)} %get-tuple-element.127.refs_0_), channel_id=1, source_target_pairs={{0,6},{1,7},{2,4},{3,5},{4,2},{5,3},{6,0},{7,1},{8,14},{9,15},{10,... | collective-permute-start | bytes 307208 | tf_op jit(solution)/shard_map/ppermute | solution.py:416
  105.2 9.0 %collective-permute-start.6 = (bf16[400,128]{1,0:T(8,128)(2,1)S(1)}, bf16[400,128]{1,0:T(8,128)(2,1)S(1)}, u32[]{:S(2)}, u32[]{:S(2)}) collective-permute-start(bf16[400,128]{1,0:T(8,128)(2,1)S(1)} %get-tuple-element.127.refs_0_), channel_id=1, source_target_pairs={{0,7},{1,6},{2,5},{3,4},{4,3},{5,2},{6,1},{7,0},{8,15},{9,14},{10,... | collective-permute-start | bytes 307208 | tf_op jit(solution)/shard_map/ppermute | solution.py:416
  120.5 4.9 %collective-permute-start.7 = (bf16[400,128]{1,0:T(8,128)(2,1)S(1)}, bf16[400,128]{1,0:T(8,128)(2,1)S(1)}, u32[]{:S(2)}, u32[]{:S(2)}) collective-permute-start(bf16[400,128]{1,0:T(8,128)(2,1)S(1)} %get-tuple-element.138), channel_id=1, source_target_pairs={{0,1},{1,0},{2,3},{3,2},{4,5},{5,4},{6,7},{7,6},{8,9},{9,8},{10,11... | collective-permute-start | bytes 307208 | tf_op jit(solution)/shard_map/ppermute | solution.py:416
  121.8 5.7 %collective-permute-start.8 = (bf16[400,128]{1,0:T(8,128)(2,1)S(1)}, bf16[400,128]{1,0:T(8,128)(2,1)S(1)}, u32[]{:S(2)}, u32[]{:S(2)}) collective-permute-start(bf16[400,128]{1,0:T(8,128)(2,1)S(1)} %get-tuple-element.139), channel_id=1, source_target_pairs={{0,2},{1,3},{2,0},{3,1},{4,6},{5,7},{6,4},{7,5},{8,10},{9,11},{10,... | collective-permute-start | bytes 307208 | tf_op jit(solution)/shard_map/ppermute | solution.py:416
  122.3 11.0 %collective-permute-start.9 = (bf16[400,128]{1,0:T(8,128)(2,1)S(1)}, bf16[400,128]{1,0:T(8,128)(2,1)S(1)}, u32[]{:S(2)}, u32[]{:S(2)}) collective-permute-start(bf16[400,128]{1,0:T(8,128)(2,1)S(1)} %get-tuple-element.140), channel_id=1, source_target_pairs={{0,3},{1,2},{2,1},{3,0},{4,7},{5,6},{6,5},{7,4},{8,11},{9,10},{10,... | collective-permute-start | bytes 307208 | tf_op jit(solution)/shard_map/ppermute | solution.py:416
  123.3 10.1 %collective-permute-start.10 = (bf16[400,128]{1,0:T(8,128)(2,1)S(1)}, bf16[400,128]{1,0:T(8,128)(2,1)S(1)}, u32[]{:S(2)}, u32[]{:S(2)}) collective-permute-start(bf16[400,128]{1,0:T(8,128)(2,1)S(1)} %get-tuple-element.141), channel_id=1, source_target_pairs={{0,4},{1,5},{2,6},{3,7},{4,0},{5,1},{6,2},{7,3},{8,12},{9,13},{10,... | collective-permute-start | bytes 307208 | tf_op jit(solution)/shard_map/ppermute | solution.py:416
  123.8 11.3 %collective-permute-start.11 = (bf16[400,128]{1,0:T(8,128)(2,1)S(1)}, bf16[400,128]{1,0:T(8,128)(2,1)S(1)}, u32[]{:S(2)}, u32[]{:S(2)}) collective-permute-start(bf16[400,128]{1,0:T(8,128)(2,1)S(1)} %get-tuple-element.142), channel_id=1, source_target_pairs={{0,5},{1,4},{2,7},{3,6},{4,1},{5,0},{6,3},{7,2},{8,13},{9,12},{10,... | collective-permute-start | bytes 307208 | tf_op jit(solution)/shard_map/ppermute | solution.py:416
  125.3 9.7 %collective-permute-start.12 = (bf16[400,128]{1,0:T(8,128)(2,1)S(1)}, bf16[400,128]{1,0:T(8,128)(2,1)S(1)}, u32[]{:S(2)}, u32[]{:S(2)}) collective-permute-start(bf16[400,128]{1,0:T(8,128)(2,1)S(1)} %get-tuple-element.143), channel_id=1, source_target_pairs={{0,6},{1,7},{2,4},{3,5},{4,2},{5,3},{6,0},{7,1},{8,14},{9,15},{10,... | collective-permute-start | bytes 307208 | tf_op jit(solution)/shard_map/ppermute | solution.py:416
  127.6 7.5 %collective-permute-start.13 = (bf16[400,128]{1,0:T(8,128)(2,1)S(1)}, bf16[400,128]{1,0:T(8,128)(2,1)S(1)}, u32[]{:S(2)}, u32[]{:S(2)}) collective-permute-start(bf16[400,128]{1,0:T(8,128)(2,1)S(1)} %get-tuple-element.144), channel_id=1, source_target_pairs={{0,7},{1,6},{2,5},{3,4},{4,3},{5,2},{6,1},{7,0},{8,15},{9,14},{10,... | collective-permute-start | bytes 307208 | tf_op jit(solution)/shard_map/ppermute | solution.py:416
  136.0 19.9 %collective-permute-start.26 = (s16[408,128]{1,0:T(8,128)(2,1)S(1)}, s16[408,128]{1,0:T(8,128)(2,1)S(1)}, u32[]{:S(2)}, u32[]{:S(2)}) collective-permute-start(s16[408,128]{1,0:T(8,128)(2,1)S(1)} %get-tuple-element.176), channel_id=1, source_target_pairs={{0,31},{1,30},{2,29},{3,28},{4,27},{5,26},{6,25},{7,24},{8,23},{9,... | collective-permute-start | bytes 313352 | tf_op jit(solution)/shard_map/ppermute | solution.py:416
  139.2 16.8 %collective-permute-start.15 = (s16[408,128]{1,0:T(8,128)(2,1)S(1)}, s16[408,128]{1,0:T(8,128)(2,1)S(1)}, u32[]{:S(2)}, u32[]{:S(2)}) collective-permute-start(s16[408,128]{1,0:T(8,128)(2,1)S(1)} %get-tuple-element.155), channel_id=1, source_target_pairs={{0,28},{1,29},{2,30},{3,31},{4,24},{5,25},{6,26},{7,27},{8,20},{9,... | collective-permute-start | bytes 313352 | tf_op jit(solution)/shard_map/ppermute | solution.py:416
  141.3 16.8 %collective-permute-start.31 = (s16[408,128]{1,0:T(8,128)(2,1)S(1)}, s16[408,128]{1,0:T(8,128)(2,1)S(1)}, u32[]{:S(2)}, u32[]{:S(2)}) collective-permute-start(s16[408,128]{1,0:T(8,128)(2,1)S(1)} %get-tuple-element.186), channel_id=1, source_target_pairs={{0,30},{1,31},{2,28},{3,29},{4,26},{5,27},{6,24},{7,25},{8,22},{9,... | collective-permute-start | bytes 313352 | tf_op jit(solution)/shard_map/ppermute | solution.py:416
  143.8 16.9 %collective-permute-start.33 = (s16[408,128]{1,0:T(8,128)(2,1)S(1)}, s16[408,128]{1,0:T(8,128)(2,1)S(1)}, u32[]{:S(2)}, u32[]{:S(2)}) collective-permute-start(s16[408,128]{1,0:T(8,128)(2,1)S(1)} %get-tuple-element.191), channel_id=1, source_target_pairs={{0,29},{1,28},{2,31},{3,30},{4,25},{5,24},{6,27},{7,26},{8,21},{9,... | collective-permute-start | bytes 313352 | tf_op jit(solution)/shard_map/ppermute | solution.py:416
  153.9 8.5 %collective-permute-start.14 = (s16[408,128]{1,0:T(8,128)(2,1)S(1)}, s16[408,128]{1,0:T(8,128)(2,1)S(1)}, u32[]{:S(2)}, u32[]{:S(2)}) collective-permute-start(s16[408,128]{1,0:T(8,128)(2,1)S(1)} %get-tuple-element.146), channel_id=1, source_target_pairs={{0,27},{1,26},{2,25},{3,24},{4,31},{5,30},{6,29},{7,28},{8,19},{9,... | collective-permute-start | bytes 313352 | tf_op jit(solution)/shard_map/ppermute | solution.py:416
  155.9 11.1 %collective-permute-start.27 = (s16[408,128]{1,0:T(8,128)(2,1)S(1)}, s16[408,128]{1,0:T(8,128)(2,1)S(1)}, u32[]{:S(2)}, u32[]{:S(2)}) collective-permute-start(s16[408,128]{1,0:T(8,128)(2,1)S(1)} %get-tuple-element.177), channel_id=1, source_target_pairs={{0,15},{1,14},{2,13},{3,12},{4,11},{5,10},{6,9},{7,8},{8,7},{9,6},... | collective-permute-start | bytes 313352 | tf_op jit(solution)/shard_map/ppermute | solution.py:416
  155.9 17.0 %collective-permute-start.16 = (s16[408,128]{1,0:T(8,128)(2,1)S(1)}, s16[408,128]{1,0:T(8,128)(2,1)S(1)}, u32[]{:S(2)}, u32[]{:S(2)}) collective-permute-start(s16[408,128]{1,0:T(8,128)(2,1)S(1)} %get-tuple-element.156), channel_id=1, source_target_pairs={{0,25},{1,24},{2,27},{3,26},{4,29},{5,28},{6,31},{7,30},{8,17},{9,... | collective-permute-start | bytes 313352 | tf_op jit(solution)/shard_map/ppermute | solution.py:416
  158.1 14.9 %collective-permute-start.32 = (s16[408,128]{1,0:T(8,128)(2,1)S(1)}, s16[408,128]{1,0:T(8,128)(2,1)S(1)}, u32[]{:S(2)}, u32[]{:S(2)}) collective-permute-start(s16[408,128]{1,0:T(8,128)(2,1)S(1)} %get-tuple-element.187), channel_id=1, source_target_pairs={{0,26},{1,27},{2,24},{3,25},{4,30},{5,31},{6,28},{7,29},{8,18},{9,... | collective-permute-start | bytes 313352 | tf_op jit(solution)/shard_map/ppermute | solution.py:416
  160.7 16.5 %collective-permute-start.34 = (s16[408,128]{1,0:T(8,128)(2,1)S(1)}, s16[408,128]{1,0:T(8,128)(2,1)S(1)}, u32[]{:S(2)}, u32[]{:S(2)}) collective-permute-start(s16[408,128]{1,0:T(8,128)(2,1)S(1)} %get-tuple-element.192), channel_id=1, source_target_pairs={{0,14},{1,15},{2,12},{3,13},{4,10},{5,11},{6,8},{7,9},{8,6},{9,7},... | collective-permute-start | bytes 313352 | tf_op jit(solution)/shard_map/ppermute | solution.py:416
  162.4 16.7 %collective-permute-start.21 = (s16[408,128]{1,0:T(8,128)(2,1)S(1)}, s16[408,128]{1,0:T(8,128)(2,1)S(1)}, u32[]{:S(2)}, u32[]{:S(2)}) collective-permute-start(s16[408,128]{1,0:T(8,128)(2,1)S(1)} %get-tuple-element.165), channel_id=1, source_target_pairs={{0,13},{1,12},{2,15},{3,14},{4,9},{5,8},{6,11},{7,10},{8,5},{9,4},... | collective-permute-start | bytes 313352 | tf_op jit(solution)/shard_map/ppermute | solution.py:416
  167.0 16.4 %collective-permute-start.28 = (s16[408,128]{1,0:T(8,128)(2,1)S(1)}, s16[408,128]{1,0:T(8,128)(2,1)S(1)}, u32[]{:S(2)}, u32[]{:S(2)}) collective-permute-start(s16[408,128]{1,0:T(8,128)(2,1)S(1)} %get-tuple-element.178), channel_id=1, source_target_pairs={{0,24},{1,25},{2,26},{3,27},{4,28},{5,29},{6,30},{7,31},{8,16},{9,... | collective-permute-start | bytes 313352 | tf_op jit(solution)/shard_map/ppermute | solution.py:416
  172.9 13.1 %collective-permute-start.17 = (s16[408,128]{1,0:T(8,128)(2,1)S(1)}, s16[408,128]{1,0:T(8,128)(2,1)S(1)}, u32[]{:S(2)}, u32[]{:S(2)}) collective-permute-start(s16[408,128]{1,0:T(8,128)(2,1)S(1)} %get-tuple-element.157), channel_id=1, source_target_pairs={{0,11},{1,10},{2,9},{3,8},{4,15},{5,14},{6,13},{7,12},{8,3},{9,2},... | collective-permute-start | bytes 313352 | tf_op jit(solution)/shard_map/ppermute | solution.py:416
  173.0 15.9 %collective-permute-start.35 = (s16[408,128]{1,0:T(8,128)(2,1)S(1)}, s16[408,128]{1,0:T(8,128)(2,1)S(1)}, u32[]{:S(2)}, u32[]{:S(2)}) collective-permute-start(s16[408,128]{1,0:T(8,128)(2,1)S(1)} %get-tuple-element.198), channel_id=1, source_target_pairs={{0,12},{1,13},{2,14},{3,15},{4,8},{5,9},{6,10},{7,11},{8,4},{9,5},... | collective-permute-start | bytes 313352 | tf_op jit(solution)/shard_map/ppermute | solution.py:416
  177.2 13.1 %collective-permute-start.36 = (s16[408,128]{1,0:T(8,128)(2,1)S(1)}, s16[408,128]{1,0:T(8,128)(2,1)S(1)}, u32[]{:S(2)}, u32[]{:S(2)}) collective-permute-start(s16[408,128]{1,0:T(8,128)(2,1)S(1)} %get-tuple-element.201), channel_id=1, source_target_pairs={{0,23},{1,22},{2,21},{3,20},{4,19},{5,18},{6,17},{7,16},{8,31},{9,... | collective-permute-start | bytes 313352 | tf_op jit(solution)/shard_map/ppermute | solution.py:416
  179.2 13.9 %collective-permute-start.22 = (s16[408,128]{1,0:T(8,128)(2,1)S(1)}, s16[408,128]{1,0:T(8,128)(2,1)S(1)}, u32[]{:S(2)}, u32[]{:S(2)}) collective-permute-start(s16[408,128]{1,0:T(8,128)(2,1)S(1)} %get-tuple-element.166), channel_id=1, source_target_pairs={{0,22},{1,23},{2,20},{3,21},{4,18},{5,19},{6,16},{7,17},{8,30},{9,... | collective-permute-start | bytes 313352 | tf_op jit(solution)/shard_map/ppermute | solution.py:416
  183.4 9.6 %collective-permute-start.29 = (s16[408,128]{1,0:T(8,128)(2,1)S(1)}, s16[408,128]{1,0:T(8,128)(2,1)S(1)}, u32[]{:S(2)}, u32[]{:S(2)}) collective-permute-start(s16[408,128]{1,0:T(8,128)(2,1)S(1)} %get-tuple-element.179), channel_id=1, source_target_pairs={{0,10},{1,11},{2,8},{3,9},{4,14},{5,15},{6,12},{7,13},{8,2},{9,3},... | collective-permute-start | bytes 313352 | tf_op jit(solution)/shard_map/ppermute | solution.py:416
  186.0 11.0 %collective-permute-start.18 = (s16[408,128]{1,0:T(8,128)(2,1)S(1)}, s16[408,128]{1,0:T(8,128)(2,1)S(1)}, u32[]{:S(2)}, u32[]{:S(2)}) collective-permute-start(s16[408,128]{1,0:T(8,128)(2,1)S(1)} %get-tuple-element.158), channel_id=1, source_target_pairs={{0,20},{1,21},{2,22},{3,23},{4,16},{5,17},{6,18},{7,19},{8,28},{9,... | collective-permute-start | bytes 313352 | tf_op jit(solution)/shard_map/ppermute | solution.py:416
  188.9 11.1 %collective-permute-start.39 = (s16[408,128]{1,0:T(8,128)(2,1)S(1)}, s16[408,128]{1,0:T(8,128)(2,1)S(1)}, u32[]{:S(2)}, u32[]{:S(2)}) collective-permute-start(s16[408,128]{1,0:T(8,128)(2,1)S(1)} %get-tuple-element.213), channel_id=1, source_target_pairs={{0,21},{1,20},{2,23},{3,22},{4,17},{5,16},{6,19},{7,18},{8,29},{9,... | collective-permute-start | bytes 313352 | tf_op jit(solution)/shard_map/ppermute | solution.py:416
  190.3 11.2 %collective-permute-start.42 = (s16[408,128]{1,0:T(8,128)(2,1)S(1)}, s16[408,128]{1,0:T(8,128)(2,1)S(1)}, u32[]{:S(2)}, u32[]{:S(2)}) collective-permute-start(s16[408,128]{1,0:T(8,128)(2,1)S(1)} %get-tuple-element.221), channel_id=1, source_target_pairs={{0,9},{1,8},{2,11},{3,10},{4,13},{5,12},{6,15},{7,14},{8,1},{9,0},... | collective-permute-start | bytes 313352 | tf_op jit(solution)/shard_map/ppermute | solution.py:416
  193.0 10.2 %collective-permute-start.23 = (s16[408,128]{1,0:T(8,128)(2,1)S(1)}, s16[408,128]{1,0:T(8,128)(2,1)S(1)}, u32[]{:S(2)}, u32[]{:S(2)}) collective-permute-start(s16[408,128]{1,0:T(8,128)(2,1)S(1)} %get-tuple-element.167), channel_id=1, source_target_pairs={{0,8},{1,9},{2,10},{3,11},{4,12},{5,13},{6,14},{7,15},{8,0},{9,1},... | collective-permute-start | bytes 313352 | tf_op jit(solution)/shard_map/ppermute | solution.py:416
  193.0 10.8 %collective-permute-start.30 = (s16[408,128]{1,0:T(8,128)(2,1)S(1)}, s16[408,128]{1,0:T(8,128)(2,1)S(1)}, u32[]{:S(2)}, u32[]{:S(2)}) collective-permute-start(s16[408,128]{1,0:T(8,128)(2,1)S(1)} %get-tuple-element.180), channel_id=1, source_target_pairs={{0,19},{1,18},{2,17},{3,16},{4,23},{5,22},{6,21},{7,20},{8,27},{9,... | collective-permute-start | bytes 313352 | tf_op jit(solution)/shard_map/ppermute | solution.py:416
  197.0 10.5 %collective-permute-start.19 = (s16[408,128]{1,0:T(8,128)(2,1)S(1)}, s16[408,128]{1,0:T(8,128)(2,1)S(1)}, u32[]{:S(2)}, u32[]{:S(2)}) collective-permute-start(s16[408,128]{1,0:T(8,128)(2,1)S(1)} %get-tuple-element.159), channel_id=1, source_target_pairs={{0,6},{1,7},{2,4},{3,5},{4,2},{5,3},{6,0},{7,1},{8,14},{9,15},{10,... | collective-permute-start | bytes 313352 | tf_op jit(solution)/shard_map/ppermute | solution.py:416
  200.0 7.9 %collective-permute-start.40 = (s16[408,128]{1,0:T(8,128)(2,1)S(1)}, s16[408,128]{1,0:T(8,128)(2,1)S(1)}, u32[]{:S(2)}, u32[]{:S(2)}) collective-permute-start(s16[408,128]{1,0:T(8,128)(2,1)S(1)} %get-tuple-element.214), channel_id=1, source_target_pairs={{0,7},{1,6},{2,5},{3,4},{4,3},{5,2},{6,1},{7,0},{8,15},{9,14},{10,... | collective-permute-start | bytes 313352 | tf_op jit(solution)/shard_map/ppermute | solution.py:416
  201.5 10.6 %collective-permute-start.43 = (s16[408,128]{1,0:T(8,128)(2,1)S(1)}, s16[408,128]{1,0:T(8,128)(2,1)S(1)}, u32[]{:S(2)}, u32[]{:S(2)}) collective-permute-start(s16[408,128]{1,0:T(8,128)(2,1)S(1)} %get-tuple-element.222), channel_id=1, source_target_pairs={{0,18},{1,19},{2,16},{3,17},{4,22},{5,23},{6,20},{7,21},{8,26},{9,... | collective-permute-start | bytes 313352 | tf_op jit(solution)/shard_map/ppermute | solution.py:416
  203.3 10.2 %collective-permute-start.24 = (s16[408,128]{1,0:T(8,128)(2,1)S(1)}, s16[408,128]{1,0:T(8,128)(2,1)S(1)}, u32[]{:S(2)}, u32[]{:S(2)}) collective-permute-start(s16[408,128]{1,0:T(8,128)(2,1)S(1)} %get-tuple-element.168), channel_id=1, source_target_pairs={{0,17},{1,16},{2,19},{3,18},{4,21},{5,20},{6,23},{7,22},{8,25},{9,... | collective-permute-start | bytes 313352 | tf_op jit(solution)/shard_map/ppermute | solution.py:416
  203.8 9.7 %collective-permute-start.37 = (s16[408,128]{1,0:T(8,128)(2,1)S(1)}, s16[408,128]{1,0:T(8,128)(2,1)S(1)}, u32[]{:S(2)}, u32[]{:S(2)}) collective-permute-start(s16[408,128]{1,0:T(8,128)(2,1)S(1)} %get-tuple-element.208), channel_id=1, source_target_pairs={{0,5},{1,4},{2,7},{3,6},{4,1},{5,0},{6,3},{7,2},{8,13},{9,12},{10,... | collective-permute-start | bytes 313352 | tf_op jit(solution)/shard_map/ppermute | solution.py:416
  207.5 11.4 %collective-permute-start.20 = (s16[408,128]{1,0:T(8,128)(2,1)S(1)}, s16[408,128]{1,0:T(8,128)(2,1)S(1)}, u32[]{:S(2)}, u32[]{:S(2)}) collective-permute-start(s16[408,128]{1,0:T(8,128)(2,1)S(1)} %get-tuple-element.160), channel_id=1, source_target_pairs={{0,3},{1,2},{2,1},{3,0},{4,7},{5,6},{6,5},{7,4},{8,11},{9,10},{10,... | collective-permute-start | bytes 313352 | tf_op jit(solution)/shard_map/ppermute | solution.py:416
  207.9 9.9 %collective-permute-start.41 = (s16[408,128]{1,0:T(8,128)(2,1)S(1)}, s16[408,128]{1,0:T(8,128)(2,1)S(1)}, u32[]{:S(2)}, u32[]{:S(2)}) collective-permute-start(s16[408,128]{1,0:T(8,128)(2,1)S(1)} %get-tuple-element.215), channel_id=1, source_target_pairs={{0,16},{1,17},{2,18},{3,19},{4,20},{5,21},{6,22},{7,23},{8,24},{9,... | collective-permute-start | bytes 313352 | tf_op jit(solution)/shard_map/ppermute | solution.py:416
  212.1 5.8 %collective-permute-start.44 = (s16[408,128]{1,0:T(8,128)(2,1)S(1)}, s16[408,128]{1,0:T(8,128)(2,1)S(1)}, u32[]{:S(2)}, u32[]{:S(2)}) collective-permute-start(s16[408,128]{1,0:T(8,128)(2,1)S(1)} %get-tuple-element.228), channel_id=1, source_target_pairs={{0,4},{1,5},{2,6},{3,7},{4,0},{5,1},{6,2},{7,3},{8,12},{9,13},{10,... | collective-permute-start | bytes 313352 | tf_op jit(solution)/shard_map/ppermute | solution.py:416
  213.5 5.5 %collective-permute-start.25 = (s16[408,128]{1,0:T(8,128)(2,1)S(1)}, s16[408,128]{1,0:T(8,128)(2,1)S(1)}, u32[]{:S(2)}, u32[]{:S(2)}) collective-permute-start(s16[408,128]{1,0:T(8,128)(2,1)S(1)} %get-tuple-element.169), channel_id=1, source_target_pairs={{0,2},{1,3},{2,0},{3,1},{4,6},{5,7},{6,4},{7,5},{8,10},{9,11},{10,... | collective-permute-start | bytes 313352 | tf_op jit(solution)/shard_map/ppermute | solution.py:416
  213.5 5.5 %collective-permute-start.38 = (s16[408,128]{1,0:T(8,128)(2,1)S(1)}, s16[408,128]{1,0:T(8,128)(2,1)S(1)}, u32[]{:S(2)}, u32[]{:S(2)}) collective-permute-start(s16[408,128]{1,0:T(8,128)(2,1)S(1)} %get-tuple-element.209), channel_id=1, source_target_pairs={{0,1},{1,0},{2,3},{3,2},{4,5},{5,4},{6,7},{7,6},{8,9},{9,8},{10,11... | collective-permute-start | bytes 313352 | tf_op jit(solution)/shard_map/ppermute | solution.py:416
  217.9 1.9 copy-start
  217.9 1.9 copy-start.1

commit v10 on v9

--- a/solution.py
+++ b/solution.py
@@ -11,7 +11,7 @@
 TAIL = 8
 CUTS = (1, 2, 2, 2, 1)
 STEPS = (3, 6, 8)
-WINDOW = 5
+WINDOW = 4
 TILE = 256
 AXES = ("src", "dst")
 F32 = jnp.float32
@@ -256,7 +256,10 @@
     outs, total, slot = refs[len(bounds) + peers : -2], refs[-2], refs[-1]
     width = slot.shape[0]
     total[:width], total[width:] = split(sum(g[...].astype(F32) for g in grads))
-    for k, out_ref in enumerate(outs):
+    seats = []
+    for out in outs:
+        seats += [out.at[0], out.at[1]] if len(out.shape) == 3 else [out]
+    for k, out_ref in enumerate(seats):
         alive = live_ref[first + k] > 0
         rank = rank_ref[first + k]
 
@@ -279,13 +282,15 @@
             out_ref[...] = jnp.zeros(out_ref.shape, jnp.int16)
 
 
-def pack(first, group, rank, live, chunks, bounds, grad_negs, npos):
+def pack(first, group, paired, rank, live, chunks, bounds, grad_negs, npos):
     width = chunks[0].shape[0]
+    block = (width + TAIL, BLK)
+    shape, outs = ((2,) + block, group // 2) if paired else (block, group)
     return pl.pallas_call(
         functools.partial(pack_kernel, first, tuple(bounds), len(grad_negs)),
-        out_shape=(jax.ShapeDtypeStruct((width + TAIL, BLK), jnp.int16),) * group,
+        out_shape=(jax.ShapeDtypeStruct(shape, jnp.int16),) * outs,
         in_specs=[smem(), smem()] + [whole()] * (1 + len(chunks) + len(grad_negs)),
-        out_specs=(whole(),) * group,
+        out_specs=(whole(),) * outs,
         scratch_shapes=[
             pltpu.VMEM((2 * width, npos.shape[1]), BF16),
             pltpu.VMEM((width, BLK), F32),
@@ -298,13 +303,15 @@
 
 def add_kernel(first, fresh, asked_ref, *refs):
     grad = refs[-1]
-    backs = refs[: -1 if fresh else -2]
+    backs = []
+    for ref in refs[: -1 if fresh else -2]:
+        backs.append(ref.at[0] if len(ref.shape) == 3 else ref)
     width = grad.shape[0]
     if fresh:
         grad[...] = jnp.zeros_like(grad)
     for k, back in enumerate(backs):
         lanes = pl.ds(pl.multiple_of(asked_ref[first + k] * BLK, BLK), BLK)
-        grad[:, lanes] += decode(back, width)
+        grad[:, lanes] += decode(back[...], width)
 
 
 def add(first, asked, backs, grad, width, rows):
@@ -378,13 +385,14 @@
     fetched = lax.all_to_all(outgoing, AXES, split_axis=0, concat_axis=0, tiled=True)
     operator = relations[rel_ids].T
 
-    half = devices // 2
-    far, near = list(range(devices - 1, half - 1, -1)), list(range(half - 1, -1, -1))
-    lead = devices // 8
-    order = far[:lead]
+    pairs = devices // 2
+    far, near = list(range(pairs - 1, pairs // 2 - 1, -1)), list(range(pairs // 2 - 1, -1, -1))
+    lead = pairs // sum(CUTS)
+    chips = far[:lead]
     for f, n in zip(far[lead:], near):
-        order += [f, n]
-    order += near[half - lead :]
+        chips += [f, n]
+    chips += near[len(far) - lead :]
+    order = [2 * chip + side for chip in chips for side in range(2)]
     partners = lax.axis_index(AXES) ^ jnp.array(order, jnp.int32)
     ids = jnp.arange(devices, dtype=jnp.int32)
     seat = partners[:, None] == ids[None, :]
@@ -421,27 +429,32 @@
     source, target, g_pos = gather_edges(rows, spos, dpos, operator)
     grads_src, grads_dst, part_negs = score(negs, source, target, operator, g_pos)
     own_grad = [part_negs[0]] + [swap(part_negs[shift], shift, "dst") for shift in range(1, peers)]
-    grad, chunks, flight, queue = None, [], [], []
+    grad, chunks, flight, arrived = None, [], [], []
     for g, (first, group) in enumerate(zip(firsts, sizes)):
+        last = g == len(sizes) - 1
         if g < len(bounds):
             edges_at = (spos, dpos)
             if g > 1:
-                edges_at, flight[-group] = lax.optimization_barrier((edges_at, flight[-group]))
+                edges_at, flight[-2] = lax.optimization_barrier((edges_at, flight[-2]))
             chunks.append(scatter(*bounds[g], grads_src, grads_dst, *edges_at))
-        packed = pack(first, group, rank, alive, chunks, bounds[: len(chunks)], own_grad, npos)
-        for k, (x, shift) in enumerate(zip(packed, order[first : first + group])):
-            i = first + k
+        packed = pack(
+            first, group, not last, rank, alive, chunks, bounds[: len(chunks)], own_grad, npos
+        )
+        shifts = order[first : first + group : 1 if last else 2]
+        for k, (x, shift) in enumerate(zip(packed, shifts)):
+            i = len(flight)
             if i >= WINDOW:
                 x, flight[i - WINDOW] = lax.optimization_barrier((x, flight[i - WINDOW]))
-            if k == WINDOW and g > 1:
+            if k == len(shifts) // 2 and g > 1:
                 x, grad = lax.optimization_barrier((x, grad))
             flight.append(swap(x, shift, AXES) if shift else x)
         if g:
-            before = firsts[g - 1]
-            grad = add(before, asked, flight[before:first], grad, width, rows_dev)
-    backs = flight[firsts[-1] :]
+            grad = add(firsts[g - 1], asked, arrived, grad, width, rows_dev)
+        arrived = []
+        for x in flight[-len(shifts) :]:
+            arrived += [x] if last else [x, swap(x[1], 1, AXES)]
     new_table, new_state = update(
-        firsts[-1], asked, backs, grad, table.T, state.reshape(1, rows_dev)
+        firsts[-1], asked, arrived, grad, table.T, state.reshape(1, rows_dev)
     )
     return (new_table.T, new_state.reshape(rows_dev))
 

time: 224 us -> 240 us (1.071)
  waiting for transfers between devices: 72 us -> 103 us
  starting transfers between devices: 67.3 us -> 53.2 us
    ppermute x45, waiting for transfers between devices: 19.9 us -> 50.9 us  [swap(): return lax.ppermute(x, axis, [(i, i ^ shift) for i in range(count)])]
    ppermute x45, starting transfers between devices: 56.5 us -> 42.3 us  [swap(): return lax.ppermute(x, axis, [(i, i ^ shift) for i in range(count)])]
  transfers between devices with their start and end apart: 47 -> 47, of which waited for: 15 -> 14; matrix products, arithmetic and copies ran while one was open for 13% -> 12% of each run, Pallas kernels for 16% -> 15%
where the time goes in v10:
time: 240 us
  waiting for transfers between devices  103 us (43%)
  starting transfers between devices  53.2 us (22%)
  Pallas kernels  51.5 us (21%)
  local copies, waits for them, and re-layouts  26.8 us (11%)
  other arithmetic  3.85 us (2%)
    ppermute x45, waiting for transfers between devices, swap(): return lax.ppermute(x, axis, [(i, i ^ shift) for i in range(count)])  50.9 us
    all_to_all x1, waiting for transfers between devices, per_device(): lax.all_to_all(outgoing, AXES, split_axis=0, concat_axis=0, tiled=True)  47.1 us
    ppermute x45, starting transfers between devices, swap(): return lax.ppermute(x, axis, [(i, i ^ shift) for i in range(count)])  42.3 us
    gather x2, local copies, waits for them, and re-layouts, per_device(): operator = relations[rel_ids].T  16.7 us
    pallas_call x3, Pallas kernels, scatter(): pl.pallas_call(functools.partial(scatter_kernel, first * BLK), out_shape=...  15.1 us
    pallas_call x5, Pallas kernels, pack(): pl.pallas_call(functools.partial(pack_kernel, first, tuple(bounds), len(g...  9.45 us
    unnamed x15, local copies, waits for them, and re-layouts  8.62 us
    pallas_call x1, Pallas kernels, gather_edges(): pl.pallas_call(edge_kernel, grid=(edges // tile,), out_shape=(jax.ShapeDt...  8.04 us
  transfers between devices with their start and end apart: 47, of which 14 were waited for; matrix products, arithmetic and copies ran while one was open for 12% of the time, Pallas kernels for 15%

profile of v10, /device:TPU:0, one launch (start us, length us, event | category | flops | bytes accessed | tf_op | source)
XLA Modules:
  0.0 239.7 jit_solution(14135293455798216152)
XLA Ops:
  0.6 1.3 copy.21
  2.0 7.3 %all-to-all-start = ((s32[32,1,1]{2,1,0:T(1,128)}), s32[32,1,1]{2,1,0:T(1,128)S(1)}, u32[]{:S(2)}, u32[]{:S(2)}) async-start(s32[32,1,1]{2,1,0:T(1,128)} %copy.21), calls=%async_computation | async-start | bytes 32768 | tf_op jit(solution)/shard_map/all_to_all | solution.py:379
  9.3 2.1 bitcast_bitcast_fusion.blocks_ref
  11.4 4.9 %all-to-all-done.asked_ref = s32[32,1,1]{2,1,0:T(1,128)S(1)} async-done(((s32[32,1,1]{2,1,0:T(1,128)}), s32[32,1,1]{2,1,0:T(1,128)S(1)}, u32[]{:S(2)}, u32[]{:S(2)}) %all-to-all-start) | async-done | bytes 160 | tf_op jit(solution)/shard_map/all_to_all | solution.py:379
  16.3 2.5 %select.19 = bf16[32,400,128]{2,1,0:T(8,128)(2,1)} custom-call(s32[32,1,1]{2,1,0:T(1,128)S(1)} %all-to-all-done.asked_ref, bf16[16,400,128]{2,1,0:T(8,128)(2,1)S(1)} %bitcast_bitcast_fusion.blocks_ref), custom_call_target="tpu_custom_call" | custom-call | tf_op jit(solution)/shard_map/select/pallas_call | solution.py:65
  18.9 3.6 %all-to-all-start.1 = ((bf16[32,400,128]{2,1,0:T(8,128)(2,1)}), bf16[32,400,128]{2,1,0:T(8,128)(2,1)}, u32[]{:S(2)}, u32[]{:S(2)}) async-start(bf16[32,400,128]{2,1,0:T(8,128)(2,1)} %select.19), calls=%async_computation.1 | async-start | bytes 6553600 | tf_op jit(solution)/shard_map/all_to_all | solution.py:385
  22.4 8.6 %copy.23 = f32[4096,400]{1,0:T(8,128)} copy(f32[4096,400]{0,1:T(8,128)} %param.11) | data formatting | bytes 13107200 | tf_op args[2]
  31.0 12.9 %gather_fusion = f32[2048,400]{1,0:T(8,128)} fusion(f32[4096,400]{1,0:T(8,128)} %copy.23, s32[2048]{0:T(1024)S(1)} %fusion.3), kind=kCustom, calls=%fused_computation | custom fusion | bytes 6561792 | tf_op jit(solution)/shard_map/gather | solution.py:386
  44.0 3.8 %copy.24 = f32[2048,400]{0,1:T(8,128)S(1)} copy(f32[2048,400]{1,0:T(8,128)} %gather_fusion) | data formatting | bytes 6553600 | tf_op jit(solution)/shard_map/gather | solution.py:386
  48.5 0.7 reduce
  49.6 47.1 %all-to-all-done.1.fetched = bf16[32,400,128]{2,1,0:T(8,128)(2,1)} async-done(((bf16[32,400,128]{2,1,0:T(8,128)(2,1)}), bf16[32,400,128]{2,1,0:T(8,128)(2,1)}, u32[]{:S(2)}, u32[]{:S(2)}) %all-to-all-start.1) | async-done | bytes 3276832 | tf_op jit(solution)/shard_map/all_to_all | solution.py:385
  96.7 2.6 %gather_negs.1 = (bf16[400,128]{1,0:T(8,128)(2,1)S(1)}, bf16[400,2048]{1,0:T(8,128)(2,1)S(1)}) custom-call(s32[16]{0:T(128)S(1)} %select_reduce_fusion.7.live_ref, bf16[32,400,128]{2,1,0:T(8,128)(2,1)} %all-to-all-done.1.fetched, s32[1,128]{1,0:T(1,128)S(1)} %fusion.10.pos_ref.npos), custom_call_target="tpu_custom_call" | custom-call | tf_op jit(solution)/shard_map/gather_negs/pallas_call | solution.py:115
  99.5 1.3 collective-permute-start.1
  100.7 0.6 collective-permute-start.2
  101.3 1.2 collective-permute-start.3
  102.5 0.5 collective-permute-start.4
  103.0 2.1 collective-permute-start.5
  105.2 0.9 collective-permute-start.6
  106.1 8.0 %gather_edges.1 = (bf16[400,2048]{1,0:T(8,128)(2,1)S(1)}, bf16[400,2048]{1,0:T(8,128)(2,1)S(1)}, f32[1,2048]{1,0:T(1,128)S(1)}) custom-call(bf16[400,2048]{1,0:T(8,128)(2,1)S(1)} %get-tuple-element.74.rows, s32[1,2048]{1,0:T(1,128)S(1)} %bitcast.48, s32[1,2048]{1,0:T(1,128)S(1)} %bitcast.52, f32[400,2048]{1,0:T(8,128)S(1)} %bitcast.45), custom_call_target="tpu_custom_call" | custom-call | flops 104857600 | bytes 204800 | tf_op jit(solution)/shard_map/gather_edges/pallas_call | solution.py:144
  114.2 6.1 %score.1 = (bf16[2,400,2048]{2,1,0:T(8,128)(2,1)S(1)}, bf16[2,400,2048]{2,1,0:T(8,128)(2,1)S(1)}, bf16[400,128]{1,0:T(8,128)(2,1)S(1)}, bf16[400,128]{1,0:T(8,12...) custom-call(bf16[400,128]{1,0:T(8,128)(2,1)S(1)} %get-tuple-element., ...), custom_call_target="tpu_custom_call" | custom-call | flops 78643200 | bytes 153600 | tf_op jit(solution)/shard_map/score/pallas_call | solution.py:191
  120.3 1.4 collective-permute-start.7
  121.7 0.5 collective-permute-start.8
  122.2 0.9 collective-permute-start.9
  123.1 0.5 collective-permute-start.10
  123.6 1.5 collective-permute-start.11
  125.2 0.8 collective-permute-start.12
  126.0 1.4 collective-permute-done.8.refs_4_.refs_3_.refs_5_
  127.5 5.7 %scatter.3.refs_0_ = f32[400,768]{1,0:T(8,128)S(1)} custom-call(bf16[2,400,2048]{2,1,0:T(8,128)(2,1)S(1)} %get-tuple-element.81.gs_ref, bf16[2,400,2048]{2,1,0:T(8,128)(2,1)S(1)} %get-tuple-element.82.gd_ref, s32[1,2048]{1,0:T(1,128)S(1)} %bitcast.49, s32[1,2048]{1,0:T(1,128)S(1)} %bitcast.53), custom_call_target="tpu_custom_call" | custom-call | flops 39321600 | bytes 76800 | tf_op jit(solution)/shard_map/scatter/pallas_call | solution.py:228
  133.2 1.7 collective-permute-done.11.refs_7_.refs_6_.refs_8_
  134.9 1.2 pack.6
  136.2 2.2 collective-permute-start.14
  138.3 5.7 %scatter.4.refs_1_ = f32[400,768]{1,0:T(8,128)S(1)} custom-call(bf16[2,400,2048]{2,1,0:T(8,128)(2,1)S(1)} %get-tuple-element.81.gs_ref, bf16[2,400,2048]{2,1,0:T(8,128)(2,1)S(1)} %get-tuple-element.82.gd_ref, s32[1,2048]{1,0:T(1,128)S(1)} %bitcast.50, s32[1,2048]{1,0:T(1,128)S(1)} %bitcast.54), custom_call_target="tpu_custom_call" | custom-call | flops 39321600 | bytes 76800 | tf_op jit(solution)/shard_map/scatter/pallas_call | solution.py:228
  144.0 1.8 pack.5
  145.8 2.7 %collective-permute-start.16 = (s16[2,408,128]{2,1,0:T(8,128)(2,1)S(1)}, s16[2,408,128]{2,1,0:T(8,128)(2,1)S(1)}, u32[]{:S(2)}, u32[]{:S(2)}) collective-permute-start(s16[2,408,128]{2,1,0:T(8,128)(2,1)S(1)} %get-tuple-element.99), channel_id=1, source_target_pairs={{0,26},{1,27},{2,24},{3,25},{4,30},{5,31},{6,28},{7,29},{8,18},{9,... | collective-permute-start | bytes 626696 | tf_op jit(solution)/shard_map/ppermute | solution.py:424
  148.5 3.4 %collective-permute-start.25 = (s16[2,408,128]{2,1,0:T(8,128)(2,1)S(1)}, s16[2,408,128]{2,1,0:T(8,128)(2,1)S(1)}, u32[]{:S(2)}, u32[]{:S(2)}) collective-permute-start(s16[2,408,128]{2,1,0:T(8,128)(2,1)S(1)} %get-tuple-element.113), channel_id=1, source_target_pairs={{0,28},{1,29},{2,30},{3,31},{4,24},{5,25},{6,26},{7,27},{8,20},{9,... | collective-permute-start | bytes 626696 | tf_op jit(solution)/shard_map/ppermute | solution.py:424
  151.9 1.7 collective-permute-start.15
  153.6 13.7 %collective-permute-done.25.refs_2_ = s16[2,408,128]{2,1,0:T(8,128)(2,1)S(1)} collective-permute-done((s16[2,408,128]{2,1,0:T(8,128)(2,1)S(1)}, s16[2,408,128]{2,1,0:T(8,128)(2,1)S(1)}, u32[]{:S(2)}, u32[]{:S(2)}) %collective-permute-start.25) | collective-permute-done | bytes 208928 | tf_op jit(solution)/shard_map/ppermute | solution.py:424
  167.4 0.5 collective-permute-start.28
  168.1 6.8 %collective-permute-start.31 = (s16[2,408,128]{2,1,0:T(8,128)(2,1)S(1)}, s16[2,408,128]{2,1,0:T(8,128)(2,1)S(1)}, u32[]{:S(2)}, u32[]{:S(2)}) collective-permute-start(s16[2,408,128]{2,1,0:T(8,128)(2,1)S(1)} %get-tuple-element.117), channel_id=1, source_target_pairs={{0,12},{1,13},{2,14},{3,15},{4,8},{5,9},{6,10},{7,11},{8,4},{9,5},... | collective-permute-start | bytes 626696 | tf_op jit(solution)/shard_map/ppermute | solution.py:424
  174.9 1.0 add.71.refs_8_
  176.0 3.8 %scatter.5.refs_2_ = f32[400,512]{1,0:T(8,128)S(1)} custom-call(bf16[2,400,2048]{2,1,0:T(8,128)(2,1)S(1)} %get-tuple-element.81.gs_ref, bf16[2,400,2048]{2,1,0:T(8,128)(2,1)S(1)} %get-tuple-element.82.gd_ref, s32[1,2048]{1,0:T(1,128)S(1)} %bitcast.51, s32[1,2048]{1,0:T(1,128)S(1)} %bitcast.55), custom_call_target="tpu_custom_call" | custom-call | flops 26214400 | bytes 51200 | tf_op jit(solution)/shard_map/scatter/pallas_call | solution.py:228
  179.7 2.7 %pack.9 = (s16[2,408,128]{2,1,0:T(8,128)(2,1)S(1)}, s16[2,408,128]{2,1,0:T(8,128)(2,1)S(1)}, s16[2,408,128]{2,1,0:T(8,128)(2,1)S(1)}, s16[2,408,128]{2,1,0:T(8,128)(2,1)S(1)}) custom-call(s32[32]{0:T(128)S(1)} %select_reduce_fusion.5.rank_ref, s32[32]{0:T(128)S(1)} %select_reduce_fusion.6.live_ref, s32[1,128]{1,0:T(1,128)S(1)} %fusion.10.pos_ref.npos, ...), custom_call_target="tpu_custom_call" | custom-call | flops 3276800 | bytes 6400 | tf_op jit(solution)/shard_map/pack/pallas_call | solution.py:289
  182.8 1.5 collective-permute-start.21
  184.3 4.2 %collective-permute-start.27 = (s16[2,408,128]{2,1,0:T(8,128)(2,1)S(1)}, s16[2,408,128]{2,1,0:T(8,128)(2,1)S(1)}, u32[]{:S(2)}, u32[]{:S(2)}) collective-permute-start(s16[2,408,128]{2,1,0:T(8,128)(2,1)S(1)} %get-tuple-element.114), channel_id=1, source_target_pairs={{0,20},{1,21},{2,22},{3,23},{4,16},{5,17},{6,18},{7,19},{8,28},{9,... | collective-permute-start | bytes 626696 | tf_op jit(solution)/shard_map/ppermute | solution.py:424
  188.5 0.6 collective-permute-start.32
  189.0 1.7 pack.7
  190.7 2.1 pack.8
  192.8 0.7 collective-permute-start.37
  193.5 1.0 add.72.refs_8_
  194.6 6.2 %collective-permute-done.17.refs_0_ = s16[2,408,128]{2,1,0:T(8,128)(2,1)S(1)} collective-permute-done((s16[2,408,128]{2,1,0:T(8,128)(2,1)S(1)}, s16[2,408,128]{2,1,0:T(8,128)(2,1)S(1)}, u32[]{:S(2)}, u32[]{:S(2)}) %collective-permute-start.17) | collective-permute-done | bytes 208928 | tf_op jit(solution)/shard_map/ppermute | solution.py:424
  200.8 4.5 %collective-permute-done.27.refs_4_ = s16[2,408,128]{2,1,0:T(8,128)(2,1)S(1)} collective-permute-done((s16[2,408,128]{2,1,0:T(8,128)(2,1)S(1)}, s16[2,408,128]{2,1,0:T(8,128)(2,1)S(1)}, u32[]{:S(2)}, u32[]{:S(2)}) %collective-permute-start.27) | collective-permute-done | bytes 208928 | tf_op jit(solution)/shard_map/ppermute | solution.py:424
  205.4 0.6 collective-permute-start.35
  206.0 12.8 %collective-permute-done.18.refs_0_ = s16[2,408,128]{2,1,0:T(8,128)(2,1)S(1)} collective-permute-done((s16[2,408,128]{2,1,0:T(8,128)(2,1)S(1)}, s16[2,408,128]{2,1,0:T(8,128)(2,1)S(1)}, u32[]{:S(2)}, u32[]{:S(2)}) %collective-permute-start.18) | collective-permute-done | bytes 208928 | tf_op jit(solution)/shard_map/ppermute | solution.py:424
  218.8 0.6 collective-permute-start.38
  219.4 2.5 %collective-permute-done.33.refs_4_ = s16[2,408,128]{2,1,0:T(8,128)(2,1)S(1)} collective-permute-done((s16[2,408,128]{2,1,0:T(8,128)(2,1)S(1)}, s16[2,408,128]{2,1,0:T(8,128)(2,1)S(1)}, u32[]{:S(2)}, u32[]{:S(2)}) %collective-permute-start.33) | collective-permute-done | bytes 208928 | tf_op jit(solution)/shard_map/ppermute | solution.py:424
  221.9 1.1 collective-permute-start.39
  223.2 5.5 %collective-permute-done.39.refs_6_ = s16[2,408,128]{2,1,0:T(8,128)(2,1)S(1)} collective-permute-done((s16[2,408,128]{2,1,0:T(8,128)(2,1)S(1)}, s16[2,408,128]{2,1,0:T(8,128)(2,1)S(1)}, u32[]{:S(2)}, u32[]{:S(2)}) %collective-permute-start.39) | collective-permute-done | bytes 208928 | tf_op jit(solution)/shard_map/ppermute | solution.py:424
  228.7 0.8 collective-permute-start.19
  230.0 1.1 collective-permute-start.23
  231.4 1.0 add.73.refs_8_
  232.5 1.0 add.74.refs_4_
  233.5 0.9 collective-permute-done.19.refs_0_
  234.5 1.5 collective-permute-done.23.refs_1_
  235.9 3.6 %update.1 = (f32[400,2048]{1,0:T(8,128)}, f32[1,2048]{1,0:T(1,128)}) custom-call(s32[32]{0:T(128)S(1)} %get-tuple-element.67.asked_ref, s16[408,128]{1,0:T(8,128)(2,1)S(1)} %collective-permute-done.19.refs_0_, s16[408,128]{1,0:T(8,128)(2,1)S(1)} %collective-permute-done.23.refs_1_, s16[408,128]{1,0:T(8,128)(2,1)S(1)} %get-tuple-element.124.refs_2_, ...), custom_call_target="tpu_custom_call" | custom-call | flops 819200 | bytes 1600 | tf_op jit(solution)/shard_map/update/pallas_call | solution.py:359
  (97 shorter events, 3.1 us)
Async XLA Ops:
  2.0 14.4 %all-to-all-start = ((s32[32,1,1]{2,1,0:T(1,128)}), s32[32,1,1]{2,1,0:T(1,128)S(1)}, u32[]{:S(2)}, u32[]{:S(2)}) async-start(s32[32,1,1]{2,1,0:T(1,128)} %copy.21), calls=%async_computation | async-start | bytes 32768 | tf_op jit(solution)/shard_map/all_to_all | solution.py:379
  18.9 77.9 %all-to-all-start.1 = ((bf16[32,400,128]{2,1,0:T(8,128)(2,1)}), bf16[32,400,128]{2,1,0:T(8,128)(2,1)}, u32[]{:S(2)}, u32[]{:S(2)}) async-start(bf16[32,400,128]{2,1,0:T(8,128)(2,1)} %select.19), calls=%async_computation.1 | async-start | bytes 6553600 | tf_op jit(solution)/shard_map/all_to_all | solution.py:385
  22.4 8.6 %copy-start.4 = (s32[2048]{0:T(1024)S(1)}, s32[2048]{0:T(1024)}, u32[]{:S(2)}) copy-start(s32[2048]{0:T(1024)} %param.12) | copy-start | bytes 24580
  44.0 3.8 %copy-start.2 = (s32[2048]{0:T(1024)S(1)}, s32[2048]{0:T(1024)}, u32[]{:S(2)}) copy-start(s32[2048]{0:T(1024)} %param.14) | copy-start | bytes 24580
  44.0 4.0 %copy-start.6 = (s32[32]{0:T(128)S(1)}, s32[32]{0:T(128)}, u32[]{:S(2)}) copy-start(s32[32]{0:T(128)} %constant.80.clone) | copy-start | bytes 388
  44.0 4.4 %copy-start.5 = (s32[128]{0:T(128)S(1)}, s32[128]{0:T(128)}, u32[]{:S(2)}) copy-start(s32[128]{0:T(128)} %param.16) | copy-start | bytes 1540
  44.0 4.4 %copy-start.3 = (s32[2048]{0:T(1024)S(1)}, s32[2048]{0:T(1024)}, u32[]{:S(2)}) copy-start(s32[2048]{0:T(1024)} %param.15) | copy-start | bytes 24580
  99.4 3.6 %collective-permute-start = (bf16[400,128]{1,0:T(8,128)(2,1)S(1)}, bf16[400,128]{1,0:T(8,128)(2,1)S(1)}, u32[]{:S(2)}, u32[]{:S(2)}) collective-permute-start(bf16[400,128]{1,0:T(8,128)(2,1)S(1)} %get-tuple-element.73.refs_0_), channel_id=1, source_target_pairs={{0,1},{1,0},{2,3},{3,2},{4,5},{5,4},{6,7},{7,6},{8,9},{9,8},{10,11... | collective-permute-start | bytes 307208 | tf_op jit(solution)/shard_map/ppermute | solution.py:424
  99.5 5.7 %collective-permute-start.1 = (bf16[400,128]{1,0:T(8,128)(2,1)S(1)}, bf16[400,128]{1,0:T(8,128)(2,1)S(1)}, u32[]{:S(2)}, u32[]{:S(2)}) collective-permute-start(bf16[400,128]{1,0:T(8,128)(2,1)S(1)} %get-tuple-element.73.refs_0_), channel_id=1, source_target_pairs={{0,2},{1,3},{2,0},{3,1},{4,6},{5,7},{6,4},{7,5},{8,10},{9,11},{10,... | collective-permute-start | bytes 307208 | tf_op jit(solution)/shard_map/ppermute | solution.py:424
  100.7 13.5 %collective-permute-start.2 = (bf16[400,128]{1,0:T(8,128)(2,1)S(1)}, bf16[400,128]{1,0:T(8,128)(2,1)S(1)}, u32[]{:S(2)}, u32[]{:S(2)}) collective-permute-start(bf16[400,128]{1,0:T(8,128)(2,1)S(1)} %get-tuple-element.73.refs_0_), channel_id=1, source_target_pairs={{0,3},{1,2},{2,1},{3,0},{4,7},{5,6},{6,5},{7,4},{8,11},{9,10},{10,... | collective-permute-start | bytes 307208 | tf_op jit(solution)/shard_map/ppermute | solution.py:424
  101.3 12.9 %collective-permute-start.3 = (bf16[400,128]{1,0:T(8,128)(2,1)S(1)}, bf16[400,128]{1,0:T(8,128)(2,1)S(1)}, u32[]{:S(2)}, u32[]{:S(2)}) collective-permute-start(bf16[400,128]{1,0:T(8,128)(2,1)S(1)} %get-tuple-element.73.refs_0_), channel_id=1, source_target_pairs={{0,4},{1,5},{2,6},{3,7},{4,0},{5,1},{6,2},{7,3},{8,12},{9,13},{10,... | collective-permute-start | bytes 307208 | tf_op jit(solution)/shard_map/ppermute | solution.py:424
  102.5 11.7 %collective-permute-start.4 = (bf16[400,128]{1,0:T(8,128)(2,1)S(1)}, bf16[400,128]{1,0:T(8,128)(2,1)S(1)}, u32[]{:S(2)}, u32[]{:S(2)}) collective-permute-start(bf16[400,128]{1,0:T(8,128)(2,1)S(1)} %get-tuple-element.73.refs_0_), channel_id=1, source_target_pairs={{0,5},{1,4},{2,7},{3,6},{4,1},{5,0},{6,3},{7,2},{8,13},{9,12},{10,... | collective-permute-start | bytes 307208 | tf_op jit(solution)/shard_map/ppermute | solution.py:424
  103.0 11.2 %collective-permute-start.5 = (bf16[400,128]{1,0:T(8,128)(2,1)S(1)}, bf16[400,128]{1,0:T(8,128)(2,1)S(1)}, u32[]{:S(2)}, u32[]{:S(2)}) collective-permute-start(bf16[400,128]{1,0:T(8,128)(2,1)S(1)} %get-tuple-element.73.refs_0_), channel_id=1, source_target_pairs={{0,6},{1,7},{2,4},{3,5},{4,2},{5,3},{6,0},{7,1},{8,14},{9,15},{10,... | collective-permute-start | bytes 307208 | tf_op jit(solution)/shard_map/ppermute | solution.py:424
  105.2 9.0 %collective-permute-start.6 = (bf16[400,128]{1,0:T(8,128)(2,1)S(1)}, bf16[400,128]{1,0:T(8,128)(2,1)S(1)}, u32[]{:S(2)}, u32[]{:S(2)}) collective-permute-start(bf16[400,128]{1,0:T(8,128)(2,1)S(1)} %get-tuple-element.73.refs_0_), channel_id=1, source_target_pairs={{0,7},{1,6},{2,5},{3,4},{4,3},{5,2},{6,1},{7,0},{8,15},{9,14},{10,... | collective-permute-start | bytes 307208 | tf_op jit(solution)/shard_map/ppermute | solution.py:424
  120.3 4.9 %collective-permute-start.7 = (bf16[400,128]{1,0:T(8,128)(2,1)S(1)}, bf16[400,128]{1,0:T(8,128)(2,1)S(1)}, u32[]{:S(2)}, u32[]{:S(2)}) collective-permute-start(bf16[400,128]{1,0:T(8,128)(2,1)S(1)} %get-tuple-element.84), channel_id=1, source_target_pairs={{0,1},{1,0},{2,3},{3,2},{4,5},{5,4},{6,7},{7,6},{8,9},{9,8},{10,11... | collective-permute-start | bytes 307208 | tf_op jit(solution)/shard_map/ppermute | solution.py:424
  121.7 5.7 %collective-permute-start.8 = (bf16[400,128]{1,0:T(8,128)(2,1)S(1)}, bf16[400,128]{1,0:T(8,128)(2,1)S(1)}, u32[]{:S(2)}, u32[]{:S(2)}) collective-permute-start(bf16[400,128]{1,0:T(8,128)(2,1)S(1)} %get-tuple-element.85), channel_id=1, source_target_pairs={{0,2},{1,3},{2,0},{3,1},{4,6},{5,7},{6,4},{7,5},{8,10},{9,11},{10,... | collective-permute-start | bytes 307208 | tf_op jit(solution)/shard_map/ppermute | solution.py:424
  122.2 11.0 %collective-permute-start.9 = (bf16[400,128]{1,0:T(8,128)(2,1)S(1)}, bf16[400,128]{1,0:T(8,128)(2,1)S(1)}, u32[]{:S(2)}, u32[]{:S(2)}) collective-permute-start(bf16[400,128]{1,0:T(8,128)(2,1)S(1)} %get-tuple-element.86), channel_id=1, source_target_pairs={{0,3},{1,2},{2,1},{3,0},{4,7},{5,6},{6,5},{7,4},{8,11},{9,10},{10,... | collective-permute-start | bytes 307208 | tf_op jit(solution)/shard_map/ppermute | solution.py:424
  123.1 10.1 %collective-permute-start.10 = (bf16[400,128]{1,0:T(8,128)(2,1)S(1)}, bf16[400,128]{1,0:T(8,128)(2,1)S(1)}, u32[]{:S(2)}, u32[]{:S(2)}) collective-permute-start(bf16[400,128]{1,0:T(8,128)(2,1)S(1)} %get-tuple-element.87), channel_id=1, source_target_pairs={{0,4},{1,5},{2,6},{3,7},{4,0},{5,1},{6,2},{7,3},{8,12},{9,13},{10,... | collective-permute-start | bytes 307208 | tf_op jit(solution)/shard_map/ppermute | solution.py:424
  123.6 11.3 %collective-permute-start.11 = (bf16[400,128]{1,0:T(8,128)(2,1)S(1)}, bf16[400,128]{1,0:T(8,128)(2,1)S(1)}, u32[]{:S(2)}, u32[]{:S(2)}) collective-permute-start(bf16[400,128]{1,0:T(8,128)(2,1)S(1)} %get-tuple-element.88), channel_id=1, source_target_pairs={{0,5},{1,4},{2,7},{3,6},{4,1},{5,0},{6,3},{7,2},{8,13},{9,12},{10,... | collective-permute-start | bytes 307208 | tf_op jit(solution)/shard_map/ppermute | solution.py:424
  125.2 9.7 %collective-permute-start.12 = (bf16[400,128]{1,0:T(8,128)(2,1)S(1)}, bf16[400,128]{1,0:T(8,128)(2,1)S(1)}, u32[]{:S(2)}, u32[]{:S(2)}) collective-permute-start(bf16[400,128]{1,0:T(8,128)(2,1)S(1)} %get-tuple-element.89), channel_id=1, source_target_pairs={{0,6},{1,7},{2,4},{3,5},{4,2},{5,3},{6,0},{7,1},{8,14},{9,15},{10,... | collective-permute-start | bytes 307208 | tf_op jit(solution)/shard_map/ppermute | solution.py:424
  127.4 7.5 %collective-permute-start.13 = (bf16[400,128]{1,0:T(8,128)(2,1)S(1)}, bf16[400,128]{1,0:T(8,128)(2,1)S(1)}, u32[]{:S(2)}, u32[]{:S(2)}) collective-permute-start(bf16[400,128]{1,0:T(8,128)(2,1)S(1)} %get-tuple-element.90), channel_id=1, source_target_pairs={{0,7},{1,6},{2,5},{3,4},{4,3},{5,2},{6,1},{7,0},{8,15},{9,14},{10,... | collective-permute-start | bytes 307208 | tf_op jit(solution)/shard_map/ppermute | solution.py:424
  136.2 15.7 %collective-permute-start.14 = (s16[2,408,128]{2,1,0:T(8,128)(2,1)S(1)}, s16[2,408,128]{2,1,0:T(8,128)(2,1)S(1)}, u32[]{:S(2)}, u32[]{:S(2)}) collective-permute-start(s16[2,408,128]{2,1,0:T(8,128)(2,1)S(1)} %get-tuple-element.92), channel_id=1, source_target_pairs={{0,30},{1,31},{2,28},{3,29},{4,26},{5,27},{6,24},{7,25},{8,22},{9,... | collective-permute-start | bytes 626696 | tf_op jit(solution)/shard_map/ppermute | solution.py:424
  145.8 21.6 %collective-permute-start.16 = (s16[2,408,128]{2,1,0:T(8,128)(2,1)S(1)}, s16[2,408,128]{2,1,0:T(8,128)(2,1)S(1)}, u32[]{:S(2)}, u32[]{:S(2)}) collective-permute-start(s16[2,408,128]{2,1,0:T(8,128)(2,1)S(1)} %get-tuple-element.99), channel_id=1, source_target_pairs={{0,26},{1,27},{2,24},{3,25},{4,30},{5,31},{6,28},{7,29},{8,18},{9,... | collective-permute-start | bytes 626696 | tf_op jit(solution)/shard_map/ppermute | solution.py:424
  148.4 19.6 %collective-permute-start.20 = (s16[2,408,128]{2,1,0:T(8,128)(2,1)S(1)}, s16[2,408,128]{2,1,0:T(8,128)(2,1)S(1)}, u32[]{:S(2)}, u32[]{:S(2)}) collective-permute-start(s16[2,408,128]{2,1,0:T(8,128)(2,1)S(1)} %get-tuple-element.106), channel_id=1, source_target_pairs={{0,14},{1,15},{2,12},{3,13},{4,10},{5,11},{6,8},{7,9},{8,6},{9,7},... | collective-permute-start | bytes 626696 | tf_op jit(solution)/shard_map/ppermute | solution.py:424
  148.5 18.9 %collective-permute-start.25 = (s16[2,408,128]{2,1,0:T(8,128)(2,1)S(1)}, s16[2,408,128]{2,1,0:T(8,128)(2,1)S(1)}, u32[]{:S(2)}, u32[]{:S(2)}) collective-permute-start(s16[2,408,128]{2,1,0:T(8,128)(2,1)S(1)} %get-tuple-element.113), channel_id=1, source_target_pairs={{0,28},{1,29},{2,30},{3,31},{4,24},{5,25},{6,26},{7,27},{8,20},{9,... | collective-permute-start | bytes 626696 | tf_op jit(solution)/shard_map/ppermute | solution.py:424
  151.9 24.1 %collective-permute-start.15 = (s16[2,408,128]{2,1,0:T(8,128)(2,1)S(1)}, s16[2,408,128]{2,1,0:T(8,128)(2,1)S(1)}, u32[]{:S(2)}, u32[]{:S(2)}) collective-permute-start(s16[2,408,128]{2,1,0:T(8,128)(2,1)S(1)} %get-tuple-element.93), channel_id=1, source_target_pairs={{0,24},{1,25},{2,26},{3,27},{4,28},{5,29},{6,30},{7,31},{8,16},{9,... | collective-permute-start | bytes 626696 | tf_op jit(solution)/shard_map/ppermute | solution.py:424
  153.5 14.6 %collective-permute-start.24 = (s16[408,128]{1,0:T(8,128)(2,1)S(1)}, s16[408,128]{1,0:T(8,128)(2,1)S(1)}, u32[]{:S(2)}, u32[]{:S(2)}) collective-permute-start(s16[408,128]{1,0:T(8,128)(2,1)S(1)} %slice_bitcast_fusion.13), channel_id=1, source_target_pairs={{0,1},{1,0},{2,3},{3,2},{4,5},{5,4},{6,7},{7,6},{8,9},{9,8},{10,11... | collective-permute-start | bytes 313352 | tf_op jit(solution)/shard_map/ppermute | solution.py:424
  167.3 7.6 %collective-permute-start.26 = (s16[408,128]{1,0:T(8,128)(2,1)S(1)}, s16[408,128]{1,0:T(8,128)(2,1)S(1)}, u32[]{:S(2)}, u32[]{:S(2)}) collective-permute-start(s16[408,128]{1,0:T(8,128)(2,1)S(1)} %slice_bitcast_fusion.12), channel_id=1, source_target_pairs={{0,1},{1,0},{2,3},{3,2},{4,5},{5,4},{6,7},{7,6},{8,9},{9,8},{10,11... | collective-permute-start | bytes 313352 | tf_op jit(solution)/shard_map/ppermute | solution.py:424
  167.4 16.8 %collective-permute-start.28 = (s16[408,128]{1,0:T(8,128)(2,1)S(1)}, s16[408,128]{1,0:T(8,128)(2,1)S(1)}, u32[]{:S(2)}, u32[]{:S(2)}) collective-permute-start(s16[408,128]{1,0:T(8,128)(2,1)S(1)} %slice_bitcast_fusion.11), channel_id=1, source_target_pairs={{0,1},{1,0},{2,3},{3,2},{4,5},{5,4},{6,7},{7,6},{8,9},{9,8},{10,11... | collective-permute-start | bytes 313352 | tf_op jit(solution)/shard_map/ppermute | solution.py:424
  168.0 20.4 %collective-permute-start.29 = (s16[408,128]{1,0:T(8,128)(2,1)S(1)}, s16[408,128]{1,0:T(8,128)(2,1)S(1)}, u32[]{:S(2)}, u32[]{:S(2)}) collective-permute-start(s16[408,128]{1,0:T(8,128)(2,1)S(1)} %slice_bitcast_fusion.10), channel_id=1, source_target_pairs={{0,1},{1,0},{2,3},{3,2},{4,5},{5,4},{6,7},{7,6},{8,9},{9,8},{10,11... | collective-permute-start | bytes 313352 | tf_op jit(solution)/shard_map/ppermute | solution.py:424
  168.1 20.3 %collective-permute-start.31 = (s16[2,408,128]{2,1,0:T(8,128)(2,1)S(1)}, s16[2,408,128]{2,1,0:T(8,128)(2,1)S(1)}, u32[]{:S(2)}, u32[]{:S(2)}) collective-permute-start(s16[2,408,128]{2,1,0:T(8,128)(2,1)S(1)} %get-tuple-element.117), channel_id=1, source_target_pairs={{0,12},{1,13},{2,14},{3,15},{4,8},{5,9},{6,10},{7,11},{8,4},{9,5},... | collective-permute-start | bytes 626696 | tf_op jit(solution)/shard_map/ppermute | solution.py:424
  182.4 18.3 %collective-permute-start.17 = (s16[2,408,128]{2,1,0:T(8,128)(2,1)S(1)}, s16[2,408,128]{2,1,0:T(8,128)(2,1)S(1)}, u32[]{:S(2)}, u32[]{:S(2)}) collective-permute-start(s16[2,408,128]{2,1,0:T(8,128)(2,1)S(1)} %get-tuple-element.100), channel_id=1, source_target_pairs={{0,22},{1,23},{2,20},{3,21},{4,18},{5,19},{6,16},{7,17},{8,30},{9,... | collective-permute-start | bytes 626696 | tf_op jit(solution)/shard_map/ppermute | solution.py:424
  182.8 18.0 %collective-permute-start.21 = (s16[2,408,128]{2,1,0:T(8,128)(2,1)S(1)}, s16[2,408,128]{2,1,0:T(8,128)(2,1)S(1)}, u32[]{:S(2)}, u32[]{:S(2)}) collective-permute-start(s16[2,408,128]{2,1,0:T(8,128)(2,1)S(1)} %get-tuple-element.107), channel_id=1, source_target_pairs={{0,10},{1,11},{2,8},{3,9},{4,14},{5,15},{6,12},{7,13},{8,2},{9,3},... | collective-permute-start | bytes 626696 | tf_op jit(solution)/shard_map/ppermute | solution.py:424
  184.3 21.0 %collective-permute-start.27 = (s16[2,408,128]{2,1,0:T(8,128)(2,1)S(1)}, s16[2,408,128]{2,1,0:T(8,128)(2,1)S(1)}, u32[]{:S(2)}, u32[]{:S(2)}) collective-permute-start(s16[2,408,128]{2,1,0:T(8,128)(2,1)S(1)} %get-tuple-element.114), channel_id=1, source_target_pairs={{0,20},{1,21},{2,22},{3,23},{4,16},{5,17},{6,18},{7,19},{8,28},{9,... | collective-permute-start | bytes 626696 | tf_op jit(solution)/shard_map/ppermute | solution.py:424
  188.4 4.4 %collective-permute-start.30 = (s16[408,128]{1,0:T(8,128)(2,1)S(1)}, s16[408,128]{1,0:T(8,128)(2,1)S(1)}, u32[]{:S(2)}, u32[]{:S(2)}) collective-permute-start(s16[408,128]{1,0:T(8,128)(2,1)S(1)} %slice_bitcast_fusion.9), channel_id=1, source_target_pairs={{0,1},{1,0},{2,3},{3,2},{4,5},{5,4},{6,7},{7,6},{8,9},{9,8},{10,11... | collective-permute-start | bytes 313352 | tf_op jit(solution)/shard_map/ppermute | solution.py:424
  188.5 5.0 %collective-permute-start.32 = (s16[408,128]{1,0:T(8,128)(2,1)S(1)}, s16[408,128]{1,0:T(8,128)(2,1)S(1)}, u32[]{:S(2)}, u32[]{:S(2)}) collective-permute-start(s16[408,128]{1,0:T(8,128)(2,1)S(1)} %slice_bitcast_fusion.8), channel_id=1, source_target_pairs={{0,1},{1,0},{2,3},{3,2},{4,5},{5,4},{6,7},{7,6},{8,9},{9,8},{10,11... | collective-permute-start | bytes 313352 | tf_op jit(solution)/shard_map/ppermute | solution.py:424
  192.8 12.6 %collective-permute-start.37 = (s16[2,408,128]{2,1,0:T(8,128)(2,1)S(1)}, s16[2,408,128]{2,1,0:T(8,128)(2,1)S(1)}, u32[]{:S(2)}, u32[]{:S(2)}) collective-permute-start(s16[2,408,128]{2,1,0:T(8,128)(2,1)S(1)} %get-tuple-element.122), channel_id=1, source_target_pairs={{0,8},{1,9},{2,10},{3,11},{4,12},{5,13},{6,14},{7,15},{8,0},{9,1},... | collective-permute-start | bytes 626696 | tf_op jit(solution)/shard_map/ppermute | solution.py:424
  200.8 18.0 %collective-permute-start.18 = (s16[2,408,128]{2,1,0:T(8,128)(2,1)S(1)}, s16[2,408,128]{2,1,0:T(8,128)(2,1)S(1)}, u32[]{:S(2)}, u32[]{:S(2)}) collective-permute-start(s16[2,408,128]{2,1,0:T(8,128)(2,1)S(1)} %get-tuple-element.101), channel_id=1, source_target_pairs={{0,18},{1,19},{2,16},{3,17},{4,22},{5,23},{6,20},{7,21},{8,26},{9,... | collective-permute-start | bytes 626696 | tf_op jit(solution)/shard_map/ppermute | solution.py:424
  200.8 18.0 %collective-permute-start.22 = (s16[2,408,128]{2,1,0:T(8,128)(2,1)S(1)}, s16[2,408,128]{2,1,0:T(8,128)(2,1)S(1)}, u32[]{:S(2)}, u32[]{:S(2)}) collective-permute-start(s16[2,408,128]{2,1,0:T(8,128)(2,1)S(1)} %get-tuple-element.108), channel_id=1, source_target_pairs={{0,6},{1,7},{2,4},{3,5},{4,2},{5,3},{6,0},{7,1},{8,14},{9,15},{10,... | collective-permute-start | bytes 626696 | tf_op jit(solution)/shard_map/ppermute | solution.py:424
  205.3 16.6 %collective-permute-start.33 = (s16[2,408,128]{2,1,0:T(8,128)(2,1)S(1)}, s16[2,408,128]{2,1,0:T(8,128)(2,1)S(1)}, u32[]{:S(2)}, u32[]{:S(2)}) collective-permute-start(s16[2,408,128]{2,1,0:T(8,128)(2,1)S(1)} %get-tuple-element.119), channel_id=1, source_target_pairs={{0,16},{1,17},{2,18},{3,19},{4,20},{5,21},{6,22},{7,23},{8,24},{9,... | collective-permute-start | bytes 626696 | tf_op jit(solution)/shard_map/ppermute | solution.py:424
  205.3 17.8 %collective-permute-start.34 = (s16[408,128]{1,0:T(8,128)(2,1)S(1)}, s16[408,128]{1,0:T(8,128)(2,1)S(1)}, u32[]{:S(2)}, u32[]{:S(2)}) collective-permute-start(s16[408,128]{1,0:T(8,128)(2,1)S(1)} %slice_bitcast_fusion.7), channel_id=1, source_target_pairs={{0,1},{1,0},{2,3},{3,2},{4,5},{5,4},{6,7},{7,6},{8,9},{9,8},{10,11... | collective-permute-start | bytes 313352 | tf_op jit(solution)/shard_map/ppermute | solution.py:424
  205.4 23.3 %collective-permute-start.35 = (s16[408,128]{1,0:T(8,128)(2,1)S(1)}, s16[408,128]{1,0:T(8,128)(2,1)S(1)}, u32[]{:S(2)}, u32[]{:S(2)}) collective-permute-start(s16[408,128]{1,0:T(8,128)(2,1)S(1)} %slice_bitcast_fusion.6), channel_id=1, source_target_pairs={{0,1},{1,0},{2,3},{3,2},{4,5},{5,4},{6,7},{7,6},{8,9},{9,8},{10,11... | collective-permute-start | bytes 313352 | tf_op jit(solution)/shard_map/ppermute | solution.py:424
  218.8 10.7 %collective-permute-start.36 = (s16[408,128]{1,0:T(8,128)(2,1)S(1)}, s16[408,128]{1,0:T(8,128)(2,1)S(1)}, u32[]{:S(2)}, u32[]{:S(2)}) collective-permute-start(s16[408,128]{1,0:T(8,128)(2,1)S(1)} %slice_bitcast_fusion.5), channel_id=1, source_target_pairs={{0,1},{1,0},{2,3},{3,2},{4,5},{5,4},{6,7},{7,6},{8,9},{9,8},{10,11... | collective-permute-start | bytes 313352 | tf_op jit(solution)/shard_map/ppermute | solution.py:424
  218.8 10.9 %collective-permute-start.38 = (s16[408,128]{1,0:T(8,128)(2,1)S(1)}, s16[408,128]{1,0:T(8,128)(2,1)S(1)}, u32[]{:S(2)}, u32[]{:S(2)}) collective-permute-start(s16[408,128]{1,0:T(8,128)(2,1)S(1)} %slice_bitcast_fusion.4), channel_id=1, source_target_pairs={{0,1},{1,0},{2,3},{3,2},{4,5},{5,4},{6,7},{7,6},{8,9},{9,8},{10,11... | collective-permute-start | bytes 313352 | tf_op jit(solution)/shard_map/ppermute | solution.py:424
  221.9 6.7 %collective-permute-start.39 = (s16[2,408,128]{2,1,0:T(8,128)(2,1)S(1)}, s16[2,408,128]{2,1,0:T(8,128)(2,1)S(1)}, u32[]{:S(2)}, u32[]{:S(2)}) collective-permute-start(s16[2,408,128]{2,1,0:T(8,128)(2,1)S(1)} %get-tuple-element.127), channel_id=1, source_target_pairs={{0,4},{1,5},{2,6},{3,7},{4,0},{5,1},{6,2},{7,3},{8,12},{9,13},{10,... | collective-permute-start | bytes 626696 | tf_op jit(solution)/shard_map/ppermute | solution.py:424
  223.1 6.9 %collective-permute-start.41 = (s16[408,128]{1,0:T(8,128)(2,1)S(1)}, s16[408,128]{1,0:T(8,128)(2,1)S(1)}, u32[]{:S(2)}, u32[]{:S(2)}) collective-permute-start(s16[408,128]{1,0:T(8,128)(2,1)S(1)} %slice_bitcast_fusion.3), channel_id=1, source_target_pairs={{0,1},{1,0},{2,3},{3,2},{4,5},{5,4},{6,7},{7,6},{8,9},{9,8},{10,11... | collective-permute-start | bytes 313352 | tf_op jit(solution)/shard_map/ppermute | solution.py:424
  228.6 2.5 %collective-permute-start.42 = (s16[408,128]{1,0:T(8,128)(2,1)S(1)}, s16[408,128]{1,0:T(8,128)(2,1)S(1)}, u32[]{:S(2)}, u32[]{:S(2)}) collective-permute-start(s16[408,128]{1,0:T(8,128)(2,1)S(1)} %slice_bitcast_fusion.2), channel_id=1, source_target_pairs={{0,1},{1,0},{2,3},{3,2},{4,5},{5,4},{6,7},{7,6},{8,9},{9,8},{10,11... | collective-permute-start | bytes 313352 | tf_op jit(solution)/shard_map/ppermute | solution.py:424
  228.7 5.8 %collective-permute-start.19 = (s16[408,128]{1,0:T(8,128)(2,1)S(1)}, s16[408,128]{1,0:T(8,128)(2,1)S(1)}, u32[]{:S(2)}, u32[]{:S(2)}) collective-permute-start(s16[408,128]{1,0:T(8,128)(2,1)S(1)} %get-tuple-element.102), channel_id=1, source_target_pairs={{0,2},{1,3},{2,0},{3,1},{4,6},{5,7},{6,4},{7,5},{8,10},{9,11},{10,... | collective-permute-start | bytes 313352 | tf_op jit(solution)/shard_map/ppermute | solution.py:424
  229.5 3.0 %collective-permute-start.43 = (s16[408,128]{1,0:T(8,128)(2,1)S(1)}, s16[408,128]{1,0:T(8,128)(2,1)S(1)}, u32[]{:S(2)}, u32[]{:S(2)}) collective-permute-start(s16[408,128]{1,0:T(8,128)(2,1)S(1)} %slice_bitcast_fusion.1), channel_id=1, source_target_pairs={{0,1},{1,0},{2,3},{3,2},{4,5},{5,4},{6,7},{7,6},{8,9},{9,8},{10,11... | collective-permute-start | bytes 313352 | tf_op jit(solution)/shard_map/ppermute | solution.py:424
  229.7 2.8 %collective-permute-start.44 = (s16[408,128]{1,0:T(8,128)(2,1)S(1)}, s16[408,128]{1,0:T(8,128)(2,1)S(1)}, u32[]{:S(2)}, u32[]{:S(2)}) collective-permute-start(s16[408,128]{1,0:T(8,128)(2,1)S(1)} %slice_bitcast_fusion), channel_id=1, source_target_pairs={{0,1},{1,0},{2,3},{3,2},{4,5},{5,4},{6,7},{7,6},{8,9},{9,8},{10,11... | collective-permute-start | bytes 313352 | tf_op jit(solution)/shard_map/ppermute | solution.py:424
  230.0 6.0 %collective-permute-start.23 = (s16[408,128]{1,0:T(8,128)(2,1)S(1)}, s16[408,128]{1,0:T(8,128)(2,1)S(1)}, u32[]{:S(2)}, u32[]{:S(2)}) collective-permute-start(s16[408,128]{1,0:T(8,128)(2,1)S(1)} %get-tuple-element.109), channel_id=1, source_target_pairs={{0,3},{1,2},{2,1},{3,0},{4,7},{5,6},{6,5},{7,4},{8,11},{9,10},{10,... | collective-permute-start | bytes 313352 | tf_op jit(solution)/shard_map/ppermute | solution.py:424
  231.1 4.8 %collective-permute-start.40 = (s16[408,128]{1,0:T(8,128)(2,1)S(1)}, s16[408,128]{1,0:T(8,128)(2,1)S(1)}, u32[]{:S(2)}, u32[]{:S(2)}) collective-permute-start(s16[408,128]{1,0:T(8,128)(2,1)S(1)} %get-tuple-element.128), channel_id=1, source_target_pairs={{0,1},{1,0},{2,3},{3,2},{4,5},{5,4},{6,7},{7,6},{8,9},{9,8},{10,11... | collective-permute-start | bytes 313352 | tf_op jit(solution)/shard_map/ppermute | solution.py:424
  232.4 3.5 %copy-start = (f32[2048,400]{0,1:T(8,128)S(1)}, f32[2048,400]{0,1:T(8,128)}, u32[]{:S(2)}) copy-start(f32[2048,400]{0,1:T(8,128)} %param.9) | copy-start | bytes 9830404
  232.5 3.5 %copy-start.1 = (f32[2048]{0:T(1024)S(1)}, f32[2048]{0:T(1024)}, u32[]{:S(2)}) copy-start(f32[2048]{0:T(1024)} %param.10) | copy-start | bytes 24580

commit v11 on v9

--- a/solution.py
+++ b/solution.py
@@ -136,7 +136,7 @@
     dst_ref[...] = target.astype(BF16)
 
 
-def gather_edges(rows, spos, dpos, operator, tile=512):
+def gather_edges(rows, spos, dpos, operator, tile=1024):
     width, total = rows.shape
     edges = spos.shape[1]
     lane = pl.BlockSpec((1, tile), lambda i: (0, i))
@@ -174,7 +174,7 @@
     u = src_ref[...].astype(F32) * operator
     u_half = u.astype(BF16)
     scores = jnp.dot(tall, u_half, preferred_element_type=F32)
-    g_neg = (jax.nn.sigmoid(scores) / count).astype(BF16)
+    g_neg = (jax.nn.sigmoid(scores) * (1.0 / count)).astype(BF16)
     sums = lax.dot_general(u_half, g_neg, NT, preferred_element_type=F32)
     for g in range(groups):
         outs[g][...] = sums[:, g * each : (g + 1) * each].astype(BF16)
@@ -341,7 +341,7 @@
             g = grad[:, lanes]
             new_state = state_ref[:, lanes] + jnp.sum(g * g, axis=0, keepdims=True) / width
             state_out[:, lanes] = new_state
-            fresh[:, lanes] = table_ref[:, lanes] - 0.1 * g / (jnp.sqrt(new_state) + 1e-10)
+            fresh[:, lanes] = table_ref[:, lanes] - g * (0.1 / (jnp.sqrt(new_state) + 1e-10))
         copy(b).start()
     for b in range(sems.shape[0]):
         copy(b).wait()

time: 224 us -> 224 us (level)
  starting transfers between devices: 67.3 us -> 71.4 us
  waiting for transfers between devices: 72 us -> 68.5 us
    ppermute x45, starting transfers between devices: 56.5 us -> 60.6 us  [swap(): return lax.ppermute(x, axis, [(i, i ^ shift) for i in range(count)])]
    ppermute x45, waiting for transfers between devices: 19.9 us -> 16.5 us  [swap(): return lax.ppermute(x, axis, [(i, i ^ shift) for i in range(count)])]
  transfers between devices with their start and end apart: 47 -> 47, of which waited for: 15 -> 12; matrix products, arithmetic and copies ran while one was open for 13% -> 13% of each run, Pallas kernels for 16% -> 16%
where the time goes in v11:
time: 224 us; the launch traced here: 223 us
  starting transfers between devices  71.4 us (32%)
  waiting for transfers between devices  68.5 us (31%)
  Pallas kernels  51.1 us (23%)
  local copies, waits for them, and re-layouts  26.7 us (12%)
  other arithmetic  3.85 us (2%)
    ppermute x45, starting transfers between devices, swap(): return lax.ppermute(x, axis, [(i, i ^ shift) for i in range(count)])  60.6 us
    all_to_all x1, waiting for transfers between devices, per_device(): lax.all_to_all(outgoing, AXES, split_axis=0, concat_axis=0, tiled=True)  47.1 us
    gather x2, local copies, waits for them, and re-layouts, per_device(): operator = relations[rel_ids].T  16.7 us
    ppermute x45, waiting for transfers between devices, swap(): return lax.ppermute(x, axis, [(i, i ^ shift) for i in range(count)])  16.5 us
    pallas_call x3, Pallas kernels, scatter(): pl.pallas_call(functools.partial(scatter_kernel, first * BLK), out_shape=...  15.1 us
    pallas_call x5, Pallas kernels, pack(): pl.pallas_call(functools.partial(pack_kernel, first, tuple(bounds), len(g...  9.29 us
    unnamed x15, local copies, waits for them, and re-layouts  8.62 us
    pallas_call x1, Pallas kernels, gather_edges(): pl.pallas_call(edge_kernel, grid=(edges // tile,), out_shape=(jax.ShapeDt...  7.8 us
  transfers between devices with their start and end apart: 47, of which 12 were waited for; matrix products, arithmetic and copies ran while one was open for 13% of the time, Pallas kernels for 16%

profile of v11, /device:TPU:0, one launch (start us, length us, event | category | flops | bytes accessed | tf_op | source)
XLA Modules:
  0.0 222.8 jit_solution(18273799401065999908)
XLA Ops:
  0.6 1.3 copy.21
  2.0 7.3 %all-to-all-start = ((s32[32,1,1]{2,1,0:T(1,128)}), s32[32,1,1]{2,1,0:T(1,128)S(1)}, u32[]{:S(2)}, u32[]{:S(2)}) async-start(s32[32,1,1]{2,1,0:T(1,128)} %copy.21), calls=%async_computation | async-start | bytes 32768 | tf_op jit(solution)/shard_map/all_to_all | solution.py:372
  9.3 2.1 bitcast_bitcast_fusion.blocks_ref
  11.4 4.9 %all-to-all-done.asked_ref = s32[32,1,1]{2,1,0:T(1,128)S(1)} async-done(((s32[32,1,1]{2,1,0:T(1,128)}), s32[32,1,1]{2,1,0:T(1,128)S(1)}, u32[]{:S(2)}, u32[]{:S(2)}) %all-to-all-start) | async-done | bytes 160 | tf_op jit(solution)/shard_map/all_to_all | solution.py:372
  16.3 2.5 %select.19 = bf16[32,400,128]{2,1,0:T(8,128)(2,1)} custom-call(s32[32,1,1]{2,1,0:T(1,128)S(1)} %all-to-all-done.asked_ref, bf16[16,400,128]{2,1,0:T(8,128)(2,1)S(1)} %bitcast_bitcast_fusion.blocks_ref), custom_call_target="tpu_custom_call" | custom-call | tf_op jit(solution)/shard_map/select/pallas_call | solution.py:65
  18.9 3.6 %all-to-all-start.1 = ((bf16[32,400,128]{2,1,0:T(8,128)(2,1)}), bf16[32,400,128]{2,1,0:T(8,128)(2,1)}, u32[]{:S(2)}, u32[]{:S(2)}) async-start(bf16[32,400,128]{2,1,0:T(8,128)(2,1)} %select.19), calls=%async_computation.1 | async-start | bytes 6553600 | tf_op jit(solution)/shard_map/all_to_all | solution.py:378
  22.4 8.6 %copy.23 = f32[4096,400]{1,0:T(8,128)} copy(f32[4096,400]{0,1:T(8,128)} %param.11) | data formatting | bytes 13107200 | tf_op args[2]
  31.0 12.9 %gather_fusion = f32[2048,400]{1,0:T(8,128)} fusion(f32[4096,400]{1,0:T(8,128)} %copy.23, s32[2048]{0:T(1024)S(1)} %fusion.3), kind=kCustom, calls=%fused_computation | custom fusion | bytes 6561792 | tf_op jit(solution)/shard_map/gather | solution.py:379
  44.0 3.8 %copy.24 = f32[2048,400]{0,1:T(8,128)S(1)} copy(f32[2048,400]{1,0:T(8,128)} %gather_fusion) | data formatting | bytes 6553600 | tf_op jit(solution)/shard_map/gather | solution.py:379
  48.5 0.7 reduce
  49.6 47.1 %all-to-all-done.1.fetched = bf16[32,400,128]{2,1,0:T(8,128)(2,1)} async-done(((bf16[32,400,128]{2,1,0:T(8,128)(2,1)}), bf16[32,400,128]{2,1,0:T(8,128)(2,1)}, u32[]{:S(2)}, u32[]{:S(2)}) %all-to-all-start.1) | async-done | bytes 3276832 | tf_op jit(solution)/shard_map/all_to_all | solution.py:378
  96.7 2.6 %gather_negs.1 = (bf16[400,128]{1,0:T(8,128)(2,1)S(1)}, bf16[400,2048]{1,0:T(8,128)(2,1)S(1)}) custom-call(s32[16]{0:T(128)S(1)} %select_reduce_fusion.7.live_ref, bf16[32,400,128]{2,1,0:T(8,128)(2,1)} %all-to-all-done.1.fetched, s32[1,128]{1,0:T(1,128)S(1)} %fusion.10.pos_ref.npos), custom_call_target="tpu_custom_call" | custom-call | tf_op jit(solution)/shard_map/gather_negs/pallas_call | solution.py:115
  99.5 1.3 collective-permute-start.1
  101.3 1.2 collective-permute-start.3
  103.0 2.1 collective-permute-start.5
  105.2 0.9 collective-permute-start.6
  106.1 7.8 %gather_edges.1 = (bf16[400,2048]{1,0:T(8,128)(2,1)S(1)}, bf16[400,2048]{1,0:T(8,128)(2,1)S(1)}, f32[1,2048]{1,0:T(1,128)S(1)}) custom-call(bf16[400,2048]{1,0:T(8,128)(2,1)S(1)} %get-tuple-element.128.rows, s32[1,2048]{1,0:T(1,128)S(1)} %bitcast.20, s32[1,2048]{1,0:T(1,128)S(1)} %bitcast.24, f32[400,2048]{1,0:T(8,128)S(1)} %bitcast.17), custom_call_target="tpu_custom_call" | custom-call | flops 104857600 | bytes 204800 | tf_op jit(solution)/shard_map/gather_edges/pallas_call | solution.py:144
  114.0 6.2 %score.1 = (bf16[2,400,2048]{2,1,0:T(8,128)(2,1)S(1)}, bf16[2,400,2048]{2,1,0:T(8,128)(2,1)S(1)}, bf16[400,128]{1,0:T(8,128)(2,1)S(1)}, bf16[400,128]{1,0:T(8,12...) custom-call(bf16[400,128]{1,0:T(8,128)(2,1)S(1)} %get-tuple-element., ...), custom_call_target="tpu_custom_call" | custom-call | flops 78643200 | bytes 153600 | tf_op jit(solution)/shard_map/score/pallas_call | solution.py:191
  120.2 1.4 collective-permute-start.7
  122.1 0.9 collective-permute-start.9
  123.5 1.5 collective-permute-start.11
  125.1 0.8 collective-permute-start.12
  125.9 1.4 collective-permute-done.8.refs_4_.refs_5_.refs_3_
  127.4 5.7 %scatter.3.refs_0_ = f32[400,768]{1,0:T(8,128)S(1)} custom-call(bf16[2,400,2048]{2,1,0:T(8,128)(2,1)S(1)} %get-tuple-element.135.gs_ref, bf16[2,400,2048]{2,1,0:T(8,128)(2,1)S(1)} %get-tuple-element.136.gd_ref, s32[1,2048]{1,0:T(1,128)S(1)} %bitcast.21, s32[1,2048]{1,0:T(1,128)S(1)} %bitcast.25), custom_call_target="tpu_custom_call" | custom-call | flops 39321600 | bytes 76800 | tf_op jit(solution)/shard_map/scatter/pallas_call | solution.py:228
  133.2 1.7 collective-permute-done.11.refs_7_.refs_8_.refs_6_
  134.8 1.6 pack.9
  136.4 2.0 collective-permute-start.26
  138.5 2.1 collective-permute-start.15
  140.6 2.7 %collective-permute-start.31 = (s16[408,128]{1,0:T(8,128)(2,1)S(1)}, s16[408,128]{1,0:T(8,128)(2,1)S(1)}, u32[]{:S(2)}, u32[]{:S(2)}) collective-permute-start(s16[408,128]{1,0:T(8,128)(2,1)S(1)} %get-tuple-element.186), channel_id=1, source_target_pairs={{0,30},{1,31},{2,28},{3,29},{4,26},{5,27},{6,24},{7,25},{8,22},{9,... | collective-permute-start | bytes 313352 | tf_op jit(solution)/shard_map/ppermute | solution.py:416
  143.3 2.7 %collective-permute-start.33 = (s16[408,128]{1,0:T(8,128)(2,1)S(1)}, s16[408,128]{1,0:T(8,128)(2,1)S(1)}, u32[]{:S(2)}, u32[]{:S(2)}) collective-permute-start(s16[408,128]{1,0:T(8,128)(2,1)S(1)} %get-tuple-element.191), channel_id=1, source_target_pairs={{0,29},{1,28},{2,31},{3,30},{4,25},{5,24},{6,27},{7,26},{8,21},{9,... | collective-permute-start | bytes 313352 | tf_op jit(solution)/shard_map/ppermute | solution.py:416
  146.0 5.7 %scatter.4.refs_1_ = f32[400,768]{1,0:T(8,128)S(1)} custom-call(bf16[2,400,2048]{2,1,0:T(8,128)(2,1)S(1)} %get-tuple-element.135.gs_ref, bf16[2,400,2048]{2,1,0:T(8,128)(2,1)S(1)} %get-tuple-element.136.gd_ref, s32[1,2048]{1,0:T(1,128)S(1)} %bitcast.22, s32[1,2048]{1,0:T(1,128)S(1)} %bitcast.26), custom_call_target="tpu_custom_call" | custom-call | flops 39321600 | bytes 76800 | tf_op jit(solution)/shard_map/scatter/pallas_call | solution.py:228
  151.7 1.8 pack.5
  153.5 1.4 collective-permute-start.14
  155.0 2.7 %collective-permute-start.16 = (s16[408,128]{1,0:T(8,128)(2,1)S(1)}, s16[408,128]{1,0:T(8,128)(2,1)S(1)}, u32[]{:S(2)}, u32[]{:S(2)}) collective-permute-start(s16[408,128]{1,0:T(8,128)(2,1)S(1)} %get-tuple-element.156), channel_id=1, source_target_pairs={{0,25},{1,24},{2,27},{3,26},{4,29},{5,28},{6,31},{7,30},{8,17},{9,... | collective-permute-start | bytes 313352 | tf_op jit(solution)/shard_map/ppermute | solution.py:416
  157.7 2.3 %collective-permute-start.32 = (s16[408,128]{1,0:T(8,128)(2,1)S(1)}, s16[408,128]{1,0:T(8,128)(2,1)S(1)}, u32[]{:S(2)}, u32[]{:S(2)}) collective-permute-start(s16[408,128]{1,0:T(8,128)(2,1)S(1)} %get-tuple-element.187), channel_id=1, source_target_pairs={{0,26},{1,27},{2,24},{3,25},{4,30},{5,31},{6,28},{7,29},{8,18},{9,... | collective-permute-start | bytes 313352 | tf_op jit(solution)/shard_map/ppermute | solution.py:416
  160.0 2.3 %collective-permute-start.34 = (s16[408,128]{1,0:T(8,128)(2,1)S(1)}, s16[408,128]{1,0:T(8,128)(2,1)S(1)}, u32[]{:S(2)}, u32[]{:S(2)}) collective-permute-start(s16[408,128]{1,0:T(8,128)(2,1)S(1)} %get-tuple-element.192), channel_id=1, source_target_pairs={{0,14},{1,15},{2,12},{3,13},{4,10},{5,11},{6,8},{7,9},{8,6},{9,7},... | collective-permute-start | bytes 313352 | tf_op jit(solution)/shard_map/ppermute | solution.py:416
  162.4 1.9 collective-permute-done.27.refs_1_
  164.2 1.1 collective-permute-start.28
  165.4 3.8 %scatter.5.refs_2_ = f32[400,512]{1,0:T(8,128)S(1)} custom-call(bf16[2,400,2048]{2,1,0:T(8,128)(2,1)S(1)} %get-tuple-element.135.gs_ref, bf16[2,400,2048]{2,1,0:T(8,128)(2,1)S(1)} %get-tuple-element.136.gd_ref, s32[1,2048]{1,0:T(1,128)S(1)} %bitcast.23, s32[1,2048]{1,0:T(1,128)S(1)} %bitcast.27), custom_call_target="tpu_custom_call" | custom-call | flops 26214400 | bytes 51200 | tf_op jit(solution)/shard_map/scatter/pallas_call | solution.py:228
  169.2 2.4 %pack.8 = (s16[408,128]{1,0:T(8,128)(2,1)S(1)}, s16[408,128]{1,0:T(8,128)(2,1)S(1)}, s16[408,128]{1,0:T(8,128)(2,1)S(1)}, s16[408,128]{1,0:T(8,128)(2,1)S(1)}, s...) custom-call(s32[32]{0:T(128)S(1)} %select_reduce_fusion.5.rank_ref, ...), custom_call_target="tpu_custom_call" | custom-call | flops 3276800 | bytes 6400 | tf_op jit(solution)/shard_map/pack/pallas_call | solution.py:284
  172.1 1.2 collective-permute-start.35
  173.3 6.0 %collective-permute-start.36 = (s16[408,128]{1,0:T(8,128)(2,1)S(1)}, s16[408,128]{1,0:T(8,128)(2,1)S(1)}, u32[]{:S(2)}, u32[]{:S(2)}) collective-permute-start(s16[408,128]{1,0:T(8,128)(2,1)S(1)} %get-tuple-element.201), channel_id=1, source_target_pairs={{0,23},{1,22},{2,21},{3,20},{4,19},{5,18},{6,17},{7,16},{8,31},{9,... | collective-permute-start | bytes 313352 | tf_op jit(solution)/shard_map/ppermute | solution.py:416
  179.5 3.0 %collective-permute-start.29 = (s16[408,128]{1,0:T(8,128)(2,1)S(1)}, s16[408,128]{1,0:T(8,128)(2,1)S(1)}, u32[]{:S(2)}, u32[]{:S(2)}) collective-permute-start(s16[408,128]{1,0:T(8,128)(2,1)S(1)} %get-tuple-element.179), channel_id=1, source_target_pairs={{0,10},{1,11},{2,8},{3,9},{4,14},{5,15},{6,12},{7,13},{8,2},{9,3},... | collective-permute-start | bytes 313352 | tf_op jit(solution)/shard_map/ppermute | solution.py:416
  182.5 1.0 add.71.refs_8_
  183.5 2.1 pack.7
  185.6 1.3 collective-permute-start.18
  186.9 1.7 collective-permute-start.39
  188.7 1.2 collective-permute-start.42
  189.9 1.3 collective-permute-start.23
  191.3 2.4 %collective-permute-start.30 = (s16[408,128]{1,0:T(8,128)(2,1)S(1)}, s16[408,128]{1,0:T(8,128)(2,1)S(1)}, u32[]{:S(2)}, u32[]{:S(2)}) collective-permute-start(s16[408,128]{1,0:T(8,128)(2,1)S(1)} %get-tuple-element.180), channel_id=1, source_target_pairs={{0,19},{1,18},{2,17},{3,16},{4,23},{5,22},{6,21},{7,20},{8,27},{9,... | collective-permute-start | bytes 313352 | tf_op jit(solution)/shard_map/ppermute | solution.py:416
  193.6 1.0 add.72.refs_8_
  194.7 3.2 %collective-permute-done.18.refs_6_ = s16[408,128]{1,0:T(8,128)(2,1)S(1)} collective-permute-done((s16[408,128]{1,0:T(8,128)(2,1)S(1)}, s16[408,128]{1,0:T(8,128)(2,1)S(1)}, u32[]{:S(2)}, u32[]{:S(2)}) %collective-permute-start.18) | collective-permute-done | bytes 104480 | tf_op jit(solution)/shard_map/ppermute | solution.py:416
  197.8 1.5 collective-permute-start.19
  199.3 1.9 collective-permute-start.40
  201.2 1.3 collective-permute-start.24
  202.5 3.9 %collective-permute-done.30.refs_0_ = s16[408,128]{1,0:T(8,128)(2,1)S(1)} collective-permute-done((s16[408,128]{1,0:T(8,128)(2,1)S(1)}, s16[408,128]{1,0:T(8,128)(2,1)S(1)}, u32[]{:S(2)}, u32[]{:S(2)}) %collective-permute-start.30) | collective-permute-done | bytes 104480 | tf_op jit(solution)/shard_map/ppermute | solution.py:416
  206.5 1.4 pack.6
  208.0 3.2 %collective-permute-done.43.refs_2_ = s16[408,128]{1,0:T(8,128)(2,1)S(1)} collective-permute-done((s16[408,128]{1,0:T(8,128)(2,1)S(1)}, s16[408,128]{1,0:T(8,128)(2,1)S(1)}, u32[]{:S(2)}, u32[]{:S(2)}) %collective-permute-start.43) | collective-permute-done | bytes 104480 | tf_op jit(solution)/shard_map/ppermute | solution.py:416
  211.2 1.1 collective-permute-start.44
  212.3 3.6 %collective-permute-start.25 = (s16[408,128]{1,0:T(8,128)(2,1)S(1)}, s16[408,128]{1,0:T(8,128)(2,1)S(1)}, u32[]{:S(2)}, u32[]{:S(2)}) collective-permute-start(s16[408,128]{1,0:T(8,128)(2,1)S(1)} %get-tuple-element.169), channel_id=1, source_target_pairs={{0,2},{1,3},{2,0},{3,1},{4,6},{5,7},{6,4},{7,5},{8,10},{9,11},{10,... | collective-permute-start | bytes 313352 | tf_op jit(solution)/shard_map/ppermute | solution.py:416
  216.0 1.0 add.73.refs_8_
  217.2 1.0 add.74.refs_4_
  218.2 0.9 collective-permute-done.25.refs_1_
  219.2 3.5 %update.1 = (f32[400,2048]{1,0:T(8,128)}, f32[1,2048]{1,0:T(1,128)}) custom-call(s32[32]{0:T(128)S(1)} %get-tuple-element.121.asked_ref, s16[408,128]{1,0:T(8,128)(2,1)S(1)} %collective-permute-done.20.refs_0_, s16[408,128]{1,0:T(8,128)(2,1)S(1)} %collective-permute-done.25.refs_1_, s16[408,128]{1,0:T(8,128)(2,1)S(1)} %collective-permute-done.38.refs_2_, ...), custom_call_target="tpu_custom_call" | custom-call | flops 819200 | bytes 1600 | tf_op jit(solution)/shard_map/update/pallas_call | solution.py:352
  (83 shorter events, 4.8 us)
Async XLA Ops:
  2.0 14.4 %all-to-all-start = ((s32[32,1,1]{2,1,0:T(1,128)}), s32[32,1,1]{2,1,0:T(1,128)S(1)}, u32[]{:S(2)}, u32[]{:S(2)}) async-start(s32[32,1,1]{2,1,0:T(1,128)} %copy.21), calls=%async_computation | async-start | bytes 32768 | tf_op jit(solution)/shard_map/all_to_all | solution.py:372
  18.9 77.9 %all-to-all-start.1 = ((bf16[32,400,128]{2,1,0:T(8,128)(2,1)}), bf16[32,400,128]{2,1,0:T(8,128)(2,1)}, u32[]{:S(2)}, u32[]{:S(2)}) async-start(bf16[32,400,128]{2,1,0:T(8,128)(2,1)} %select.19), calls=%async_computation.1 | async-start | bytes 6553600 | tf_op jit(solution)/shard_map/all_to_all | solution.py:378
  22.4 8.6 %copy-start.4 = (s32[2048]{0:T(1024)S(1)}, s32[2048]{0:T(1024)}, u32[]{:S(2)}) copy-start(s32[2048]{0:T(1024)} %param.12) | copy-start | bytes 24580
  44.0 3.8 %copy-start.2 = (s32[2048]{0:T(1024)S(1)}, s32[2048]{0:T(1024)}, u32[]{:S(2)}) copy-start(s32[2048]{0:T(1024)} %param.14) | copy-start | bytes 24580
  44.0 4.0 %copy-start.6 = (s32[32]{0:T(128)S(1)}, s32[32]{0:T(128)}, u32[]{:S(2)}) copy-start(s32[32]{0:T(128)} %constant.80.clone) | copy-start | bytes 388
  44.0 4.4 %copy-start.5 = (s32[128]{0:T(128)S(1)}, s32[128]{0:T(128)}, u32[]{:S(2)}) copy-start(s32[128]{0:T(128)} %param.16) | copy-start | bytes 1540
  44.0 4.4 %copy-start.3 = (s32[2048]{0:T(1024)S(1)}, s32[2048]{0:T(1024)}, u32[]{:S(2)}) copy-start(s32[2048]{0:T(1024)} %param.15) | copy-start | bytes 24580
  99.4 3.6 %collective-permute-start = (bf16[400,128]{1,0:T(8,128)(2,1)S(1)}, bf16[400,128]{1,0:T(8,128)(2,1)S(1)}, u32[]{:S(2)}, u32[]{:S(2)}) collective-permute-start(bf16[400,128]{1,0:T(8,128)(2,1)S(1)} %get-tuple-element.127.refs_0_), channel_id=1, source_target_pairs={{0,1},{1,0},{2,3},{3,2},{4,5},{5,4},{6,7},{7,6},{8,9},{9,8},{10,11... | collective-permute-start | bytes 307208 | tf_op jit(solution)/shard_map/ppermute | solution.py:416
  99.5 5.7 %collective-permute-start.1 = (bf16[400,128]{1,0:T(8,128)(2,1)S(1)}, bf16[400,128]{1,0:T(8,128)(2,1)S(1)}, u32[]{:S(2)}, u32[]{:S(2)}) collective-permute-start(bf16[400,128]{1,0:T(8,128)(2,1)S(1)} %get-tuple-element.127.refs_0_), channel_id=1, source_target_pairs={{0,2},{1,3},{2,0},{3,1},{4,6},{5,7},{6,4},{7,5},{8,10},{9,11},{10,... | collective-permute-start | bytes 307208 | tf_op jit(solution)/shard_map/ppermute | solution.py:416
  100.7 13.2 %collective-permute-start.2 = (bf16[400,128]{1,0:T(8,128)(2,1)S(1)}, bf16[400,128]{1,0:T(8,128)(2,1)S(1)}, u32[]{:S(2)}, u32[]{:S(2)}) collective-permute-start(bf16[400,128]{1,0:T(8,128)(2,1)S(1)} %get-tuple-element.127.refs_0_), channel_id=1, source_target_pairs={{0,3},{1,2},{2,1},{3,0},{4,7},{5,6},{6,5},{7,4},{8,11},{9,10},{10,... | collective-permute-start | bytes 307208 | tf_op jit(solution)/shard_map/ppermute | solution.py:416
  101.3 12.6 %collective-permute-start.3 = (bf16[400,128]{1,0:T(8,128)(2,1)S(1)}, bf16[400,128]{1,0:T(8,128)(2,1)S(1)}, u32[]{:S(2)}, u32[]{:S(2)}) collective-permute-start(bf16[400,128]{1,0:T(8,128)(2,1)S(1)} %get-tuple-element.127.refs_0_), channel_id=1, source_target_pairs={{0,4},{1,5},{2,6},{3,7},{4,0},{5,1},{6,2},{7,3},{8,12},{9,13},{10,... | collective-permute-start | bytes 307208 | tf_op jit(solution)/shard_map/ppermute | solution.py:416
  102.5 11.5 %collective-permute-start.4 = (bf16[400,128]{1,0:T(8,128)(2,1)S(1)}, bf16[400,128]{1,0:T(8,128)(2,1)S(1)}, u32[]{:S(2)}, u32[]{:S(2)}) collective-permute-start(bf16[400,128]{1,0:T(8,128)(2,1)S(1)} %get-tuple-element.127.refs_0_), channel_id=1, source_target_pairs={{0,5},{1,4},{2,7},{3,6},{4,1},{5,0},{6,3},{7,2},{8,13},{9,12},{10,... | collective-permute-start | bytes 307208 | tf_op jit(solution)/shard_map/ppermute | solution.py:416
  103.0 11.0 %collective-permute-start.5 = (bf16[400,128]{1,0:T(8,128)(2,1)S(1)}, bf16[400,128]{1,0:T(8,128)(2,1)S(1)}, u32[]{:S(2)}, u32[]{:S(2)}) collective-permute-start(bf16[400,128]{1,0:T(8,128)(2,1)S(1)} %get-tuple-element.127.refs_0_), channel_id=1, source_target_pairs={{0,6},{1,7},{2,4},{3,5},{4,2},{5,3},{6,0},{7,1},{8,14},{9,15},{10,... | collective-permute-start | bytes 307208 | tf_op jit(solution)/shard_map/ppermute | solution.py:416
  105.2 8.8 %collective-permute-start.6 = (bf16[400,128]{1,0:T(8,128)(2,1)S(1)}, bf16[400,128]{1,0:T(8,128)(2,1)S(1)}, u32[]{:S(2)}, u32[]{:S(2)}) collective-permute-start(bf16[400,128]{1,0:T(8,128)(2,1)S(1)} %get-tuple-element.127.refs_0_), channel_id=1, source_target_pairs={{0,7},{1,6},{2,5},{3,4},{4,3},{5,2},{6,1},{7,0},{8,15},{9,14},{10,... | collective-permute-start | bytes 307208 | tf_op jit(solution)/shard_map/ppermute | solution.py:416
  120.2 4.9 %collective-permute-start.7 = (bf16[400,128]{1,0:T(8,128)(2,1)S(1)}, bf16[400,128]{1,0:T(8,128)(2,1)S(1)}, u32[]{:S(2)}, u32[]{:S(2)}) collective-permute-start(bf16[400,128]{1,0:T(8,128)(2,1)S(1)} %get-tuple-element.138), channel_id=1, source_target_pairs={{0,1},{1,0},{2,3},{3,2},{4,5},{5,4},{6,7},{7,6},{8,9},{9,8},{10,11... | collective-permute-start | bytes 307208 | tf_op jit(solution)/shard_map/ppermute | solution.py:416
  121.6 5.7 %collective-permute-start.8 = (bf16[400,128]{1,0:T(8,128)(2,1)S(1)}, bf16[400,128]{1,0:T(8,128)(2,1)S(1)}, u32[]{:S(2)}, u32[]{:S(2)}) collective-permute-start(bf16[400,128]{1,0:T(8,128)(2,1)S(1)} %get-tuple-element.139), channel_id=1, source_target_pairs={{0,2},{1,3},{2,0},{3,1},{4,6},{5,7},{6,4},{7,5},{8,10},{9,11},{10,... | collective-permute-start | bytes 307208 | tf_op jit(solution)/shard_map/ppermute | solution.py:416
  122.1 11.0 %collective-permute-start.9 = (bf16[400,128]{1,0:T(8,128)(2,1)S(1)}, bf16[400,128]{1,0:T(8,128)(2,1)S(1)}, u32[]{:S(2)}, u32[]{:S(2)}) collective-permute-start(bf16[400,128]{1,0:T(8,128)(2,1)S(1)} %get-tuple-element.140), channel_id=1, source_target_pairs={{0,3},{1,2},{2,1},{3,0},{4,7},{5,6},{6,5},{7,4},{8,11},{9,10},{10,... | collective-permute-start | bytes 307208 | tf_op jit(solution)/shard_map/ppermute | solution.py:416
  123.0 10.1 %collective-permute-start.10 = (bf16[400,128]{1,0:T(8,128)(2,1)S(1)}, bf16[400,128]{1,0:T(8,128)(2,1)S(1)}, u32[]{:S(2)}, u32[]{:S(2)}) collective-permute-start(bf16[400,128]{1,0:T(8,128)(2,1)S(1)} %get-tuple-element.141), channel_id=1, source_target_pairs={{0,4},{1,5},{2,6},{3,7},{4,0},{5,1},{6,2},{7,3},{8,12},{9,13},{10,... | collective-permute-start | bytes 307208 | tf_op jit(solution)/shard_map/ppermute | solution.py:416
  123.5 11.3 %collective-permute-start.11 = (bf16[400,128]{1,0:T(8,128)(2,1)S(1)}, bf16[400,128]{1,0:T(8,128)(2,1)S(1)}, u32[]{:S(2)}, u32[]{:S(2)}) collective-permute-start(bf16[400,128]{1,0:T(8,128)(2,1)S(1)} %get-tuple-element.142), channel_id=1, source_target_pairs={{0,5},{1,4},{2,7},{3,6},{4,1},{5,0},{6,3},{7,2},{8,13},{9,12},{10,... | collective-permute-start | bytes 307208 | tf_op jit(solution)/shard_map/ppermute | solution.py:416
  125.1 9.7 %collective-permute-start.12 = (bf16[400,128]{1,0:T(8,128)(2,1)S(1)}, bf16[400,128]{1,0:T(8,128)(2,1)S(1)}, u32[]{:S(2)}, u32[]{:S(2)}) collective-permute-start(bf16[400,128]{1,0:T(8,128)(2,1)S(1)} %get-tuple-element.143), channel_id=1, source_target_pairs={{0,6},{1,7},{2,4},{3,5},{4,2},{5,3},{6,0},{7,1},{8,14},{9,15},{10,... | collective-permute-start | bytes 307208 | tf_op jit(solution)/shard_map/ppermute | solution.py:416
  127.3 7.5 %collective-permute-start.13 = (bf16[400,128]{1,0:T(8,128)(2,1)S(1)}, bf16[400,128]{1,0:T(8,128)(2,1)S(1)}, u32[]{:S(2)}, u32[]{:S(2)}) collective-permute-start(bf16[400,128]{1,0:T(8,128)(2,1)S(1)} %get-tuple-element.144), channel_id=1, source_target_pairs={{0,7},{1,6},{2,5},{3,4},{4,3},{5,2},{6,1},{7,0},{8,15},{9,14},{10,... | collective-permute-start | bytes 307208 | tf_op jit(solution)/shard_map/ppermute | solution.py:416
  136.4 18.5 %collective-permute-start.26 = (s16[408,128]{1,0:T(8,128)(2,1)S(1)}, s16[408,128]{1,0:T(8,128)(2,1)S(1)}, u32[]{:S(2)}, u32[]{:S(2)}) collective-permute-start(s16[408,128]{1,0:T(8,128)(2,1)S(1)} %get-tuple-element.176), channel_id=1, source_target_pairs={{0,31},{1,30},{2,29},{3,28},{4,27},{5,26},{6,25},{7,24},{8,23},{9,... | collective-permute-start | bytes 313352 | tf_op jit(solution)/shard_map/ppermute | solution.py:416
  138.5 16.5 %collective-permute-start.15 = (s16[408,128]{1,0:T(8,128)(2,1)S(1)}, s16[408,128]{1,0:T(8,128)(2,1)S(1)}, u32[]{:S(2)}, u32[]{:S(2)}) collective-permute-start(s16[408,128]{1,0:T(8,128)(2,1)S(1)} %get-tuple-element.155), channel_id=1, source_target_pairs={{0,28},{1,29},{2,30},{3,31},{4,24},{5,25},{6,26},{7,27},{8,20},{9,... | collective-permute-start | bytes 313352 | tf_op jit(solution)/shard_map/ppermute | solution.py:416
  140.6 17.1 %collective-permute-start.31 = (s16[408,128]{1,0:T(8,128)(2,1)S(1)}, s16[408,128]{1,0:T(8,128)(2,1)S(1)}, u32[]{:S(2)}, u32[]{:S(2)}) collective-permute-start(s16[408,128]{1,0:T(8,128)(2,1)S(1)} %get-tuple-element.186), channel_id=1, source_target_pairs={{0,30},{1,31},{2,28},{3,29},{4,26},{5,27},{6,24},{7,25},{8,22},{9,... | collective-permute-start | bytes 313352 | tf_op jit(solution)/shard_map/ppermute | solution.py:416
  143.3 16.7 %collective-permute-start.33 = (s16[408,128]{1,0:T(8,128)(2,1)S(1)}, s16[408,128]{1,0:T(8,128)(2,1)S(1)}, u32[]{:S(2)}, u32[]{:S(2)}) collective-permute-start(s16[408,128]{1,0:T(8,128)(2,1)S(1)} %get-tuple-element.191), channel_id=1, source_target_pairs={{0,29},{1,28},{2,31},{3,30},{4,25},{5,24},{6,27},{7,26},{8,21},{9,... | collective-permute-start | bytes 313352 | tf_op jit(solution)/shard_map/ppermute | solution.py:416
  153.5 8.8 %collective-permute-start.14 = (s16[408,128]{1,0:T(8,128)(2,1)S(1)}, s16[408,128]{1,0:T(8,128)(2,1)S(1)}, u32[]{:S(2)}, u32[]{:S(2)}) collective-permute-start(s16[408,128]{1,0:T(8,128)(2,1)S(1)} %get-tuple-element.146), channel_id=1, source_target_pairs={{0,27},{1,26},{2,25},{3,24},{4,31},{5,30},{6,29},{7,28},{8,19},{9,... | collective-permute-start | bytes 313352 | tf_op jit(solution)/shard_map/ppermute | solution.py:416
  155.0 9.3 %collective-permute-start.27 = (s16[408,128]{1,0:T(8,128)(2,1)S(1)}, s16[408,128]{1,0:T(8,128)(2,1)S(1)}, u32[]{:S(2)}, u32[]{:S(2)}) collective-permute-start(s16[408,128]{1,0:T(8,128)(2,1)S(1)} %get-tuple-element.177), channel_id=1, source_target_pairs={{0,15},{1,14},{2,13},{3,12},{4,11},{5,10},{6,9},{7,8},{8,7},{9,6},... | collective-permute-start | bytes 313352 | tf_op jit(solution)/shard_map/ppermute | solution.py:416
  155.0 16.6 %collective-permute-start.16 = (s16[408,128]{1,0:T(8,128)(2,1)S(1)}, s16[408,128]{1,0:T(8,128)(2,1)S(1)}, u32[]{:S(2)}, u32[]{:S(2)}) collective-permute-start(s16[408,128]{1,0:T(8,128)(2,1)S(1)} %get-tuple-element.156), channel_id=1, source_target_pairs={{0,25},{1,24},{2,27},{3,26},{4,29},{5,28},{6,31},{7,30},{8,17},{9,... | collective-permute-start | bytes 313352 | tf_op jit(solution)/shard_map/ppermute | solution.py:416
  157.7 14.4 %collective-permute-start.32 = (s16[408,128]{1,0:T(8,128)(2,1)S(1)}, s16[408,128]{1,0:T(8,128)(2,1)S(1)}, u32[]{:S(2)}, u32[]{:S(2)}) collective-permute-start(s16[408,128]{1,0:T(8,128)(2,1)S(1)} %get-tuple-element.187), channel_id=1, source_target_pairs={{0,26},{1,27},{2,24},{3,25},{4,30},{5,31},{6,28},{7,29},{8,18},{9,... | collective-permute-start | bytes 313352 | tf_op jit(solution)/shard_map/ppermute | solution.py:416
  160.0 13.3 %collective-permute-start.34 = (s16[408,128]{1,0:T(8,128)(2,1)S(1)}, s16[408,128]{1,0:T(8,128)(2,1)S(1)}, u32[]{:S(2)}, u32[]{:S(2)}) collective-permute-start(s16[408,128]{1,0:T(8,128)(2,1)S(1)} %get-tuple-element.192), channel_id=1, source_target_pairs={{0,14},{1,15},{2,12},{3,13},{4,10},{5,11},{6,8},{7,9},{8,6},{9,7},... | collective-permute-start | bytes 313352 | tf_op jit(solution)/shard_map/ppermute | solution.py:416
  162.3 17.0 %collective-permute-start.21 = (s16[408,128]{1,0:T(8,128)(2,1)S(1)}, s16[408,128]{1,0:T(8,128)(2,1)S(1)}, u32[]{:S(2)}, u32[]{:S(2)}) collective-permute-start(s16[408,128]{1,0:T(8,128)(2,1)S(1)} %get-tuple-element.165), channel_id=1, source_target_pairs={{0,13},{1,12},{2,15},{3,14},{4,9},{5,8},{6,11},{7,10},{8,5},{9,4},... | collective-permute-start | bytes 313352 | tf_op jit(solution)/shard_map/ppermute | solution.py:416
  164.2 15.2 %collective-permute-start.28 = (s16[408,128]{1,0:T(8,128)(2,1)S(1)}, s16[408,128]{1,0:T(8,128)(2,1)S(1)}, u32[]{:S(2)}, u32[]{:S(2)}) collective-permute-start(s16[408,128]{1,0:T(8,128)(2,1)S(1)} %get-tuple-element.178), channel_id=1, source_target_pairs={{0,24},{1,25},{2,26},{3,27},{4,28},{5,29},{6,30},{7,31},{8,16},{9,... | collective-permute-start | bytes 313352 | tf_op jit(solution)/shard_map/ppermute | solution.py:416
  171.6 14.0 %collective-permute-start.17 = (s16[408,128]{1,0:T(8,128)(2,1)S(1)}, s16[408,128]{1,0:T(8,128)(2,1)S(1)}, u32[]{:S(2)}, u32[]{:S(2)}) collective-permute-start(s16[408,128]{1,0:T(8,128)(2,1)S(1)} %get-tuple-element.157), channel_id=1, source_target_pairs={{0,11},{1,10},{2,9},{3,8},{4,15},{5,14},{6,13},{7,12},{8,3},{9,2},... | collective-permute-start | bytes 313352 | tf_op jit(solution)/shard_map/ppermute | solution.py:416
  172.1 14.8 %collective-permute-start.35 = (s16[408,128]{1,0:T(8,128)(2,1)S(1)}, s16[408,128]{1,0:T(8,128)(2,1)S(1)}, u32[]{:S(2)}, u32[]{:S(2)}) collective-permute-start(s16[408,128]{1,0:T(8,128)(2,1)S(1)} %get-tuple-element.198), channel_id=1, source_target_pairs={{0,12},{1,13},{2,14},{3,15},{4,8},{5,9},{6,10},{7,11},{8,4},{9,5},... | collective-permute-start | bytes 313352 | tf_op jit(solution)/shard_map/ppermute | solution.py:416
  173.3 15.4 %collective-permute-start.36 = (s16[408,128]{1,0:T(8,128)(2,1)S(1)}, s16[408,128]{1,0:T(8,128)(2,1)S(1)}, u32[]{:S(2)}, u32[]{:S(2)}) collective-permute-start(s16[408,128]{1,0:T(8,128)(2,1)S(1)} %get-tuple-element.201), channel_id=1, source_target_pairs={{0,23},{1,22},{2,21},{3,20},{4,19},{5,18},{6,17},{7,16},{8,31},{9,... | collective-permute-start | bytes 313352 | tf_op jit(solution)/shard_map/ppermute | solution.py:416
  179.3 10.6 %collective-permute-start.22 = (s16[408,128]{1,0:T(8,128)(2,1)S(1)}, s16[408,128]{1,0:T(8,128)(2,1)S(1)}, u32[]{:S(2)}, u32[]{:S(2)}) collective-permute-start(s16[408,128]{1,0:T(8,128)(2,1)S(1)} %get-tuple-element.166), channel_id=1, source_target_pairs={{0,22},{1,23},{2,20},{3,21},{4,18},{5,19},{6,16},{7,17},{8,30},{9,... | collective-permute-start | bytes 313352 | tf_op jit(solution)/shard_map/ppermute | solution.py:416
  179.5 11.8 %collective-permute-start.29 = (s16[408,128]{1,0:T(8,128)(2,1)S(1)}, s16[408,128]{1,0:T(8,128)(2,1)S(1)}, u32[]{:S(2)}, u32[]{:S(2)}) collective-permute-start(s16[408,128]{1,0:T(8,128)(2,1)S(1)} %get-tuple-element.179), channel_id=1, source_target_pairs={{0,10},{1,11},{2,8},{3,9},{4,14},{5,15},{6,12},{7,13},{8,2},{9,3},... | collective-permute-start | bytes 313352 | tf_op jit(solution)/shard_map/ppermute | solution.py:416
  185.6 12.2 %collective-permute-start.18 = (s16[408,128]{1,0:T(8,128)(2,1)S(1)}, s16[408,128]{1,0:T(8,128)(2,1)S(1)}, u32[]{:S(2)}, u32[]{:S(2)}) collective-permute-start(s16[408,128]{1,0:T(8,128)(2,1)S(1)} %get-tuple-element.158), channel_id=1, source_target_pairs={{0,20},{1,21},{2,22},{3,23},{4,16},{5,17},{6,18},{7,19},{8,28},{9,... | collective-permute-start | bytes 313352 | tf_op jit(solution)/shard_map/ppermute | solution.py:416
  186.9 12.4 %collective-permute-start.39 = (s16[408,128]{1,0:T(8,128)(2,1)S(1)}, s16[408,128]{1,0:T(8,128)(2,1)S(1)}, u32[]{:S(2)}, u32[]{:S(2)}) collective-permute-start(s16[408,128]{1,0:T(8,128)(2,1)S(1)} %get-tuple-element.213), channel_id=1, source_target_pairs={{0,21},{1,20},{2,23},{3,22},{4,17},{5,16},{6,19},{7,18},{8,29},{9,... | collective-permute-start | bytes 313352 | tf_op jit(solution)/shard_map/ppermute | solution.py:416
  188.7 12.5 %collective-permute-start.42 = (s16[408,128]{1,0:T(8,128)(2,1)S(1)}, s16[408,128]{1,0:T(8,128)(2,1)S(1)}, u32[]{:S(2)}, u32[]{:S(2)}) collective-permute-start(s16[408,128]{1,0:T(8,128)(2,1)S(1)} %get-tuple-element.221), channel_id=1, source_target_pairs={{0,9},{1,8},{2,11},{3,10},{4,13},{5,12},{6,15},{7,14},{8,1},{9,0},... | collective-permute-start | bytes 313352 | tf_op jit(solution)/shard_map/ppermute | solution.py:416
  189.9 11.3 %collective-permute-start.23 = (s16[408,128]{1,0:T(8,128)(2,1)S(1)}, s16[408,128]{1,0:T(8,128)(2,1)S(1)}, u32[]{:S(2)}, u32[]{:S(2)}) collective-permute-start(s16[408,128]{1,0:T(8,128)(2,1)S(1)} %get-tuple-element.167), channel_id=1, source_target_pairs={{0,8},{1,9},{2,10},{3,11},{4,12},{5,13},{6,14},{7,15},{8,0},{9,1},... | collective-permute-start | bytes 313352 | tf_op jit(solution)/shard_map/ppermute | solution.py:416
  191.3 15.2 %collective-permute-start.30 = (s16[408,128]{1,0:T(8,128)(2,1)S(1)}, s16[408,128]{1,0:T(8,128)(2,1)S(1)}, u32[]{:S(2)}, u32[]{:S(2)}) collective-permute-start(s16[408,128]{1,0:T(8,128)(2,1)S(1)} %get-tuple-element.180), channel_id=1, source_target_pairs={{0,19},{1,18},{2,17},{3,16},{4,23},{5,22},{6,21},{7,20},{8,27},{9,... | collective-permute-start | bytes 313352 | tf_op jit(solution)/shard_map/ppermute | solution.py:416
  197.8 10.0 %collective-permute-start.19 = (s16[408,128]{1,0:T(8,128)(2,1)S(1)}, s16[408,128]{1,0:T(8,128)(2,1)S(1)}, u32[]{:S(2)}, u32[]{:S(2)}) collective-permute-start(s16[408,128]{1,0:T(8,128)(2,1)S(1)} %get-tuple-element.159), channel_id=1, source_target_pairs={{0,6},{1,7},{2,4},{3,5},{4,2},{5,3},{6,0},{7,1},{8,14},{9,15},{10,... | collective-permute-start | bytes 313352 | tf_op jit(solution)/shard_map/ppermute | solution.py:416
  199.3 8.7 %collective-permute-start.40 = (s16[408,128]{1,0:T(8,128)(2,1)S(1)}, s16[408,128]{1,0:T(8,128)(2,1)S(1)}, u32[]{:S(2)}, u32[]{:S(2)}) collective-permute-start(s16[408,128]{1,0:T(8,128)(2,1)S(1)} %get-tuple-element.214), channel_id=1, source_target_pairs={{0,7},{1,6},{2,5},{3,4},{4,3},{5,2},{6,1},{7,0},{8,15},{9,14},{10,... | collective-permute-start | bytes 313352 | tf_op jit(solution)/shard_map/ppermute | solution.py:416
  201.2 10.0 %collective-permute-start.43 = (s16[408,128]{1,0:T(8,128)(2,1)S(1)}, s16[408,128]{1,0:T(8,128)(2,1)S(1)}, u32[]{:S(2)}, u32[]{:S(2)}) collective-permute-start(s16[408,128]{1,0:T(8,128)(2,1)S(1)} %get-tuple-element.222), channel_id=1, source_target_pairs={{0,18},{1,19},{2,16},{3,17},{4,22},{5,23},{6,20},{7,21},{8,26},{9,... | collective-permute-start | bytes 313352 | tf_op jit(solution)/shard_map/ppermute | solution.py:416
  201.2 11.1 %collective-permute-start.24 = (s16[408,128]{1,0:T(8,128)(2,1)S(1)}, s16[408,128]{1,0:T(8,128)(2,1)S(1)}, u32[]{:S(2)}, u32[]{:S(2)}) collective-permute-start(s16[408,128]{1,0:T(8,128)(2,1)S(1)} %get-tuple-element.168), channel_id=1, source_target_pairs={{0,17},{1,16},{2,19},{3,18},{4,21},{5,20},{6,23},{7,22},{8,25},{9,... | collective-permute-start | bytes 313352 | tf_op jit(solution)/shard_map/ppermute | solution.py:416
  206.5 9.5 %collective-permute-start.37 = (s16[408,128]{1,0:T(8,128)(2,1)S(1)}, s16[408,128]{1,0:T(8,128)(2,1)S(1)}, u32[]{:S(2)}, u32[]{:S(2)}) collective-permute-start(s16[408,128]{1,0:T(8,128)(2,1)S(1)} %get-tuple-element.208), channel_id=1, source_target_pairs={{0,5},{1,4},{2,7},{3,6},{4,1},{5,0},{6,3},{7,2},{8,13},{9,12},{10,... | collective-permute-start | bytes 313352 | tf_op jit(solution)/shard_map/ppermute | solution.py:416
  207.9 10.4 %collective-permute-start.20 = (s16[408,128]{1,0:T(8,128)(2,1)S(1)}, s16[408,128]{1,0:T(8,128)(2,1)S(1)}, u32[]{:S(2)}, u32[]{:S(2)}) collective-permute-start(s16[408,128]{1,0:T(8,128)(2,1)S(1)} %get-tuple-element.160), channel_id=1, source_target_pairs={{0,3},{1,2},{2,1},{3,0},{4,7},{5,6},{6,5},{7,4},{8,11},{9,10},{10,... | collective-permute-start | bytes 313352 | tf_op jit(solution)/shard_map/ppermute | solution.py:416
  208.0 9.2 %collective-permute-start.41 = (s16[408,128]{1,0:T(8,128)(2,1)S(1)}, s16[408,128]{1,0:T(8,128)(2,1)S(1)}, u32[]{:S(2)}, u32[]{:S(2)}) collective-permute-start(s16[408,128]{1,0:T(8,128)(2,1)S(1)} %get-tuple-element.215), channel_id=1, source_target_pairs={{0,16},{1,17},{2,18},{3,19},{4,20},{5,21},{6,22},{7,23},{8,24},{9,... | collective-permute-start | bytes 313352 | tf_op jit(solution)/shard_map/ppermute | solution.py:416
  211.2 6.0 %collective-permute-start.44 = (s16[408,128]{1,0:T(8,128)(2,1)S(1)}, s16[408,128]{1,0:T(8,128)(2,1)S(1)}, u32[]{:S(2)}, u32[]{:S(2)}) collective-permute-start(s16[408,128]{1,0:T(8,128)(2,1)S(1)} %get-tuple-element.228), channel_id=1, source_target_pairs={{0,4},{1,5},{2,6},{3,7},{4,0},{5,1},{6,2},{7,3},{8,12},{9,13},{10,... | collective-permute-start | bytes 313352 | tf_op jit(solution)/shard_map/ppermute | solution.py:416
  212.3 6.8 %collective-permute-start.25 = (s16[408,128]{1,0:T(8,128)(2,1)S(1)}, s16[408,128]{1,0:T(8,128)(2,1)S(1)}, u32[]{:S(2)}, u32[]{:S(2)}) collective-permute-start(s16[408,128]{1,0:T(8,128)(2,1)S(1)} %get-tuple-element.169), channel_id=1, source_target_pairs={{0,2},{1,3},{2,0},{3,1},{4,6},{5,7},{6,4},{7,5},{8,10},{9,11},{10,... | collective-permute-start | bytes 313352 | tf_op jit(solution)/shard_map/ppermute | solution.py:416
  216.0 3.2 %collective-permute-start.38 = (s16[408,128]{1,0:T(8,128)(2,1)S(1)}, s16[408,128]{1,0:T(8,128)(2,1)S(1)}, u32[]{:S(2)}, u32[]{:S(2)}) collective-permute-start(s16[408,128]{1,0:T(8,128)(2,1)S(1)} %get-tuple-element.209), channel_id=1, source_target_pairs={{0,1},{1,0},{2,3},{3,2},{4,5},{5,4},{6,7},{7,6},{8,9},{9,8},{10,11... | collective-permute-start | bytes 313352 | tf_op jit(solution)/shard_map/ppermute | solution.py:416
  217.2 2.0 copy-start
  217.2 2.0 copy-start.1

commit v12 on v11

--- a/solution.py
+++ b/solution.py
@@ -9,7 +9,7 @@
 
 BLK = 128
 TAIL = 8
-CUTS = (1, 2, 2, 2, 1)
+CUTS = (3, 3, 4, 4, 2)
 STEPS = (3, 6, 8)
 WINDOW = 5
 TILE = 256
@@ -254,8 +254,7 @@
 def pack_kernel(first, bounds, peers, rank_ref, live_ref, npos, *refs):
     chunks, grads = refs[: len(bounds)], refs[len(bounds) : len(bounds) + peers]
     outs, total, slot = refs[len(bounds) + peers : -2], refs[-2], refs[-1]
-    width = slot.shape[0]
-    total[:width], total[width:] = split(sum(g[...].astype(F32) for g in grads))
+    total[...] = sum(g[...].astype(F32) for g in grads).astype(BF16)
     for k, out_ref in enumerate(outs):
         alive = live_ref[first + k] > 0
         rank = rank_ref[first + k]
@@ -271,8 +270,8 @@
         def _():
             index = lax.broadcasted_iota(jnp.int32, (BLK, npos.shape[1]), 0) + rank * BLK
             hot = jnp.where(index == npos[...], 1.0, 0.0).astype(BF16)
-            both = lax.dot_general(total[...], hot, NT, preferred_element_type=F32)
-            encode(slot[...] + (both[:width] + both[width:]), out_ref)
+            part = lax.dot_general(total[...], hot, NT, preferred_element_type=F32)
+            encode(slot[...] + part, out_ref)
 
         @pl.when(jnp.logical_not(alive))
         def _():
@@ -287,7 +286,7 @@
         in_specs=[smem(), smem()] + [whole()] * (1 + len(chunks) + len(grad_negs)),
         out_specs=(whole(),) * group,
         scratch_shapes=[
-            pltpu.VMEM((2 * width, npos.shape[1]), BF16),
+            pltpu.VMEM((width, npos.shape[1]), BF16),
             pltpu.VMEM((width, BLK), F32),
         ],
         compiler_params=params(0),

time: 224 us -> 227 us (1.013)
  starting transfers between devices: 71.4 us -> 77.4 us
  waiting for transfers between devices: 68.5 us -> 66.1 us
    ppermute x45, starting transfers between devices: 60.6 us -> 66.6 us  [swap(): return lax.ppermute(x, axis, [(i, i ^ shift) for i in range(count)])]
    ppermute x45, waiting for transfers between devices: 16.5 us -> 14 us  [swap(): return lax.ppermute(x, axis, [(i, i ^ shift) for i in range(count)])]
  transfers between devices with their start and end apart: 47 -> 47, of which waited for: 12 -> 12; matrix products, arithmetic and copies ran while one was open for 13% -> 13% of each run, Pallas kernels for 16% -> 15%
where the time goes in v12:
time: 227 us; the launch traced here: 226 us
  starting transfers between devices  77.4 us (34%)
  waiting for transfers between devices  66.1 us (29%)
  Pallas kernels  50.9 us (22%)
  local copies, waits for them, and re-layouts  26.7 us (12%)
  other arithmetic  3.85 us (2%)
    ppermute x45, starting transfers between devices, swap(): return lax.ppermute(x, axis, [(i, i ^ shift) for i in range(count)])  66.6 us
    all_to_all x1, waiting for transfers between devices, per_device(): lax.all_to_all(outgoing, AXES, split_axis=0, concat_axis=0, tiled=True)  47.1 us
    gather x2, local copies, waits for them, and re-layouts, per_device(): operator = relations[rel_ids].T  16.7 us
    pallas_call x3, Pallas kernels, scatter(): pl.pallas_call(functools.partial(scatter_kernel, first * BLK), out_shape=...  15.1 us
    ppermute x45, waiting for transfers between devices, swap(): return lax.ppermute(x, axis, [(i, i ^ shift) for i in range(count)])  14 us
    pallas_call x5, Pallas kernels, pack(): pl.pallas_call(functools.partial(pack_kernel, first, tuple(bounds), len(g...  9.08 us
    unnamed x15, local copies, waits for them, and re-layouts  8.62 us
    pallas_call x1, Pallas kernels, gather_edges(): pl.pallas_call(edge_kernel, grid=(edges // tile,), out_shape=(jax.ShapeDt...  7.8 us
  transfers between devices with their start and end apart: 47, of which 12 were waited for; matrix products, arithmetic and copies ran while one was open for 13% of the time, Pallas kernels for 15%

profile of v12, /device:TPU:0, one launch (start us, length us, event | category | flops | bytes accessed | tf_op | source)
XLA Modules:
  0.0 226.2 jit_solution(18311534569905323056)
XLA Ops:
  0.6 1.3 copy.21
  2.0 7.3 %all-to-all-start = ((s32[32,1,1]{2,1,0:T(1,128)}), s32[32,1,1]{2,1,0:T(1,128)S(1)}, u32[]{:S(2)}, u32[]{:S(2)}) async-start(s32[32,1,1]{2,1,0:T(1,128)} %copy.21), calls=%async_computation | async-start | bytes 32768 | tf_op jit(solution)/shard_map/all_to_all | solution.py:371
  9.3 2.1 bitcast_bitcast_fusion.blocks_ref
  11.4 4.9 %all-to-all-done.asked_ref = s32[32,1,1]{2,1,0:T(1,128)S(1)} async-done(((s32[32,1,1]{2,1,0:T(1,128)}), s32[32,1,1]{2,1,0:T(1,128)S(1)}, u32[]{:S(2)}, u32[]{:S(2)}) %all-to-all-start) | async-done | bytes 160 | tf_op jit(solution)/shard_map/all_to_all | solution.py:371
  16.3 2.5 %select.19 = bf16[32,400,128]{2,1,0:T(8,128)(2,1)} custom-call(s32[32,1,1]{2,1,0:T(1,128)S(1)} %all-to-all-done.asked_ref, bf16[16,400,128]{2,1,0:T(8,128)(2,1)S(1)} %bitcast_bitcast_fusion.blocks_ref), custom_call_target="tpu_custom_call" | custom-call | tf_op jit(solution)/shard_map/select/pallas_call | solution.py:65
  18.9 3.6 %all-to-all-start.1 = ((bf16[32,400,128]{2,1,0:T(8,128)(2,1)}), bf16[32,400,128]{2,1,0:T(8,128)(2,1)}, u32[]{:S(2)}, u32[]{:S(2)}) async-start(bf16[32,400,128]{2,1,0:T(8,128)(2,1)} %select.19), calls=%async_computation.1 | async-start | bytes 6553600 | tf_op jit(solution)/shard_map/all_to_all | solution.py:377
  22.4 8.6 %copy.23 = f32[4096,400]{1,0:T(8,128)} copy(f32[4096,400]{0,1:T(8,128)} %param.11) | data formatting | bytes 13107200 | tf_op args[2]
  31.0 12.9 %gather_fusion = f32[2048,400]{1,0:T(8,128)} fusion(f32[4096,400]{1,0:T(8,128)} %copy.23, s32[2048]{0:T(1024)S(1)} %fusion.3), kind=kCustom, calls=%fused_computation | custom fusion | bytes 6561792 | tf_op jit(solution)/shard_map/gather | solution.py:378
  44.0 3.8 %copy.24 = f32[2048,400]{0,1:T(8,128)S(1)} copy(f32[2048,400]{1,0:T(8,128)} %gather_fusion) | data formatting | bytes 6553600 | tf_op jit(solution)/shard_map/gather | solution.py:378
  49.6 47.1 %all-to-all-done.1.fetched = bf16[32,400,128]{2,1,0:T(8,128)(2,1)} async-done(((bf16[32,400,128]{2,1,0:T(8,128)(2,1)}), bf16[32,400,128]{2,1,0:T(8,128)(2,1)}, u32[]{:S(2)}, u32[]{:S(2)}) %all-to-all-start.1) | async-done | bytes 3276832 | tf_op jit(solution)/shard_map/all_to_all | solution.py:377
  96.7 2.6 %gather_negs.1 = (bf16[400,128]{1,0:T(8,128)(2,1)S(1)}, bf16[400,2048]{1,0:T(8,128)(2,1)S(1)}) custom-call(s32[16]{0:T(128)S(1)} %select_reduce_fusion.7.live_ref, bf16[32,400,128]{2,1,0:T(8,128)(2,1)} %all-to-all-done.1.fetched, s32[1,128]{1,0:T(1,128)S(1)} %fusion.10.pos_ref.npos), custom_call_target="tpu_custom_call" | custom-call | tf_op jit(solution)/shard_map/gather_negs/pallas_call | solution.py:115
  99.5 1.3 collective-permute-start.1
  101.3 1.2 collective-permute-start.3
  103.0 2.1 collective-permute-start.5
  105.2 0.9 collective-permute-start.6
  106.1 7.8 %gather_edges.1 = (bf16[400,2048]{1,0:T(8,128)(2,1)S(1)}, bf16[400,2048]{1,0:T(8,128)(2,1)S(1)}, f32[1,2048]{1,0:T(1,128)S(1)}) custom-call(bf16[400,2048]{1,0:T(8,128)(2,1)S(1)} %get-tuple-element.127.rows, s32[1,2048]{1,0:T(1,128)S(1)} %bitcast.20, s32[1,2048]{1,0:T(1,128)S(1)} %bitcast.24, f32[400,2048]{1,0:T(8,128)S(1)} %bitcast.17), custom_call_target="tpu_custom_call" | custom-call | flops 104857600 | bytes 204800 | tf_op jit(solution)/shard_map/gather_edges/pallas_call | solution.py:144
  114.0 6.2 %score.1 = (bf16[2,400,2048]{2,1,0:T(8,128)(2,1)S(1)}, bf16[2,400,2048]{2,1,0:T(8,128)(2,1)S(1)}, bf16[400,128]{1,0:T(8,128)(2,1)S(1)}, bf16[400,128]{1,0:T(8,12...) custom-call(bf16[400,128]{1,0:T(8,128)(2,1)S(1)} %get-tuple-element., ...), custom_call_target="tpu_custom_call" | custom-call | flops 78643200 | bytes 153600 | tf_op jit(solution)/shard_map/score/pallas_call | solution.py:191
  120.2 1.4 collective-permute-start.7
  122.1 0.9 collective-permute-start.9
  123.5 1.5 collective-permute-start.11
  125.1 0.8 collective-permute-start.12
  125.9 1.4 collective-permute-done.8.refs_4_.refs_3_.refs_5_
  127.4 5.7 %scatter.3.refs_0_ = f32[400,768]{1,0:T(8,128)S(1)} custom-call(bf16[2,400,2048]{2,1,0:T(8,128)(2,1)S(1)} %get-tuple-element.134.gs_ref, bf16[2,400,2048]{2,1,0:T(8,128)(2,1)S(1)} %get-tuple-element.135.gd_ref, s32[1,2048]{1,0:T(1,128)S(1)} %bitcast.21, s32[1,2048]{1,0:T(1,128)S(1)} %bitcast.25), custom_call_target="tpu_custom_call" | custom-call | flops 39321600 | bytes 76800 | tf_op jit(solution)/shard_map/scatter/pallas_call | solution.py:228
  133.2 1.7 collective-permute-done.11.refs_7_.refs_6_.refs_8_
  134.8 1.9 pack.6
  136.7 1.8 collective-permute-start.26
  138.5 1.9 collective-permute-start.15
  140.4 2.7 %collective-permute-start.31 = (s16[408,128]{1,0:T(8,128)(2,1)S(1)}, s16[408,128]{1,0:T(8,128)(2,1)S(1)}, u32[]{:S(2)}, u32[]{:S(2)}) collective-permute-start(s16[408,128]{1,0:T(8,128)(2,1)S(1)} %get-tuple-element.183), channel_id=1, source_target_pairs={{0,30},{1,31},{2,28},{3,29},{4,26},{5,27},{6,24},{7,25},{8,22},{9,... | collective-permute-start | bytes 313352 | tf_op jit(solution)/shard_map/ppermute | solution.py:415
  143.1 3.2 %collective-permute-start.33 = (s16[408,128]{1,0:T(8,128)(2,1)S(1)}, s16[408,128]{1,0:T(8,128)(2,1)S(1)}, u32[]{:S(2)}, u32[]{:S(2)}) collective-permute-start(s16[408,128]{1,0:T(8,128)(2,1)S(1)} %get-tuple-element.188), channel_id=1, source_target_pairs={{0,29},{1,28},{2,31},{3,30},{4,25},{5,24},{6,27},{7,26},{8,21},{9,... | collective-permute-start | bytes 313352 | tf_op jit(solution)/shard_map/ppermute | solution.py:415
  146.3 1.9 collective-permute-start.14
  148.2 5.7 %scatter.4.refs_1_ = f32[400,768]{1,0:T(8,128)S(1)} custom-call(bf16[2,400,2048]{2,1,0:T(8,128)(2,1)S(1)} %get-tuple-element.134.gs_ref, bf16[2,400,2048]{2,1,0:T(8,128)(2,1)S(1)} %get-tuple-element.135.gd_ref, s32[1,2048]{1,0:T(1,128)S(1)} %bitcast.22, s32[1,2048]{1,0:T(1,128)S(1)} %bitcast.26), custom_call_target="tpu_custom_call" | custom-call | flops 39321600 | bytes 76800 | tf_op jit(solution)/shard_map/scatter/pallas_call | solution.py:228
  153.9 1.7 pack.5
  155.6 1.6 collective-permute-start.16
  157.2 2.6 %collective-permute-start.32 = (s16[408,128]{1,0:T(8,128)(2,1)S(1)}, s16[408,128]{1,0:T(8,128)(2,1)S(1)}, u32[]{:S(2)}, u32[]{:S(2)}) collective-permute-start(s16[408,128]{1,0:T(8,128)(2,1)S(1)} %get-tuple-element.184), channel_id=1, source_target_pairs={{0,26},{1,27},{2,24},{3,25},{4,30},{5,31},{6,28},{7,29},{8,18},{9,... | collective-permute-start | bytes 313352 | tf_op jit(solution)/shard_map/ppermute | solution.py:415
  159.9 3.0 %collective-permute-start.34 = (s16[408,128]{1,0:T(8,128)(2,1)S(1)}, s16[408,128]{1,0:T(8,128)(2,1)S(1)}, u32[]{:S(2)}, u32[]{:S(2)}) collective-permute-start(s16[408,128]{1,0:T(8,128)(2,1)S(1)} %get-tuple-element.189), channel_id=1, source_target_pairs={{0,14},{1,15},{2,12},{3,13},{4,10},{5,11},{6,8},{7,9},{8,6},{9,7},... | collective-permute-start | bytes 313352 | tf_op jit(solution)/shard_map/ppermute | solution.py:415
  162.9 6.4 %collective-permute-start.21 = (s16[408,128]{1,0:T(8,128)(2,1)S(1)}, s16[408,128]{1,0:T(8,128)(2,1)S(1)}, u32[]{:S(2)}, u32[]{:S(2)}) collective-permute-start(s16[408,128]{1,0:T(8,128)(2,1)S(1)} %get-tuple-element.164), channel_id=1, source_target_pairs={{0,13},{1,12},{2,15},{3,14},{4,9},{5,8},{6,11},{7,10},{8,5},{9,4},... | collective-permute-start | bytes 313352 | tf_op jit(solution)/shard_map/ppermute | solution.py:415
  169.2 1.7 collective-permute-start.28
  170.9 3.8 %scatter.5.refs_2_ = f32[400,512]{1,0:T(8,128)S(1)} custom-call(bf16[2,400,2048]{2,1,0:T(8,128)(2,1)S(1)} %get-tuple-element.134.gs_ref, bf16[2,400,2048]{2,1,0:T(8,128)(2,1)S(1)} %get-tuple-element.135.gd_ref, s32[1,2048]{1,0:T(1,128)S(1)} %bitcast.23, s32[1,2048]{1,0:T(1,128)S(1)} %bitcast.27), custom_call_target="tpu_custom_call" | custom-call | flops 26214400 | bytes 51200 | tf_op jit(solution)/shard_map/scatter/pallas_call | solution.py:228
  174.7 2.4 %pack.9 = (s16[408,128]{1,0:T(8,128)(2,1)S(1)}, s16[408,128]{1,0:T(8,128)(2,1)S(1)}, s16[408,128]{1,0:T(8,128)(2,1)S(1)}, s16[408,128]{1,0:T(8,128)(2,1)S(1)}, s...) custom-call(s32[32]{0:T(128)S(1)} %select_reduce_fusion.5.rank_ref, ...), custom_call_target="tpu_custom_call" | custom-call | flops 3276800 | bytes 6400 | tf_op jit(solution)/shard_map/pack/pallas_call | solution.py:283
  177.2 0.9 collective-permute-start.35
  178.1 2.5 %collective-permute-start.36 = (s16[408,128]{1,0:T(8,128)(2,1)S(1)}, s16[408,128]{1,0:T(8,128)(2,1)S(1)}, u32[]{:S(2)}, u32[]{:S(2)}) collective-permute-start(s16[408,128]{1,0:T(8,128)(2,1)S(1)} %get-tuple-element.198), channel_id=1, source_target_pairs={{0,23},{1,22},{2,21},{3,20},{4,19},{5,18},{6,17},{7,16},{8,31},{9,... | collective-permute-start | bytes 313352 | tf_op jit(solution)/shard_map/ppermute | solution.py:415
  180.6 2.8 %collective-permute-start.22 = (s16[408,128]{1,0:T(8,128)(2,1)S(1)}, s16[408,128]{1,0:T(8,128)(2,1)S(1)}, u32[]{:S(2)}, u32[]{:S(2)}) collective-permute-start(s16[408,128]{1,0:T(8,128)(2,1)S(1)} %get-tuple-element.165), channel_id=1, source_target_pairs={{0,22},{1,23},{2,20},{3,21},{4,18},{5,19},{6,16},{7,17},{8,30},{9,... | collective-permute-start | bytes 313352 | tf_op jit(solution)/shard_map/ppermute | solution.py:415
  183.4 1.2 collective-permute-start.29
  184.6 2.0 pack.8
  186.6 1.1 add.71.refs_6_
  187.8 3.6 %collective-permute-start.18 = (s16[408,128]{1,0:T(8,128)(2,1)S(1)}, s16[408,128]{1,0:T(8,128)(2,1)S(1)}, u32[]{:S(2)}, u32[]{:S(2)}) collective-permute-start(s16[408,128]{1,0:T(8,128)(2,1)S(1)} %get-tuple-element.157), channel_id=1, source_target_pairs={{0,20},{1,21},{2,22},{3,23},{4,16},{5,17},{6,18},{7,19},{8,28},{9,... | collective-permute-start | bytes 313352 | tf_op jit(solution)/shard_map/ppermute | solution.py:415
  191.4 2.1 collective-permute-start.42
  193.5 3.9 %collective-permute-done.22.refs_2_ = s16[408,128]{1,0:T(8,128)(2,1)S(1)} collective-permute-done((s16[408,128]{1,0:T(8,128)(2,1)S(1)}, s16[408,128]{1,0:T(8,128)(2,1)S(1)}, u32[]{:S(2)}, u32[]{:S(2)}) %collective-permute-start.22) | collective-permute-done | bytes 104480 | tf_op jit(solution)/shard_map/ppermute | solution.py:415
  197.4 0.9 add.72.refs_8_
  198.3 1.6 collective-permute-done.18.refs_6_
  200.1 0.7 collective-permute-done.39.refs_4_
  200.8 2.1 collective-permute-start.40
  203.0 1.6 collective-permute-start.43
  204.6 2.4 %collective-permute-start.24 = (s16[408,128]{1,0:T(8,128)(2,1)S(1)}, s16[408,128]{1,0:T(8,128)(2,1)S(1)}, u32[]{:S(2)}, u32[]{:S(2)}) collective-permute-start(s16[408,128]{1,0:T(8,128)(2,1)S(1)} %get-tuple-element.167), channel_id=1, source_target_pairs={{0,17},{1,16},{2,19},{3,18},{4,21},{5,20},{6,23},{7,22},{8,25},{9,... | collective-permute-start | bytes 313352 | tf_op jit(solution)/shard_map/ppermute | solution.py:415
  207.2 1.1 pack.7
  208.3 1.4 collective-permute-start.20
  210.3 1.4 collective-permute-start.41
  211.7 2.5 %collective-permute-done.43.refs_2_ = s16[408,128]{1,0:T(8,128)(2,1)S(1)} collective-permute-done((s16[408,128]{1,0:T(8,128)(2,1)S(1)}, s16[408,128]{1,0:T(8,128)(2,1)S(1)}, u32[]{:S(2)}, u32[]{:S(2)}) %collective-permute-start.43) | collective-permute-done | bytes 104480 | tf_op jit(solution)/shard_map/ppermute | solution.py:415
  214.1 1.2 collective-permute-start.44
  215.3 3.6 %collective-permute-start.25 = (s16[408,128]{1,0:T(8,128)(2,1)S(1)}, s16[408,128]{1,0:T(8,128)(2,1)S(1)}, u32[]{:S(2)}, u32[]{:S(2)}) collective-permute-start(s16[408,128]{1,0:T(8,128)(2,1)S(1)} %get-tuple-element.168), channel_id=1, source_target_pairs={{0,2},{1,3},{2,0},{3,1},{4,6},{5,7},{6,4},{7,5},{8,10},{9,11},{10,... | collective-permute-start | bytes 313352 | tf_op jit(solution)/shard_map/ppermute | solution.py:415
  219.0 1.0 add.73.refs_8_
  220.1 1.0 add.74.refs_4_
  221.1 1.4 collective-permute-done.25.refs_1_
  222.6 3.5 %update.1 = (f32[400,2048]{1,0:T(8,128)}, f32[1,2048]{1,0:T(1,128)}) custom-call(s32[32]{0:T(128)S(1)} %get-tuple-element.120.asked_ref, s16[408,128]{1,0:T(8,128)(2,1)S(1)} %collective-permute-done.20.refs_0_, s16[408,128]{1,0:T(8,128)(2,1)S(1)} %collective-permute-done.25.refs_1_, s16[408,128]{1,0:T(8,128)(2,1)S(1)} %collective-permute-done.38.refs_2_, ...), custom_call_target="tpu_custom_call" | custom-call | flops 819200 | bytes 1600 | tf_op jit(solution)/shard_map/update/pallas_call | solution.py:351
  (83 shorter events, 5.4 us)
Async XLA Ops:
  2.0 14.4 %all-to-all-start = ((s32[32,1,1]{2,1,0:T(1,128)}), s32[32,1,1]{2,1,0:T(1,128)S(1)}, u32[]{:S(2)}, u32[]{:S(2)}) async-start(s32[32,1,1]{2,1,0:T(1,128)} %copy.21), calls=%async_computation | async-start | bytes 32768 | tf_op jit(solution)/shard_map/all_to_all | solution.py:371
  18.9 77.9 %all-to-all-start.1 = ((bf16[32,400,128]{2,1,0:T(8,128)(2,1)}), bf16[32,400,128]{2,1,0:T(8,128)(2,1)}, u32[]{:S(2)}, u32[]{:S(2)}) async-start(bf16[32,400,128]{2,1,0:T(8,128)(2,1)} %select.19), calls=%async_computation.1 | async-start | bytes 6553600 | tf_op jit(solution)/shard_map/all_to_all | solution.py:377
  22.4 8.6 %copy-start.4 = (s32[2048]{0:T(1024)S(1)}, s32[2048]{0:T(1024)}, u32[]{:S(2)}) copy-start(s32[2048]{0:T(1024)} %param.12) | copy-start | bytes 24580
  44.0 3.8 %copy-start.2 = (s32[2048]{0:T(1024)S(1)}, s32[2048]{0:T(1024)}, u32[]{:S(2)}) copy-start(s32[2048]{0:T(1024)} %param.14) | copy-start | bytes 24580
  44.0 4.0 %copy-start.6 = (s32[32]{0:T(128)S(1)}, s32[32]{0:T(128)}, u32[]{:S(2)}) copy-start(s32[32]{0:T(128)} %constant.80.clone) | copy-start | bytes 388
  44.0 4.4 %copy-start.5 = (s32[128]{0:T(128)S(1)}, s32[128]{0:T(128)}, u32[]{:S(2)}) copy-start(s32[128]{0:T(128)} %param.16) | copy-start | bytes 1540
  44.0 4.4 %copy-start.3 = (s32[2048]{0:T(1024)S(1)}, s32[2048]{0:T(1024)}, u32[]{:S(2)}) copy-start(s32[2048]{0:T(1024)} %param.15) | copy-start | bytes 24580
  99.4 3.6 %collective-permute-start = (bf16[400,128]{1,0:T(8,128)(2,1)S(1)}, bf16[400,128]{1,0:T(8,128)(2,1)S(1)}, u32[]{:S(2)}, u32[]{:S(2)}) collective-permute-start(bf16[400,128]{1,0:T(8,128)(2,1)S(1)} %get-tuple-element.126.refs_0_), channel_id=1, source_target_pairs={{0,1},{1,0},{2,3},{3,2},{4,5},{5,4},{6,7},{7,6},{8,9},{9,8},{10,11... | collective-permute-start | bytes 307208 | tf_op jit(solution)/shard_map/ppermute | solution.py:415
  99.5 5.7 %collective-permute-start.1 = (bf16[400,128]{1,0:T(8,128)(2,1)S(1)}, bf16[400,128]{1,0:T(8,128)(2,1)S(1)}, u32[]{:S(2)}, u32[]{:S(2)}) collective-permute-start(bf16[400,128]{1,0:T(8,128)(2,1)S(1)} %get-tuple-element.126.refs_0_), channel_id=1, source_target_pairs={{0,2},{1,3},{2,0},{3,1},{4,6},{5,7},{6,4},{7,5},{8,10},{9,11},{10,... | collective-permute-start | bytes 307208 | tf_op jit(solution)/shard_map/ppermute | solution.py:415
  100.7 13.2 %collective-permute-start.2 = (bf16[400,128]{1,0:T(8,128)(2,1)S(1)}, bf16[400,128]{1,0:T(8,128)(2,1)S(1)}, u32[]{:S(2)}, u32[]{:S(2)}) collective-permute-start(bf16[400,128]{1,0:T(8,128)(2,1)S(1)} %get-tuple-element.126.refs_0_), channel_id=1, source_target_pairs={{0,3},{1,2},{2,1},{3,0},{4,7},{5,6},{6,5},{7,4},{8,11},{9,10},{10,... | collective-permute-start | bytes 307208 | tf_op jit(solution)/shard_map/ppermute | solution.py:415
  101.3 12.6 %collective-permute-start.3 = (bf16[400,128]{1,0:T(8,128)(2,1)S(1)}, bf16[400,128]{1,0:T(8,128)(2,1)S(1)}, u32[]{:S(2)}, u32[]{:S(2)}) collective-permute-start(bf16[400,128]{1,0:T(8,128)(2,1)S(1)} %get-tuple-element.126.refs_0_), channel_id=1, source_target_pairs={{0,4},{1,5},{2,6},{3,7},{4,0},{5,1},{6,2},{7,3},{8,12},{9,13},{10,... | collective-permute-start | bytes 307208 | tf_op jit(solution)/shard_map/ppermute | solution.py:415
  102.5 11.5 %collective-permute-start.4 = (bf16[400,128]{1,0:T(8,128)(2,1)S(1)}, bf16[400,128]{1,0:T(8,128)(2,1)S(1)}, u32[]{:S(2)}, u32[]{:S(2)}) collective-permute-start(bf16[400,128]{1,0:T(8,128)(2,1)S(1)} %get-tuple-element.126.refs_0_), channel_id=1, source_target_pairs={{0,5},{1,4},{2,7},{3,6},{4,1},{5,0},{6,3},{7,2},{8,13},{9,12},{10,... | collective-permute-start | bytes 307208 | tf_op jit(solution)/shard_map/ppermute | solution.py:415
  103.0 11.0 %collective-permute-start.5 = (bf16[400,128]{1,0:T(8,128)(2,1)S(1)}, bf16[400,128]{1,0:T(8,128)(2,1)S(1)}, u32[]{:S(2)}, u32[]{:S(2)}) collective-permute-start(bf16[400,128]{1,0:T(8,128)(2,1)S(1)} %get-tuple-element.126.refs_0_), channel_id=1, source_target_pairs={{0,6},{1,7},{2,4},{3,5},{4,2},{5,3},{6,0},{7,1},{8,14},{9,15},{10,... | collective-permute-start | bytes 307208 | tf_op jit(solution)/shard_map/ppermute | solution.py:415
  105.2 8.8 %collective-permute-start.6 = (bf16[400,128]{1,0:T(8,128)(2,1)S(1)}, bf16[400,128]{1,0:T(8,128)(2,1)S(1)}, u32[]{:S(2)}, u32[]{:S(2)}) collective-permute-start(bf16[400,128]{1,0:T(8,128)(2,1)S(1)} %get-tuple-element.126.refs_0_), channel_id=1, source_target_pairs={{0,7},{1,6},{2,5},{3,4},{4,3},{5,2},{6,1},{7,0},{8,15},{9,14},{10,... | collective-permute-start | bytes 307208 | tf_op jit(solution)/shard_map/ppermute | solution.py:415
  120.2 4.9 %collective-permute-start.7 = (bf16[400,128]{1,0:T(8,128)(2,1)S(1)}, bf16[400,128]{1,0:T(8,128)(2,1)S(1)}, u32[]{:S(2)}, u32[]{:S(2)}) collective-permute-start(bf16[400,128]{1,0:T(8,128)(2,1)S(1)} %get-tuple-element.137), channel_id=1, source_target_pairs={{0,1},{1,0},{2,3},{3,2},{4,5},{5,4},{6,7},{7,6},{8,9},{9,8},{10,11... | collective-permute-start | bytes 307208 | tf_op jit(solution)/shard_map/ppermute | solution.py:415
  121.6 5.7 %collective-permute-start.8 = (bf16[400,128]{1,0:T(8,128)(2,1)S(1)}, bf16[400,128]{1,0:T(8,128)(2,1)S(1)}, u32[]{:S(2)}, u32[]{:S(2)}) collective-permute-start(bf16[400,128]{1,0:T(8,128)(2,1)S(1)} %get-tuple-element.138), channel_id=1, source_target_pairs={{0,2},{1,3},{2,0},{3,1},{4,6},{5,7},{6,4},{7,5},{8,10},{9,11},{10,... | collective-permute-start | bytes 307208 | tf_op jit(solution)/shard_map/ppermute | solution.py:415
  122.1 11.0 %collective-permute-start.9 = (bf16[400,128]{1,0:T(8,128)(2,1)S(1)}, bf16[400,128]{1,0:T(8,128)(2,1)S(1)}, u32[]{:S(2)}, u32[]{:S(2)}) collective-permute-start(bf16[400,128]{1,0:T(8,128)(2,1)S(1)} %get-tuple-element.139), channel_id=1, source_target_pairs={{0,3},{1,2},{2,1},{3,0},{4,7},{5,6},{6,5},{7,4},{8,11},{9,10},{10,... | collective-permute-start | bytes 307208 | tf_op jit(solution)/shard_map/ppermute | solution.py:415
  123.0 10.1 %collective-permute-start.10 = (bf16[400,128]{1,0:T(8,128)(2,1)S(1)}, bf16[400,128]{1,0:T(8,128)(2,1)S(1)}, u32[]{:S(2)}, u32[]{:S(2)}) collective-permute-start(bf16[400,128]{1,0:T(8,128)(2,1)S(1)} %get-tuple-element.140), channel_id=1, source_target_pairs={{0,4},{1,5},{2,6},{3,7},{4,0},{5,1},{6,2},{7,3},{8,12},{9,13},{10,... | collective-permute-start | bytes 307208 | tf_op jit(solution)/shard_map/ppermute | solution.py:415
  123.5 11.3 %collective-permute-start.11 = (bf16[400,128]{1,0:T(8,128)(2,1)S(1)}, bf16[400,128]{1,0:T(8,128)(2,1)S(1)}, u32[]{:S(2)}, u32[]{:S(2)}) collective-permute-start(bf16[400,128]{1,0:T(8,128)(2,1)S(1)} %get-tuple-element.141), channel_id=1, source_target_pairs={{0,5},{1,4},{2,7},{3,6},{4,1},{5,0},{6,3},{7,2},{8,13},{9,12},{10,... | collective-permute-start | bytes 307208 | tf_op jit(solution)/shard_map/ppermute | solution.py:415
  125.1 9.7 %collective-permute-start.12 = (bf16[400,128]{1,0:T(8,128)(2,1)S(1)}, bf16[400,128]{1,0:T(8,128)(2,1)S(1)}, u32[]{:S(2)}, u32[]{:S(2)}) collective-permute-start(bf16[400,128]{1,0:T(8,128)(2,1)S(1)} %get-tuple-element.142), channel_id=1, source_target_pairs={{0,6},{1,7},{2,4},{3,5},{4,2},{5,3},{6,0},{7,1},{8,14},{9,15},{10,... | collective-permute-start | bytes 307208 | tf_op jit(solution)/shard_map/ppermute | solution.py:415
  127.3 7.5 %collective-permute-start.13 = (bf16[400,128]{1,0:T(8,128)(2,1)S(1)}, bf16[400,128]{1,0:T(8,128)(2,1)S(1)}, u32[]{:S(2)}, u32[]{:S(2)}) collective-permute-start(bf16[400,128]{1,0:T(8,128)(2,1)S(1)} %get-tuple-element.143), channel_id=1, source_target_pairs={{0,7},{1,6},{2,5},{3,4},{4,3},{5,2},{6,1},{7,0},{8,15},{9,14},{10,... | collective-permute-start | bytes 307208 | tf_op jit(solution)/shard_map/ppermute | solution.py:415
  136.7 11.5 %collective-permute-start.26 = (s16[408,128]{1,0:T(8,128)(2,1)S(1)}, s16[408,128]{1,0:T(8,128)(2,1)S(1)}, u32[]{:S(2)}, u32[]{:S(2)}) collective-permute-start(s16[408,128]{1,0:T(8,128)(2,1)S(1)} %get-tuple-element.175), channel_id=1, source_target_pairs={{0,31},{1,30},{2,29},{3,28},{4,27},{5,26},{6,25},{7,24},{8,23},{9,... | collective-permute-start | bytes 313352 | tf_op jit(solution)/shard_map/ppermute | solution.py:415
  138.5 17.1 %collective-permute-start.15 = (s16[408,128]{1,0:T(8,128)(2,1)S(1)}, s16[408,128]{1,0:T(8,128)(2,1)S(1)}, u32[]{:S(2)}, u32[]{:S(2)}) collective-permute-start(s16[408,128]{1,0:T(8,128)(2,1)S(1)} %get-tuple-element.154), channel_id=1, source_target_pairs={{0,28},{1,29},{2,30},{3,31},{4,24},{5,25},{6,26},{7,27},{8,20},{9,... | collective-permute-start | bytes 313352 | tf_op jit(solution)/shard_map/ppermute | solution.py:415
  140.4 16.8 %collective-permute-start.31 = (s16[408,128]{1,0:T(8,128)(2,1)S(1)}, s16[408,128]{1,0:T(8,128)(2,1)S(1)}, u32[]{:S(2)}, u32[]{:S(2)}) collective-permute-start(s16[408,128]{1,0:T(8,128)(2,1)S(1)} %get-tuple-element.183), channel_id=1, source_target_pairs={{0,30},{1,31},{2,28},{3,29},{4,26},{5,27},{6,24},{7,25},{8,22},{9,... | collective-permute-start | bytes 313352 | tf_op jit(solution)/shard_map/ppermute | solution.py:415
  143.1 16.8 %collective-permute-start.33 = (s16[408,128]{1,0:T(8,128)(2,1)S(1)}, s16[408,128]{1,0:T(8,128)(2,1)S(1)}, u32[]{:S(2)}, u32[]{:S(2)}) collective-permute-start(s16[408,128]{1,0:T(8,128)(2,1)S(1)} %get-tuple-element.188), channel_id=1, source_target_pairs={{0,29},{1,28},{2,31},{3,30},{4,25},{5,24},{6,27},{7,26},{8,21},{9,... | collective-permute-start | bytes 313352 | tf_op jit(solution)/shard_map/ppermute | solution.py:415
  146.3 16.6 %collective-permute-start.14 = (s16[408,128]{1,0:T(8,128)(2,1)S(1)}, s16[408,128]{1,0:T(8,128)(2,1)S(1)}, u32[]{:S(2)}, u32[]{:S(2)}) collective-permute-start(s16[408,128]{1,0:T(8,128)(2,1)S(1)} %get-tuple-element.145), channel_id=1, source_target_pairs={{0,27},{1,26},{2,25},{3,24},{4,31},{5,30},{6,29},{7,28},{8,19},{9,... | collective-permute-start | bytes 313352 | tf_op jit(solution)/shard_map/ppermute | solution.py:415
  148.2 21.0 %collective-permute-start.27 = (s16[408,128]{1,0:T(8,128)(2,1)S(1)}, s16[408,128]{1,0:T(8,128)(2,1)S(1)}, u32[]{:S(2)}, u32[]{:S(2)}) collective-permute-start(s16[408,128]{1,0:T(8,128)(2,1)S(1)} %get-tuple-element.176), channel_id=1, source_target_pairs={{0,15},{1,14},{2,13},{3,12},{4,11},{5,10},{6,9},{7,8},{8,7},{9,6},... | collective-permute-start | bytes 313352 | tf_op jit(solution)/shard_map/ppermute | solution.py:415
  155.6 21.4 %collective-permute-start.16 = (s16[408,128]{1,0:T(8,128)(2,1)S(1)}, s16[408,128]{1,0:T(8,128)(2,1)S(1)}, u32[]{:S(2)}, u32[]{:S(2)}) collective-permute-start(s16[408,128]{1,0:T(8,128)(2,1)S(1)} %get-tuple-element.155), channel_id=1, source_target_pairs={{0,25},{1,24},{2,27},{3,26},{4,29},{5,28},{6,31},{7,30},{8,17},{9,... | collective-permute-start | bytes 313352 | tf_op jit(solution)/shard_map/ppermute | solution.py:415
  157.2 19.9 %collective-permute-start.32 = (s16[408,128]{1,0:T(8,128)(2,1)S(1)}, s16[408,128]{1,0:T(8,128)(2,1)S(1)}, u32[]{:S(2)}, u32[]{:S(2)}) collective-permute-start(s16[408,128]{1,0:T(8,128)(2,1)S(1)} %get-tuple-element.184), channel_id=1, source_target_pairs={{0,26},{1,27},{2,24},{3,25},{4,30},{5,31},{6,28},{7,29},{8,18},{9,... | collective-permute-start | bytes 313352 | tf_op jit(solution)/shard_map/ppermute | solution.py:415
  159.9 18.3 %collective-permute-start.34 = (s16[408,128]{1,0:T(8,128)(2,1)S(1)}, s16[408,128]{1,0:T(8,128)(2,1)S(1)}, u32[]{:S(2)}, u32[]{:S(2)}) collective-permute-start(s16[408,128]{1,0:T(8,128)(2,1)S(1)} %get-tuple-element.189), channel_id=1, source_target_pairs={{0,14},{1,15},{2,12},{3,13},{4,10},{5,11},{6,8},{7,9},{8,6},{9,7},... | collective-permute-start | bytes 313352 | tf_op jit(solution)/shard_map/ppermute | solution.py:415
  162.9 17.7 %collective-permute-start.21 = (s16[408,128]{1,0:T(8,128)(2,1)S(1)}, s16[408,128]{1,0:T(8,128)(2,1)S(1)}, u32[]{:S(2)}, u32[]{:S(2)}) collective-permute-start(s16[408,128]{1,0:T(8,128)(2,1)S(1)} %get-tuple-element.164), channel_id=1, source_target_pairs={{0,13},{1,12},{2,15},{3,14},{4,9},{5,8},{6,11},{7,10},{8,5},{9,4},... | collective-permute-start | bytes 313352 | tf_op jit(solution)/shard_map/ppermute | solution.py:415
  169.2 14.2 %collective-permute-start.28 = (s16[408,128]{1,0:T(8,128)(2,1)S(1)}, s16[408,128]{1,0:T(8,128)(2,1)S(1)}, u32[]{:S(2)}, u32[]{:S(2)}) collective-permute-start(s16[408,128]{1,0:T(8,128)(2,1)S(1)} %get-tuple-element.177), channel_id=1, source_target_pairs={{0,24},{1,25},{2,26},{3,27},{4,28},{5,29},{6,30},{7,31},{8,16},{9,... | collective-permute-start | bytes 313352 | tf_op jit(solution)/shard_map/ppermute | solution.py:415
  177.1 10.7 %collective-permute-start.17 = (s16[408,128]{1,0:T(8,128)(2,1)S(1)}, s16[408,128]{1,0:T(8,128)(2,1)S(1)}, u32[]{:S(2)}, u32[]{:S(2)}) collective-permute-start(s16[408,128]{1,0:T(8,128)(2,1)S(1)} %get-tuple-element.156), channel_id=1, source_target_pairs={{0,11},{1,10},{2,9},{3,8},{4,15},{5,14},{6,13},{7,12},{8,3},{9,2},... | collective-permute-start | bytes 313352 | tf_op jit(solution)/shard_map/ppermute | solution.py:415
  177.2 14.2 %collective-permute-start.35 = (s16[408,128]{1,0:T(8,128)(2,1)S(1)}, s16[408,128]{1,0:T(8,128)(2,1)S(1)}, u32[]{:S(2)}, u32[]{:S(2)}) collective-permute-start(s16[408,128]{1,0:T(8,128)(2,1)S(1)} %get-tuple-element.195), channel_id=1, source_target_pairs={{0,12},{1,13},{2,14},{3,15},{4,8},{5,9},{6,10},{7,11},{8,4},{9,5},... | collective-permute-start | bytes 313352 | tf_op jit(solution)/shard_map/ppermute | solution.py:415
  178.1 13.3 %collective-permute-start.36 = (s16[408,128]{1,0:T(8,128)(2,1)S(1)}, s16[408,128]{1,0:T(8,128)(2,1)S(1)}, u32[]{:S(2)}, u32[]{:S(2)}) collective-permute-start(s16[408,128]{1,0:T(8,128)(2,1)S(1)} %get-tuple-element.198), channel_id=1, source_target_pairs={{0,23},{1,22},{2,21},{3,20},{4,19},{5,18},{6,17},{7,16},{8,31},{9,... | collective-permute-start | bytes 313352 | tf_op jit(solution)/shard_map/ppermute | solution.py:415
  180.6 16.8 %collective-permute-start.22 = (s16[408,128]{1,0:T(8,128)(2,1)S(1)}, s16[408,128]{1,0:T(8,128)(2,1)S(1)}, u32[]{:S(2)}, u32[]{:S(2)}) collective-permute-start(s16[408,128]{1,0:T(8,128)(2,1)S(1)} %get-tuple-element.165), channel_id=1, source_target_pairs={{0,22},{1,23},{2,20},{3,21},{4,18},{5,19},{6,16},{7,17},{8,30},{9,... | collective-permute-start | bytes 313352 | tf_op jit(solution)/shard_map/ppermute | solution.py:415
  183.4 14.0 %collective-permute-start.29 = (s16[408,128]{1,0:T(8,128)(2,1)S(1)}, s16[408,128]{1,0:T(8,128)(2,1)S(1)}, u32[]{:S(2)}, u32[]{:S(2)}) collective-permute-start(s16[408,128]{1,0:T(8,128)(2,1)S(1)} %get-tuple-element.178), channel_id=1, source_target_pairs={{0,10},{1,11},{2,8},{3,9},{4,14},{5,15},{6,12},{7,13},{8,2},{9,3},... | collective-permute-start | bytes 313352 | tf_op jit(solution)/shard_map/ppermute | solution.py:415
  187.8 12.1 %collective-permute-start.18 = (s16[408,128]{1,0:T(8,128)(2,1)S(1)}, s16[408,128]{1,0:T(8,128)(2,1)S(1)}, u32[]{:S(2)}, u32[]{:S(2)}) collective-permute-start(s16[408,128]{1,0:T(8,128)(2,1)S(1)} %get-tuple-element.157), channel_id=1, source_target_pairs={{0,20},{1,21},{2,22},{3,23},{4,16},{5,17},{6,18},{7,19},{8,28},{9,... | collective-permute-start | bytes 313352 | tf_op jit(solution)/shard_map/ppermute | solution.py:415
  191.4 9.4 %collective-permute-start.39 = (s16[408,128]{1,0:T(8,128)(2,1)S(1)}, s16[408,128]{1,0:T(8,128)(2,1)S(1)}, u32[]{:S(2)}, u32[]{:S(2)}) collective-permute-start(s16[408,128]{1,0:T(8,128)(2,1)S(1)} %get-tuple-element.211), channel_id=1, source_target_pairs={{0,21},{1,20},{2,23},{3,22},{4,17},{5,16},{6,19},{7,18},{8,29},{9,... | collective-permute-start | bytes 313352 | tf_op jit(solution)/shard_map/ppermute | solution.py:415
  191.4 11.6 %collective-permute-start.42 = (s16[408,128]{1,0:T(8,128)(2,1)S(1)}, s16[408,128]{1,0:T(8,128)(2,1)S(1)}, u32[]{:S(2)}, u32[]{:S(2)}) collective-permute-start(s16[408,128]{1,0:T(8,128)(2,1)S(1)} %get-tuple-element.219), channel_id=1, source_target_pairs={{0,9},{1,8},{2,11},{3,10},{4,13},{5,12},{6,15},{7,14},{8,1},{9,0},... | collective-permute-start | bytes 313352 | tf_op jit(solution)/shard_map/ppermute | solution.py:415
  197.4 7.2 %collective-permute-start.23 = (s16[408,128]{1,0:T(8,128)(2,1)S(1)}, s16[408,128]{1,0:T(8,128)(2,1)S(1)}, u32[]{:S(2)}, u32[]{:S(2)}) collective-permute-start(s16[408,128]{1,0:T(8,128)(2,1)S(1)} %get-tuple-element.166), channel_id=1, source_target_pairs={{0,8},{1,9},{2,10},{3,11},{4,12},{5,13},{6,14},{7,15},{8,0},{9,1},... | collective-permute-start | bytes 313352 | tf_op jit(solution)/shard_map/ppermute | solution.py:415
  197.4 9.6 %collective-permute-start.30 = (s16[408,128]{1,0:T(8,128)(2,1)S(1)}, s16[408,128]{1,0:T(8,128)(2,1)S(1)}, u32[]{:S(2)}, u32[]{:S(2)}) collective-permute-start(s16[408,128]{1,0:T(8,128)(2,1)S(1)} %get-tuple-element.179), channel_id=1, source_target_pairs={{0,19},{1,18},{2,17},{3,16},{4,23},{5,22},{6,21},{7,20},{8,27},{9,... | collective-permute-start | bytes 313352 | tf_op jit(solution)/shard_map/ppermute | solution.py:415
  199.9 8.4 %collective-permute-start.19 = (s16[408,128]{1,0:T(8,128)(2,1)S(1)}, s16[408,128]{1,0:T(8,128)(2,1)S(1)}, u32[]{:S(2)}, u32[]{:S(2)}) collective-permute-start(s16[408,128]{1,0:T(8,128)(2,1)S(1)} %get-tuple-element.158), channel_id=1, source_target_pairs={{0,6},{1,7},{2,4},{3,5},{4,2},{5,3},{6,0},{7,1},{8,14},{9,15},{10,... | collective-permute-start | bytes 313352 | tf_op jit(solution)/shard_map/ppermute | solution.py:415
  200.8 9.5 %collective-permute-start.40 = (s16[408,128]{1,0:T(8,128)(2,1)S(1)}, s16[408,128]{1,0:T(8,128)(2,1)S(1)}, u32[]{:S(2)}, u32[]{:S(2)}) collective-permute-start(s16[408,128]{1,0:T(8,128)(2,1)S(1)} %get-tuple-element.212), channel_id=1, source_target_pairs={{0,7},{1,6},{2,5},{3,4},{4,3},{5,2},{6,1},{7,0},{8,15},{9,14},{10,... | collective-permute-start | bytes 313352 | tf_op jit(solution)/shard_map/ppermute | solution.py:415
  203.0 11.2 %collective-permute-start.43 = (s16[408,128]{1,0:T(8,128)(2,1)S(1)}, s16[408,128]{1,0:T(8,128)(2,1)S(1)}, u32[]{:S(2)}, u32[]{:S(2)}) collective-permute-start(s16[408,128]{1,0:T(8,128)(2,1)S(1)} %get-tuple-element.220), channel_id=1, source_target_pairs={{0,18},{1,19},{2,16},{3,17},{4,22},{5,23},{6,20},{7,21},{8,26},{9,... | collective-permute-start | bytes 313352 | tf_op jit(solution)/shard_map/ppermute | solution.py:415
  204.6 10.7 %collective-permute-start.24 = (s16[408,128]{1,0:T(8,128)(2,1)S(1)}, s16[408,128]{1,0:T(8,128)(2,1)S(1)}, u32[]{:S(2)}, u32[]{:S(2)}) collective-permute-start(s16[408,128]{1,0:T(8,128)(2,1)S(1)} %get-tuple-element.167), channel_id=1, source_target_pairs={{0,17},{1,16},{2,19},{3,18},{4,21},{5,20},{6,23},{7,22},{8,25},{9,... | collective-permute-start | bytes 313352 | tf_op jit(solution)/shard_map/ppermute | solution.py:415
  207.0 12.0 %collective-permute-start.37 = (s16[408,128]{1,0:T(8,128)(2,1)S(1)}, s16[408,128]{1,0:T(8,128)(2,1)S(1)}, u32[]{:S(2)}, u32[]{:S(2)}) collective-permute-start(s16[408,128]{1,0:T(8,128)(2,1)S(1)} %get-tuple-element.206), channel_id=1, source_target_pairs={{0,5},{1,4},{2,7},{3,6},{4,1},{5,0},{6,3},{7,2},{8,13},{9,12},{10,... | collective-permute-start | bytes 313352 | tf_op jit(solution)/shard_map/ppermute | solution.py:415
  208.3 12.8 %collective-permute-start.20 = (s16[408,128]{1,0:T(8,128)(2,1)S(1)}, s16[408,128]{1,0:T(8,128)(2,1)S(1)}, u32[]{:S(2)}, u32[]{:S(2)}) collective-permute-start(s16[408,128]{1,0:T(8,128)(2,1)S(1)} %get-tuple-element.159), channel_id=1, source_target_pairs={{0,3},{1,2},{2,1},{3,0},{4,7},{5,6},{6,5},{7,4},{8,11},{9,10},{10,... | collective-permute-start | bytes 313352 | tf_op jit(solution)/shard_map/ppermute | solution.py:415
  210.3 9.7 %collective-permute-start.41 = (s16[408,128]{1,0:T(8,128)(2,1)S(1)}, s16[408,128]{1,0:T(8,128)(2,1)S(1)}, u32[]{:S(2)}, u32[]{:S(2)}) collective-permute-start(s16[408,128]{1,0:T(8,128)(2,1)S(1)} %get-tuple-element.213), channel_id=1, source_target_pairs={{0,16},{1,17},{2,18},{3,19},{4,20},{5,21},{6,22},{7,23},{8,24},{9,... | collective-permute-start | bytes 313352 | tf_op jit(solution)/shard_map/ppermute | solution.py:415
  214.1 5.9 %collective-permute-start.44 = (s16[408,128]{1,0:T(8,128)(2,1)S(1)}, s16[408,128]{1,0:T(8,128)(2,1)S(1)}, u32[]{:S(2)}, u32[]{:S(2)}) collective-permute-start(s16[408,128]{1,0:T(8,128)(2,1)S(1)} %get-tuple-element.226), channel_id=1, source_target_pairs={{0,4},{1,5},{2,6},{3,7},{4,0},{5,1},{6,2},{7,3},{8,12},{9,13},{10,... | collective-permute-start | bytes 313352 | tf_op jit(solution)/shard_map/ppermute | solution.py:415
  215.3 7.2 %collective-permute-start.25 = (s16[408,128]{1,0:T(8,128)(2,1)S(1)}, s16[408,128]{1,0:T(8,128)(2,1)S(1)}, u32[]{:S(2)}, u32[]{:S(2)}) collective-permute-start(s16[408,128]{1,0:T(8,128)(2,1)S(1)} %get-tuple-element.168), channel_id=1, source_target_pairs={{0,2},{1,3},{2,0},{3,1},{4,6},{5,7},{6,4},{7,5},{8,10},{9,11},{10,... | collective-permute-start | bytes 313352 | tf_op jit(solution)/shard_map/ppermute | solution.py:415
  219.0 3.6 %collective-permute-start.38 = (s16[408,128]{1,0:T(8,128)(2,1)S(1)}, s16[408,128]{1,0:T(8,128)(2,1)S(1)}, u32[]{:S(2)}, u32[]{:S(2)}) collective-permute-start(s16[408,128]{1,0:T(8,128)(2,1)S(1)} %get-tuple-element.207), channel_id=1, source_target_pairs={{0,1},{1,0},{2,3},{3,2},{4,5},{5,4},{6,7},{7,6},{8,9},{9,8},{10,11... | collective-permute-start | bytes 313352 | tf_op jit(solution)/shard_map/ppermute | solution.py:415
  220.0 2.5 %copy-start = (f32[2048,400]{0,1:T(8,128)S(1)}, f32[2048,400]{0,1:T(8,128)}, u32[]{:S(2)}) copy-start(f32[2048,400]{0,1:T(8,128)} %param.9) | copy-start | bytes 9830404
  220.0 2.5 %copy-start.1 = (f32[2048]{0:T(1024)S(1)}, f32[2048]{0:T(1024)}, u32[]{:S(2)}) copy-start(f32[2048]{0:T(1024)} %param.10) | copy-start | bytes 24580

commit v13 on v12

--- a/solution.py
+++ b/solution.py
@@ -9,7 +9,7 @@
 
 BLK = 128
 TAIL = 8
-CUTS = (3, 3, 4, 4, 2)
+CUTS = (1, 2, 2, 2, 1)
 STEPS = (3, 6, 8)
 WINDOW = 5
 TILE = 256
@@ -136,7 +136,7 @@
     dst_ref[...] = target.astype(BF16)
 
 
-def gather_edges(rows, spos, dpos, operator, tile=1024):
+def gather_edges(rows, spos, dpos, operator, tile=512):
     width, total = rows.shape
     edges = spos.shape[1]
     lane = pl.BlockSpec((1, tile), lambda i: (0, i))
@@ -174,7 +174,7 @@
     u = src_ref[...].astype(F32) * operator
     u_half = u.astype(BF16)
     scores = jnp.dot(tall, u_half, preferred_element_type=F32)
-    g_neg = (jax.nn.sigmoid(scores) * (1.0 / count)).astype(BF16)
+    g_neg = (jax.nn.sigmoid(scores) / count).astype(BF16)
     sums = lax.dot_general(u_half, g_neg, NT, preferred_element_type=F32)
     for g in range(groups):
         outs[g][...] = sums[:, g * each : (g + 1) * each].astype(BF16)
@@ -340,7 +340,7 @@
             g = grad[:, lanes]
             new_state = state_ref[:, lanes] + jnp.sum(g * g, axis=0, keepdims=True) / width
             state_out[:, lanes] = new_state
-            fresh[:, lanes] = table_ref[:, lanes] - g * (0.1 / (jnp.sqrt(new_state) + 1e-10))
+            fresh[:, lanes] = table_ref[:, lanes] - 0.1 * g / (jnp.sqrt(new_state) + 1e-10)
         copy(b).start()
     for b in range(sems.shape[0]):
         copy(b).wait()

time: 227 us -> 225 us (level)
  transfers between devices with their start and end apart: 47 -> 47, of which waited for: 12 -> 12; matrix products, arithmetic and copies ran while one was open for 13% -> 13% of each run, Pallas kernels for 15% -> 16%
where the time goes in v13:
time: 225 us
  starting transfers between devices  75.8 us (34%)
  waiting for transfers between devices  65.8 us (29%)
  Pallas kernels  51.1 us (23%)
  local copies, waits for them, and re-layouts  26.7 us (12%)
  other arithmetic  3.85 us (2%)
    ppermute x45, starting transfers between devices, swap(): return lax.ppermute(x, axis, [(i, i ^ shift) for i in range(count)])  65 us
    all_to_all x1, waiting for transfers between devices, per_device(): lax.all_to_all(outgoing, AXES, split_axis=0, concat_axis=0, tiled=True)  47.1 us
    gather x2, local copies, waits for them, and re-layouts, per_device(): operator = relations[rel_ids].T  16.7 us
    pallas_call x3, Pallas kernels, scatter(): pl.pallas_call(functools.partial(scatter_kernel, first * BLK), out_shape=...  15.1 us
    ppermute x45, waiting for transfers between devices, swap(): return lax.ppermute(x, axis, [(i, i ^ shift) for i in range(count)])  13.7 us
    pallas_call x5, Pallas kernels, pack(): pl.pallas_call(functools.partial(pack_kernel, first, tuple(bounds), len(g...  9.04 us
    unnamed x15, local copies, waits for them, and re-layouts  8.7 us
    pallas_call x1, Pallas kernels, gather_edges(): pl.pallas_call(edge_kernel, grid=(edges // tile,), out_shape=(jax.ShapeDt...  8.04 us
  transfers between devices with their start and end apart: 47, of which 12 were waited for; matrix products, arithmetic and copies ran while one was open for 13% of the time, Pallas kernels for 16%

profile of v13, /device:TPU:0, one launch (start us, length us, event | category | flops | bytes accessed | tf_op | source)
XLA Modules:
  0.0 224.5 jit_solution(17294109677071575645)
XLA Ops:
  0.6 1.3 copy.21
  2.0 7.3 %all-to-all-start = ((s32[32,1,1]{2,1,0:T(1,128)}), s32[32,1,1]{2,1,0:T(1,128)S(1)}, u32[]{:S(2)}, u32[]{:S(2)}) async-start(s32[32,1,1]{2,1,0:T(1,128)} %copy.21), calls=%async_computation | async-start | bytes 32768 | tf_op jit(solution)/shard_map/all_to_all | solution.py:371
  9.3 2.1 bitcast_bitcast_fusion.blocks_ref
  11.4 4.9 %all-to-all-done.asked_ref = s32[32,1,1]{2,1,0:T(1,128)S(1)} async-done(((s32[32,1,1]{2,1,0:T(1,128)}), s32[32,1,1]{2,1,0:T(1,128)S(1)}, u32[]{:S(2)}, u32[]{:S(2)}) %all-to-all-start) | async-done | bytes 160 | tf_op jit(solution)/shard_map/all_to_all | solution.py:371
  16.3 2.5 %select.19 = bf16[32,400,128]{2,1,0:T(8,128)(2,1)} custom-call(s32[32,1,1]{2,1,0:T(1,128)S(1)} %all-to-all-done.asked_ref, bf16[16,400,128]{2,1,0:T(8,128)(2,1)S(1)} %bitcast_bitcast_fusion.blocks_ref), custom_call_target="tpu_custom_call" | custom-call | tf_op jit(solution)/shard_map/select/pallas_call | solution.py:65
  18.9 3.6 %all-to-all-start.1 = ((bf16[32,400,128]{2,1,0:T(8,128)(2,1)}), bf16[32,400,128]{2,1,0:T(8,128)(2,1)}, u32[]{:S(2)}, u32[]{:S(2)}) async-start(bf16[32,400,128]{2,1,0:T(8,128)(2,1)} %select.19), calls=%async_computation.1 | async-start | bytes 6553600 | tf_op jit(solution)/shard_map/all_to_all | solution.py:377
  22.4 8.6 %copy.23 = f32[4096,400]{1,0:T(8,128)} copy(f32[4096,400]{0,1:T(8,128)} %param.11) | data formatting | bytes 13107200 | tf_op args[2]
  31.0 12.9 %gather_fusion = f32[2048,400]{1,0:T(8,128)} fusion(f32[4096,400]{1,0:T(8,128)} %copy.23, s32[2048]{0:T(1024)S(1)} %fusion.3), kind=kCustom, calls=%fused_computation | custom fusion | bytes 6561792 | tf_op jit(solution)/shard_map/gather | solution.py:378
  44.0 3.8 %copy.24 = f32[2048,400]{0,1:T(8,128)S(1)} copy(f32[2048,400]{1,0:T(8,128)} %gather_fusion) | data formatting | bytes 6553600 | tf_op jit(solution)/shard_map/gather | solution.py:378
  49.6 47.1 %all-to-all-done.1.fetched = bf16[32,400,128]{2,1,0:T(8,128)(2,1)} async-done(((bf16[32,400,128]{2,1,0:T(8,128)(2,1)}), bf16[32,400,128]{2,1,0:T(8,128)(2,1)}, u32[]{:S(2)}, u32[]{:S(2)}) %all-to-all-start.1) | async-done | bytes 3276832 | tf_op jit(solution)/shard_map/all_to_all | solution.py:377
  96.7 2.6 %gather_negs.1 = (bf16[400,128]{1,0:T(8,128)(2,1)S(1)}, bf16[400,2048]{1,0:T(8,128)(2,1)S(1)}) custom-call(s32[16]{0:T(128)S(1)} %select_reduce_fusion.7.live_ref, bf16[32,400,128]{2,1,0:T(8,128)(2,1)} %all-to-all-done.1.fetched, s32[1,128]{1,0:T(1,128)S(1)} %fusion.10.pos_ref.npos), custom_call_target="tpu_custom_call" | custom-call | tf_op jit(solution)/shard_map/gather_negs/pallas_call | solution.py:115
  99.5 1.3 collective-permute-start.1
  101.3 1.2 collective-permute-start.3
  103.0 2.1 collective-permute-start.5
  105.2 0.9 collective-permute-start.6
  106.1 8.0 %gather_edges.1 = (bf16[400,2048]{1,0:T(8,128)(2,1)S(1)}, bf16[400,2048]{1,0:T(8,128)(2,1)S(1)}, f32[1,2048]{1,0:T(1,128)S(1)}) custom-call(bf16[400,2048]{1,0:T(8,128)(2,1)S(1)} %get-tuple-element.128.rows, s32[1,2048]{1,0:T(1,128)S(1)} %bitcast.20, s32[1,2048]{1,0:T(1,128)S(1)} %bitcast.24, f32[400,2048]{1,0:T(8,128)S(1)} %bitcast.17), custom_call_target="tpu_custom_call" | custom-call | flops 104857600 | bytes 204800 | tf_op jit(solution)/shard_map/gather_edges/pallas_call | solution.py:144
  114.2 6.2 %score.1 = (bf16[2,400,2048]{2,1,0:T(8,128)(2,1)S(1)}, bf16[2,400,2048]{2,1,0:T(8,128)(2,1)S(1)}, bf16[400,128]{1,0:T(8,128)(2,1)S(1)}, bf16[400,128]{1,0:T(8,12...) custom-call(bf16[400,128]{1,0:T(8,128)(2,1)S(1)} %get-tuple-element., ...), custom_call_target="tpu_custom_call" | custom-call | flops 78643200 | bytes 153600 | tf_op jit(solution)/shard_map/score/pallas_call | solution.py:191
  120.5 1.4 collective-permute-start.7
  122.3 0.9 collective-permute-start.9
  123.8 1.5 collective-permute-start.11
  125.3 0.8 collective-permute-start.12
  126.1 1.4 collective-permute-done.8.refs_4_.refs_5_.refs_3_
  127.7 5.7 %scatter.3.refs_0_ = f32[400,768]{1,0:T(8,128)S(1)} custom-call(bf16[2,400,2048]{2,1,0:T(8,128)(2,1)S(1)} %get-tuple-element.135.gs_ref, bf16[2,400,2048]{2,1,0:T(8,128)(2,1)S(1)} %get-tuple-element.136.gd_ref, s32[1,2048]{1,0:T(1,128)S(1)} %bitcast.21, s32[1,2048]{1,0:T(1,128)S(1)} %bitcast.25), custom_call_target="tpu_custom_call" | custom-call | flops 39321600 | bytes 76800 | tf_op jit(solution)/shard_map/scatter/pallas_call | solution.py:228
  133.4 1.7 collective-permute-done.11.refs_7_.refs_8_.refs_6_
  135.1 1.5 pack.9
  136.6 2.3 %collective-permute-start.26 = (s16[408,128]{1,0:T(8,128)(2,1)S(1)}, s16[408,128]{1,0:T(8,128)(2,1)S(1)}, u32[]{:S(2)}, u32[]{:S(2)}) collective-permute-start(s16[408,128]{1,0:T(8,128)(2,1)S(1)} %get-tuple-element.176), channel_id=1, source_target_pairs={{0,31},{1,30},{2,29},{3,28},{4,27},{5,26},{6,25},{7,24},{8,23},{9,... | collective-permute-start | bytes 313352 | tf_op jit(solution)/shard_map/ppermute | solution.py:415
  138.8 2.2 collective-permute-start.15
  141.0 2.9 %collective-permute-start.31 = (s16[408,128]{1,0:T(8,128)(2,1)S(1)}, s16[408,128]{1,0:T(8,128)(2,1)S(1)}, u32[]{:S(2)}, u32[]{:S(2)}) collective-permute-start(s16[408,128]{1,0:T(8,128)(2,1)S(1)} %get-tuple-element.186), channel_id=1, source_target_pairs={{0,30},{1,31},{2,28},{3,29},{4,26},{5,27},{6,24},{7,25},{8,22},{9,... | collective-permute-start | bytes 313352 | tf_op jit(solution)/shard_map/ppermute | solution.py:415
  144.0 2.2 collective-permute-start.33
  146.1 5.7 %scatter.4.refs_1_ = f32[400,768]{1,0:T(8,128)S(1)} custom-call(bf16[2,400,2048]{2,1,0:T(8,128)(2,1)S(1)} %get-tuple-element.135.gs_ref, bf16[2,400,2048]{2,1,0:T(8,128)(2,1)S(1)} %get-tuple-element.136.gd_ref, s32[1,2048]{1,0:T(1,128)S(1)} %bitcast.22, s32[1,2048]{1,0:T(1,128)S(1)} %bitcast.26), custom_call_target="tpu_custom_call" | custom-call | flops 39321600 | bytes 76800 | tf_op jit(solution)/shard_map/scatter/pallas_call | solution.py:228
  151.8 1.5 pack.5
  153.3 1.5 collective-permute-start.14
  154.8 2.1 collective-permute-start.16
  156.9 3.2 %collective-permute-start.32 = (s16[408,128]{1,0:T(8,128)(2,1)S(1)}, s16[408,128]{1,0:T(8,128)(2,1)S(1)}, u32[]{:S(2)}, u32[]{:S(2)}) collective-permute-start(s16[408,128]{1,0:T(8,128)(2,1)S(1)} %get-tuple-element.187), channel_id=1, source_target_pairs={{0,26},{1,27},{2,24},{3,25},{4,30},{5,31},{6,28},{7,29},{8,18},{9,... | collective-permute-start | bytes 313352 | tf_op jit(solution)/shard_map/ppermute | solution.py:415
  160.1 1.6 collective-permute-start.34
  161.8 2.1 collective-permute-start.21
  163.9 1.1 collective-permute-done.27.refs_1_
  164.9 1.4 collective-permute-start.28
  166.4 3.8 %scatter.5.refs_2_ = f32[400,512]{1,0:T(8,128)S(1)} custom-call(bf16[2,400,2048]{2,1,0:T(8,128)(2,1)S(1)} %get-tuple-element.135.gs_ref, bf16[2,400,2048]{2,1,0:T(8,128)(2,1)S(1)} %get-tuple-element.136.gd_ref, s32[1,2048]{1,0:T(1,128)S(1)} %bitcast.23, s32[1,2048]{1,0:T(1,128)S(1)} %bitcast.27), custom_call_target="tpu_custom_call" | custom-call | flops 26214400 | bytes 51200 | tf_op jit(solution)/shard_map/scatter/pallas_call | solution.py:228
  170.2 2.3 %pack.8 = (s16[408,128]{1,0:T(8,128)(2,1)S(1)}, s16[408,128]{1,0:T(8,128)(2,1)S(1)}, s16[408,128]{1,0:T(8,128)(2,1)S(1)}, s16[408,128]{1,0:T(8,128)(2,1)S(1)}, s...) custom-call(s32[32]{0:T(128)S(1)} %select_reduce_fusion.5.rank_ref, ...), custom_call_target="tpu_custom_call" | custom-call | flops 3276800 | bytes 6400 | tf_op jit(solution)/shard_map/pack/pallas_call | solution.py:283
  172.5 1.0 collective-permute-start.17
  173.6 5.5 %collective-permute-start.36 = (s16[408,128]{1,0:T(8,128)(2,1)S(1)}, s16[408,128]{1,0:T(8,128)(2,1)S(1)}, u32[]{:S(2)}, u32[]{:S(2)}) collective-permute-start(s16[408,128]{1,0:T(8,128)(2,1)S(1)} %get-tuple-element.201), channel_id=1, source_target_pairs={{0,23},{1,22},{2,21},{3,20},{4,19},{5,18},{6,17},{7,16},{8,31},{9,... | collective-permute-start | bytes 313352 | tf_op jit(solution)/shard_map/ppermute | solution.py:415
  179.0 2.0 collective-permute-start.22
  181.0 1.1 collective-permute-start.29
  182.1 1.0 add.71.refs_8_
  183.1 2.4 %pack.7 = (s16[408,128]{1,0:T(8,128)(2,1)S(1)}, s16[408,128]{1,0:T(8,128)(2,1)S(1)}, s16[408,128]{1,0:T(8,128)(2,1)S(1)}, s16[408,128]{1,0:T(8,128)(2,1)S(1)}, s...) custom-call(s32[32]{0:T(128)S(1)} %select_reduce_fusion.5.rank_ref, ...), custom_call_target="tpu_custom_call" | custom-call | flops 3276800 | bytes 6400 | tf_op jit(solution)/shard_map/pack/pallas_call | solution.py:283
  185.5 1.2 collective-permute-start.18
  186.7 1.6 collective-permute-start.39
  188.3 2.0 collective-permute-start.42
  190.4 0.8 collective-permute-start.23
  191.2 2.7 %collective-permute-start.30 = (s16[408,128]{1,0:T(8,128)(2,1)S(1)}, s16[408,128]{1,0:T(8,128)(2,1)S(1)}, u32[]{:S(2)}, u32[]{:S(2)}) collective-permute-start(s16[408,128]{1,0:T(8,128)(2,1)S(1)} %get-tuple-element.180), channel_id=1, source_target_pairs={{0,19},{1,18},{2,17},{3,16},{4,23},{5,22},{6,21},{7,20},{8,27},{9,... | collective-permute-start | bytes 313352 | tf_op jit(solution)/shard_map/ppermute | solution.py:415
  193.9 1.0 add.72.refs_8_
  195.0 3.3 %collective-permute-done.18.refs_6_ = s16[408,128]{1,0:T(8,128)(2,1)S(1)} collective-permute-done((s16[408,128]{1,0:T(8,128)(2,1)S(1)}, s16[408,128]{1,0:T(8,128)(2,1)S(1)}, u32[]{:S(2)}, u32[]{:S(2)}) %collective-permute-start.18) | collective-permute-done | bytes 104480 | tf_op jit(solution)/shard_map/ppermute | solution.py:415
  198.3 3.2 %collective-permute-start.19 = (s16[408,128]{1,0:T(8,128)(2,1)S(1)}, s16[408,128]{1,0:T(8,128)(2,1)S(1)}, u32[]{:S(2)}, u32[]{:S(2)}) collective-permute-start(s16[408,128]{1,0:T(8,128)(2,1)S(1)} %get-tuple-element.159), channel_id=1, source_target_pairs={{0,6},{1,7},{2,4},{3,5},{4,2},{5,3},{6,0},{7,1},{8,14},{9,15},{10,... | collective-permute-start | bytes 313352 | tf_op jit(solution)/shard_map/ppermute | solution.py:415
  201.9 1.6 collective-permute-start.24
  203.5 4.4 %collective-permute-start.37 = (s16[408,128]{1,0:T(8,128)(2,1)S(1)}, s16[408,128]{1,0:T(8,128)(2,1)S(1)}, u32[]{:S(2)}, u32[]{:S(2)}) collective-permute-start(s16[408,128]{1,0:T(8,128)(2,1)S(1)} %get-tuple-element.208), channel_id=1, source_target_pairs={{0,5},{1,4},{2,7},{3,6},{4,1},{5,0},{6,3},{7,2},{8,13},{9,12},{10,... | collective-permute-start | bytes 313352 | tf_op jit(solution)/shard_map/ppermute | solution.py:415
  207.9 1.4 pack.6
  209.4 0.9 collective-permute-start.41
  210.3 4.4 %collective-permute-done.43.refs_2_ = s16[408,128]{1,0:T(8,128)(2,1)S(1)} collective-permute-done((s16[408,128]{1,0:T(8,128)(2,1)S(1)}, s16[408,128]{1,0:T(8,128)(2,1)S(1)}, u32[]{:S(2)}, u32[]{:S(2)}) %collective-permute-start.43) | collective-permute-done | bytes 104480 | tf_op jit(solution)/shard_map/ppermute | solution.py:415
  214.7 0.9 collective-permute-done.24.refs_4_
  215.6 2.4 %collective-permute-start.25 = (s16[408,128]{1,0:T(8,128)(2,1)S(1)}, s16[408,128]{1,0:T(8,128)(2,1)S(1)}, u32[]{:S(2)}, u32[]{:S(2)}) collective-permute-start(s16[408,128]{1,0:T(8,128)(2,1)S(1)} %get-tuple-element.169), channel_id=1, source_target_pairs={{0,2},{1,3},{2,0},{3,1},{4,6},{5,7},{6,4},{7,5},{8,10},{9,11},{10,... | collective-permute-start | bytes 313352 | tf_op jit(solution)/shard_map/ppermute | solution.py:415
  218.0 1.0 add.73.refs_8_
  219.7 1.0 add.74.refs_4_
  220.9 3.4 %update.1 = (f32[400,2048]{1,0:T(8,128)}, f32[1,2048]{1,0:T(1,128)}) custom-call(s32[32]{0:T(128)S(1)} %get-tuple-element.121.asked_ref, s16[408,128]{1,0:T(8,128)(2,1)S(1)} %collective-permute-done.20.refs_0_, s16[408,128]{1,0:T(8,128)(2,1)S(1)} %collective-permute-done.25.refs_1_, s16[408,128]{1,0:T(8,128)(2,1)S(1)} %collective-permute-done.38.refs_2_, ...), custom_call_target="tpu_custom_call" | custom-call | flops 819200 | bytes 1600 | tf_op jit(solution)/shard_map/update/pallas_call | solution.py:351
  (83 shorter events, 5.6 us)
Async XLA Ops:
  2.0 14.4 %all-to-all-start = ((s32[32,1,1]{2,1,0:T(1,128)}), s32[32,1,1]{2,1,0:T(1,128)S(1)}, u32[]{:S(2)}, u32[]{:S(2)}) async-start(s32[32,1,1]{2,1,0:T(1,128)} %copy.21), calls=%async_computation | async-start | bytes 32768 | tf_op jit(solution)/shard_map/all_to_all | solution.py:371
  18.9 77.9 %all-to-all-start.1 = ((bf16[32,400,128]{2,1,0:T(8,128)(2,1)}), bf16[32,400,128]{2,1,0:T(8,128)(2,1)}, u32[]{:S(2)}, u32[]{:S(2)}) async-start(bf16[32,400,128]{2,1,0:T(8,128)(2,1)} %select.19), calls=%async_computation.1 | async-start | bytes 6553600 | tf_op jit(solution)/shard_map/all_to_all | solution.py:377
  22.4 8.6 %copy-start.4 = (s32[2048]{0:T(1024)S(1)}, s32[2048]{0:T(1024)}, u32[]{:S(2)}) copy-start(s32[2048]{0:T(1024)} %param.12) | copy-start | bytes 24580
  44.0 3.8 %copy-start.2 = (s32[2048]{0:T(1024)S(1)}, s32[2048]{0:T(1024)}, u32[]{:S(2)}) copy-start(s32[2048]{0:T(1024)} %param.14) | copy-start | bytes 24580
  44.0 4.0 %copy-start.6 = (s32[32]{0:T(128)S(1)}, s32[32]{0:T(128)}, u32[]{:S(2)}) copy-start(s32[32]{0:T(128)} %constant.80.clone) | copy-start | bytes 388
  44.0 4.4 %copy-start.5 = (s32[128]{0:T(128)S(1)}, s32[128]{0:T(128)}, u32[]{:S(2)}) copy-start(s32[128]{0:T(128)} %param.16) | copy-start | bytes 1540
  44.0 4.4 %copy-start.3 = (s32[2048]{0:T(1024)S(1)}, s32[2048]{0:T(1024)}, u32[]{:S(2)}) copy-start(s32[2048]{0:T(1024)} %param.15) | copy-start | bytes 24580
  99.4 3.6 %collective-permute-start = (bf16[400,128]{1,0:T(8,128)(2,1)S(1)}, bf16[400,128]{1,0:T(8,128)(2,1)S(1)}, u32[]{:S(2)}, u32[]{:S(2)}) collective-permute-start(bf16[400,128]{1,0:T(8,128)(2,1)S(1)} %get-tuple-element.127.refs_0_), channel_id=1, source_target_pairs={{0,1},{1,0},{2,3},{3,2},{4,5},{5,4},{6,7},{7,6},{8,9},{9,8},{10,11... | collective-permute-start | bytes 307208 | tf_op jit(solution)/shard_map/ppermute | solution.py:415
  99.5 5.7 %collective-permute-start.1 = (bf16[400,128]{1,0:T(8,128)(2,1)S(1)}, bf16[400,128]{1,0:T(8,128)(2,1)S(1)}, u32[]{:S(2)}, u32[]{:S(2)}) collective-permute-start(bf16[400,128]{1,0:T(8,128)(2,1)S(1)} %get-tuple-element.127.refs_0_), channel_id=1, source_target_pairs={{0,2},{1,3},{2,0},{3,1},{4,6},{5,7},{6,4},{7,5},{8,10},{9,11},{10,... | collective-permute-start | bytes 307208 | tf_op jit(solution)/shard_map/ppermute | solution.py:415
  100.7 13.5 %collective-permute-start.2 = (bf16[400,128]{1,0:T(8,128)(2,1)S(1)}, bf16[400,128]{1,0:T(8,128)(2,1)S(1)}, u32[]{:S(2)}, u32[]{:S(2)}) collective-permute-start(bf16[400,128]{1,0:T(8,128)(2,1)S(1)} %get-tuple-element.127.refs_0_), channel_id=1, source_target_pairs={{0,3},{1,2},{2,1},{3,0},{4,7},{5,6},{6,5},{7,4},{8,11},{9,10},{10,... | collective-permute-start | bytes 307208 | tf_op jit(solution)/shard_map/ppermute | solution.py:415
  101.3 12.9 %collective-permute-start.3 = (bf16[400,128]{1,0:T(8,128)(2,1)S(1)}, bf16[400,128]{1,0:T(8,128)(2,1)S(1)}, u32[]{:S(2)}, u32[]{:S(2)}) collective-permute-start(bf16[400,128]{1,0:T(8,128)(2,1)S(1)} %get-tuple-element.127.refs_0_), channel_id=1, source_target_pairs={{0,4},{1,5},{2,6},{3,7},{4,0},{5,1},{6,2},{7,3},{8,12},{9,13},{10,... | collective-permute-start | bytes 307208 | tf_op jit(solution)/shard_map/ppermute | solution.py:415
  102.5 11.7 %collective-permute-start.4 = (bf16[400,128]{1,0:T(8,128)(2,1)S(1)}, bf16[400,128]{1,0:T(8,128)(2,1)S(1)}, u32[]{:S(2)}, u32[]{:S(2)}) collective-permute-start(bf16[400,128]{1,0:T(8,128)(2,1)S(1)} %get-tuple-element.127.refs_0_), channel_id=1, source_target_pairs={{0,5},{1,4},{2,7},{3,6},{4,1},{5,0},{6,3},{7,2},{8,13},{9,12},{10,... | collective-permute-start | bytes 307208 | tf_op jit(solution)/shard_map/ppermute | solution.py:415
  103.0 11.2 %collective-permute-start.5 = (bf16[400,128]{1,0:T(8,128)(2,1)S(1)}, bf16[400,128]{1,0:T(8,128)(2,1)S(1)}, u32[]{:S(2)}, u32[]{:S(2)}) collective-permute-start(bf16[400,128]{1,0:T(8,128)(2,1)S(1)} %get-tuple-element.127.refs_0_), channel_id=1, source_target_pairs={{0,6},{1,7},{2,4},{3,5},{4,2},{5,3},{6,0},{7,1},{8,14},{9,15},{10,... | collective-permute-start | bytes 307208 | tf_op jit(solution)/shard_map/ppermute | solution.py:415
  105.2 9.0 %collective-permute-start.6 = (bf16[400,128]{1,0:T(8,128)(2,1)S(1)}, bf16[400,128]{1,0:T(8,128)(2,1)S(1)}, u32[]{:S(2)}, u32[]{:S(2)}) collective-permute-start(bf16[400,128]{1,0:T(8,128)(2,1)S(1)} %get-tuple-element.127.refs_0_), channel_id=1, source_target_pairs={{0,7},{1,6},{2,5},{3,4},{4,3},{5,2},{6,1},{7,0},{8,15},{9,14},{10,... | collective-permute-start | bytes 307208 | tf_op jit(solution)/shard_map/ppermute | solution.py:415
  120.5 4.9 %collective-permute-start.7 = (bf16[400,128]{1,0:T(8,128)(2,1)S(1)}, bf16[400,128]{1,0:T(8,128)(2,1)S(1)}, u32[]{:S(2)}, u32[]{:S(2)}) collective-permute-start(bf16[400,128]{1,0:T(8,128)(2,1)S(1)} %get-tuple-element.138), channel_id=1, source_target_pairs={{0,1},{1,0},{2,3},{3,2},{4,5},{5,4},{6,7},{7,6},{8,9},{9,8},{10,11... | collective-permute-start | bytes 307208 | tf_op jit(solution)/shard_map/ppermute | solution.py:415
  121.8 5.7 %collective-permute-start.8 = (bf16[400,128]{1,0:T(8,128)(2,1)S(1)}, bf16[400,128]{1,0:T(8,128)(2,1)S(1)}, u32[]{:S(2)}, u32[]{:S(2)}) collective-permute-start(bf16[400,128]{1,0:T(8,128)(2,1)S(1)} %get-tuple-element.139), channel_id=1, source_target_pairs={{0,2},{1,3},{2,0},{3,1},{4,6},{5,7},{6,4},{7,5},{8,10},{9,11},{10,... | collective-permute-start | bytes 307208 | tf_op jit(solution)/shard_map/ppermute | solution.py:415
  122.3 11.0 %collective-permute-start.9 = (bf16[400,128]{1,0:T(8,128)(2,1)S(1)}, bf16[400,128]{1,0:T(8,128)(2,1)S(1)}, u32[]{:S(2)}, u32[]{:S(2)}) collective-permute-start(bf16[400,128]{1,0:T(8,128)(2,1)S(1)} %get-tuple-element.140), channel_id=1, source_target_pairs={{0,3},{1,2},{2,1},{3,0},{4,7},{5,6},{6,5},{7,4},{8,11},{9,10},{10,... | collective-permute-start | bytes 307208 | tf_op jit(solution)/shard_map/ppermute | solution.py:415
  123.3 10.1 %collective-permute-start.10 = (bf16[400,128]{1,0:T(8,128)(2,1)S(1)}, bf16[400,128]{1,0:T(8,128)(2,1)S(1)}, u32[]{:S(2)}, u32[]{:S(2)}) collective-permute-start(bf16[400,128]{1,0:T(8,128)(2,1)S(1)} %get-tuple-element.141), channel_id=1, source_target_pairs={{0,4},{1,5},{2,6},{3,7},{4,0},{5,1},{6,2},{7,3},{8,12},{9,13},{10,... | collective-permute-start | bytes 307208 | tf_op jit(solution)/shard_map/ppermute | solution.py:415
  123.8 11.3 %collective-permute-start.11 = (bf16[400,128]{1,0:T(8,128)(2,1)S(1)}, bf16[400,128]{1,0:T(8,128)(2,1)S(1)}, u32[]{:S(2)}, u32[]{:S(2)}) collective-permute-start(bf16[400,128]{1,0:T(8,128)(2,1)S(1)} %get-tuple-element.142), channel_id=1, source_target_pairs={{0,5},{1,4},{2,7},{3,6},{4,1},{5,0},{6,3},{7,2},{8,13},{9,12},{10,... | collective-permute-start | bytes 307208 | tf_op jit(solution)/shard_map/ppermute | solution.py:415
  125.3 9.7 %collective-permute-start.12 = (bf16[400,128]{1,0:T(8,128)(2,1)S(1)}, bf16[400,128]{1,0:T(8,128)(2,1)S(1)}, u32[]{:S(2)}, u32[]{:S(2)}) collective-permute-start(bf16[400,128]{1,0:T(8,128)(2,1)S(1)} %get-tuple-element.143), channel_id=1, source_target_pairs={{0,6},{1,7},{2,4},{3,5},{4,2},{5,3},{6,0},{7,1},{8,14},{9,15},{10,... | collective-permute-start | bytes 307208 | tf_op jit(solution)/shard_map/ppermute | solution.py:415
  127.6 7.5 %collective-permute-start.13 = (bf16[400,128]{1,0:T(8,128)(2,1)S(1)}, bf16[400,128]{1,0:T(8,128)(2,1)S(1)}, u32[]{:S(2)}, u32[]{:S(2)}) collective-permute-start(bf16[400,128]{1,0:T(8,128)(2,1)S(1)} %get-tuple-element.144), channel_id=1, source_target_pairs={{0,7},{1,6},{2,5},{3,4},{4,3},{5,2},{6,1},{7,0},{8,15},{9,14},{10,... | collective-permute-start | bytes 307208 | tf_op jit(solution)/shard_map/ppermute | solution.py:415
  136.6 18.2 %collective-permute-start.26 = (s16[408,128]{1,0:T(8,128)(2,1)S(1)}, s16[408,128]{1,0:T(8,128)(2,1)S(1)}, u32[]{:S(2)}, u32[]{:S(2)}) collective-permute-start(s16[408,128]{1,0:T(8,128)(2,1)S(1)} %get-tuple-element.176), channel_id=1, source_target_pairs={{0,31},{1,30},{2,29},{3,28},{4,27},{5,26},{6,25},{7,24},{8,23},{9,... | collective-permute-start | bytes 313352 | tf_op jit(solution)/shard_map/ppermute | solution.py:415
  138.8 15.9 %collective-permute-start.15 = (s16[408,128]{1,0:T(8,128)(2,1)S(1)}, s16[408,128]{1,0:T(8,128)(2,1)S(1)}, u32[]{:S(2)}, u32[]{:S(2)}) collective-permute-start(s16[408,128]{1,0:T(8,128)(2,1)S(1)} %get-tuple-element.155), channel_id=1, source_target_pairs={{0,28},{1,29},{2,30},{3,31},{4,24},{5,25},{6,26},{7,27},{8,20},{9,... | collective-permute-start | bytes 313352 | tf_op jit(solution)/shard_map/ppermute | solution.py:415
  141.0 15.9 %collective-permute-start.31 = (s16[408,128]{1,0:T(8,128)(2,1)S(1)}, s16[408,128]{1,0:T(8,128)(2,1)S(1)}, u32[]{:S(2)}, u32[]{:S(2)}) collective-permute-start(s16[408,128]{1,0:T(8,128)(2,1)S(1)} %get-tuple-element.186), channel_id=1, source_target_pairs={{0,30},{1,31},{2,28},{3,29},{4,26},{5,27},{6,24},{7,25},{8,22},{9,... | collective-permute-start | bytes 313352 | tf_op jit(solution)/shard_map/ppermute | solution.py:415
  144.0 16.2 %collective-permute-start.33 = (s16[408,128]{1,0:T(8,128)(2,1)S(1)}, s16[408,128]{1,0:T(8,128)(2,1)S(1)}, u32[]{:S(2)}, u32[]{:S(2)}) collective-permute-start(s16[408,128]{1,0:T(8,128)(2,1)S(1)} %get-tuple-element.191), channel_id=1, source_target_pairs={{0,29},{1,28},{2,31},{3,30},{4,25},{5,24},{6,27},{7,26},{8,21},{9,... | collective-permute-start | bytes 313352 | tf_op jit(solution)/shard_map/ppermute | solution.py:415
  153.3 8.5 %collective-permute-start.14 = (s16[408,128]{1,0:T(8,128)(2,1)S(1)}, s16[408,128]{1,0:T(8,128)(2,1)S(1)}, u32[]{:S(2)}, u32[]{:S(2)}) collective-permute-start(s16[408,128]{1,0:T(8,128)(2,1)S(1)} %get-tuple-element.146), channel_id=1, source_target_pairs={{0,27},{1,26},{2,25},{3,24},{4,31},{5,30},{6,29},{7,28},{8,19},{9,... | collective-permute-start | bytes 313352 | tf_op jit(solution)/shard_map/ppermute | solution.py:415
  154.8 10.2 %collective-permute-start.27 = (s16[408,128]{1,0:T(8,128)(2,1)S(1)}, s16[408,128]{1,0:T(8,128)(2,1)S(1)}, u32[]{:S(2)}, u32[]{:S(2)}) collective-permute-start(s16[408,128]{1,0:T(8,128)(2,1)S(1)} %get-tuple-element.177), channel_id=1, source_target_pairs={{0,15},{1,14},{2,13},{3,12},{4,11},{5,10},{6,9},{7,8},{8,7},{9,6},... | collective-permute-start | bytes 313352 | tf_op jit(solution)/shard_map/ppermute | solution.py:415
  154.8 17.7 %collective-permute-start.16 = (s16[408,128]{1,0:T(8,128)(2,1)S(1)}, s16[408,128]{1,0:T(8,128)(2,1)S(1)}, u32[]{:S(2)}, u32[]{:S(2)}) collective-permute-start(s16[408,128]{1,0:T(8,128)(2,1)S(1)} %get-tuple-element.156), channel_id=1, source_target_pairs={{0,25},{1,24},{2,27},{3,26},{4,29},{5,28},{6,31},{7,30},{8,17},{9,... | collective-permute-start | bytes 313352 | tf_op jit(solution)/shard_map/ppermute | solution.py:415
  156.9 16.6 %collective-permute-start.32 = (s16[408,128]{1,0:T(8,128)(2,1)S(1)}, s16[408,128]{1,0:T(8,128)(2,1)S(1)}, u32[]{:S(2)}, u32[]{:S(2)}) collective-permute-start(s16[408,128]{1,0:T(8,128)(2,1)S(1)} %get-tuple-element.187), channel_id=1, source_target_pairs={{0,26},{1,27},{2,24},{3,25},{4,30},{5,31},{6,28},{7,29},{8,18},{9,... | collective-permute-start | bytes 313352 | tf_op jit(solution)/shard_map/ppermute | solution.py:415
  160.1 13.4 %collective-permute-start.34 = (s16[408,128]{1,0:T(8,128)(2,1)S(1)}, s16[408,128]{1,0:T(8,128)(2,1)S(1)}, u32[]{:S(2)}, u32[]{:S(2)}) collective-permute-start(s16[408,128]{1,0:T(8,128)(2,1)S(1)} %get-tuple-element.192), channel_id=1, source_target_pairs={{0,14},{1,15},{2,12},{3,13},{4,10},{5,11},{6,8},{7,9},{8,6},{9,7},... | collective-permute-start | bytes 313352 | tf_op jit(solution)/shard_map/ppermute | solution.py:415
  161.8 17.3 %collective-permute-start.21 = (s16[408,128]{1,0:T(8,128)(2,1)S(1)}, s16[408,128]{1,0:T(8,128)(2,1)S(1)}, u32[]{:S(2)}, u32[]{:S(2)}) collective-permute-start(s16[408,128]{1,0:T(8,128)(2,1)S(1)} %get-tuple-element.165), channel_id=1, source_target_pairs={{0,13},{1,12},{2,15},{3,14},{4,9},{5,8},{6,11},{7,10},{8,5},{9,4},... | collective-permute-start | bytes 313352 | tf_op jit(solution)/shard_map/ppermute | solution.py:415
  164.9 16.1 %collective-permute-start.28 = (s16[408,128]{1,0:T(8,128)(2,1)S(1)}, s16[408,128]{1,0:T(8,128)(2,1)S(1)}, u32[]{:S(2)}, u32[]{:S(2)}) collective-permute-start(s16[408,128]{1,0:T(8,128)(2,1)S(1)} %get-tuple-element.178), channel_id=1, source_target_pairs={{0,24},{1,25},{2,26},{3,27},{4,28},{5,29},{6,30},{7,31},{8,16},{9,... | collective-permute-start | bytes 313352 | tf_op jit(solution)/shard_map/ppermute | solution.py:415
  172.5 13.0 %collective-permute-start.17 = (s16[408,128]{1,0:T(8,128)(2,1)S(1)}, s16[408,128]{1,0:T(8,128)(2,1)S(1)}, u32[]{:S(2)}, u32[]{:S(2)}) collective-permute-start(s16[408,128]{1,0:T(8,128)(2,1)S(1)} %get-tuple-element.157), channel_id=1, source_target_pairs={{0,11},{1,10},{2,9},{3,8},{4,15},{5,14},{6,13},{7,12},{8,3},{9,2},... | collective-permute-start | bytes 313352 | tf_op jit(solution)/shard_map/ppermute | solution.py:415
  173.5 13.2 %collective-permute-start.35 = (s16[408,128]{1,0:T(8,128)(2,1)S(1)}, s16[408,128]{1,0:T(8,128)(2,1)S(1)}, u32[]{:S(2)}, u32[]{:S(2)}) collective-permute-start(s16[408,128]{1,0:T(8,128)(2,1)S(1)} %get-tuple-element.198), channel_id=1, source_target_pairs={{0,12},{1,13},{2,14},{3,15},{4,8},{5,9},{6,10},{7,11},{8,4},{9,5},... | collective-permute-start | bytes 313352 | tf_op jit(solution)/shard_map/ppermute | solution.py:415
  173.6 14.8 %collective-permute-start.36 = (s16[408,128]{1,0:T(8,128)(2,1)S(1)}, s16[408,128]{1,0:T(8,128)(2,1)S(1)}, u32[]{:S(2)}, u32[]{:S(2)}) collective-permute-start(s16[408,128]{1,0:T(8,128)(2,1)S(1)} %get-tuple-element.201), channel_id=1, source_target_pairs={{0,23},{1,22},{2,21},{3,20},{4,19},{5,18},{6,17},{7,16},{8,31},{9,... | collective-permute-start | bytes 313352 | tf_op jit(solution)/shard_map/ppermute | solution.py:415
  179.0 11.3 %collective-permute-start.22 = (s16[408,128]{1,0:T(8,128)(2,1)S(1)}, s16[408,128]{1,0:T(8,128)(2,1)S(1)}, u32[]{:S(2)}, u32[]{:S(2)}) collective-permute-start(s16[408,128]{1,0:T(8,128)(2,1)S(1)} %get-tuple-element.166), channel_id=1, source_target_pairs={{0,22},{1,23},{2,20},{3,21},{4,18},{5,19},{6,16},{7,17},{8,30},{9,... | collective-permute-start | bytes 313352 | tf_op jit(solution)/shard_map/ppermute | solution.py:415
  181.0 10.2 %collective-permute-start.29 = (s16[408,128]{1,0:T(8,128)(2,1)S(1)}, s16[408,128]{1,0:T(8,128)(2,1)S(1)}, u32[]{:S(2)}, u32[]{:S(2)}) collective-permute-start(s16[408,128]{1,0:T(8,128)(2,1)S(1)} %get-tuple-element.179), channel_id=1, source_target_pairs={{0,10},{1,11},{2,8},{3,9},{4,14},{5,15},{6,12},{7,13},{8,2},{9,3},... | collective-permute-start | bytes 313352 | tf_op jit(solution)/shard_map/ppermute | solution.py:415
  185.5 12.7 %collective-permute-start.18 = (s16[408,128]{1,0:T(8,128)(2,1)S(1)}, s16[408,128]{1,0:T(8,128)(2,1)S(1)}, u32[]{:S(2)}, u32[]{:S(2)}) collective-permute-start(s16[408,128]{1,0:T(8,128)(2,1)S(1)} %get-tuple-element.158), channel_id=1, source_target_pairs={{0,20},{1,21},{2,22},{3,23},{4,16},{5,17},{6,18},{7,19},{8,28},{9,... | collective-permute-start | bytes 313352 | tf_op jit(solution)/shard_map/ppermute | solution.py:415
  186.7 14.7 %collective-permute-start.39 = (s16[408,128]{1,0:T(8,128)(2,1)S(1)}, s16[408,128]{1,0:T(8,128)(2,1)S(1)}, u32[]{:S(2)}, u32[]{:S(2)}) collective-permute-start(s16[408,128]{1,0:T(8,128)(2,1)S(1)} %get-tuple-element.213), channel_id=1, source_target_pairs={{0,21},{1,20},{2,23},{3,22},{4,17},{5,16},{6,19},{7,18},{8,29},{9,... | collective-permute-start | bytes 313352 | tf_op jit(solution)/shard_map/ppermute | solution.py:415
  188.3 13.1 %collective-permute-start.42 = (s16[408,128]{1,0:T(8,128)(2,1)S(1)}, s16[408,128]{1,0:T(8,128)(2,1)S(1)}, u32[]{:S(2)}, u32[]{:S(2)}) collective-permute-start(s16[408,128]{1,0:T(8,128)(2,1)S(1)} %get-tuple-element.221), channel_id=1, source_target_pairs={{0,9},{1,8},{2,11},{3,10},{4,13},{5,12},{6,15},{7,14},{8,1},{9,0},... | collective-permute-start | bytes 313352 | tf_op jit(solution)/shard_map/ppermute | solution.py:415
  190.4 11.5 %collective-permute-start.23 = (s16[408,128]{1,0:T(8,128)(2,1)S(1)}, s16[408,128]{1,0:T(8,128)(2,1)S(1)}, u32[]{:S(2)}, u32[]{:S(2)}) collective-permute-start(s16[408,128]{1,0:T(8,128)(2,1)S(1)} %get-tuple-element.167), channel_id=1, source_target_pairs={{0,8},{1,9},{2,10},{3,11},{4,12},{5,13},{6,14},{7,15},{8,0},{9,1},... | collective-permute-start | bytes 313352 | tf_op jit(solution)/shard_map/ppermute | solution.py:415
  191.2 12.3 %collective-permute-start.30 = (s16[408,128]{1,0:T(8,128)(2,1)S(1)}, s16[408,128]{1,0:T(8,128)(2,1)S(1)}, u32[]{:S(2)}, u32[]{:S(2)}) collective-permute-start(s16[408,128]{1,0:T(8,128)(2,1)S(1)} %get-tuple-element.180), channel_id=1, source_target_pairs={{0,19},{1,18},{2,17},{3,16},{4,23},{5,22},{6,21},{7,20},{8,27},{9,... | collective-permute-start | bytes 313352 | tf_op jit(solution)/shard_map/ppermute | solution.py:415
  198.3 11.0 %collective-permute-start.19 = (s16[408,128]{1,0:T(8,128)(2,1)S(1)}, s16[408,128]{1,0:T(8,128)(2,1)S(1)}, u32[]{:S(2)}, u32[]{:S(2)}) collective-permute-start(s16[408,128]{1,0:T(8,128)(2,1)S(1)} %get-tuple-element.159), channel_id=1, source_target_pairs={{0,6},{1,7},{2,4},{3,5},{4,2},{5,3},{6,0},{7,1},{8,14},{9,15},{10,... | collective-permute-start | bytes 313352 | tf_op jit(solution)/shard_map/ppermute | solution.py:415
  201.4 8.0 %collective-permute-start.40 = (s16[408,128]{1,0:T(8,128)(2,1)S(1)}, s16[408,128]{1,0:T(8,128)(2,1)S(1)}, u32[]{:S(2)}, u32[]{:S(2)}) collective-permute-start(s16[408,128]{1,0:T(8,128)(2,1)S(1)} %get-tuple-element.214), channel_id=1, source_target_pairs={{0,7},{1,6},{2,5},{3,4},{4,3},{5,2},{6,1},{7,0},{8,15},{9,14},{10,... | collective-permute-start | bytes 313352 | tf_op jit(solution)/shard_map/ppermute | solution.py:415
  201.4 13.3 %collective-permute-start.43 = (s16[408,128]{1,0:T(8,128)(2,1)S(1)}, s16[408,128]{1,0:T(8,128)(2,1)S(1)}, u32[]{:S(2)}, u32[]{:S(2)}) collective-permute-start(s16[408,128]{1,0:T(8,128)(2,1)S(1)} %get-tuple-element.222), channel_id=1, source_target_pairs={{0,18},{1,19},{2,16},{3,17},{4,22},{5,23},{6,20},{7,21},{8,26},{9,... | collective-permute-start | bytes 313352 | tf_op jit(solution)/shard_map/ppermute | solution.py:415
  201.9 13.7 %collective-permute-start.24 = (s16[408,128]{1,0:T(8,128)(2,1)S(1)}, s16[408,128]{1,0:T(8,128)(2,1)S(1)}, u32[]{:S(2)}, u32[]{:S(2)}) collective-permute-start(s16[408,128]{1,0:T(8,128)(2,1)S(1)} %get-tuple-element.168), channel_id=1, source_target_pairs={{0,17},{1,16},{2,19},{3,18},{4,21},{5,20},{6,23},{7,22},{8,25},{9,... | collective-permute-start | bytes 313352 | tf_op jit(solution)/shard_map/ppermute | solution.py:415
  203.5 14.5 %collective-permute-start.37 = (s16[408,128]{1,0:T(8,128)(2,1)S(1)}, s16[408,128]{1,0:T(8,128)(2,1)S(1)}, u32[]{:S(2)}, u32[]{:S(2)}) collective-permute-start(s16[408,128]{1,0:T(8,128)(2,1)S(1)} %get-tuple-element.208), channel_id=1, source_target_pairs={{0,5},{1,4},{2,7},{3,6},{4,1},{5,0},{6,3},{7,2},{8,13},{9,12},{10,... | collective-permute-start | bytes 313352 | tf_op jit(solution)/shard_map/ppermute | solution.py:415
  209.3 11.4 %collective-permute-start.20 = (s16[408,128]{1,0:T(8,128)(2,1)S(1)}, s16[408,128]{1,0:T(8,128)(2,1)S(1)}, u32[]{:S(2)}, u32[]{:S(2)}) collective-permute-start(s16[408,128]{1,0:T(8,128)(2,1)S(1)} %get-tuple-element.160), channel_id=1, source_target_pairs={{0,3},{1,2},{2,1},{3,0},{4,7},{5,6},{6,5},{7,4},{8,11},{9,10},{10,... | collective-permute-start | bytes 313352 | tf_op jit(solution)/shard_map/ppermute | solution.py:415
  209.4 9.6 %collective-permute-start.41 = (s16[408,128]{1,0:T(8,128)(2,1)S(1)}, s16[408,128]{1,0:T(8,128)(2,1)S(1)}, u32[]{:S(2)}, u32[]{:S(2)}) collective-permute-start(s16[408,128]{1,0:T(8,128)(2,1)S(1)} %get-tuple-element.215), channel_id=1, source_target_pairs={{0,16},{1,17},{2,18},{3,19},{4,20},{5,21},{6,22},{7,23},{8,24},{9,... | collective-permute-start | bytes 313352 | tf_op jit(solution)/shard_map/ppermute | solution.py:415
  214.7 4.9 %collective-permute-start.44 = (s16[408,128]{1,0:T(8,128)(2,1)S(1)}, s16[408,128]{1,0:T(8,128)(2,1)S(1)}, u32[]{:S(2)}, u32[]{:S(2)}) collective-permute-start(s16[408,128]{1,0:T(8,128)(2,1)S(1)} %get-tuple-element.228), channel_id=1, source_target_pairs={{0,4},{1,5},{2,6},{3,7},{4,0},{5,1},{6,2},{7,3},{8,12},{9,13},{10,... | collective-permute-start | bytes 313352 | tf_op jit(solution)/shard_map/ppermute | solution.py:415
  215.6 5.3 %collective-permute-start.25 = (s16[408,128]{1,0:T(8,128)(2,1)S(1)}, s16[408,128]{1,0:T(8,128)(2,1)S(1)}, u32[]{:S(2)}, u32[]{:S(2)}) collective-permute-start(s16[408,128]{1,0:T(8,128)(2,1)S(1)} %get-tuple-element.169), channel_id=1, source_target_pairs={{0,2},{1,3},{2,0},{3,1},{4,6},{5,7},{6,4},{7,5},{8,10},{9,11},{10,... | collective-permute-start | bytes 313352 | tf_op jit(solution)/shard_map/ppermute | solution.py:415
  218.0 2.9 %collective-permute-start.38 = (s16[408,128]{1,0:T(8,128)(2,1)S(1)}, s16[408,128]{1,0:T(8,128)(2,1)S(1)}, u32[]{:S(2)}, u32[]{:S(2)}) collective-permute-start(s16[408,128]{1,0:T(8,128)(2,1)S(1)} %get-tuple-element.209), channel_id=1, source_target_pairs={{0,1},{1,0},{2,3},{3,2},{4,5},{5,4},{6,7},{7,6},{8,9},{9,8},{10,11... | collective-permute-start | bytes 313352 | tf_op jit(solution)/shard_map/ppermute | solution.py:415
  219.0 1.9 copy-start
  219.0 1.9 copy-start.1

commit v14 on v9

--- a/solution.py
+++ b/solution.py
@@ -10,7 +10,7 @@
 BLK = 128
 TAIL = 8
 CUTS = (1, 2, 2, 2, 1)
-STEPS = (3, 6, 8)
+STEPS = (2, 6, 8)
 WINDOW = 5
 TILE = 256
 AXES = ("src", "dst")

time: 224 us -> 226 us (level)
  transfers between devices with their start and end apart: 47 -> 47, of which waited for: 15 -> 14; matrix products, arithmetic and copies ran while one was open for 13% -> 13% of each run, Pallas kernels for 16% -> 16%
where the time goes in v14:
time: 226 us
  waiting for transfers between devices  73.6 us (33%)
  starting transfers between devices  67.7 us (30%)
  Pallas kernels  51.7 us (23%)
  local copies, waits for them, and re-layouts  27.5 us (12%)
  other arithmetic  3.85 us (2%)
    ppermute x45, starting transfers between devices, swap(): return lax.ppermute(x, axis, [(i, i ^ shift) for i in range(count)])  56.8 us
    all_to_all x1, waiting for transfers between devices, per_device(): lax.all_to_all(outgoing, AXES, split_axis=0, concat_axis=0, tiled=True)  47.1 us
    ppermute x45, waiting for transfers between devices, swap(): return lax.ppermute(x, axis, [(i, i ^ shift) for i in range(count)])  21.6 us
    gather x2, local copies, waits for them, and re-layouts, per_device(): operator = relations[rel_ids].T  16.7 us
    pallas_call x3, Pallas kernels, scatter(): pl.pallas_call(functools.partial(scatter_kernel, first * BLK), out_shape=...  15.1 us
    pallas_call x5, Pallas kernels, pack(): pl.pallas_call(functools.partial(pack_kernel, first, tuple(bounds), len(g...  9.63 us
    unnamed x15, local copies, waits for them, and re-layouts  9.47 us
    pallas_call x1, Pallas kernels, gather_edges(): pl.pallas_call(edge_kernel, grid=(edges // tile,), out_shape=(jax.ShapeDt...  8.04 us
  transfers between devices with their start and end apart: 47, of which 14 were waited for; matrix products, arithmetic and copies ran while one was open for 13% of the time, Pallas kernels for 16%

profile of v14, /device:TPU:0, one launch (start us, length us, event | category | flops | bytes accessed | tf_op | source)
XLA Modules:
  0.0 225.7 jit_solution(8218741567021078553)
XLA Ops:
  0.6 1.3 copy.21
  2.0 7.3 %all-to-all-start = ((s32[32,1,1]{2,1,0:T(1,128)}), s32[32,1,1]{2,1,0:T(1,128)S(1)}, u32[]{:S(2)}, u32[]{:S(2)}) async-start(s32[32,1,1]{2,1,0:T(1,128)} %copy.21), calls=%async_computation | async-start | bytes 32768 | tf_op jit(solution)/shard_map/all_to_all | solution.py:372
  9.3 2.1 bitcast_bitcast_fusion.blocks_ref
  11.4 4.9 %all-to-all-done.asked_ref = s32[32,1,1]{2,1,0:T(1,128)S(1)} async-done(((s32[32,1,1]{2,1,0:T(1,128)}), s32[32,1,1]{2,1,0:T(1,128)S(1)}, u32[]{:S(2)}, u32[]{:S(2)}) %all-to-all-start) | async-done | bytes 160 | tf_op jit(solution)/shard_map/all_to_all | solution.py:372
  16.3 2.5 %select.19 = bf16[32,400,128]{2,1,0:T(8,128)(2,1)} custom-call(s32[32,1,1]{2,1,0:T(1,128)S(1)} %all-to-all-done.asked_ref, bf16[16,400,128]{2,1,0:T(8,128)(2,1)S(1)} %bitcast_bitcast_fusion.blocks_ref), custom_call_target="tpu_custom_call" | custom-call | tf_op jit(solution)/shard_map/select/pallas_call | solution.py:65
  18.9 3.6 %all-to-all-start.1 = ((bf16[32,400,128]{2,1,0:T(8,128)(2,1)}), bf16[32,400,128]{2,1,0:T(8,128)(2,1)}, u32[]{:S(2)}, u32[]{:S(2)}) async-start(bf16[32,400,128]{2,1,0:T(8,128)(2,1)} %select.19), calls=%async_computation.1 | async-start | bytes 6553600 | tf_op jit(solution)/shard_map/all_to_all | solution.py:378
  22.4 8.6 %copy.23 = f32[4096,400]{1,0:T(8,128)} copy(f32[4096,400]{0,1:T(8,128)} %param.11) | data formatting | bytes 13107200 | tf_op args[2]
  31.0 12.9 %gather_fusion = f32[2048,400]{1,0:T(8,128)} fusion(f32[4096,400]{1,0:T(8,128)} %copy.23, s32[2048]{0:T(1024)S(1)} %fusion.3), kind=kCustom, calls=%fused_computation | custom fusion | bytes 6561792 | tf_op jit(solution)/shard_map/gather | solution.py:379
  44.0 3.8 %copy.24 = f32[2048,400]{0,1:T(8,128)S(1)} copy(f32[2048,400]{1,0:T(8,128)} %gather_fusion) | data formatting | bytes 6553600 | tf_op jit(solution)/shard_map/gather | solution.py:379
  49.6 47.1 %all-to-all-done.1.fetched = bf16[32,400,128]{2,1,0:T(8,128)(2,1)} async-done(((bf16[32,400,128]{2,1,0:T(8,128)(2,1)}), bf16[32,400,128]{2,1,0:T(8,128)(2,1)}, u32[]{:S(2)}, u32[]{:S(2)}) %all-to-all-start.1) | async-done | bytes 3276832 | tf_op jit(solution)/shard_map/all_to_all | solution.py:378
  96.7 2.6 %gather_negs.1 = (bf16[400,128]{1,0:T(8,128)(2,1)S(1)}, bf16[400,2048]{1,0:T(8,128)(2,1)S(1)}) custom-call(s32[16]{0:T(128)S(1)} %select_reduce_fusion.7.live_ref, bf16[32,400,128]{2,1,0:T(8,128)(2,1)} %all-to-all-done.1.fetched, s32[1,128]{1,0:T(1,128)S(1)} %fusion.10.pos_ref.npos), custom_call_target="tpu_custom_call" | custom-call | tf_op jit(solution)/shard_map/gather_negs/pallas_call | solution.py:115
  99.5 1.3 collective-permute-start.1
  101.3 1.2 collective-permute-start.3
  103.0 2.1 collective-permute-start.5
  105.2 0.9 collective-permute-start.6
  106.1 8.0 %gather_edges.1 = (bf16[400,2048]{1,0:T(8,128)(2,1)S(1)}, bf16[400,2048]{1,0:T(8,128)(2,1)S(1)}, f32[1,2048]{1,0:T(1,128)S(1)}) custom-call(bf16[400,2048]{1,0:T(8,128)(2,1)S(1)} %get-tuple-element.128.rows, s32[1,2048]{1,0:T(1,128)S(1)} %bitcast.20, s32[1,2048]{1,0:T(1,128)S(1)} %bitcast.24, f32[400,2048]{1,0:T(8,128)S(1)} %bitcast.17), custom_call_target="tpu_custom_call" | custom-call | flops 104857600 | bytes 204800 | tf_op jit(solution)/shard_map/gather_edges/pallas_call | solution.py:144
  114.2 6.2 %score.1 = (bf16[2,400,2048]{2,1,0:T(8,128)(2,1)S(1)}, bf16[2,400,2048]{2,1,0:T(8,128)(2,1)S(1)}, bf16[400,128]{1,0:T(8,128)(2,1)S(1)}, bf16[400,128]{1,0:T(8,12...) custom-call(bf16[400,128]{1,0:T(8,128)(2,1)S(1)} %get-tuple-element., ...), custom_call_target="tpu_custom_call" | custom-call | flops 78643200 | bytes 153600 | tf_op jit(solution)/shard_map/score/pallas_call | solution.py:191
  120.5 1.4 collective-permute-start.7
  122.3 0.9 collective-permute-start.9
  123.8 1.5 collective-permute-start.11
  125.3 0.8 collective-permute-start.12
  126.1 1.4 collective-permute-done.8.refs_4_.refs_5_.refs_3_
  127.7 3.8 %scatter.3.refs_0_ = f32[400,512]{1,0:T(8,128)S(1)} custom-call(bf16[2,400,2048]{2,1,0:T(8,128)(2,1)S(1)} %get-tuple-element.135.gs_ref, bf16[2,400,2048]{2,1,0:T(8,128)(2,1)S(1)} %get-tuple-element.136.gd_ref, s32[1,2048]{1,0:T(1,128)S(1)} %bitcast.21, s32[1,2048]{1,0:T(1,128)S(1)} %bitcast.25), custom_call_target="tpu_custom_call" | custom-call | flops 26214400 | bytes 51200 | tf_op jit(solution)/shard_map/scatter/pallas_call | solution.py:228
  131.4 2.0 collective-permute-done.10.refs_6_.refs_7_.refs_5_
  133.4 1.7 collective-permute-done.11.refs_7_.refs_8_.refs_6_
  135.1 1.2 pack.9
  136.3 1.9 collective-permute-start.26
  138.2 2.3 %collective-permute-start.15 = (s16[408,128]{1,0:T(8,128)(2,1)S(1)}, s16[408,128]{1,0:T(8,128)(2,1)S(1)}, u32[]{:S(2)}, u32[]{:S(2)}) collective-permute-start(s16[408,128]{1,0:T(8,128)(2,1)S(1)} %get-tuple-element.155), channel_id=1, source_target_pairs={{0,28},{1,29},{2,30},{3,31},{4,24},{5,25},{6,26},{7,27},{8,20},{9,... | collective-permute-start | bytes 313352 | tf_op jit(solution)/shard_map/ppermute | solution.py:416
  140.5 3.6 %collective-permute-start.31 = (s16[408,128]{1,0:T(8,128)(2,1)S(1)}, s16[408,128]{1,0:T(8,128)(2,1)S(1)}, u32[]{:S(2)}, u32[]{:S(2)}) collective-permute-start(s16[408,128]{1,0:T(8,128)(2,1)S(1)} %get-tuple-element.186), channel_id=1, source_target_pairs={{0,30},{1,31},{2,28},{3,29},{4,26},{5,27},{6,24},{7,25},{8,22},{9,... | collective-permute-start | bytes 313352 | tf_op jit(solution)/shard_map/ppermute | solution.py:416
  144.1 1.8 collective-permute-start.33
  145.9 7.6 %scatter.4.refs_1_ = f32[400,1024]{1,0:T(8,128)S(1)} custom-call(bf16[2,400,2048]{2,1,0:T(8,128)(2,1)S(1)} %get-tuple-element.135.gs_ref, bf16[2,400,2048]{2,1,0:T(8,128)(2,1)S(1)} %get-tuple-element.136.gd_ref, s32[1,2048]{1,0:T(1,128)S(1)} %bitcast.22, s32[1,2048]{1,0:T(1,128)S(1)} %bitcast.26), custom_call_target="tpu_custom_call" | custom-call | flops 52428800 | bytes 102400 | tf_op jit(solution)/shard_map/scatter/pallas_call | solution.py:228
  153.5 2.7 %pack.5 = (s16[408,128]{1,0:T(8,128)(2,1)S(1)}, s16[408,128]{1,0:T(8,128)(2,1)S(1)}, s16[408,128]{1,0:T(8,128)(2,1)S(1)}, s16[408,128]{1,0:T(8,128)(2,1)S(1)}, s...) custom-call(s32[32]{0:T(128)S(1)} %select_reduce_fusion.5.rank_ref, ...), custom_call_target="tpu_custom_call" | custom-call | flops 3276800 | bytes 6400 | tf_op jit(solution)/shard_map/pack/pallas_call | solution.py:284
  156.2 2.0 collective-permute-start.14
  158.2 2.2 collective-permute-start.16
  160.4 2.0 collective-permute-start.32
  162.4 2.0 collective-permute-start.34
  165.1 2.1 collective-permute-done.27.refs_1_
  167.2 4.0 %collective-permute-start.28 = (s16[408,128]{1,0:T(8,128)(2,1)S(1)}, s16[408,128]{1,0:T(8,128)(2,1)S(1)}, u32[]{:S(2)}, u32[]{:S(2)}) collective-permute-start(s16[408,128]{1,0:T(8,128)(2,1)S(1)} %get-tuple-element.178), channel_id=1, source_target_pairs={{0,24},{1,25},{2,26},{3,27},{4,28},{5,29},{6,30},{7,31},{8,16},{9,... | collective-permute-start | bytes 313352 | tf_op jit(solution)/shard_map/ppermute | solution.py:416
  171.2 3.8 %scatter.5.refs_2_ = f32[400,512]{1,0:T(8,128)S(1)} custom-call(bf16[2,400,2048]{2,1,0:T(8,128)(2,1)S(1)} %get-tuple-element.135.gs_ref, bf16[2,400,2048]{2,1,0:T(8,128)(2,1)S(1)} %get-tuple-element.136.gd_ref, s32[1,2048]{1,0:T(1,128)S(1)} %bitcast.23, s32[1,2048]{1,0:T(1,128)S(1)} %bitcast.27), custom_call_target="tpu_custom_call" | custom-call | flops 26214400 | bytes 51200 | tf_op jit(solution)/shard_map/scatter/pallas_call | solution.py:228
  175.0 1.9 pack.8
  177.0 4.1 %collective-permute-start.35 = (s16[408,128]{1,0:T(8,128)(2,1)S(1)}, s16[408,128]{1,0:T(8,128)(2,1)S(1)}, u32[]{:S(2)}, u32[]{:S(2)}) collective-permute-start(s16[408,128]{1,0:T(8,128)(2,1)S(1)} %get-tuple-element.198), channel_id=1, source_target_pairs={{0,12},{1,13},{2,14},{3,15},{4,8},{5,9},{6,10},{7,11},{8,4},{9,5},... | collective-permute-start | bytes 313352 | tf_op jit(solution)/shard_map/ppermute | solution.py:416
  181.1 4.8 %collective-permute-start.22 = (s16[408,128]{1,0:T(8,128)(2,1)S(1)}, s16[408,128]{1,0:T(8,128)(2,1)S(1)}, u32[]{:S(2)}, u32[]{:S(2)}) collective-permute-start(s16[408,128]{1,0:T(8,128)(2,1)S(1)} %get-tuple-element.166), channel_id=1, source_target_pairs={{0,22},{1,23},{2,20},{3,21},{4,18},{5,19},{6,16},{7,17},{8,30},{9,... | collective-permute-start | bytes 313352 | tf_op jit(solution)/shard_map/ppermute | solution.py:416
  185.8 1.0 add.71.refs_8_
  186.8 2.2 pack.7
  189.6 2.8 %collective-permute-done.35.refs_7_ = s16[408,128]{1,0:T(8,128)(2,1)S(1)} collective-permute-done((s16[408,128]{1,0:T(8,128)(2,1)S(1)}, s16[408,128]{1,0:T(8,128)(2,1)S(1)}, u32[]{:S(2)}, u32[]{:S(2)}) %collective-permute-start.35) | collective-permute-done | bytes 104480 | tf_op jit(solution)/shard_map/ppermute | solution.py:416
  192.7 2.0 collective-permute-done.22.refs_2_
  194.8 1.0 add.72.refs_8_
  195.8 3.8 %collective-permute-done.18.refs_6_ = s16[408,128]{1,0:T(8,128)(2,1)S(1)} collective-permute-done((s16[408,128]{1,0:T(8,128)(2,1)S(1)}, s16[408,128]{1,0:T(8,128)(2,1)S(1)}, u32[]{:S(2)}, u32[]{:S(2)}) %collective-permute-start.18) | collective-permute-done | bytes 104480 | tf_op jit(solution)/shard_map/ppermute | solution.py:416
  199.6 1.1 collective-permute-start.19
  200.8 1.0 collective-permute-done.39.refs_4_
  201.8 1.3 collective-permute-start.40
  203.1 1.6 collective-permute-done.23.refs_7_
  204.7 1.8 collective-permute-start.24
  206.5 3.8 %collective-permute-start.37 = (s16[408,128]{1,0:T(8,128)(2,1)S(1)}, s16[408,128]{1,0:T(8,128)(2,1)S(1)}, u32[]{:S(2)}, u32[]{:S(2)}) collective-permute-start(s16[408,128]{1,0:T(8,128)(2,1)S(1)} %get-tuple-element.208), channel_id=1, source_target_pairs={{0,5},{1,4},{2,7},{3,6},{4,1},{5,0},{6,3},{7,2},{8,13},{9,12},{10,... | collective-permute-start | bytes 313352 | tf_op jit(solution)/shard_map/ppermute | solution.py:416
  210.3 1.6 pack.6
  212.3 2.0 collective-permute-done.43.refs_2_
  214.2 1.6 collective-permute-start.44
  215.8 0.9 collective-permute-start.25
  216.7 1.2 collective-permute-start.38
  217.9 1.0 add.73.refs_8_
  219.0 1.1 collective-permute-done.41.refs_6_
  220.1 1.0 add.74.refs_4_
  221.1 0.9 copy-done
  222.0 3.5 %update.1 = (f32[400,2048]{1,0:T(8,128)}, f32[1,2048]{1,0:T(1,128)}) custom-call(s32[32]{0:T(128)S(1)} %get-tuple-element.121.asked_ref, s16[408,128]{1,0:T(8,128)(2,1)S(1)} %collective-permute-done.20.refs_0_, s16[408,128]{1,0:T(8,128)(2,1)S(1)} %collective-permute-done.25.refs_1_, s16[408,128]{1,0:T(8,128)(2,1)S(1)} %collective-permute-done.38.refs_2_, ...), custom_call_target="tpu_custom_call" | custom-call | flops 819200 | bytes 1600 | tf_op jit(solution)/shard_map/update/pallas_call | solution.py:352
  (83 shorter events, 6.2 us)
Async XLA Ops:
  2.0 14.4 %all-to-all-start = ((s32[32,1,1]{2,1,0:T(1,128)}), s32[32,1,1]{2,1,0:T(1,128)S(1)}, u32[]{:S(2)}, u32[]{:S(2)}) async-start(s32[32,1,1]{2,1,0:T(1,128)} %copy.21), calls=%async_computation | async-start | bytes 32768 | tf_op jit(solution)/shard_map/all_to_all | solution.py:372
  18.9 77.9 %all-to-all-start.1 = ((bf16[32,400,128]{2,1,0:T(8,128)(2,1)}), bf16[32,400,128]{2,1,0:T(8,128)(2,1)}, u32[]{:S(2)}, u32[]{:S(2)}) async-start(bf16[32,400,128]{2,1,0:T(8,128)(2,1)} %select.19), calls=%async_computation.1 | async-start | bytes 6553600 | tf_op jit(solution)/shard_map/all_to_all | solution.py:378
  22.4 8.6 %copy-start.4 = (s32[2048]{0:T(1024)S(1)}, s32[2048]{0:T(1024)}, u32[]{:S(2)}) copy-start(s32[2048]{0:T(1024)} %param.12) | copy-start | bytes 24580
  44.0 3.8 %copy-start.2 = (s32[2048]{0:T(1024)S(1)}, s32[2048]{0:T(1024)}, u32[]{:S(2)}) copy-start(s32[2048]{0:T(1024)} %param.14) | copy-start | bytes 24580
  44.0 4.0 %copy-start.6 = (s32[32]{0:T(128)S(1)}, s32[32]{0:T(128)}, u32[]{:S(2)}) copy-start(s32[32]{0:T(128)} %constant.80.clone) | copy-start | bytes 388
  44.0 4.4 %copy-start.5 = (s32[128]{0:T(128)S(1)}, s32[128]{0:T(128)}, u32[]{:S(2)}) copy-start(s32[128]{0:T(128)} %param.16) | copy-start | bytes 1540
  44.0 4.4 %copy-start.3 = (s32[2048]{0:T(1024)S(1)}, s32[2048]{0:T(1024)}, u32[]{:S(2)}) copy-start(s32[2048]{0:T(1024)} %param.15) | copy-start | bytes 24580
  99.4 3.6 %collective-permute-start = (bf16[400,128]{1,0:T(8,128)(2,1)S(1)}, bf16[400,128]{1,0:T(8,128)(2,1)S(1)}, u32[]{:S(2)}, u32[]{:S(2)}) collective-permute-start(bf16[400,128]{1,0:T(8,128)(2,1)S(1)} %get-tuple-element.127.refs_0_), channel_id=1, source_target_pairs={{0,1},{1,0},{2,3},{3,2},{4,5},{5,4},{6,7},{7,6},{8,9},{9,8},{10,11... | collective-permute-start | bytes 307208 | tf_op jit(solution)/shard_map/ppermute | solution.py:416
  99.5 5.7 %collective-permute-start.1 = (bf16[400,128]{1,0:T(8,128)(2,1)S(1)}, bf16[400,128]{1,0:T(8,128)(2,1)S(1)}, u32[]{:S(2)}, u32[]{:S(2)}) collective-permute-start(bf16[400,128]{1,0:T(8,128)(2,1)S(1)} %get-tuple-element.127.refs_0_), channel_id=1, source_target_pairs={{0,2},{1,3},{2,0},{3,1},{4,6},{5,7},{6,4},{7,5},{8,10},{9,11},{10,... | collective-permute-start | bytes 307208 | tf_op jit(solution)/shard_map/ppermute | solution.py:416
  100.7 13.5 %collective-permute-start.2 = (bf16[400,128]{1,0:T(8,128)(2,1)S(1)}, bf16[400,128]{1,0:T(8,128)(2,1)S(1)}, u32[]{:S(2)}, u32[]{:S(2)}) collective-permute-start(bf16[400,128]{1,0:T(8,128)(2,1)S(1)} %get-tuple-element.127.refs_0_), channel_id=1, source_target_pairs={{0,3},{1,2},{2,1},{3,0},{4,7},{5,6},{6,5},{7,4},{8,11},{9,10},{10,... | collective-permute-start | bytes 307208 | tf_op jit(solution)/shard_map/ppermute | solution.py:416
  101.3 12.9 %collective-permute-start.3 = (bf16[400,128]{1,0:T(8,128)(2,1)S(1)}, bf16[400,128]{1,0:T(8,128)(2,1)S(1)}, u32[]{:S(2)}, u32[]{:S(2)}) collective-permute-start(bf16[400,128]{1,0:T(8,128)(2,1)S(1)} %get-tuple-element.127.refs_0_), channel_id=1, source_target_pairs={{0,4},{1,5},{2,6},{3,7},{4,0},{5,1},{6,2},{7,3},{8,12},{9,13},{10,... | collective-permute-start | bytes 307208 | tf_op jit(solution)/shard_map/ppermute | solution.py:416
  102.5 11.7 %collective-permute-start.4 = (bf16[400,128]{1,0:T(8,128)(2,1)S(1)}, bf16[400,128]{1,0:T(8,128)(2,1)S(1)}, u32[]{:S(2)}, u32[]{:S(2)}) collective-permute-start(bf16[400,128]{1,0:T(8,128)(2,1)S(1)} %get-tuple-element.127.refs_0_), channel_id=1, source_target_pairs={{0,5},{1,4},{2,7},{3,6},{4,1},{5,0},{6,3},{7,2},{8,13},{9,12},{10,... | collective-permute-start | bytes 307208 | tf_op jit(solution)/shard_map/ppermute | solution.py:416
  103.0 11.2 %collective-permute-start.5 = (bf16[400,128]{1,0:T(8,128)(2,1)S(1)}, bf16[400,128]{1,0:T(8,128)(2,1)S(1)}, u32[]{:S(2)}, u32[]{:S(2)}) collective-permute-start(bf16[400,128]{1,0:T(8,128)(2,1)S(1)} %get-tuple-element.127.refs_0_), channel_id=1, source_target_pairs={{0,6},{1,7},{2,4},{3,5},{4,2},{5,3},{6,0},{7,1},{8,14},{9,15},{10,... | collective-permute-start | bytes 307208 | tf_op jit(solution)/shard_map/ppermute | solution.py:416
  105.2 9.0 %collective-permute-start.6 = (bf16[400,128]{1,0:T(8,128)(2,1)S(1)}, bf16[400,128]{1,0:T(8,128)(2,1)S(1)}, u32[]{:S(2)}, u32[]{:S(2)}) collective-permute-start(bf16[400,128]{1,0:T(8,128)(2,1)S(1)} %get-tuple-element.127.refs_0_), channel_id=1, source_target_pairs={{0,7},{1,6},{2,5},{3,4},{4,3},{5,2},{6,1},{7,0},{8,15},{9,14},{10,... | collective-permute-start | bytes 307208 | tf_op jit(solution)/shard_map/ppermute | solution.py:416
  120.5 4.9 %collective-permute-start.7 = (bf16[400,128]{1,0:T(8,128)(2,1)S(1)}, bf16[400,128]{1,0:T(8,128)(2,1)S(1)}, u32[]{:S(2)}, u32[]{:S(2)}) collective-permute-start(bf16[400,128]{1,0:T(8,128)(2,1)S(1)} %get-tuple-element.138), channel_id=1, source_target_pairs={{0,1},{1,0},{2,3},{3,2},{4,5},{5,4},{6,7},{7,6},{8,9},{9,8},{10,11... | collective-permute-start | bytes 307208 | tf_op jit(solution)/shard_map/ppermute | solution.py:416
  121.8 5.7 %collective-permute-start.8 = (bf16[400,128]{1,0:T(8,128)(2,1)S(1)}, bf16[400,128]{1,0:T(8,128)(2,1)S(1)}, u32[]{:S(2)}, u32[]{:S(2)}) collective-permute-start(bf16[400,128]{1,0:T(8,128)(2,1)S(1)} %get-tuple-element.139), channel_id=1, source_target_pairs={{0,2},{1,3},{2,0},{3,1},{4,6},{5,7},{6,4},{7,5},{8,10},{9,11},{10,... | collective-permute-start | bytes 307208 | tf_op jit(solution)/shard_map/ppermute | solution.py:416
  122.3 9.1 %collective-permute-start.9 = (bf16[400,128]{1,0:T(8,128)(2,1)S(1)}, bf16[400,128]{1,0:T(8,128)(2,1)S(1)}, u32[]{:S(2)}, u32[]{:S(2)}) collective-permute-start(bf16[400,128]{1,0:T(8,128)(2,1)S(1)} %get-tuple-element.140), channel_id=1, source_target_pairs={{0,3},{1,2},{2,1},{3,0},{4,7},{5,6},{6,5},{7,4},{8,11},{9,10},{10,... | collective-permute-start | bytes 307208 | tf_op jit(solution)/shard_map/ppermute | solution.py:416
  123.3 10.1 %collective-permute-start.10 = (bf16[400,128]{1,0:T(8,128)(2,1)S(1)}, bf16[400,128]{1,0:T(8,128)(2,1)S(1)}, u32[]{:S(2)}, u32[]{:S(2)}) collective-permute-start(bf16[400,128]{1,0:T(8,128)(2,1)S(1)} %get-tuple-element.141), channel_id=1, source_target_pairs={{0,4},{1,5},{2,6},{3,7},{4,0},{5,1},{6,2},{7,3},{8,12},{9,13},{10,... | collective-permute-start | bytes 307208 | tf_op jit(solution)/shard_map/ppermute | solution.py:416
  123.8 11.3 %collective-permute-start.11 = (bf16[400,128]{1,0:T(8,128)(2,1)S(1)}, bf16[400,128]{1,0:T(8,128)(2,1)S(1)}, u32[]{:S(2)}, u32[]{:S(2)}) collective-permute-start(bf16[400,128]{1,0:T(8,128)(2,1)S(1)} %get-tuple-element.142), channel_id=1, source_target_pairs={{0,5},{1,4},{2,7},{3,6},{4,1},{5,0},{6,3},{7,2},{8,13},{9,12},{10,... | collective-permute-start | bytes 307208 | tf_op jit(solution)/shard_map/ppermute | solution.py:416
  125.3 9.7 %collective-permute-start.12 = (bf16[400,128]{1,0:T(8,128)(2,1)S(1)}, bf16[400,128]{1,0:T(8,128)(2,1)S(1)}, u32[]{:S(2)}, u32[]{:S(2)}) collective-permute-start(bf16[400,128]{1,0:T(8,128)(2,1)S(1)} %get-tuple-element.143), channel_id=1, source_target_pairs={{0,6},{1,7},{2,4},{3,5},{4,2},{5,3},{6,0},{7,1},{8,14},{9,15},{10,... | collective-permute-start | bytes 307208 | tf_op jit(solution)/shard_map/ppermute | solution.py:416
  127.6 7.5 %collective-permute-start.13 = (bf16[400,128]{1,0:T(8,128)(2,1)S(1)}, bf16[400,128]{1,0:T(8,128)(2,1)S(1)}, u32[]{:S(2)}, u32[]{:S(2)}) collective-permute-start(bf16[400,128]{1,0:T(8,128)(2,1)S(1)} %get-tuple-element.144), channel_id=1, source_target_pairs={{0,7},{1,6},{2,5},{3,4},{4,3},{5,2},{6,1},{7,0},{8,15},{9,14},{10,... | collective-permute-start | bytes 307208 | tf_op jit(solution)/shard_map/ppermute | solution.py:416
  136.3 21.9 %collective-permute-start.26 = (s16[408,128]{1,0:T(8,128)(2,1)S(1)}, s16[408,128]{1,0:T(8,128)(2,1)S(1)}, u32[]{:S(2)}, u32[]{:S(2)}) collective-permute-start(s16[408,128]{1,0:T(8,128)(2,1)S(1)} %get-tuple-element.176), channel_id=1, source_target_pairs={{0,31},{1,30},{2,29},{3,28},{4,27},{5,26},{6,25},{7,24},{8,23},{9,... | collective-permute-start | bytes 313352 | tf_op jit(solution)/shard_map/ppermute | solution.py:416
  138.2 20.0 %collective-permute-start.15 = (s16[408,128]{1,0:T(8,128)(2,1)S(1)}, s16[408,128]{1,0:T(8,128)(2,1)S(1)}, u32[]{:S(2)}, u32[]{:S(2)}) collective-permute-start(s16[408,128]{1,0:T(8,128)(2,1)S(1)} %get-tuple-element.155), channel_id=1, source_target_pairs={{0,28},{1,29},{2,30},{3,31},{4,24},{5,25},{6,26},{7,27},{8,20},{9,... | collective-permute-start | bytes 313352 | tf_op jit(solution)/shard_map/ppermute | solution.py:416
  140.5 19.9 %collective-permute-start.31 = (s16[408,128]{1,0:T(8,128)(2,1)S(1)}, s16[408,128]{1,0:T(8,128)(2,1)S(1)}, u32[]{:S(2)}, u32[]{:S(2)}) collective-permute-start(s16[408,128]{1,0:T(8,128)(2,1)S(1)} %get-tuple-element.186), channel_id=1, source_target_pairs={{0,30},{1,31},{2,28},{3,29},{4,26},{5,27},{6,24},{7,25},{8,22},{9,... | collective-permute-start | bytes 313352 | tf_op jit(solution)/shard_map/ppermute | solution.py:416
  144.1 18.3 %collective-permute-start.33 = (s16[408,128]{1,0:T(8,128)(2,1)S(1)}, s16[408,128]{1,0:T(8,128)(2,1)S(1)}, u32[]{:S(2)}, u32[]{:S(2)}) collective-permute-start(s16[408,128]{1,0:T(8,128)(2,1)S(1)} %get-tuple-element.191), channel_id=1, source_target_pairs={{0,29},{1,28},{2,31},{3,30},{4,25},{5,24},{6,27},{7,26},{8,21},{9,... | collective-permute-start | bytes 313352 | tf_op jit(solution)/shard_map/ppermute | solution.py:416
  156.2 8.2 %collective-permute-start.14 = (s16[408,128]{1,0:T(8,128)(2,1)S(1)}, s16[408,128]{1,0:T(8,128)(2,1)S(1)}, u32[]{:S(2)}, u32[]{:S(2)}) collective-permute-start(s16[408,128]{1,0:T(8,128)(2,1)S(1)} %get-tuple-element.146), channel_id=1, source_target_pairs={{0,27},{1,26},{2,25},{3,24},{4,31},{5,30},{6,29},{7,28},{8,19},{9,... | collective-permute-start | bytes 313352 | tf_op jit(solution)/shard_map/ppermute | solution.py:416
  158.2 9.0 %collective-permute-start.27 = (s16[408,128]{1,0:T(8,128)(2,1)S(1)}, s16[408,128]{1,0:T(8,128)(2,1)S(1)}, u32[]{:S(2)}, u32[]{:S(2)}) collective-permute-start(s16[408,128]{1,0:T(8,128)(2,1)S(1)} %get-tuple-element.177), channel_id=1, source_target_pairs={{0,15},{1,14},{2,13},{3,12},{4,11},{5,10},{6,9},{7,8},{8,7},{9,6},... | collective-permute-start | bytes 313352 | tf_op jit(solution)/shard_map/ppermute | solution.py:416
  158.2 18.6 %collective-permute-start.16 = (s16[408,128]{1,0:T(8,128)(2,1)S(1)}, s16[408,128]{1,0:T(8,128)(2,1)S(1)}, u32[]{:S(2)}, u32[]{:S(2)}) collective-permute-start(s16[408,128]{1,0:T(8,128)(2,1)S(1)} %get-tuple-element.156), channel_id=1, source_target_pairs={{0,25},{1,24},{2,27},{3,26},{4,29},{5,28},{6,31},{7,30},{8,17},{9,... | collective-permute-start | bytes 313352 | tf_op jit(solution)/shard_map/ppermute | solution.py:416
  160.4 16.6 %collective-permute-start.32 = (s16[408,128]{1,0:T(8,128)(2,1)S(1)}, s16[408,128]{1,0:T(8,128)(2,1)S(1)}, u32[]{:S(2)}, u32[]{:S(2)}) collective-permute-start(s16[408,128]{1,0:T(8,128)(2,1)S(1)} %get-tuple-element.187), channel_id=1, source_target_pairs={{0,26},{1,27},{2,24},{3,25},{4,30},{5,31},{6,28},{7,29},{8,18},{9,... | collective-permute-start | bytes 313352 | tf_op jit(solution)/shard_map/ppermute | solution.py:416
  162.4 18.7 %collective-permute-start.34 = (s16[408,128]{1,0:T(8,128)(2,1)S(1)}, s16[408,128]{1,0:T(8,128)(2,1)S(1)}, u32[]{:S(2)}, u32[]{:S(2)}) collective-permute-start(s16[408,128]{1,0:T(8,128)(2,1)S(1)} %get-tuple-element.192), channel_id=1, source_target_pairs={{0,14},{1,15},{2,12},{3,13},{4,10},{5,11},{6,8},{7,9},{8,6},{9,7},... | collective-permute-start | bytes 313352 | tf_op jit(solution)/shard_map/ppermute | solution.py:416
  164.4 16.7 %collective-permute-start.21 = (s16[408,128]{1,0:T(8,128)(2,1)S(1)}, s16[408,128]{1,0:T(8,128)(2,1)S(1)}, u32[]{:S(2)}, u32[]{:S(2)}) collective-permute-start(s16[408,128]{1,0:T(8,128)(2,1)S(1)} %get-tuple-element.165), channel_id=1, source_target_pairs={{0,13},{1,12},{2,15},{3,14},{4,9},{5,8},{6,11},{7,10},{8,5},{9,4},... | collective-permute-start | bytes 313352 | tf_op jit(solution)/shard_map/ppermute | solution.py:416
  167.2 18.6 %collective-permute-start.28 = (s16[408,128]{1,0:T(8,128)(2,1)S(1)}, s16[408,128]{1,0:T(8,128)(2,1)S(1)}, u32[]{:S(2)}, u32[]{:S(2)}) collective-permute-start(s16[408,128]{1,0:T(8,128)(2,1)S(1)} %get-tuple-element.178), channel_id=1, source_target_pairs={{0,24},{1,25},{2,26},{3,27},{4,28},{5,29},{6,30},{7,31},{8,16},{9,... | collective-permute-start | bytes 313352 | tf_op jit(solution)/shard_map/ppermute | solution.py:416
  176.9 12.2 %collective-permute-start.17 = (s16[408,128]{1,0:T(8,128)(2,1)S(1)}, s16[408,128]{1,0:T(8,128)(2,1)S(1)}, u32[]{:S(2)}, u32[]{:S(2)}) collective-permute-start(s16[408,128]{1,0:T(8,128)(2,1)S(1)} %get-tuple-element.157), channel_id=1, source_target_pairs={{0,11},{1,10},{2,9},{3,8},{4,15},{5,14},{6,13},{7,12},{8,3},{9,2},... | collective-permute-start | bytes 313352 | tf_op jit(solution)/shard_map/ppermute | solution.py:416
  177.0 15.5 %collective-permute-start.35 = (s16[408,128]{1,0:T(8,128)(2,1)S(1)}, s16[408,128]{1,0:T(8,128)(2,1)S(1)}, u32[]{:S(2)}, u32[]{:S(2)}) collective-permute-start(s16[408,128]{1,0:T(8,128)(2,1)S(1)} %get-tuple-element.198), channel_id=1, source_target_pairs={{0,12},{1,13},{2,14},{3,15},{4,8},{5,9},{6,10},{7,11},{8,4},{9,5},... | collective-permute-start | bytes 313352 | tf_op jit(solution)/shard_map/ppermute | solution.py:416
  181.1 11.7 %collective-permute-start.36 = (s16[408,128]{1,0:T(8,128)(2,1)S(1)}, s16[408,128]{1,0:T(8,128)(2,1)S(1)}, u32[]{:S(2)}, u32[]{:S(2)}) collective-permute-start(s16[408,128]{1,0:T(8,128)(2,1)S(1)} %get-tuple-element.201), channel_id=1, source_target_pairs={{0,23},{1,22},{2,21},{3,20},{4,19},{5,18},{6,17},{7,16},{8,31},{9,... | collective-permute-start | bytes 313352 | tf_op jit(solution)/shard_map/ppermute | solution.py:416
  181.1 13.7 %collective-permute-start.22 = (s16[408,128]{1,0:T(8,128)(2,1)S(1)}, s16[408,128]{1,0:T(8,128)(2,1)S(1)}, u32[]{:S(2)}, u32[]{:S(2)}) collective-permute-start(s16[408,128]{1,0:T(8,128)(2,1)S(1)} %get-tuple-element.166), channel_id=1, source_target_pairs={{0,22},{1,23},{2,20},{3,21},{4,18},{5,19},{6,16},{7,17},{8,30},{9,... | collective-permute-start | bytes 313352 | tf_op jit(solution)/shard_map/ppermute | solution.py:416
  185.8 8.9 %collective-permute-start.29 = (s16[408,128]{1,0:T(8,128)(2,1)S(1)}, s16[408,128]{1,0:T(8,128)(2,1)S(1)}, u32[]{:S(2)}, u32[]{:S(2)}) collective-permute-start(s16[408,128]{1,0:T(8,128)(2,1)S(1)} %get-tuple-element.179), channel_id=1, source_target_pairs={{0,10},{1,11},{2,8},{3,9},{4,14},{5,15},{6,12},{7,13},{8,2},{9,3},... | collective-permute-start | bytes 313352 | tf_op jit(solution)/shard_map/ppermute | solution.py:416
  189.0 10.6 %collective-permute-start.18 = (s16[408,128]{1,0:T(8,128)(2,1)S(1)}, s16[408,128]{1,0:T(8,128)(2,1)S(1)}, u32[]{:S(2)}, u32[]{:S(2)}) collective-permute-start(s16[408,128]{1,0:T(8,128)(2,1)S(1)} %get-tuple-element.158), channel_id=1, source_target_pairs={{0,20},{1,21},{2,22},{3,23},{4,16},{5,17},{6,18},{7,19},{8,28},{9,... | collective-permute-start | bytes 313352 | tf_op jit(solution)/shard_map/ppermute | solution.py:416
  192.4 9.3 %collective-permute-start.39 = (s16[408,128]{1,0:T(8,128)(2,1)S(1)}, s16[408,128]{1,0:T(8,128)(2,1)S(1)}, u32[]{:S(2)}, u32[]{:S(2)}) collective-permute-start(s16[408,128]{1,0:T(8,128)(2,1)S(1)} %get-tuple-element.213), channel_id=1, source_target_pairs={{0,21},{1,20},{2,23},{3,22},{4,17},{5,16},{6,19},{7,18},{8,29},{9,... | collective-permute-start | bytes 313352 | tf_op jit(solution)/shard_map/ppermute | solution.py:416
  192.7 10.4 %collective-permute-start.42 = (s16[408,128]{1,0:T(8,128)(2,1)S(1)}, s16[408,128]{1,0:T(8,128)(2,1)S(1)}, u32[]{:S(2)}, u32[]{:S(2)}) collective-permute-start(s16[408,128]{1,0:T(8,128)(2,1)S(1)} %get-tuple-element.221), channel_id=1, source_target_pairs={{0,9},{1,8},{2,11},{3,10},{4,13},{5,12},{6,15},{7,14},{8,1},{9,0},... | collective-permute-start | bytes 313352 | tf_op jit(solution)/shard_map/ppermute | solution.py:416
  194.8 9.9 %collective-permute-start.23 = (s16[408,128]{1,0:T(8,128)(2,1)S(1)}, s16[408,128]{1,0:T(8,128)(2,1)S(1)}, u32[]{:S(2)}, u32[]{:S(2)}) collective-permute-start(s16[408,128]{1,0:T(8,128)(2,1)S(1)} %get-tuple-element.167), channel_id=1, source_target_pairs={{0,8},{1,9},{2,10},{3,11},{4,12},{5,13},{6,14},{7,15},{8,0},{9,1},... | collective-permute-start | bytes 313352 | tf_op jit(solution)/shard_map/ppermute | solution.py:416
  194.8 11.7 %collective-permute-start.30 = (s16[408,128]{1,0:T(8,128)(2,1)S(1)}, s16[408,128]{1,0:T(8,128)(2,1)S(1)}, u32[]{:S(2)}, u32[]{:S(2)}) collective-permute-start(s16[408,128]{1,0:T(8,128)(2,1)S(1)} %get-tuple-element.180), channel_id=1, source_target_pairs={{0,19},{1,18},{2,17},{3,16},{4,23},{5,22},{6,21},{7,20},{8,27},{9,... | collective-permute-start | bytes 313352 | tf_op jit(solution)/shard_map/ppermute | solution.py:416
  199.6 12.3 %collective-permute-start.19 = (s16[408,128]{1,0:T(8,128)(2,1)S(1)}, s16[408,128]{1,0:T(8,128)(2,1)S(1)}, u32[]{:S(2)}, u32[]{:S(2)}) collective-permute-start(s16[408,128]{1,0:T(8,128)(2,1)S(1)} %get-tuple-element.159), channel_id=1, source_target_pairs={{0,6},{1,7},{2,4},{3,5},{4,2},{5,3},{6,0},{7,1},{8,14},{9,15},{10,... | collective-permute-start | bytes 313352 | tf_op jit(solution)/shard_map/ppermute | solution.py:416
  201.8 10.2 %collective-permute-start.40 = (s16[408,128]{1,0:T(8,128)(2,1)S(1)}, s16[408,128]{1,0:T(8,128)(2,1)S(1)}, u32[]{:S(2)}, u32[]{:S(2)}) collective-permute-start(s16[408,128]{1,0:T(8,128)(2,1)S(1)} %get-tuple-element.214), channel_id=1, source_target_pairs={{0,7},{1,6},{2,5},{3,4},{4,3},{5,2},{6,1},{7,0},{8,15},{9,14},{10,... | collective-permute-start | bytes 313352 | tf_op jit(solution)/shard_map/ppermute | solution.py:416
  203.1 11.1 %collective-permute-start.43 = (s16[408,128]{1,0:T(8,128)(2,1)S(1)}, s16[408,128]{1,0:T(8,128)(2,1)S(1)}, u32[]{:S(2)}, u32[]{:S(2)}) collective-permute-start(s16[408,128]{1,0:T(8,128)(2,1)S(1)} %get-tuple-element.222), channel_id=1, source_target_pairs={{0,18},{1,19},{2,16},{3,17},{4,22},{5,23},{6,20},{7,21},{8,26},{9,... | collective-permute-start | bytes 313352 | tf_op jit(solution)/shard_map/ppermute | solution.py:416
  204.7 11.1 %collective-permute-start.24 = (s16[408,128]{1,0:T(8,128)(2,1)S(1)}, s16[408,128]{1,0:T(8,128)(2,1)S(1)}, u32[]{:S(2)}, u32[]{:S(2)}) collective-permute-start(s16[408,128]{1,0:T(8,128)(2,1)S(1)} %get-tuple-element.168), channel_id=1, source_target_pairs={{0,17},{1,16},{2,19},{3,18},{4,21},{5,20},{6,23},{7,22},{8,25},{9,... | collective-permute-start | bytes 313352 | tf_op jit(solution)/shard_map/ppermute | solution.py:416
  206.5 10.2 %collective-permute-start.37 = (s16[408,128]{1,0:T(8,128)(2,1)S(1)}, s16[408,128]{1,0:T(8,128)(2,1)S(1)}, u32[]{:S(2)}, u32[]{:S(2)}) collective-permute-start(s16[408,128]{1,0:T(8,128)(2,1)S(1)} %get-tuple-element.208), channel_id=1, source_target_pairs={{0,5},{1,4},{2,7},{3,6},{4,1},{5,0},{6,3},{7,2},{8,13},{9,12},{10,... | collective-permute-start | bytes 313352 | tf_op jit(solution)/shard_map/ppermute | solution.py:416
  211.9 9.2 %collective-permute-start.20 = (s16[408,128]{1,0:T(8,128)(2,1)S(1)}, s16[408,128]{1,0:T(8,128)(2,1)S(1)}, u32[]{:S(2)}, u32[]{:S(2)}) collective-permute-start(s16[408,128]{1,0:T(8,128)(2,1)S(1)} %get-tuple-element.160), channel_id=1, source_target_pairs={{0,3},{1,2},{2,1},{3,0},{4,7},{5,6},{6,5},{7,4},{8,11},{9,10},{10,... | collective-permute-start | bytes 313352 | tf_op jit(solution)/shard_map/ppermute | solution.py:416
  212.0 8.0 %collective-permute-start.41 = (s16[408,128]{1,0:T(8,128)(2,1)S(1)}, s16[408,128]{1,0:T(8,128)(2,1)S(1)}, u32[]{:S(2)}, u32[]{:S(2)}) collective-permute-start(s16[408,128]{1,0:T(8,128)(2,1)S(1)} %get-tuple-element.215), channel_id=1, source_target_pairs={{0,16},{1,17},{2,18},{3,19},{4,20},{5,21},{6,22},{7,23},{8,24},{9,... | collective-permute-start | bytes 313352 | tf_op jit(solution)/shard_map/ppermute | solution.py:416
  214.2 5.9 %collective-permute-start.44 = (s16[408,128]{1,0:T(8,128)(2,1)S(1)}, s16[408,128]{1,0:T(8,128)(2,1)S(1)}, u32[]{:S(2)}, u32[]{:S(2)}) collective-permute-start(s16[408,128]{1,0:T(8,128)(2,1)S(1)} %get-tuple-element.228), channel_id=1, source_target_pairs={{0,4},{1,5},{2,6},{3,7},{4,0},{5,1},{6,2},{7,3},{8,12},{9,13},{10,... | collective-permute-start | bytes 313352 | tf_op jit(solution)/shard_map/ppermute | solution.py:416
  215.8 5.3 %collective-permute-start.25 = (s16[408,128]{1,0:T(8,128)(2,1)S(1)}, s16[408,128]{1,0:T(8,128)(2,1)S(1)}, u32[]{:S(2)}, u32[]{:S(2)}) collective-permute-start(s16[408,128]{1,0:T(8,128)(2,1)S(1)} %get-tuple-element.169), channel_id=1, source_target_pairs={{0,2},{1,3},{2,0},{3,1},{4,6},{5,7},{6,4},{7,5},{8,10},{9,11},{10,... | collective-permute-start | bytes 313352 | tf_op jit(solution)/shard_map/ppermute | solution.py:416
  216.7 4.4 %collective-permute-start.38 = (s16[408,128]{1,0:T(8,128)(2,1)S(1)}, s16[408,128]{1,0:T(8,128)(2,1)S(1)}, u32[]{:S(2)}, u32[]{:S(2)}) collective-permute-start(s16[408,128]{1,0:T(8,128)(2,1)S(1)} %get-tuple-element.209), channel_id=1, source_target_pairs={{0,1},{1,0},{2,3},{3,2},{4,5},{5,4},{6,7},{7,6},{8,9},{9,8},{10,11... | collective-permute-start | bytes 313352 | tf_op jit(solution)/shard_map/ppermute | solution.py:416
  220.1 1.9 copy-start
  220.1 1.9 copy-start.1
